TPU v7x, 256 devices: a whole 4x4x8 slice. The times are simulated.
256 devices in a mesh: sub: 4 (over y), row: 4 (over x_lo, core), col: 16 (over z, x_hi).
Axes of the slice: x: 4 (x_hi: 2, x_lo: 2; x = x_hi * 2 + x_lo), y: 4, z: 8, core: 2. Of those that a mesh axis runs over, the one named last changes fastest.
Arguments:
- pressure_rhs: float32 [3, 4, 4096, 128], P(None, 'sub', 'col'), may hold values from -6 to 6
- diag_inverse: float32 [4, 4096, 7, 4096], P('sub', 'row', None, 'col'), as said below
- factor_blocks: float32 [3, 4, 2048, 4096], P(None, 'sub', 'col', 'row'), may hold values from -0.09375 to 0.09375
- row_lists: int32 [3, 4, 2048], P(None, 'sub', 'col'), may hold values from 0 to 16383, as said below
Outputs:
- solution: float32 [3, 4, 4096, 128], P(None, 'sub', 'col')
Inputs may be any that keep to these rules, and one draw needn't show every extreme that they name: `diag_inverse`: in slot 2^l - 1 + q the block of row panel s is zero where q > s mod 2^l, and lower triangular with diagonal entries between 0.5 and 2 where q = s mod 2^l. row_lists[t, s, k] = q * 4096 + 2 k + e with e 0 or 1 and q below 2^m, m the upper level of pair t; entry 0 of every list is 0 and entry 2047 is 2^m * 4096 - 1.
All inputs are finite; a program needn't handle non-finite values.
Results may differ from a plain program's by a relative error of at most 0.00012.
Values sent between devices are 32-bit elements; how exact they have to be, the bound alone decides.
No kernel may reach another device: no remote copies, remote signals or barrier semaphores. Data moves between devices by JAX's collectives and lax.ppermute only.
A program may use at most 64 MiB of HBM per device.

v0:
```python
import jax
import jax.numpy as jnp
from jax import lax
from jax.sharding import PartitionSpec as P

S = 4096
NRHS = 128


exact_mode = lax.Precision.HIGHEST


def swapped(value, axis, bit):
    mask = 2**bit
    pairs = [(source, source ^ mask) for source in range(lax.axis_size(axis))]
    return lax.ppermute(value, axis, pairs)


def pair_slot(low_level, high_level, level_count):
    return (
        low_level * (level_count - 1)
        - low_level * (low_level - 1) // 2
        + high_level
        - low_level
        - 1
    )


def local_rows(row_lists, slot_index, col_block):
    targets = row_lists[slot_index, 0]
    panel_of = targets // S
    offset_in = targets % S - lax.axis_index("col") * col_block
    return panel_of * col_block + offset_in


def pick_half(stacked, which):
    return lax.dynamic_index_in_dim(stacked, which, 0, keepdims=False)


def fold_halves(values, level_num):
    sub_place = lax.axis_index("sub")
    for bit_index in reversed(range(level_num)):
        own_bit = sub_place >> bit_index & 1
        halves = values.reshape((2, values.shape[0] // 2) + values.shape[1:])
        keeper = pick_half(halves, own_bit)
        giving = pick_half(halves, 1 - own_bit)
        values = keeper + swapped(giving, "sub", bit_index)
    return values


def spread_panels(values, level_num):
    sub_place = lax.axis_index("sub")
    for bit_index in range(level_num):
        own_bit = sub_place >> bit_index & 1
        partner = swapped(values, "sub", bit_index)
        values = jnp.where(
            own_bit == 0,
            jnp.concatenate([values, partner], 0),
            jnp.concatenate([partner, values], 0),
        )
    return values


def separator_sum(values, level_num, own_rhs):
    own_part = fold_halves(values, level_num)[0]
    own_part = lax.psum(own_part, "row")
    if own_rhs is not None:
        own_part = own_rhs - own_part
    return spread_panels(own_part[None], level_num)


def on_device(pressure_rhs, diag_inverse, factor_blocks, row_lists):
    level_count = pressure_rhs.shape[0]
    col_block = pressure_rhs.shape[2]
    row_block = diag_inverse.shape[1]
    pending = {}
    for high_level in range(1, level_count):
        pending[high_level] = jnp.zeros((2**high_level * col_block, NRHS), jnp.float32)
    solved = []
    for level_num in range(level_count):
        span_size = 2**level_num
        own_rhs = pressure_rhs[level_num, 0]
        if level_num == 0:
            gathered = own_rhs[None]
        else:
            gathered = separator_sum(
                pending[level_num].reshape(span_size, col_block, NRHS), level_num, own_rhs
            )
        diag_blocks = diag_inverse[0, :, span_size - 1 : 2 * span_size - 1, :]
        column_part = jnp.einsum("ias,asn->in", diag_blocks, gathered, precision=exact_mode)
        solved_panel = lax.psum(column_part, "col")
        solved.append(solved_panel)
        for high_level in range(level_num + 1, level_count):
            slot_index = pair_slot(level_num, high_level, level_count)
            update_rows = jnp.dot(factor_blocks[slot_index, 0], solved_panel, precision=exact_mode)
            where_to = local_rows(row_lists, slot_index, col_block)
            pending[high_level] = pending[high_level].at[where_to].add(update_rows)
    finished = [None] * level_count
    for level_num in reversed(range(level_count)):
        span_size = 2**level_num
        residue = solved[level_num]
        if level_num < level_count - 1:
            correction = jnp.zeros((row_block, NRHS), jnp.float32)
            for high_level in range(level_num + 1, level_count):
                slot_index = pair_slot(level_num, high_level, level_count)
                where_from = local_rows(row_lists, slot_index, col_block)
                picked = finished[high_level].reshape(-1, NRHS)[where_from]
                correction = correction + jnp.einsum(
                    "ks,kn->sn", factor_blocks[slot_index, 0], picked, precision=exact_mode
                )
            residue = residue - lax.psum(correction, "col")
        diag_blocks = diag_inverse[0, :, span_size - 1 : 2 * span_size - 1, :]
        pieces = jnp.einsum("ias,in->asn", diag_blocks, residue, precision=exact_mode)
        finished[level_num] = separator_sum(pieces, level_num, None)
    sub_place = lax.axis_index("sub")
    outputs = []
    for level_num in range(level_count):
        outputs.append(
            lax.dynamic_index_in_dim(
                finished[level_num], sub_place % 2**level_num, 0, keepdims=False
            )
        )
    return jnp.stack(outputs)[:, None]


def solution(mesh):
    in_specs = (
        P(None, "sub", "col", None),
        P("sub", "row", None, "col"),
        P(None, "sub", "col", "row"),
        P(None, "sub", "col"),
    )
    out_specs = P(None, "sub", "col", None)
    return jax.shard_map(
        on_device, mesh=mesh, in_specs=in_specs, out_specs=out_specs, check_vma=False
    )
```

profile of v0, /device:TPU:1, one launch (start us, length us, event | category | flops | bytes accessed | tf_op | source)
XLA Modules:
  0.0 1141.2 jit_solution(4845397803051537167)
XLA Ops:
  6.5 3.1 fusion.20
  9.7 0.8 fusion.68
  10.5 151.3 %all-reduce.11.cloned.1.call-done = f32[1024,128]{1,0:T(8,128)} async-done(((f32[1024,128]{1,0:T(8,128)}), f32[1024,128]{1,0:T(8,128)}) %all-reduce.11.cloned.1.call-update) | async-done | bytes 524304 | tf_op jit(solution)/shard_map/psum | solution.py:91
  161.8 2.2 convolution_bitcast_fusion.4
  164.2 1.1 scatter_custom_fusion
  165.4 1.3 collective-permute-start
  166.8 2.9 collective-permute-done
  169.7 0.7 fusion.55
  170.6 51.3 %all-reduce.13.cloned.1.call-done = f32[256,128]{0,1:T(8,128)} async-done(((f32[256,128]{0,1:T(8,128)}), f32[256,128]{0,1:T(8,128)}) %all-reduce.13.cloned.1.call-update) | async-done | bytes 131088 | tf_op jit(solution)/shard_map/psum | solution.py:66
  221.9 0.9 fusion.56
  222.8 1.3 collective-permute-start.1
  224.1 3.7 collective-permute-done.1
  227.8 4.7 fusion.12
  232.6 1.0 convolution_bitcast_fusion.3
  233.7 1.1 scatter_custom_fusion.1
  234.9 147.3 %all-reduce.15.cloned.1.call-done = f32[1024,128]{0,1:T(8,128)} async-done(((f32[1024,128]{0,1:T(8,128)}), f32[1024,128]{0,1:T(8,128)}) %all-reduce.15.cloned.1.call-update) | async-done | bytes 524304 | tf_op jit(solution)/shard_map/psum | solution.py:91
  382.2 1.6 convolution_bitcast_fusion.2
  383.9 1.5 scatter_fusion
  385.6 2.8 collective-permute-start.2
  388.5 4.2 collective-permute-done.2
  392.8 1.3 collective-permute-start.3
  394.1 2.6 collective-permute-done.3
  396.7 0.7 add_bitcast_fusion
  397.6 52.5 %all-reduce.17.cloned.1.call-done = f32[256,128]{0,1:T(8,128)} async-done(((f32[256,128]{0,1:T(8,128)}), f32[256,128]{0,1:T(8,128)}) %all-reduce.17.cloned.1.call-update) | async-done | bytes 131088 | tf_op jit(solution)/shard_map/psum | solution.py:66
  450.1 0.9 fusion.54
  451.0 1.3 collective-permute-start.4
  452.3 3.7 collective-permute-done.4
  456.0 3.0 collective-permute-start.5
  459.0 5.7 collective-permute-done.5
  464.7 7.4 fusion.15
  472.1 150.5 %all-reduce.19.cloned.1.call-done = f32[1024,128]{0,1:T(8,128)} async-done(((f32[1024,128]{0,1:T(8,128)}), f32[1024,128]{0,1:T(8,128)}) %all-reduce.19.cloned.1.call-update) | async-done | bytes 524304 | tf_op jit(solution)/shard_map/psum | solution.py:91
  622.6 4.8 fusion
  627.4 2.8 collective-permute-start.6
  630.2 4.0 collective-permute-done.6
  634.3 1.3 collective-permute-start.7
  635.6 2.6 collective-permute-done.7
  638.2 0.7 dynamic-slice_add_fusion
  638.9 53.0 %all-reduce.21.cloned.1.call-done = f32[1,256,128]{1,2,0:T(8,128)} async-done(((f32[1,256,128]{1,2,0:T(8,128)}), f32[1,256,128]{1,2,0:T(8,128)}) %all-reduce.21.cloned.1.call-update) | async-done | bytes 131088 | tf_op jit(solution)/shard_map/psum | solution.py:66
  691.9 1.2 collective-permute-start.8
  693.1 3.9 collective-permute-done.8
  697.1 1.0 maximum_select_fusion.6
  698.1 2.8 collective-permute-start.9
  700.9 5.6 collective-permute-done.9
  706.6 0.2 copy.24
  706.8 0.7 gather_fusion
  707.4 1.4 convolution_bitcast_fusion
  709.0 150.5 %all-reduce.23.cloned.1.call-done = f32[1024,128]{0,1:T(8,128)} async-done(((f32[1024,128]{0,1:T(8,128)}), f32[1024,128]{0,1:T(8,128)}) %all-reduce.23.cloned.1.call-update) | async-done | bytes 524304 | tf_op jit(solution)/shard_map/psum | solution.py:111
  859.4 3.2 fusion.6
  862.7 1.3 collective-permute-start.10
  864.0 3.0 collective-permute-done.10
  867.0 0.7 bitcast_add_fusion.2
  867.7 51.4 %all-reduce.25.cloned.1.call-done = f32[1,256,128]{1,2,0:T(8,128)} async-done(((f32[1,256,128]{1,2,0:T(8,128)}), f32[1,256,128]{1,2,0:T(8,128)}) %all-reduce.25.cloned.1.call-update) | async-done | bytes 131088 | tf_op jit(solution)/shard_map/psum | solution.py:66
  919.2 1.2 collective-permute-start.11
  920.4 0.6 gather_fusion.2
  921.0 3.3 collective-permute-done.11
  924.3 1.0 maximum_select_fusion.7
  925.4 0.7 gather_fusion.1
  926.1 1.0 fusion.35
  927.1 1.8 fusion.18
  929.0 149.6 %all-reduce.27.cloned.1.call-done = f32[1024,128]{1,0:T(8,128)} async-done(((f32[1024,128]{1,0:T(8,128)}), f32[1024,128]{1,0:T(8,128)}) %all-reduce.27.cloned.1.call-update) | async-done | bytes 524304 | tf_op jit(solution)/shard_map/psum | solution.py:111
  1078.6 3.1 convolution_bitcast_fusion.1
  1081.8 50.7 %all-reduce.29.cloned.1.call-done = f32[1,256,128]{1,2,0:T(8,128)} async-done(((f32[1,256,128]{1,2,0:T(8,128)}), f32[1,256,128]{1,2,0:T(8,128)}) %all-reduce.29.cloned.1.call-update) | async-done | bytes 131088 | tf_op jit(solution)/shard_map/psum | solution.py:66
  1132.5 0.9 maximum_bitcast_fusion
  1133.4 0.9 copy.26
  (51 shorter events, 1.9 us)
Async XLA Ops:
  6.5 163.9 %copy-start.2 = (f32[3,1,256,128]{3,2,1,0:T(8,128)S(1)}, f32[3,1,256,128]{3,2,1,0:T(8,128)}, u32[]{:S(2)}) copy-start(f32[3,1,256,128]{3,2,1,0:T(8,128)} %param.4) | copy-start | bytes 1179652
  6.5 155.3 %all-reduce.11.cloned.1.call-start = ((), (), s32[]{:S(2)}) async-start(), calls=%async_computation | async-start | bytes 1048576 | tf_op jit(solution)/shard_map/psum | solution.py:91
  9.6 223.0 %copy-start = (f32[3,1,128,1024]{3,2,1,0:T(8,128)S(1)}, f32[3,1,128,1024]{3,2,1,0:T(8,128)}, u32[]{:S(2)}) copy-start(f32[3,1,128,1024]{3,2,1,0:T(8,128)} %param.6) | copy-start | bytes 4718596
  9.6 212.3 %all-reduce.13.cloned.1.call-start = ((), (), s32[]{:S(2)}) async-start(), calls=%async_computation.1 | async-start | bytes 262144 | tf_op jit(solution)/shard_map/psum | solution.py:66
  161.8 70.8 %copy-start.1 = (f32[1024,128]{1,0:T(8,128)S(1)}, f32[1024,128]{1,0:T(8,128)}, u32[]{:S(2)}) copy-start(f32[1024,128]{1,0:T(8,128)} %all-reduce.11.cloned.1.call-done) | copy-start | bytes 1572868
  165.4 4.3 collective-permute-start
  170.4 211.8 %all-reduce.15.cloned.1.call-start = ((), (), s32[]{:S(2)}) async-start(), calls=%async_computation.2 | async-start | bytes 1048576 | tf_op jit(solution)/shard_map/psum | solution.py:91
  222.8 5.0 collective-permute-start.1
  232.5 217.5 %all-reduce.17.cloned.1.call-start = ((), (), s32[]{:S(2)}) async-start(), calls=%async_computation.3 | async-start | bytes 262144 | tf_op jit(solution)/shard_map/psum | solution.py:66
  385.6 7.2 collective-permute-start.2
  392.8 3.9 collective-permute-start.3
  397.4 225.2 %all-reduce.19.cloned.1.call-start = ((), (), s32[]{:S(2)}) async-start(), calls=%async_computation.4 | async-start | bytes 1048576 | tf_op jit(solution)/shard_map/psum | solution.py:91
  451.0 5.0 collective-permute-start.4
  456.0 8.7 collective-permute-start.5
  472.1 219.8 %all-reduce.21.cloned.1.call-start = ((), (), s32[]{:S(2)}) async-start(), calls=%async_computation.5 | async-start | bytes 262144 | tf_op jit(solution)/shard_map/psum | solution.py:66
  627.4 6.8 collective-permute-start.6
  634.3 3.9 collective-permute-start.7
  638.9 220.5 %all-reduce.23.cloned.1.call-start = ((), (), s32[]{:S(2)}) async-start(), calls=%async_computation.6 | async-start | bytes 1048576 | tf_op jit(solution)/shard_map/psum | solution.py:111
  691.9 5.1 collective-permute-start.8
  698.1 8.5 collective-permute-start.9
  708.9 210.3 %all-reduce.25.cloned.1.call-start = ((), (), s32[]{:S(2)}) async-start(), calls=%async_computation.7 | async-start | bytes 262144 | tf_op jit(solution)/shard_map/psum | solution.py:66
  862.7 4.3 collective-permute-start.10
  867.7 210.9 %all-reduce.27.cloned.1.call-start = ((), (), s32[]{:S(2)}) async-start(), calls=%async_computation.8 | async-start | bytes 1048576 | tf_op jit(solution)/shard_map/psum | solution.py:111
  919.2 5.1 collective-permute-start.11
  928.9 203.6 %all-reduce.29.cloned.1.call-start = ((), (), s32[]{:S(2)}) async-start(), calls=%async_computation.9 | async-start | bytes 262144 | tf_op jit(solution)/shard_map/psum | solution.py:66
Sparse Core Ops, SparseCore 0:
  9.9 151.8 all-reduce.10
  170.5 51.3 all-reduce.12
  232.7 149.4 all-reduce.14
  397.6 52.4 all-reduce.16
  472.2 150.3 all-reduce.18
  639.0 52.8 all-reduce.20
  709.0 150.3 all-reduce.22
  867.8 51.3 all-reduce.24
  929.0 149.5 all-reduce.26
  1081.8 50.5 all-reduce.28
where the time goes:
time: 1140 us
  waiting for transfers between devices  1050 us (92%)
  matrix products  35.2 us (3%)
  starting transfers between devices  22 us (2%)
  between operations  13.9 us (1%)
  other arithmetic  12.1 us (1%)
    psum x3, waiting for transfers between devices, on_device(): solved_panel = lax.psum(column_part, 'col')  449 us
    psum x2, waiting for transfers between devices, on_device(): residue = residue - lax.psum(correction, 'col')  300 us
    psum x5, waiting for transfers between devices, separator_sum(): own_part = lax.psum(own_part, 'row')  259 us
    ppermute x12, waiting for transfers between devices, swapped(): return lax.ppermute(value, axis, pairs)  45.3 us
  transfers between devices with their start and end apart: 22, of which 22 were waited for; matrix products, arithmetic and copies ran while one was open for 0% of the time, Pallas kernels for 0%

commit v1 on v0

v1 whole, which is shorter than its diff:
```python
import jax
import jax.numpy as jnp
from jax import lax
from jax.sharding import PartitionSpec as P

S = 4096
NRHS = 128
mode = lax.Precision.HIGH


def swapped(value, axis, mask):
    pairs = [(source, source ^ mask) for source in range(lax.axis_size(axis))]
    return lax.ppermute(value, axis, pairs)


def col_sum(part):
    cols = lax.axis_size("col")
    blocks = part.reshape(cols, -1, NRHS)
    own = lax.all_to_all(blocks, "col", 0, 0).sum(0)
    full = lax.all_to_all(jnp.broadcast_to(own, blocks.shape), "col", 0, 0)
    return full.reshape(part.shape)


def row_sum(part):
    part = part + swapped(part, "row", 1)
    return part + swapped(part, "row", 2)


def spread(update, lists, panels):
    keep = (lists // S == jnp.arange(panels)[:, None])[:, :, None] & (
        (lists % 2)[:, None] == jnp.arange(2)
    )
    placed = jnp.where(keep[..., None], update[None, :, None, :], 0.0)
    return placed.reshape(panels, -1, NRHS)


def pick(values, lists):
    panels = values.shape[0]
    keep = (lists // S == jnp.arange(panels)[:, None])[:, :, None] & (
        (lists % 2)[:, None] == jnp.arange(2)
    )
    parts = values.reshape(panels, -1, 2, NRHS)
    return jnp.where(keep[..., None], parts, 0.0).sum((0, 2))


def on_device(pressure_rhs, diag_inverse, factor_blocks, row_lists):
    sub = lax.axis_index("sub")
    rhs = pressure_rhs[:, 0]
    diag = diag_inverse[0]
    factor = factor_blocks[:, 0]
    lists = row_lists[:, 0]
    col_block = rhs.shape[1]

    packed = jnp.concatenate(
        [
            rhs[1:].reshape(-1, NRHS),
            lists.astype(jnp.float32),
            jnp.zeros((5, NRHS), jnp.float32),
        ]
    )
    seen = jnp.stack([packed] + [swapped(packed, "sub", m) for m in (1, 2, 3)])
    order = jnp.arange(4) ^ sub
    seen = seen[order]
    rhs_all = seen[:, : 2 * col_block].reshape(4, 2, col_block, NRHS)
    lists_all = seen[:, 2 * col_block : 2 * col_block + 3].astype(jnp.int32)
    mate = sub ^ 1

    def forward(level, right):
        first = 2**level - 1
        blocks = diag[:, first : first + 2**level, :]
        part = jnp.einsum("ias,asn->in", blocks, right, precision=mode)
        return col_sum(part)

    def backward(level, residue):
        first = 2**level - 1
        blocks = diag[:, first : first + 2**level, :]
        return jnp.einsum("ias,in->asn", blocks, residue, precision=mode)

    def update(slot, solved):
        return jnp.dot(factor[slot], solved, precision=mode)

    def correct(slot, picked):
        return jnp.einsum("ks,kn->sn", factor[slot], picked, precision=mode)

    y0 = forward(0, rhs[:1])
    u01 = row_sum(update(0, y0))
    u02 = update(1, y0)
    other = swapped(u01, "sub", 1)
    base = sub // 2 * 2
    rhs1 = lax.dynamic_slice_in_dim(rhs_all[:, 0], base, 2, 0)
    b1 = rhs1 - spread(u01, lists[0], 2) - spread(other, lists_all[mate, 0], 2)
    y1 = forward(1, b1)
    u2 = row_sum(jnp.concatenate([u02, update(2, y1)]))
    b2 = rhs_all[:, 1]
    for m in range(4):
        far = swapped(u2, "sub", m) if m else u2
        from_lists = lists_all[sub ^ m]
        b2 = b2 - spread(far[:NRHS], from_lists[1], 4) - spread(far[NRHS:], from_lists[2], 4)
    y2 = forward(2, b2)

    pieces2 = backward(2, y2)
    wanted = jnp.stack(
        [
            jnp.concatenate(
                [pick(pieces2, lists_all[s, 1]), pick(pieces2, lists_all[s, 2]), pieces2[s]]
            )
            for s in range(4)
        ]
    )
    mine = lax.all_to_all(wanted, "sub", 0, 0).sum(0)
    mine = row_sum(mine)
    pick02, pick12, x2 = mine[:NRHS], mine[NRHS : 2 * NRHS], mine[2 * NRHS :]
    w1 = y1 - col_sum(correct(2, pick12))
    pieces1 = backward(1, w1)
    keep = lax.dynamic_index_in_dim(pieces1, sub % 2, 0, keepdims=False)
    give = lax.dynamic_index_in_dim(pieces1, 1 - sub % 2, 0, keepdims=False)
    keep = jnp.concatenate([pick(pieces1, lists[0]), keep])
    give = jnp.concatenate([pick(pieces1, lists_all[mate, 0]), give])
    mine1 = row_sum(keep + swapped(give, "sub", 1))
    pick01, x1 = mine1[:NRHS], mine1[NRHS:]
    w0 = y0 - col_sum(correct(0, pick01) + correct(1, pick02))
    x0 = row_sum(backward(0, w0)[0])
    return jnp.stack([x0, x1, x2])[:, None]


def solution(mesh):
    in_specs = (
        P(None, "sub", "col", None),
        P("sub", "row", None, "col"),
        P(None, "sub", "col", "row"),
        P(None, "sub", "col"),
    )
    out_specs = P(None, "sub", "col", None)
    return jax.shard_map(
        on_device, mesh=mesh, in_specs=in_specs, out_specs=out_specs, check_vma=False
    )
```

time: 1140 us -> 378 us (0.33)
  waiting for transfers between devices: 1050 us -> 116 us
  blocking collectives: 0 us -> 75.4 us
  local copies, waits for them, and re-layouts: 4.29 us -> 62.8 us
  starting transfers between devices: 22 us -> 71 us
  other arithmetic: 12.1 us -> 25.3 us
  between operations: 13.9 us -> 1.41 us
  matrix products: 35.2 us -> 23 us
    psum x10 -> x0, waiting for transfers between devices: 1010 us -> none  [the longest x3 449 us: on_device(): solved_panel = lax.psum(column_part, 'col')]
    all_to_all x0 -> x7, waiting for transfers between devices: none -> 82.1 us  [the longest x4 51.5 us: col_sum(): full = lax.all_to_all(jnp.broadcast_to(own, blocks.shape), 'col', 0, 0)]
    all_to_all x0 -> x4, blocking collectives: none -> 75.4 us  [the longest x2 41.1 us: col_sum(): own = lax.all_to_all(blocks, 'col', 0, 0).sum(0)]
    all_to_all x0 -> x7, starting transfers between devices: none -> 35.2 us  [the longest x3 17.9 us: col_sum(): own = lax.all_to_all(blocks, 'col', 0, 0).sum(0)]
    broadcast_in_dim x1 -> x25, local copies, waits for them, and re-layouts: 0.91 us -> 23.1 us  [the longest x18 18.8 us: spread(): placed = jnp.where(keep[..., None], update[None, :, None, :], 0.0)]
    reduce_sum x0 -> x20, local copies, waits for them, and re-layouts: none -> 15.9 us  [pick(): return jnp.where(keep[..., None], parts, 0.0).sum((0, 2))]
    ppermute x12 -> x18, starting transfers between devices: 21.6 us -> 35.8 us  [swapped(): return lax.ppermute(value, axis, pairs)]
    dot_general x12, matrix products: 35.2 us -> 23 us  [the longest x3 10.9 us: forward(): part = jnp.einsum('ias,asn->in', blocks, right, precision=mode)]
  transfers between devices with their start and end apart: 22 -> 25, of which waited for: 22 -> 19; matrix products, arithmetic and copies ran while one was open for 0% -> 13% of each run, Pallas kernels for 0% -> 0%
where the time goes in v1:
time: 378 us; the launch traced here: 375 us
  waiting for transfers between devices  116 us (31%)
  blocking collectives  75.4 us (20%)
  starting transfers between devices  71 us (19%)
  local copies, waits for them, and re-layouts  62.8 us (17%)
  other arithmetic  25.3 us (7%)
  matrix products  23 us (6%)
    all_to_all x4, waiting for transfers between devices, col_sum(): full = lax.all_to_all(jnp.broadcast_to(own, blocks.shape), 'col', 0, 0)  51.5 us
    all_to_all x2, blocking collectives, col_sum(): own = lax.all_to_all(blocks, 'col', 0, 0).sum(0)  41.1 us
    ppermute x18, starting transfers between devices, swapped(): return lax.ppermute(value, axis, pairs)  35.8 us
    ppermute x18, waiting for transfers between devices, swapped(): return lax.ppermute(value, axis, pairs)  34.4 us
    all_to_all x3, waiting for transfers between devices, col_sum(): own = lax.all_to_all(blocks, 'col', 0, 0).sum(0)  30.6 us
    all_to_all x1, blocking collectives, col_sum(): full = lax.all_to_all(jnp.broadcast_to(own, blocks.shape), 'col', 0, 0)  20.9 us
    broadcast_in_dim x18, local copies, waits for them, and re-layouts, spread(): placed = jnp.where(keep[..., None], update[None, :, None, :], 0.0)  18.8 us
    all_to_all x3, starting transfers between devices, col_sum(): own = lax.all_to_all(blocks, 'col', 0, 0).sum(0)  17.9 us
  transfers between devices with their start and end apart: 25, of which 19 were waited for; matrix products, arithmetic and copies ran while one was open for 13% of the time, Pallas kernels for 0%

profile of v1, /device:TPU:1, one launch (start us, length us, event | category | flops | bytes accessed | tf_op | source)
XLA Modules:
  0.0 375.5 jit_solution(9090235042414137707)
XLA Ops:
  1.9 3.8 %collective-permute-start.1 = (f32[520,128]{1,0:T(8,128)S(1)}, f32[520,128]{1,0:T(8,128)S(1)}, u32[]{:S(2)}, u32[]{:S(2)}) collective-permute-start(f32[520,128]{1,0:T(8,128)S(1)} %maximum_maximum_fusion), channel_id=1, source_target_pairs={{0,128},{64,192},{128,0},{192,64},{1,129},{65,193},{129,1},{193,65... | collective-permute-start | bytes 798728 | tf_op jit(solution)/shard_map/ppermute | solution.py:13
  6.5 1.3 slice.207
  7.8 2.3 fusion.71
  10.1 10.8 %all-to-all-start = ((f32[16,64,128]{2,1,0:T(8,128)}), f32[16,64,128]{2,1,0:T(8,128)}, u32[]{:S(2)}, u32[]{:S(2)}) async-start(f32[16,64,128]{2,1,0:T(8,128)} %fusion.71), calls=%async_computation | async-start | bytes 1048576 | tf_op jit(solution)/shard_map/all_to_all | solution.py:19
  30.1 7.8 %all-to-all-done = f32[16,64,128]{2,1,0:T(8,128)} async-done(((f32[16,64,128]{2,1,0:T(8,128)}), f32[16,64,128]{2,1,0:T(8,128)}, u32[]{:S(2)}, u32[]{:S(2)}) %all-to-all-start) | async-done | bytes 524320 | tf_op jit(solution)/shard_map/all_to_all | solution.py:19
  37.8 1.1 reduce_sum.171
  39.8 4.3 %all-to-all-start.1 = ((f32[16,64,128]{2,1,0:T(8,128)}), f32[16,64,128]{2,1,0:T(8,128)S(1)}, u32[]{:S(2)}, u32[]{:S(2)}) async-start(f32[16,64,128]{2,1,0:T(8,128)} %broadcast_in_dim.410), calls=%async_computation.1 | async-start | bytes 1048576 | tf_op jit(solution)/shard_map/all_to_all | solution.py:20
  45.9 14.6 %all-to-all-done.1 = f32[16,64,128]{2,1,0:T(8,128)S(1)} async-done(((f32[16,64,128]{2,1,0:T(8,128)}), f32[16,64,128]{2,1,0:T(8,128)S(1)}, u32[]{:S(2)}, u32[]{:S(2)}) %all-to-all-start.1) | async-done | bytes 524320 | tf_op jit(solution)/shard_map/all_to_all | solution.py:20
  61.1 3.8 %collective-permute-start.3 = (f32[128,128]{0,1:T(8,128)S(1)}, f32[128,128]{0,1:T(8,128)S(1)}, u32[]{:S(2)}, u32[]{:S(2)}) collective-permute-start(f32[128,128]{0,1:T(8,128)S(1)} %convolution_bitcast_fusion.4), channel_id=1, source_target_pairs={{0,16},{16,0},{32,48},{48,32},{1,17},{17,1},{33,49},{49,33},{2,18}... | collective-permute-start | bytes 196616 | tf_op jit(solution)/shard_map/ppermute | solution.py:13
  66.2 2.8 collective-permute-done.4
  69.4 2.8 collective-permute-done.5
  72.4 3.0 fusion.8
  76.5 3.6 all-to-all-start.2
  84.3 11.0 %all-to-all-done.2 = f32[16,64,128]{2,1,0:T(8,128)S(1)} async-done(((f32[16,64,128]{2,1,0:T(8,128)}), f32[16,64,128]{2,1,0:T(8,128)S(1)}, u32[]{:S(2)}, u32[]{:S(2)}) %all-to-all-start.2) | async-done | bytes 524320 | tf_op jit(solution)/shard_map/all_to_all | solution.py:19
  96.2 4.3 %all-to-all-start.3 = ((f32[16,64,128]{2,1,0:T(8,128)}), f32[16,64,128]{2,1,0:T(8,128)S(1)}, u32[]{:S(2)}, u32[]{:S(2)}) async-start(f32[16,64,128]{2,1,0:T(8,128)} %broadcast_in_dim.422), calls=%async_computation.3 | async-start | bytes 1048576 | tf_op jit(solution)/shard_map/all_to_all | solution.py:20
  101.1 1.2 copy.152
  104.9 9.1 %all-to-all-done.3 = f32[16,64,128]{2,1,0:T(8,128)S(1)} async-done(((f32[16,64,128]{2,1,0:T(8,128)}), f32[16,64,128]{2,1,0:T(8,128)S(1)}, u32[]{:S(2)}, u32[]{:S(2)}) %all-to-all-start.3) | async-done | bytes 524320 | tf_op jit(solution)/shard_map/all_to_all | solution.py:20
  114.3 6.4 %collective-permute-start.6 = (f32[256,128]{1,0:T(8,128)S(1)}, f32[256,128]{1,0:T(8,128)S(1)}, u32[]{:S(2)}, u32[]{:S(2)}) collective-permute-start(f32[256,128]{1,0:T(8,128)S(1)} %pad_maximum_fusion.3), channel_id=1, source_target_pairs={{0,16},{16,0},{32,48},{48,32},{1,17},{17,1},{33,49},{49,33},{2,18}... | collective-permute-start | bytes 393224 | tf_op jit(solution)/shard_map/ppermute | solution.py:13
  122.7 3.8 %collective-permute-done.7 = f32[256,128]{1,0:T(8,128)S(1)} collective-permute-done((f32[256,128]{1,0:T(8,128)S(1)}, f32[256,128]{1,0:T(8,128)S(1)}, u32[]{:S(2)}, u32[]{:S(2)}) %collective-permute-start.7) | collective-permute-done | bytes 131104 | tf_op jit(solution)/shard_map/ppermute | solution.py:13
  126.5 1.9 collective-permute-start.9
  130.6 1.5 broadcast_in_dim.430
  133.2 1.5 fusion.92
  135.4 1.6 copy.116
  137.1 1.5 broadcast_in_dim.446
  138.6 1.7 copy.117
  140.2 1.5 fusion.91
  142.5 1.7 copy.114
  144.1 1.5 broadcast_in_dim.438
  145.7 1.7 copy.115
  147.3 1.5 fusion.93
  150.5 1.5 broadcast_in_dim.454
  152.1 1.7 copy.119
  153.7 5.6 %fusion.11 = f32[1024,128]{0,1:T(8,128)} fusion(f32[1024,7,256]{2,0,1:T(8,128)} %bitcast.332, f32[4,1,256,128]{2,3,0,1:T(8,128)S(1)} %copy.152, f32[256,128]{0,1:T(8,128)} %copy.119, f32[256,128]{0,1:T(8,128)S(1)} %copy.118, f32[256,128]{0,1:T(8,128)} %copy.117, f32[256,128]{0,1:T(8,128)} %copy.116, f32[256,128]{0,1:T(8,128)} %copy.115, ...), kind=kOutput, calls=%fused_computation.11 | convolution fusion | flops 807403520 | bytes 6299648 | tf_op jit(solution)/shard_map/ias,asn->in/dot_general | solution.py:71
  159.4 2.0 copy.120
  161.5 3.6 all-to-all-start.4
  168.9 11.8 %all-to-all-done.4 = f32[16,64,128]{2,1,0:T(8,128)S(1)} async-done(((f32[16,64,128]{2,1,0:T(8,128)}), f32[16,64,128]{2,1,0:T(8,128)S(1)}, u32[]{:S(2)}, u32[]{:S(2)}) %all-to-all-start.4) | async-done | bytes 524320 | tf_op jit(solution)/shard_map/all_to_all | solution.py:19
  181.6 4.4 %all-to-all-start.5 = ((f32[16,64,128]{2,1,0:T(8,128)}), f32[16,64,128]{2,1,0:T(8,128)S(1)}, u32[]{:S(2)}, u32[]{:S(2)}) async-start(f32[16,64,128]{2,1,0:T(8,128)} %broadcast_in_dim.457), calls=%async_computation.5 | async-start | bytes 1048576 | tf_op jit(solution)/shard_map/all_to_all | solution.py:20
  188.5 11.4 %all-to-all-done.5 = f32[16,64,128]{2,1,0:T(8,128)S(1)} async-done(((f32[16,64,128]{2,1,0:T(8,128)}), f32[16,64,128]{2,1,0:T(8,128)S(1)}, u32[]{:S(2)}, u32[]{:S(2)}) %all-to-all-start.5) | async-done | bytes 524320 | tf_op jit(solution)/shard_map/all_to_all | solution.py:20
  199.9 5.5 %select_reduce_fusion.7 = (f32[256,128]{0,1:T(8,128)}, f32[256,128]{0,1:T(8,128)}, f32[256,128]{0,1:T(8,128)}, f32[256,128]{0,1:T(8,128)}, f32[256,128]{0,1:T(8,...) fusion(pred[4,256]{1,0:T(4,128)(4,1)S(1)} %broadcast_and_fusion.15, ...), kind=kOutput, calls=%fused_computation.46 | convolution fusion | flops 807141376 | bytes 6299648 | tf_op jit(solution)/shard_map/ias,in->asn/dot_general | solution.py:77
  211.0 1.6 copy.136
  212.6 1.7 copy.131
  214.2 1.7 reduce_sum.238
  215.9 1.6 copy.133
  217.5 1.7 copy.130
  219.1 1.7 reduce_sum.235
  220.8 1.6 copy.132
  228.1 13.4 %all_to_all.55 = f32[4,512,128]{1,2,0:T(8,128)} all-to-all(f32[4,512,128]{1,2,0:T(8,128)S(1)} %pad_maximum_fusion.1), channel_id=1, replica_groups=mesh['sub'=4,'row'=4,'col'=16] {'sub'}, dimensions={0} | all-to-all | bytes 2097152 | tf_op jit(solution)/shard_map/all_to_all | solution.py:110
  241.5 1.3 reduce_sum.245
  242.9 6.7 %collective-permute-start.11 = (f32[512,128]{0,1:T(8,128)S(1)}, f32[512,128]{0,1:T(8,128)S(1)}, u32[]{:S(2)}, u32[]{:S(2)}) collective-permute-start(f32[512,128]{0,1:T(8,128)S(1)} %reduce_sum.245), channel_id=1, source_target_pairs={{0,16},{16,0},{32,48},{48,32},{1,17},{17,1},{33,49},{49,33},{2,18}... | collective-permute-start | bytes 786440 | tf_op jit(solution)/shard_map/ppermute | solution.py:13
  249.6 1.2 collective-permute-done.11
  251.3 7.0 %collective-permute-done.12 = f32[512,128]{0,1:T(8,128)S(1)} collective-permute-done((f32[512,128]{0,1:T(8,128)S(1)}, f32[512,128]{0,1:T(8,128)S(1)}, u32[]{:S(2)}, u32[]{:S(2)}) %collective-permute-start.12) | collective-permute-done | bytes 262176 | tf_op jit(solution)/shard_map/ppermute | solution.py:13
  259.8 21.2 %all_to_all.56 = f32[16,64,128]{2,1,0:T(8,128)S(1)} all-to-all(f32[16,64,128]{2,1,0:T(8,128)} %bitcast.346), channel_id=1, replica_groups=mesh['sub'=4,'row'=4,'col'=16] {'col'}, dimensions={0} | all-to-all | bytes 1048576 | tf_op jit(solution)/shard_map/all_to_all | solution.py:19
  281.9 4.3 %all-to-all-start.8 = ((f32[16,64,128]{2,1,0:T(8,128)}), f32[16,64,128]{2,1,0:T(8,128)S(1)}, u32[]{:S(2)}, u32[]{:S(2)}) async-start(f32[16,64,128]{2,1,0:T(8,128)} %broadcast_in_dim.465), calls=%async_computation.8 | async-start | bytes 1048576 | tf_op jit(solution)/shard_map/all_to_all | solution.py:20
  286.3 16.4 %all-to-all-done.8 = f32[16,64,128]{2,1,0:T(8,128)S(1)} async-done(((f32[16,64,128]{2,1,0:T(8,128)}), f32[16,64,128]{2,1,0:T(8,128)S(1)}, u32[]{:S(2)}, u32[]{:S(2)}) %all-to-all-start.8) | async-done | bytes 524320 | tf_op jit(solution)/shard_map/all_to_all | solution.py:20
  302.8 2.3 select_reduce_fusion.9
  306.3 3.9 %collective-permute-done.13 = f32[384,128]{0,1:T(8,128)S(1)} collective-permute-done((f32[384,128]{0,1:T(8,128)S(1)}, f32[384,128]{0,1:T(8,128)S(1)}, u32[]{:S(2)}, u32[]{:S(2)}) %collective-permute-start.13) | collective-permute-done | bytes 196640 | tf_op jit(solution)/shard_map/ppermute | solution.py:13
  310.2 4.9 %collective-permute-start.14 = (f32[384,128]{0,1:T(8,128)S(1)}, f32[384,128]{0,1:T(8,128)S(1)}, u32[]{:S(2)}, u32[]{:S(2)}) collective-permute-start(f32[384,128]{0,1:T(8,128)S(1)} %maximum_add_fusion), channel_id=1, source_target_pairs={{0,16},{16,0},{32,48},{48,32},{1,17},{17,1},{33,49},{49,33},{2,18}... | collective-permute-start | bytes 589832 | tf_op jit(solution)/shard_map/ppermute | solution.py:13
  315.1 1.1 collective-permute-done.14
  317.1 5.3 %collective-permute-done.15 = f32[384,128]{0,1:T(8,128)S(1)} collective-permute-done((f32[384,128]{0,1:T(8,128)S(1)}, f32[384,128]{0,1:T(8,128)S(1)}, u32[]{:S(2)}, u32[]{:S(2)}) %collective-permute-start.15) | collective-permute-done | bytes 196640 | tf_op jit(solution)/shard_map/ppermute | solution.py:13
  323.0 19.9 %all_to_all.57 = f32[16,64,128]{2,1,0:T(8,128)S(1)} all-to-all(f32[16,64,128]{2,1,0:T(8,128)S(1)} %bitcast.347), channel_id=1, replica_groups=mesh['sub'=4,'row'=4,'col'=16] {'col'}, dimensions={0} | all-to-all | bytes 1048576 | tf_op jit(solution)/shard_map/all_to_all | solution.py:19
  343.0 20.9 %all_to_all.58 = f32[16,64,128]{2,1,0:T(8,128)S(1)} all-to-all(f32[16,64,128]{2,1,0:T(8,128)S(1)} %broadcast_in_dim.468), channel_id=1, replica_groups=mesh['sub'=4,'row'=4,'col'=16] {'col'}, dimensions={0} | all-to-all | bytes 1048576 | tf_op jit(solution)/shard_map/all_to_all | solution.py:20
  363.9 1.8 convolution_bitcast_fusion.1
  365.7 3.0 collective-permute-start.16
  370.3 4.2 %collective-permute-done.17 = f32[256,128]{0,1:T(8,128)S(1)} collective-permute-done((f32[256,128]{0,1:T(8,128)S(1)}, f32[256,128]{0,1:T(8,128)S(1)}, u32[]{:S(2)}, u32[]{:S(2)}) %collective-permute-start.17) | collective-permute-done | bytes 131104 | tf_op jit(solution)/shard_map/ppermute | solution.py:13
  (275 shorter events, 60.9 us)
Async XLA Ops:
  1.9 20.4 %collective-permute-start.1 = (f32[520,128]{1,0:T(8,128)S(1)}, f32[520,128]{1,0:T(8,128)S(1)}, u32[]{:S(2)}, u32[]{:S(2)}) collective-permute-start(f32[520,128]{1,0:T(8,128)S(1)} %maximum_maximum_fusion), channel_id=1, source_target_pairs={{0,128},{64,192},{128,0},{192,64},{1,129},{65,193},{129,1},{193,65... | collective-permute-start | bytes 798728 | tf_op jit(solution)/shard_map/ppermute | solution.py:13
  5.7 16.6 %collective-permute-start = (f32[520,128]{1,0:T(8,128)S(1)}, f32[520,128]{1,0:T(8,128)S(1)}, u32[]{:S(2)}, u32[]{:S(2)}) collective-permute-start(f32[520,128]{1,0:T(8,128)S(1)} %maximum_maximum_fusion), channel_id=1, source_target_pairs={{0,64},{64,0},{128,192},{192,128},{1,65},{65,1},{129,193},{193,129... | collective-permute-start | bytes 798728 | tf_op jit(solution)/shard_map/ppermute | solution.py:13
  6.1 16.2 %collective-permute-start.2 = (f32[520,128]{1,0:T(8,128)S(1)}, f32[520,128]{1,0:T(8,128)S(1)}, u32[]{:S(2)}, u32[]{:S(2)}) collective-permute-start(f32[520,128]{1,0:T(8,128)S(1)} %maximum_maximum_fusion), channel_id=1, source_target_pairs={{0,192},{64,128},{128,64},{192,0},{1,193},{65,129},{129,65},{193,1... | collective-permute-start | bytes 798728 | tf_op jit(solution)/shard_map/ppermute | solution.py:13
  10.1 27.8 %all-to-all-start = ((f32[16,64,128]{2,1,0:T(8,128)}), f32[16,64,128]{2,1,0:T(8,128)}, u32[]{:S(2)}, u32[]{:S(2)}) async-start(f32[16,64,128]{2,1,0:T(8,128)} %fusion.71), calls=%async_computation | async-start | bytes 1048576 | tf_op jit(solution)/shard_map/all_to_all | solution.py:19
  22.3 0.7 copy-start.2
  29.9 42.5 %copy-start.17 = (pred[2,256]{1,0:T(4,128)(4,1)}, pred[2,256]{1,0:T(4,128)(4,1)S(1)}, u32[]{:S(2)}) copy-start(pred[2,256]{1,0:T(4,128)(4,1)S(1)} %get-tuple-element.97) | copy-start | bytes 1540
  29.9 42.5 %copy-start.19 = (pred[2,256]{1,0:T(4,128)(4,1)}, pred[2,256]{1,0:T(4,128)(4,1)S(1)}, u32[]{:S(2)}) copy-start(pred[2,256]{1,0:T(4,128)(4,1)S(1)} %get-tuple-element.98) | copy-start | bytes 1540
  39.8 20.8 %all-to-all-start.1 = ((f32[16,64,128]{2,1,0:T(8,128)}), f32[16,64,128]{2,1,0:T(8,128)S(1)}, u32[]{:S(2)}, u32[]{:S(2)}) async-start(f32[16,64,128]{2,1,0:T(8,128)} %broadcast_in_dim.410), calls=%async_computation.1 | async-start | bytes 1048576 | tf_op jit(solution)/shard_map/all_to_all | solution.py:20
  44.7 15.8 %copy-start = (f32[3,1,128,1024]{3,2,1,0:T(8,128)S(1)}, f32[3,1,128,1024]{3,2,1,0:T(8,128)}, u32[]{:S(2)}) copy-start(f32[3,1,128,1024]{3,2,1,0:T(8,128)} %param.6) | copy-start | bytes 4718596
  61.1 4.7 %collective-permute-start.3 = (f32[128,128]{0,1:T(8,128)S(1)}, f32[128,128]{0,1:T(8,128)S(1)}, u32[]{:S(2)}, u32[]{:S(2)}) collective-permute-start(f32[128,128]{0,1:T(8,128)S(1)} %convolution_bitcast_fusion.4), channel_id=1, source_target_pairs={{0,16},{16,0},{32,48},{48,32},{1,17},{17,1},{33,49},{49,33},{2,18}... | collective-permute-start | bytes 196616 | tf_op jit(solution)/shard_map/ppermute | solution.py:13
  65.8 3.2 collective-permute-start.4
  69.0 3.2 collective-permute-start.5
  76.5 18.9 %all-to-all-start.2 = ((f32[16,64,128]{2,1,0:T(8,128)}), f32[16,64,128]{2,1,0:T(8,128)S(1)}, u32[]{:S(2)}, u32[]{:S(2)}) async-start(f32[16,64,128]{2,1,0:T(8,128)} %bitcast.21), calls=%async_computation.2 | async-start | bytes 1048576 | tf_op jit(solution)/shard_map/all_to_all | solution.py:19
  96.2 17.7 %all-to-all-start.3 = ((f32[16,64,128]{2,1,0:T(8,128)}), f32[16,64,128]{2,1,0:T(8,128)S(1)}, u32[]{:S(2)}, u32[]{:S(2)}) async-start(f32[16,64,128]{2,1,0:T(8,128)} %broadcast_in_dim.422), calls=%async_computation.3 | async-start | bytes 1048576 | tf_op jit(solution)/shard_map/all_to_all | solution.py:20
  114.3 7.4 %collective-permute-start.6 = (f32[256,128]{1,0:T(8,128)S(1)}, f32[256,128]{1,0:T(8,128)S(1)}, u32[]{:S(2)}, u32[]{:S(2)}) collective-permute-start(f32[256,128]{1,0:T(8,128)S(1)} %pad_maximum_fusion.3), channel_id=1, source_target_pairs={{0,16},{16,0},{32,48},{48,32},{1,17},{17,1},{33,49},{49,33},{2,18}... | collective-permute-start | bytes 393224 | tf_op jit(solution)/shard_map/ppermute | solution.py:13
  121.7 4.8 %collective-permute-start.7 = (f32[256,128]{1,0:T(8,128)S(1)}, f32[256,128]{1,0:T(8,128)S(1)}, u32[]{:S(2)}, u32[]{:S(2)}) collective-permute-start(f32[256,128]{1,0:T(8,128)S(1)} %fusion.87), channel_id=1, source_target_pairs={{0,32},{16,48},{32,0},{48,16},{1,33},{17,49},{33,1},{49,17},{2,34}... | collective-permute-start | bytes 393224 | tf_op jit(solution)/shard_map/ppermute | solution.py:13
  126.5 6.7 %collective-permute-start.9 = (f32[256,128]{1,0:T(8,128)S(1)}, f32[256,128]{1,0:T(8,128)}, u32[]{:S(2)}, u32[]{:S(2)}) collective-permute-start(f32[256,128]{1,0:T(8,128)S(1)} %add.331), channel_id=1, source_target_pairs={{0,128},{64,192},{128,0},{192,64},{1,129},{65,193},{129,1},{193,65... | collective-permute-start | bytes 393224 | tf_op jit(solution)/shard_map/ppermute | solution.py:13
  128.4 11.8 %collective-permute-start.8 = (f32[256,128]{1,0:T(8,128)S(1)}, f32[256,128]{1,0:T(8,128)}, u32[]{:S(2)}, u32[]{:S(2)}) collective-permute-start(f32[256,128]{1,0:T(8,128)S(1)} %add.331), channel_id=1, source_target_pairs={{0,64},{64,0},{128,192},{192,128},{1,65},{65,1},{129,193},{193,129... | collective-permute-start | bytes 393224 | tf_op jit(solution)/shard_map/ppermute | solution.py:13
  128.8 18.5 %collective-permute-start.10 = (f32[256,128]{1,0:T(8,128)S(1)}, f32[256,128]{1,0:T(8,128)}, u32[]{:S(2)}, u32[]{:S(2)}) collective-permute-start(f32[256,128]{1,0:T(8,128)S(1)} %add.331), channel_id=1, source_target_pairs={{0,192},{64,128},{128,64},{192,0},{1,193},{65,129},{129,65},{193,1... | collective-permute-start | bytes 393224 | tf_op jit(solution)/shard_map/ppermute | solution.py:13
  159.3 5.8 %copy-start.27 = (s32[128]{0:T(128)S(1)}, s32[128]{0:T(128)}, u32[]{:S(2)}) copy-start(s32[128]{0:T(128)} %get-tuple-element.39) | copy-start | bytes 1540
  159.3 5.8 %copy-start.28 = (s32[128]{0:T(128)S(1)}, s32[128]{0:T(128)}, u32[]{:S(2)}) copy-start(s32[128]{0:T(128)} %get-tuple-element.40) | copy-start | bytes 1540
  159.4 5.8 %copy-start.13 = (pred[128,2]{1,0:T(8,128)(4,1)S(1)}, pred[128,2]{1,0:T(8,128)(4,1)}, u32[]{:S(2)}) copy-start(pred[128,2]{1,0:T(8,128)(4,1)} %get-tuple-element.87) | copy-start | bytes 772
  159.4 5.9 %copy-start.14 = (pred[128,2]{1,0:T(8,128)(4,1)S(1)}, pred[128,2]{1,0:T(8,128)(4,1)}, u32[]{:S(2)}) copy-start(pred[128,2]{1,0:T(8,128)(4,1)} %get-tuple-element.81) | copy-start | bytes 772
  159.4 6.1 %copy-start.15 = (pred[128,2]{1,0:T(8,128)(4,1)S(1)}, pred[128,2]{1,0:T(8,128)(4,1)}, u32[]{:S(2)}) copy-start(pred[128,2]{1,0:T(8,128)(4,1)} %get-tuple-element.83) | copy-start | bytes 772
  159.4 6.2 %copy-start.16 = (pred[128,2]{1,0:T(8,128)(4,1)S(1)}, pred[128,2]{1,0:T(8,128)(4,1)}, u32[]{:S(2)}) copy-start(pred[128,2]{1,0:T(8,128)(4,1)} %get-tuple-element.85) | copy-start | bytes 772
  159.4 6.7 %copy-start.24 = (pred[4,128]{1,0:T(4,128)(4,1)S(1)}, pred[4,128]{1,0:T(4,128)(4,1)}, u32[]{:S(2)}) copy-start(pred[4,128]{1,0:T(4,128)(4,1)} %get-tuple-element.93) | copy-start | bytes 1540
  159.4 7.0 %copy-start.23 = (pred[4,128]{1,0:T(4,128)(4,1)S(1)}, pred[4,128]{1,0:T(4,128)(4,1)}, u32[]{:S(2)}) copy-start(pred[4,128]{1,0:T(4,128)(4,1)} %get-tuple-element.91) | copy-start | bytes 1540
  159.4 7.3 %copy-start.25 = (s32[128]{0:T(128)S(1)}, s32[128]{0:T(128)}, u32[]{:S(2)}) copy-start(s32[128]{0:T(128)} %get-tuple-element.33) | copy-start | bytes 1540
  159.4 7.3 %copy-start.26 = (s32[128]{0:T(128)S(1)}, s32[128]{0:T(128)}, u32[]{:S(2)}) copy-start(s32[128]{0:T(128)} %get-tuple-element.34) | copy-start | bytes 1540
  161.5 19.2 %all-to-all-start.4 = ((f32[16,64,128]{2,1,0:T(8,128)}), f32[16,64,128]{2,1,0:T(8,128)S(1)}, u32[]{:S(2)}, u32[]{:S(2)}) async-start(f32[16,64,128]{2,1,0:T(8,128)} %bitcast.345), calls=%async_computation.4 | async-start | bytes 1048576 | tf_op jit(solution)/shard_map/all_to_all | solution.py:19
  165.1 21.6 %copy-start.10 = (pred[128,2]{1,0:T(8,128)(4,1)S(1)}, pred[128,2]{1,0:T(8,128)(4,1)}, u32[]{:S(2)}) copy-start(pred[128,2]{1,0:T(8,128)(4,1)} %get-tuple-element.82) | copy-start | bytes 772
  165.1 21.8 %copy-start.11 = (pred[128,2]{1,0:T(8,128)(4,1)S(1)}, pred[128,2]{1,0:T(8,128)(4,1)}, u32[]{:S(2)}) copy-start(pred[128,2]{1,0:T(8,128)(4,1)} %get-tuple-element.84) | copy-start | bytes 772
  165.1 21.9 %copy-start.12 = (pred[128,2]{1,0:T(8,128)(4,1)S(1)}, pred[128,2]{1,0:T(8,128)(4,1)}, u32[]{:S(2)}) copy-start(pred[128,2]{1,0:T(8,128)(4,1)} %get-tuple-element.86) | copy-start | bytes 772
  165.1 22.4 %copy-start.22 = (pred[4,128]{1,0:T(4,128)(4,1)S(1)}, pred[4,128]{1,0:T(4,128)(4,1)}, u32[]{:S(2)}) copy-start(pred[4,128]{1,0:T(4,128)(4,1)} %get-tuple-element.94) | copy-start | bytes 1540
  165.1 22.7 %copy-start.21 = (pred[4,128]{1,0:T(4,128)(4,1)S(1)}, pred[4,128]{1,0:T(4,128)(4,1)}, u32[]{:S(2)}) copy-start(pred[4,128]{1,0:T(4,128)(4,1)} %get-tuple-element.92) | copy-start | bytes 1540
  181.6 18.4 %all-to-all-start.5 = ((f32[16,64,128]{2,1,0:T(8,128)}), f32[16,64,128]{2,1,0:T(8,128)S(1)}, u32[]{:S(2)}, u32[]{:S(2)}) async-start(f32[16,64,128]{2,1,0:T(8,128)} %broadcast_in_dim.457), calls=%async_computation.5 | async-start | bytes 1048576 | tf_op jit(solution)/shard_map/all_to_all | solution.py:20
  211.0 16.0 %copy-start.1 = (f32[4,256,128]{1,2,0:T(8,128)S(1)}, f32[4,256,128]{1,2,0:T(8,128)}, u32[]{:S(2)}) copy-start(f32[4,256,128]{1,2,0:T(8,128)} %get-tuple-element.71) | copy-start | bytes 1572868
  225.2 1.8 copy-start.3
  225.2 2.7 copy-start.4
  226.0 1.9 copy-start.5
  226.2 1.8 copy-start.6
  226.2 1.8 copy-start.7
  227.0 1.0 copy-start.8
  227.0 1.1 copy-start.9
  242.9 7.9 %collective-permute-start.11 = (f32[512,128]{0,1:T(8,128)S(1)}, f32[512,128]{0,1:T(8,128)S(1)}, u32[]{:S(2)}, u32[]{:S(2)}) collective-permute-start(f32[512,128]{0,1:T(8,128)S(1)} %reduce_sum.245), channel_id=1, source_target_pairs={{0,16},{16,0},{32,48},{48,32},{1,17},{17,1},{33,49},{49,33},{2,18}... | collective-permute-start | bytes 786440 | tf_op jit(solution)/shard_map/ppermute | solution.py:13
  250.8 7.6 %collective-permute-start.12 = (f32[512,128]{0,1:T(8,128)S(1)}, f32[512,128]{0,1:T(8,128)S(1)}, u32[]{:S(2)}, u32[]{:S(2)}) collective-permute-start(f32[512,128]{0,1:T(8,128)S(1)} %add.348), channel_id=1, source_target_pairs={{0,32},{16,48},{32,0},{48,16},{1,33},{17,49},{33,1},{49,17},{2,34}... | collective-permute-start | bytes 786440 | tf_op jit(solution)/shard_map/ppermute | solution.py:13
  281.1 21.7 %copy-start.18 = (pred[2,256]{1,0:T(4,128)(4,1)S(1)}, pred[2,256]{1,0:T(4,128)(4,1)}, u32[]{:S(2)}) copy-start(pred[2,256]{1,0:T(4,128)(4,1)} %copy-done.17) | copy-start | bytes 1540
  281.1 21.7 %copy-start.20 = (pred[2,256]{1,0:T(4,128)(4,1)S(1)}, pred[2,256]{1,0:T(4,128)(4,1)}, u32[]{:S(2)}) copy-start(pred[2,256]{1,0:T(4,128)(4,1)} %copy-done.19) | copy-start | bytes 1540
  281.9 20.7 %all-to-all-start.8 = ((f32[16,64,128]{2,1,0:T(8,128)}), f32[16,64,128]{2,1,0:T(8,128)S(1)}, u32[]{:S(2)}, u32[]{:S(2)}) async-start(f32[16,64,128]{2,1,0:T(8,128)} %broadcast_in_dim.465), calls=%async_computation.8 | async-start | bytes 1048576 | tf_op jit(solution)/shard_map/all_to_all | solution.py:20
  305.5 4.6 %collective-permute-start.13 = (f32[384,128]{0,1:T(8,128)S(1)}, f32[384,128]{0,1:T(8,128)S(1)}, u32[]{:S(2)}, u32[]{:S(2)}) collective-permute-start(f32[384,128]{0,1:T(8,128)S(1)} %pad_maximum_fusion.2), channel_id=1, source_target_pairs={{0,64},{64,0},{128,192},{192,128},{1,65},{65,1},{129,193},{193,129... | collective-permute-start | bytes 589832 | tf_op jit(solution)/shard_map/ppermute | solution.py:13
  310.2 6.0 %collective-permute-start.14 = (f32[384,128]{0,1:T(8,128)S(1)}, f32[384,128]{0,1:T(8,128)S(1)}, u32[]{:S(2)}, u32[]{:S(2)}) collective-permute-start(f32[384,128]{0,1:T(8,128)S(1)} %maximum_add_fusion), channel_id=1, source_target_pairs={{0,16},{16,0},{32,48},{48,32},{1,17},{17,1},{33,49},{49,33},{2,18}... | collective-permute-start | bytes 589832 | tf_op jit(solution)/shard_map/ppermute | solution.py:13
  316.2 6.2 %collective-permute-start.15 = (f32[384,128]{0,1:T(8,128)S(1)}, f32[384,128]{0,1:T(8,128)S(1)}, u32[]{:S(2)}, u32[]{:S(2)}) collective-permute-start(f32[384,128]{0,1:T(8,128)S(1)} %add.354), channel_id=1, source_target_pairs={{0,32},{16,48},{32,0},{48,16},{1,33},{17,49},{33,1},{49,17},{2,34}... | collective-permute-start | bytes 589832 | tf_op jit(solution)/shard_map/ppermute | solution.py:13
  365.7 4.0 %collective-permute-start.16 = (f32[256,128]{0,1:T(8,128)S(1)}, f32[256,128]{0,1:T(8,128)S(1)}, u32[]{:S(2)}, u32[]{:S(2)}) collective-permute-start(f32[256,128]{0,1:T(8,128)S(1)} %convolution_bitcast_fusion.1), channel_id=1, source_target_pairs={{0,16},{16,0},{32,48},{48,32},{1,17},{17,1},{33,49},{49,33},{2,18}... | collective-permute-start | bytes 393224 | tf_op jit(solution)/shard_map/ppermute | solution.py:13
  369.7 4.8 %collective-permute-start.17 = (f32[256,128]{0,1:T(8,128)S(1)}, f32[256,128]{0,1:T(8,128)S(1)}, u32[]{:S(2)}, u32[]{:S(2)}) collective-permute-start(f32[256,128]{0,1:T(8,128)S(1)} %add.358), channel_id=1, source_target_pairs={{0,32},{16,48},{32,0},{48,16},{1,33},{17,49},{33,1},{49,17},{2,34}... | collective-permute-start | bytes 393224 | tf_op jit(solution)/shard_map/ppermute | solution.py:13

commit v2 on v1

v2 whole, which is shorter than its diff:
```python
import functools

import jax
import jax.numpy as jnp
from jax import lax
from jax.experimental import pallas as pl
from jax.experimental.pallas import tpu as pltpu
from jax.sharding import PartitionSpec as P

S = 4096
N = 128
C = 256
R = 1024
K = 128
STEP = 256
LIST_AT = 2 * C
PACKED = 2 * C + 8
mode = lax.Precision.HIGH


def halves(value):
    high = value.astype(jnp.bfloat16)
    low = (value - high.astype(jnp.float32)).astype(jnp.bfloat16)
    return high, low


def mm(a, b):
    return jnp.dot(a, b, preferred_element_type=jnp.float32)


def hits(seen_ref, place, slots, panels):
    targets = jnp.concatenate(
        [seen_ref[place, LIST_AT + t : LIST_AT + t + 1, :] for t in slots], axis=1
    ).astype(jnp.int32)
    shape = (panels * C, K * len(slots))
    rows = lax.broadcasted_iota(jnp.int32, shape, 0)
    return jnp.where(rows == targets, 1.0, 0.0).astype(jnp.bfloat16)


SLOTS_OF = {1: (0,), 2: (1, 2)}


def forward_kernel(level, sub_ref, *refs):
    spans = 2**level
    updates = spans if level else 0
    seen_ref, refs = refs[0], refs[1:]
    update_refs, refs = refs[:updates], refs[updates:]
    diag_refs, (out_ref, right_ref) = refs[:spans], refs[spans:]

    @pl.when(pl.program_id(0) == 0)
    def _():
        if level == 0:
            high, low = halves(seen_ref[...])
            right_ref[0] = jnp.concatenate([high, low], axis=1)
        else:
            sub = sub_ref[0] % spans
            total = None
            for m in range(spans):
                high, low = halves(update_refs[m][...])
                pair = jnp.concatenate([high, low], axis=1)
                term = mm(hits(seen_ref, m, SLOTS_OF[level], spans), pair)
                total = term if total is None else total + term
            total = total[:, :N] + total[:, N:]
            for a in range(spans):
                rhs = seen_ref[a ^ sub, (level - 1) * C : level * C, :]
                high, low = halves(rhs - total[a * C : (a + 1) * C])
                right_ref[a] = jnp.concatenate([high, low], axis=1)

    wide, thin = None, None
    for a in range(spans):
        high, low = halves(diag_refs[a][0])
        one, two = mm(high, right_ref[a]), mm(low, right_ref[a, :, :N])
        wide = one if wide is None else wide + one
        thin = two if thin is None else thin + two
    out_ref[...] = wide[:, :N] + wide[:, N:] + thin


def diag_specs(level):
    spans = 2**level
    return [
        pl.BlockSpec((1, STEP, C), lambda i, s, a=a: (spans - 1 + a, i, 0)) for a in range(spans)
    ]


def whole(*shape):
    return pl.BlockSpec(shape, lambda i, s: (0,) * len(shape))


def forward(level, sub, seen, updates, diag):
    spans = 2**level
    return pl.pallas_call(
        functools.partial(forward_kernel, level),
        grid_spec=pltpu.PrefetchScalarGridSpec(
            num_scalar_prefetch=1,
            grid=(R // STEP,),
            in_specs=[whole(*seen.shape)] + [whole(*u.shape) for u in updates] + diag_specs(level),
            out_specs=pl.BlockSpec((STEP, N), lambda i, s: (i, 0)),
            scratch_shapes=[pltpu.VMEM((spans, C, 2 * N), jnp.bfloat16)],
        ),
        out_shape=jax.ShapeDtypeStruct((R, N), jnp.float32),
        cost_estimate=pl.CostEstimate(
            flops=6 * R * spans * C * N, bytes_accessed=4 * R * spans * C, transcendentals=0
        ),
        name=f"forward{level}",
    )(sub, seen, *updates, *[diag] * spans)


def backward_kernel(level, sub_ref, seen_ref, residue_ref, *refs):
    spans = 2**level
    diag_refs, refs = refs[:spans], refs[spans:]
    out_refs, total_ref = refs[:-1], refs[-1]
    step = pl.program_id(0)

    @pl.when(step == 0)
    def _():
        total_ref[...] = jnp.zeros_like(total_ref)

    high, low = halves(residue_ref[...].T)
    both = jnp.concatenate([high, low], axis=0)
    for a in range(spans):
        diag_high, diag_low = halves(diag_refs[a][0])
        one = mm(both, diag_high)
        total_ref[a] += one[:N] + one[N:] + mm(high, diag_low)

    @pl.when(step == R // STEP - 1)
    def _():
        if level == 0:
            out_refs[0][...] = total_ref[0].T
            return
        sub = sub_ref[0] % spans
        pieces = jnp.concatenate([total_ref[a] for a in range(spans)], axis=1)
        high, low = halves(pieces)
        both = jnp.concatenate([high, low], axis=0)
        for m in range(spans):
            picked = mm(both, hits(seen_ref, m, SLOTS_OF[level], spans))
            picked = (picked[:N] + picked[N:]).T
            own = total_ref[m ^ sub].T
            if level == 2:
                out_refs[2 * m][...] = picked[K:]
                out_refs[2 * m + 1][:K, :] = picked[:K]
                out_refs[2 * m + 1][K:, :] = own
            else:
                out_refs[m][:K, :] = picked
                out_refs[m][K:, :] = own


def backward(level, sub, seen, residue, diag):
    spans = 2**level
    heights = {0: [C], 1: [K + C] * 2, 2: [K, K + C] * 4}[level]
    return pl.pallas_call(
        functools.partial(backward_kernel, level),
        grid_spec=pltpu.PrefetchScalarGridSpec(
            num_scalar_prefetch=1,
            grid=(R // STEP,),
            in_specs=[whole(*seen.shape), pl.BlockSpec((STEP, N), lambda i, s: (i, 0))]
            + diag_specs(level),
            out_specs=[whole(h, N) for h in heights],
            scratch_shapes=[pltpu.VMEM((spans, N, C), jnp.float32)],
        ),
        out_shape=[jax.ShapeDtypeStruct((h, N), jnp.float32) for h in heights],
        cost_estimate=pl.CostEstimate(
            flops=6 * R * spans * C * N, bytes_accessed=4 * R * spans * C, transcendentals=0
        ),
        name=f"backward{level}",
    )(sub, seen, residue, *[diag] * spans)


def swapped(value, axis, mask):
    pairs = [(source, source ^ mask) for source in range(lax.axis_size(axis))]
    return lax.ppermute(value, axis, pairs)


def col_sum(part):
    cols = lax.axis_size("col")
    blocks = part.reshape(cols, -1, N)
    own = lax.all_to_all(blocks, "col", 0, 0).sum(0)
    full = lax.all_to_all(jnp.broadcast_to(own, blocks.shape), "col", 0, 0)
    return full.reshape(part.shape)


def row_sum(part):
    part = part + swapped(part, "row", 1)
    return part + swapped(part, "row", 2)


def on_device(pressure_rhs, diag_inverse, factor_blocks, row_lists):
    sub = lax.axis_index("sub").astype(jnp.int32).reshape(1)
    rhs = pressure_rhs[:, 0]
    diag = diag_inverse[0].transpose(1, 0, 2)
    factor = factor_blocks[:, 0]
    lists = row_lists[:, 0]
    targets = lists // S * C + lists % S - lax.axis_index("col") * C

    packed = jnp.concatenate(
        [
            rhs[1:].reshape(-1, N),
            targets.astype(jnp.float32),
            jnp.zeros((PACKED - LIST_AT - 3, N), jnp.float32),
        ]
    )
    seen = jnp.stack([packed] + [swapped(packed, "sub", m) for m in (1, 2, 3)])

    def update(slot, solved):
        return jnp.dot(factor[slot], solved, precision=mode)

    def correct(slot, picked):
        return jnp.einsum("ks,kn->sn", factor[slot], picked, precision=mode)

    y0 = col_sum(forward(0, sub, rhs[0], [], diag))
    u01 = row_sum(update(0, y0))
    u02 = update(1, y0)
    y1 = col_sum(forward(1, sub, seen, [u01, swapped(u01, "sub", 1)], diag))
    u2 = row_sum(jnp.concatenate([u02, update(2, y1)]))
    far = [swapped(u2, "sub", m) for m in (1, 2, 3)]
    y2 = col_sum(forward(2, sub, seen, [u2] + far, diag))

    out2 = backward(2, sub, seen, y2, diag)
    soon, later = list(out2[0::2]), list(out2[1::2])
    pick12 = row_sum(soon[0] + sum(swapped(soon[m], "sub", m) for m in (1, 2, 3)))
    pick12, *later = lax.optimization_barrier([pick12] + later)
    later = row_sum(later[0] + sum(swapped(later[m], "sub", m) for m in (1, 2, 3)))
    pick02, x2 = later[:K], later[K:]
    w1 = y1 - col_sum(correct(2, pick12))
    near, away = backward(1, sub, seen, w1, diag)
    mine = row_sum(near + swapped(away, "sub", 1))
    pick01, x1 = mine[:K], mine[K:]
    w0 = y0 - col_sum(correct(0, pick01) + correct(1, pick02))
    (x0,) = backward(0, sub, rhs[0], w0, diag)
    x0 = row_sum(x0)
    return jnp.stack([x0, x1, x2])[:, None]


def solution(mesh):
    in_specs = (
        P(None, "sub", "col", None),
        P("sub", "row", None, "col"),
        P(None, "sub", "col", "row"),
        P(None, "sub", "col"),
    )
    out_specs = P(None, "sub", "col", None)
    return jax.shard_map(
        on_device, mesh=mesh, in_specs=in_specs, out_specs=out_specs, check_vma=False
    )
```

time: 378 us -> 343 us (0.907)
  blocking collectives: 75.4 us -> 154 us
  local copies, waits for them, and re-layouts: 62.8 us -> 6.89 us
  waiting for transfers between devices: 116 us -> 84.1 us
  Pallas kernels: 0 us -> 29.3 us
  matrix products: 23 us -> 2.37 us
  other arithmetic: 25.3 us -> 6.97 us
  starting transfers between devices: 71 us -> 57.8 us
    all_to_all x2 -> x5, blocking collectives: 41.1 us -> 113 us  [col_sum(): own = lax.all_to_all(blocks, 'col', 0, 0).sum(0)]
    all_to_all x3 -> x0, waiting for transfers between devices: 30.6 us -> none  [col_sum(): own = lax.all_to_all(blocks, 'col', 0, 0).sum(0)]
    pallas_call x0 -> x6, Pallas kernels: none -> 29.3 us  [the longest x3 14.9 us: backward(): pl.pallas_call(functools.partial(backward_kernel, level), grid_spec=pltpu...]
    dot_general x6 -> x0, matrix products: 20.6 us -> none  [the longest x3 10.9 us: forward(): part = jnp.einsum('ias,asn->in', blocks, right, precision=mode)]
    all_to_all x1 -> x2, blocking collectives: 20.9 us -> 41.3 us  [col_sum(): full = lax.all_to_all(jnp.broadcast_to(own, blocks.shape), 'col', 0, 0)]
    broadcast_in_dim x20 -> x1, local copies, waits for them, and re-layouts: 19.7 us -> 0.01 us  [on_device(): jnp.zeros((PACKED - LIST_AT - 3, N), jnp.float32)]
    all_to_all x3 -> x0, starting transfers between devices: 17.9 us -> none  [col_sum(): own = lax.all_to_all(blocks, 'col', 0, 0).sum(0)]
    all_to_all x4 -> x3, waiting for transfers between devices: 51.5 us -> 33.7 us  [col_sum(): full = lax.all_to_all(jnp.broadcast_to(own, blocks.shape), 'col', 0, 0)]
  transfers between devices with their start and end apart: 25 -> 29, of which waited for: 19 -> 22; matrix products, arithmetic and copies ran while one was open for 13% -> 1% of each run, Pallas kernels for 0% -> 1%
where the time goes in v2:
time: 343 us; the launch traced here: 342 us
  blocking collectives  154 us (45%)
  waiting for transfers between devices  84.1 us (25%)
  starting transfers between devices  57.8 us (17%)
  Pallas kernels  29.3 us (9%)
  other arithmetic  6.97 us (2%)
  local copies, waits for them, and re-layouts  6.89 us (2%)
    all_to_all x5, blocking collectives, col_sum(): own = lax.all_to_all(blocks, 'col', 0, 0).sum(0)  113 us
    ppermute x26, waiting for transfers between devices, swapped(): return lax.ppermute(value, axis, pairs)  50.3 us
    ppermute x26, starting transfers between devices, swapped(): return lax.ppermute(value, axis, pairs)  44.6 us
    all_to_all x2, blocking collectives, col_sum(): full = lax.all_to_all(jnp.broadcast_to(own, blocks.shape), 'col', 0, 0)  41.3 us
    all_to_all x3, waiting for transfers between devices, col_sum(): full = lax.all_to_all(jnp.broadcast_to(own, blocks.shape), 'col', 0, 0)  33.7 us
    pallas_call x3, Pallas kernels, backward(): pl.pallas_call(functools.partial(backward_kernel, level), grid_spec=pltpu...  14.9 us
    pallas_call x3, Pallas kernels, forward(): pl.pallas_call(functools.partial(forward_kernel, level), grid_spec=pltpu....  14.3 us
    all_to_all x3, starting transfers between devices, col_sum(): full = lax.all_to_all(jnp.broadcast_to(own, blocks.shape), 'col', 0, 0)  13.2 us
  transfers between devices with their start and end apart: 29, of which 22 were waited for; matrix products, arithmetic and copies ran while one was open for 1% of the time, Pallas kernels for 1%

profile of v2, /device:TPU:1, one launch (start us, length us, event | category | flops | bytes accessed | tf_op | source)
XLA Modules:
  0.0 341.9 jit_solution(15936061932225073158)
XLA Ops:
  0.0 1.6 slice_bitcast_fusion.2.refs_0_.seen_ref
  1.6 3.7 %forward0.1 = f32[1024,128]{1,0:T(8,128)} custom-call(s32[1]{0:T(128)} %bitcast.sub_ref, f32[256,128]{1,0:T(8,128)} %slice_bitcast_fusion.2.refs_0_.seen_ref, f32[7,1024,256]{2,1,0:T(8,128)} %bitcast.81), custom_call_target="tpu_custom_call" | custom-call | flops 201326592 | bytes 1048576 | tf_op jit(solution)/shard_map/forward0/pallas_call | solution.py:91
  5.3 28.9 %all_to_all.50 = f32[16,64,128]{2,1,0:T(8,128)S(1)} all-to-all(f32[16,64,128]{2,1,0:T(8,128)} %bitcast.103), channel_id=1, replica_groups=mesh['sub'=4,'row'=4,'col'=16] {'col'}, dimensions={0} | all-to-all | bytes 1048576 | tf_op jit(solution)/shard_map/all_to_all | solution.py:176
  34.2 0.9 broadcast_in_dim.21
  35.1 4.7 %all-to-all-start.1 = ((f32[16,64,128]{2,1,0:T(8,128)}), f32[16,64,128]{2,1,0:T(8,128)S(1)}, u32[]{:S(2)}, u32[]{:S(2)}) async-start(f32[16,64,128]{2,1,0:T(8,128)} %broadcast_in_dim.21), calls=%async_computation.1 | async-start | bytes 1048576 | tf_op jit(solution)/shard_map/all_to_all | solution.py:177
  40.0 17.2 %all-to-all-done.1 = f32[16,64,128]{2,1,0:T(8,128)S(1)} async-done(((f32[16,64,128]{2,1,0:T(8,128)}), f32[16,64,128]{2,1,0:T(8,128)S(1)}, u32[]{:S(2)}, u32[]{:S(2)}) %all-to-all-start.1) | async-done | bytes 524320 | tf_op jit(solution)/shard_map/all_to_all | solution.py:177
  57.5 2.4 collective-permute-start.3
  60.1 2.8 collective-permute-start.2
  64.2 3.0 collective-permute-done.4
  67.2 1.2 collective-permute-start.5
  68.4 6.8 %collective-permute-done.2 = f32[520,128]{1,0:T(8,128)S(1)} collective-permute-done((f32[520,128]{1,0:T(8,128)S(1)}, f32[520,128]{1,0:T(8,128)S(1)}, u32[]{:S(2)}, u32[]{:S(2)}) %collective-permute-start.2) | collective-permute-done | bytes 266272 | tf_op jit(solution)/shard_map/ppermute | solution.py:170
  75.7 1.1 pad_maximum_fusion.refs_0_.seen_ref
  77.7 4.7 %forward1.1 = f32[1024,128]{1,0:T(8,128)} custom-call(s32[1]{0:T(128)} %bitcast.sub_ref, f32[4,520,128]{2,1,0:T(8,128)} %pad_maximum_fusion.refs_0_.seen_ref, f32[128,128]{1,0:T(8,128)} %copy-done.3, f32[128,128]{1,0:T(8,128)} %copy-done.8, f32[7,1024,256]{2,1,0:T(8,128)} %bitcast.82, f32[7,1024,256]{2,1,0:T(8,128)} %bitcast.83), custom_call_target="tpu_custom_call" | custom-call | flops 402653184 | bytes 2097152 | tf_op jit(solution)/shard_map/forward1/pallas_call | solution.py:91
  82.4 20.8 %all_to_all.51 = f32[16,64,128]{2,1,0:T(8,128)S(1)} all-to-all(f32[16,64,128]{2,1,0:T(8,128)} %bitcast.102), channel_id=1, replica_groups=mesh['sub'=4,'row'=4,'col'=16] {'col'}, dimensions={0} | all-to-all | bytes 1048576 | tf_op jit(solution)/shard_map/all_to_all | solution.py:176
  103.3 0.9 broadcast_in_dim.23
  104.2 4.2 %all-to-all-start.3 = ((f32[16,64,128]{2,1,0:T(8,128)}), f32[16,64,128]{2,1,0:T(8,128)S(1)}, u32[]{:S(2)}, u32[]{:S(2)}) async-start(f32[16,64,128]{2,1,0:T(8,128)} %broadcast_in_dim.23), calls=%async_computation.3 | async-start | bytes 1048576 | tf_op jit(solution)/shard_map/all_to_all | solution.py:177
  108.8 15.6 %all-to-all-done.3 = f32[16,64,128]{2,1,0:T(8,128)S(1)} async-done(((f32[16,64,128]{2,1,0:T(8,128)}), f32[16,64,128]{2,1,0:T(8,128)S(1)}, u32[]{:S(2)}, u32[]{:S(2)}) %all-to-all-start.3) | async-done | bytes 524320 | tf_op jit(solution)/shard_map/all_to_all | solution.py:177
  124.8 4.1 %collective-permute-start.6 = (f32[256,128]{1,0:T(8,128)S(1)}, f32[256,128]{1,0:T(8,128)S(1)}, u32[]{:S(2)}, u32[]{:S(2)}) collective-permute-start(f32[256,128]{1,0:T(8,128)S(1)} %pad_maximum_fusion.1), channel_id=1, source_target_pairs={{0,16},{16,0},{32,48},{48,32},{1,17},{17,1},{33,49},{49,33},{2,18}... | collective-permute-start | bytes 393224 | tf_op jit(solution)/shard_map/ppermute | solution.py:170
  129.0 1.0 collective-permute-done.6
  130.4 4.4 %collective-permute-done.7 = f32[256,128]{1,0:T(8,128)S(1)} collective-permute-done((f32[256,128]{1,0:T(8,128)S(1)}, f32[256,128]{1,0:T(8,128)S(1)}, u32[]{:S(2)}, u32[]{:S(2)}) %collective-permute-start.7) | collective-permute-done | bytes 131104 | tf_op jit(solution)/shard_map/ppermute | solution.py:170
  135.2 2.6 collective-permute-start.9
  137.8 0.9 collective-permute-start.10
  138.7 3.9 %collective-permute-done.9.refs_3_ = f32[256,128]{1,0:T(8,128)S(1)} collective-permute-done((f32[256,128]{1,0:T(8,128)S(1)}, f32[256,128]{1,0:T(8,128)S(1)}, u32[]{:S(2)}, u32[]{:S(2)}) %collective-permute-start.9) | collective-permute-done | bytes 131104 | tf_op jit(solution)/shard_map/ppermute | solution.py:170
  142.7 2.9 collective-permute-done.10.refs_4_
  146.2 5.9 %forward2.1 = f32[1024,128]{1,0:T(8,128)} custom-call(s32[1]{0:T(128)} %bitcast.sub_ref, f32[4,520,128]{2,1,0:T(8,128)} %pad_maximum_fusion.refs_0_.seen_ref, f32[256,128]{1,0:T(8,128)} %copy-done.1, f32[256,128]{1,0:T(8,128)} %copy-done.5, f32[256,128]{1,0:T(8,128)} %copy-done.6, f32[256,128]{1,0:T(8,128)} %copy-done.7, f32[7,1024,256]{2,1,0:T(8,128)} %bitcast.84, ...), custom_call_target="tpu_custom_call" | custom-call | flops 805306368 | bytes 4194304 | tf_op jit(solution)/shard_map/forward2/pallas_call | solution.py:91
  152.1 20.7 %all_to_all.52 = f32[16,64,128]{2,1,0:T(8,128)S(1)} all-to-all(f32[16,64,128]{2,1,0:T(8,128)} %bitcast.101), channel_id=1, replica_groups=mesh['sub'=4,'row'=4,'col'=16] {'col'}, dimensions={0} | all-to-all | bytes 1048576 | tf_op jit(solution)/shard_map/all_to_all | solution.py:176
  172.9 20.2 %all_to_all.53 = f32[16,64,128]{2,1,0:T(8,128)} all-to-all(f32[16,64,128]{2,1,0:T(8,128)S(1)} %broadcast_in_dim.24), channel_id=1, replica_groups=mesh['sub'=4,'row'=4,'col'=16] {'col'}, dimensions={0} | all-to-all | bytes 1048576 | tf_op jit(solution)/shard_map/all_to_all | solution.py:177
  193.1 6.3 %backward2.1 = (f32[128,128]{1,0:T(8,128)}, f32[384,128]{1,0:T(8,128)}, f32[128,128]{1,0:T(8,128)}, f32[384,128]{1,0:T(8,128)}, f32[128,128]{1,0:T(8,128)}, /*in...) custom-call(s32[1]{0:T(128)} %bitcast.sub_ref, f32[4,520,128]{2,1,0:T(8,128)} %pad_maximum_fusion.refs_0_.seen_ref, ...), custom_call_target="tpu_custom_call" | custom-call | flops 805306368 | bytes 4194304 | tf_op jit(solution)/shard_map/backward2/pallas_call | solution.py:150
  199.4 1.0 collective-permute-start.13
  200.3 2.9 collective-permute-start.12
  203.2 0.7 collective-permute-done.13
  203.9 1.9 collective-permute-done.12
  205.8 0.9 add_add_fusion.1
  206.7 5.4 %collective-permute-start.14 = (f32[128,128]{1,0:T(8,128)S(1)}, f32[128,128]{1,0:T(8,128)S(1)}, u32[]{:S(2)}, u32[]{:S(2)}) collective-permute-start(f32[128,128]{1,0:T(8,128)S(1)} %add_add_fusion.1), channel_id=1, source_target_pairs={{0,16},{16,0},{32,48},{48,32},{1,17},{17,1},{33,49},{49,33},{2,18}... | collective-permute-start | bytes 196616 | tf_op jit(solution)/shard_map/ppermute | solution.py:170
  212.1 0.9 collective-permute-done.14
  213.4 2.8 collective-permute-done.15
  216.7 1.0 copy.8
  217.7 20.6 %all_to_all.54 = f32[16,64,128]{2,1,0:T(8,128)S(1)} all-to-all(f32[16,64,128]{2,1,0:T(8,128)} %bitcast.104), channel_id=1, replica_groups=mesh['sub'=4,'row'=4,'col'=16] {'col'}, dimensions={0} | all-to-all | bytes 1048576 | tf_op jit(solution)/shard_map/all_to_all | solution.py:176
  238.3 0.9 broadcast_in_dim.25
  239.1 4.3 %all-to-all-start.7 = ((f32[16,64,128]{2,1,0:T(8,128)}), f32[16,64,128]{2,1,0:T(8,128)S(1)}, u32[]{:S(2)}, u32[]{:S(2)}) async-start(f32[16,64,128]{2,1,0:T(8,128)} %broadcast_in_dim.25), calls=%async_computation.7 | async-start | bytes 1048576 | tf_op jit(solution)/shard_map/all_to_all | solution.py:177
  243.4 1.2 collective-permute-start.21
  244.6 1.1 collective-permute-start.19
  245.7 1.6 collective-permute-start.20
  247.4 2.1 collective-permute-done.21
  249.5 4.1 %collective-permute-done.20 = f32[384,128]{1,0:T(8,128)S(1)} collective-permute-done((f32[384,128]{1,0:T(8,128)}, f32[384,128]{1,0:T(8,128)S(1)}, u32[]{:S(2)}, u32[]{:S(2)}) %collective-permute-start.20) | collective-permute-done | bytes 196640 | tf_op jit(solution)/shard_map/ppermute | solution.py:170
  253.6 4.2 %collective-permute-start.22 = (f32[384,128]{1,0:T(8,128)S(1)}, f32[384,128]{1,0:T(8,128)S(1)}, u32[]{:S(2)}, u32[]{:S(2)}) collective-permute-start(f32[384,128]{1,0:T(8,128)S(1)} %add_add_fusion), channel_id=1, source_target_pairs={{0,16},{16,0},{32,48},{48,32},{1,17},{17,1},{33,49},{49,33},{2,18}... | collective-permute-start | bytes 589832 | tf_op jit(solution)/shard_map/ppermute | solution.py:170
  257.8 0.9 all-to-all-done.7
  258.7 0.9 bitcast_subtract_fusion.1.residue_ref
  259.6 4.8 %backward1.1 = (f32[384,128]{1,0:T(8,128)}, f32[384,128]{1,0:T(8,128)}) custom-call(s32[1]{0:T(128)} %bitcast.sub_ref, f32[4,520,128]{2,1,0:T(8,128)} %pad_maximum_fusion.refs_0_.seen_ref, f32[1024,128]{1,0:T(8,128)} %bitcast_subtract_fusion.1.residue_ref, f32[7,1024,256]{2,1,0:T(8,128)} %bitcast.92, f32[7,1024,256]{2,1,0:T(8,128)} %bitcast.93), custom_call_target="tpu_custom_call" | custom-call | flops 402653184 | bytes 2097152 | tf_op jit(solution)/shard_map/backward1/pallas_call | solution.py:150
  264.4 1.0 collective-permute-start.16
  266.0 3.2 collective-permute-done.16
  269.2 0.9 add.84
  270.1 5.7 %collective-permute-start.17 = (f32[384,128]{1,0:T(8,128)S(1)}, f32[384,128]{1,0:T(8,128)S(1)}, u32[]{:S(2)}, u32[]{:S(2)}) collective-permute-start(f32[384,128]{1,0:T(8,128)S(1)} %add.84), channel_id=1, source_target_pairs={{0,16},{16,0},{32,48},{48,32},{1,17},{17,1},{33,49},{49,33},{2,18}... | collective-permute-start | bytes 589832 | tf_op jit(solution)/shard_map/ppermute | solution.py:170
  275.8 1.0 collective-permute-done.17
  277.7 5.3 %collective-permute-done.18 = f32[384,128]{1,0:T(8,128)S(1)} collective-permute-done((f32[384,128]{1,0:T(8,128)S(1)}, f32[384,128]{1,0:T(8,128)S(1)}, u32[]{:S(2)}, u32[]{:S(2)}) %collective-permute-start.18) | collective-permute-done | bytes 196640 | tf_op jit(solution)/shard_map/ppermute | solution.py:170
  283.7 21.9 %all_to_all.55 = f32[16,64,128]{2,1,0:T(8,128)S(1)} all-to-all(f32[16,64,128]{2,1,0:T(8,128)S(1)} %bitcast.105), channel_id=1, replica_groups=mesh['sub'=4,'row'=4,'col'=16] {'col'}, dimensions={0} | all-to-all | bytes 1048576 | tf_op jit(solution)/shard_map/all_to_all | solution.py:176
  305.8 21.2 %all_to_all.56 = f32[16,64,128]{2,1,0:T(8,128)S(1)} all-to-all(f32[16,64,128]{2,1,0:T(8,128)S(1)} %broadcast_in_dim.26), channel_id=1, replica_groups=mesh['sub'=4,'row'=4,'col'=16] {'col'}, dimensions={0} | all-to-all | bytes 1048576 | tf_op jit(solution)/shard_map/all_to_all | solution.py:177
  326.9 0.9 bitcast_subtract_fusion.residue_ref
  327.8 3.8 %backward0.1 = f32[256,128]{1,0:T(8,128)} custom-call(s32[1]{0:T(128)} %bitcast.sub_ref, f32[256,128]{1,0:T(8,128)} %slice_bitcast_fusion.2.refs_0_.seen_ref, f32[1024,128]{1,0:T(8,128)} %bitcast_subtract_fusion.residue_ref, f32[7,1024,256]{2,1,0:T(8,128)} %bitcast.94), custom_call_target="tpu_custom_call" | custom-call | flops 201326592 | bytes 1048576 | tf_op jit(solution)/shard_map/backward0/pallas_call | solution.py:150
  331.6 2.7 collective-permute-start.24
  334.2 1.2 collective-permute-done.24
  335.4 0.9 add.94
  336.8 4.4 %collective-permute-done.25 = f32[256,128]{1,0:T(8,128)S(1)} collective-permute-done((f32[256,128]{1,0:T(8,128)S(1)}, f32[256,128]{1,0:T(8,128)S(1)}, u32[]{:S(2)}, u32[]{:S(2)}) %collective-permute-start.25) | collective-permute-done | bytes 131104 | tf_op jit(solution)/shard_map/ppermute | solution.py:170
  341.1 0.8 maximum_bitcast_fusion
  (74 shorter events, 9.2 us)
Async XLA Ops:
  5.3 34.5 %copy-start.2 = (f32[3,1,256,128]{3,2,1,0:T(8,128)S(1)}, f32[3,1,256,128]{3,2,1,0:T(8,128)}, u32[]{:S(2)}) copy-start(f32[3,1,256,128]{3,2,1,0:T(8,128)} %param.4) | copy-start | bytes 1179652
  34.2 5.8 %copy-start.9 = (s32[3,1,128]{2,1,0:T(1,128)S(1)}, s32[3,1,128]{2,1,0:T(1,128)}, u32[]{:S(2)}) copy-start(s32[3,1,128]{2,1,0:T(1,128)} %param.7) | copy-start | bytes 4612
  34.2 22.9 %copy-start = (f32[3,1,128,1024]{3,2,1,0:T(8,128)S(1)}, f32[3,1,128,1024]{3,2,1,0:T(8,128)}, u32[]{:S(2)}) copy-start(f32[3,1,128,1024]{3,2,1,0:T(8,128)} %param.6) | copy-start | bytes 4718596
  35.1 22.0 %all-to-all-start.1 = ((f32[16,64,128]{2,1,0:T(8,128)}), f32[16,64,128]{2,1,0:T(8,128)S(1)}, u32[]{:S(2)}, u32[]{:S(2)}) async-start(f32[16,64,128]{2,1,0:T(8,128)} %broadcast_in_dim.21), calls=%async_computation.1 | async-start | bytes 1048576 | tf_op jit(solution)/shard_map/all_to_all | solution.py:177
  57.5 6.1 %collective-permute-start.3 = (f32[128,128]{1,0:T(8,128)S(1)}, f32[128,128]{1,0:T(8,128)S(1)}, u32[]{:S(2)}, u32[]{:S(2)}) collective-permute-start(f32[128,128]{1,0:T(8,128)S(1)} %convolution_bitcast_fusion.3), channel_id=1, source_target_pairs={{0,16},{16,0},{32,48},{48,32},{1,17},{17,1},{33,49},{49,33},{2,18}... | collective-permute-start | bytes 196616 | tf_op jit(solution)/shard_map/ppermute | solution.py:170
  60.1 15.1 %collective-permute-start.2 = (f32[520,128]{1,0:T(8,128)S(1)}, f32[520,128]{1,0:T(8,128)S(1)}, u32[]{:S(2)}, u32[]{:S(2)}) collective-permute-start(f32[520,128]{1,0:T(8,128)S(1)} %maximum_maximum_fusion), channel_id=1, source_target_pairs={{0,192},{64,128},{128,64},{192,0},{1,193},{65,129},{129,65},{193,1... | collective-permute-start | bytes 798728 | tf_op jit(solution)/shard_map/ppermute | solution.py:170
  62.9 12.2 %collective-permute-start.1 = (f32[520,128]{1,0:T(8,128)S(1)}, f32[520,128]{1,0:T(8,128)S(1)}, u32[]{:S(2)}, u32[]{:S(2)}) collective-permute-start(f32[520,128]{1,0:T(8,128)S(1)} %maximum_maximum_fusion), channel_id=1, source_target_pairs={{0,128},{64,192},{128,0},{192,64},{1,129},{65,193},{129,1},{193,65... | collective-permute-start | bytes 798728 | tf_op jit(solution)/shard_map/ppermute | solution.py:170
  63.3 12.4 %collective-permute-start = (f32[520,128]{1,0:T(8,128)S(1)}, f32[520,128]{1,0:T(8,128)S(1)}, u32[]{:S(2)}, u32[]{:S(2)}) collective-permute-start(f32[520,128]{1,0:T(8,128)S(1)} %maximum_maximum_fusion), channel_id=1, source_target_pairs={{0,64},{64,0},{128,192},{192,128},{1,65},{65,1},{129,193},{193,129... | collective-permute-start | bytes 798728 | tf_op jit(solution)/shard_map/ppermute | solution.py:170
  63.6 3.5 %collective-permute-start.4 = (f32[128,128]{1,0:T(8,128)S(1)}, f32[128,128]{1,0:T(8,128)S(1)}, u32[]{:S(2)}, u32[]{:S(2)}) collective-permute-start(f32[128,128]{1,0:T(8,128)S(1)} %add.75), channel_id=1, source_target_pairs={{0,32},{16,48},{32,0},{48,16},{1,33},{17,49},{33,1},{49,17},{2,34}... | collective-permute-start | bytes 196616 | tf_op jit(solution)/shard_map/ppermute | solution.py:170
  67.1 10.0 %copy-start.3 = (f32[128,128]{1,0:T(8,128)}, f32[128,128]{1,0:T(8,128)S(1)}, u32[]{:S(2)}) copy-start(f32[128,128]{1,0:T(8,128)S(1)} %add.76.refs_1_) | copy-start | bytes 196612
  67.2 10.0 %collective-permute-start.5 = (f32[128,128]{1,0:T(8,128)S(1)}, f32[128,128]{1,0:T(8,128)S(1)}, u32[]{:S(2)}, u32[]{:S(2)}) collective-permute-start(f32[128,128]{1,0:T(8,128)S(1)} %add.76.refs_1_), channel_id=1, source_target_pairs={{0,64},{64,0},{128,192},{192,128},{1,65},{65,1},{129,193},{193,129... | collective-permute-start | bytes 196616 | tf_op jit(solution)/shard_map/ppermute | solution.py:170
  77.1 0.6 copy-start.8
  104.2 20.3 %all-to-all-start.3 = ((f32[16,64,128]{2,1,0:T(8,128)}), f32[16,64,128]{2,1,0:T(8,128)S(1)}, u32[]{:S(2)}, u32[]{:S(2)}) async-start(f32[16,64,128]{2,1,0:T(8,128)} %broadcast_in_dim.23), calls=%async_computation.3 | async-start | bytes 1048576 | tf_op jit(solution)/shard_map/all_to_all | solution.py:177
  124.8 5.1 %collective-permute-start.6 = (f32[256,128]{1,0:T(8,128)S(1)}, f32[256,128]{1,0:T(8,128)S(1)}, u32[]{:S(2)}, u32[]{:S(2)}) collective-permute-start(f32[256,128]{1,0:T(8,128)S(1)} %pad_maximum_fusion.1), channel_id=1, source_target_pairs={{0,16},{16,0},{32,48},{48,32},{1,17},{17,1},{33,49},{49,33},{2,18}... | collective-permute-start | bytes 393224 | tf_op jit(solution)/shard_map/ppermute | solution.py:170
  130.0 4.8 %collective-permute-start.7 = (f32[256,128]{1,0:T(8,128)S(1)}, f32[256,128]{1,0:T(8,128)S(1)}, u32[]{:S(2)}, u32[]{:S(2)}) collective-permute-start(f32[256,128]{1,0:T(8,128)S(1)} %fusion.23), channel_id=1, source_target_pairs={{0,32},{16,48},{32,0},{48,16},{1,33},{17,49},{33,1},{49,17},{2,34}... | collective-permute-start | bytes 393224 | tf_op jit(solution)/shard_map/ppermute | solution.py:170
  134.8 10.8 %copy-start.1 = (f32[256,128]{1,0:T(8,128)}, f32[256,128]{1,0:T(8,128)S(1)}, u32[]{:S(2)}) copy-start(f32[256,128]{1,0:T(8,128)S(1)} %add.78.refs_1_) | copy-start | bytes 393220
  134.8 3.9 %collective-permute-start.8 = (f32[256,128]{1,0:T(8,128)S(1)}, f32[256,128]{1,0:T(8,128)S(1)}, u32[]{:S(2)}, u32[]{:S(2)}) collective-permute-start(f32[256,128]{1,0:T(8,128)S(1)} %add.78.refs_1_), channel_id=1, source_target_pairs={{0,64},{64,0},{128,192},{192,128},{1,65},{65,1},{129,193},{193,129... | collective-permute-start | bytes 393224 | tf_op jit(solution)/shard_map/ppermute | solution.py:170
  135.2 7.5 %collective-permute-start.9 = (f32[256,128]{1,0:T(8,128)S(1)}, f32[256,128]{1,0:T(8,128)S(1)}, u32[]{:S(2)}, u32[]{:S(2)}) collective-permute-start(f32[256,128]{1,0:T(8,128)S(1)} %add.78.refs_1_), channel_id=1, source_target_pairs={{0,128},{64,192},{128,0},{192,64},{1,129},{65,193},{129,1},{193,65... | collective-permute-start | bytes 393224 | tf_op jit(solution)/shard_map/ppermute | solution.py:170
  137.8 7.8 %collective-permute-start.10 = (f32[256,128]{1,0:T(8,128)S(1)}, f32[256,128]{1,0:T(8,128)S(1)}, u32[]{:S(2)}, u32[]{:S(2)}) collective-permute-start(f32[256,128]{1,0:T(8,128)S(1)} %add.78.refs_1_), channel_id=1, source_target_pairs={{0,192},{64,128},{128,64},{192,0},{1,193},{65,129},{129,65},{193,1... | collective-permute-start | bytes 393224 | tf_op jit(solution)/shard_map/ppermute | solution.py:170
  138.7 6.8 %copy-start.5 = (f32[256,128]{1,0:T(8,128)}, f32[256,128]{1,0:T(8,128)S(1)}, u32[]{:S(2)}) copy-start(f32[256,128]{1,0:T(8,128)S(1)} %collective-permute-done.8.refs_2_) | copy-start | bytes 393220
  142.7 2.9 copy-start.6
  145.6 0.6 copy-start.7
  199.4 4.5 %collective-permute-start.13 = (f32[128,128]{1,0:T(8,128)}, f32[128,128]{1,0:T(8,128)S(1)}, u32[]{:S(2)}, u32[]{:S(2)}) collective-permute-start(f32[128,128]{1,0:T(8,128)} %get-tuple-element.23), channel_id=1, source_target_pairs={{0,192},{64,128},{128,64},{192,0},{1,193},{65,129},{129,65},{193,1... | collective-permute-start | bytes 196616 | tf_op jit(solution)/shard_map/ppermute | solution.py:170
  200.3 3.6 %collective-permute-start.11 = (f32[128,128]{1,0:T(8,128)}, f32[128,128]{1,0:T(8,128)S(1)}, u32[]{:S(2)}, u32[]{:S(2)}) collective-permute-start(f32[128,128]{1,0:T(8,128)} %get-tuple-element.21), channel_id=1, source_target_pairs={{0,64},{64,0},{128,192},{192,128},{1,65},{65,1},{129,193},{193,129... | collective-permute-start | bytes 196616 | tf_op jit(solution)/shard_map/ppermute | solution.py:170
  200.3 5.5 %collective-permute-start.12 = (f32[128,128]{1,0:T(8,128)}, f32[128,128]{1,0:T(8,128)S(1)}, u32[]{:S(2)}, u32[]{:S(2)}) collective-permute-start(f32[128,128]{1,0:T(8,128)} %get-tuple-element.22), channel_id=1, source_target_pairs={{0,128},{64,192},{128,0},{192,64},{1,129},{65,193},{129,1},{193,65... | collective-permute-start | bytes 196616 | tf_op jit(solution)/shard_map/ppermute | solution.py:170
  206.7 6.3 %collective-permute-start.14 = (f32[128,128]{1,0:T(8,128)S(1)}, f32[128,128]{1,0:T(8,128)S(1)}, u32[]{:S(2)}, u32[]{:S(2)}) collective-permute-start(f32[128,128]{1,0:T(8,128)S(1)} %add_add_fusion.1), channel_id=1, source_target_pairs={{0,16},{16,0},{32,48},{48,32},{1,17},{17,1},{33,49},{49,33},{2,18}... | collective-permute-start | bytes 196616 | tf_op jit(solution)/shard_map/ppermute | solution.py:170
  213.0 3.2 collective-permute-start.15
  217.7 35.8 %copy-start.4 = (f32[384,128]{1,0:T(8,128)S(1)}, f32[384,128]{1,0:T(8,128)}, u32[]{:S(2)}) copy-start(f32[384,128]{1,0:T(8,128)} %get-tuple-element.31) | copy-start | bytes 589828
  239.1 19.6 %all-to-all-start.7 = ((f32[16,64,128]{2,1,0:T(8,128)}), f32[16,64,128]{2,1,0:T(8,128)S(1)}, u32[]{:S(2)}, u32[]{:S(2)}) async-start(f32[16,64,128]{2,1,0:T(8,128)} %broadcast_in_dim.25), calls=%async_computation.7 | async-start | bytes 1048576 | tf_op jit(solution)/shard_map/all_to_all | solution.py:177
  243.4 6.0 %collective-permute-start.21 = (f32[384,128]{1,0:T(8,128)}, f32[384,128]{1,0:T(8,128)S(1)}, u32[]{:S(2)}, u32[]{:S(2)}) collective-permute-start(f32[384,128]{1,0:T(8,128)} %get-tuple-element.34), channel_id=1, source_target_pairs={{0,192},{64,128},{128,64},{192,0},{1,193},{65,129},{129,65},{193,1... | collective-permute-start | bytes 589832 | tf_op jit(solution)/shard_map/ppermute | solution.py:170
  244.6 4.9 %collective-permute-start.19 = (f32[384,128]{1,0:T(8,128)}, f32[384,128]{1,0:T(8,128)S(1)}, u32[]{:S(2)}, u32[]{:S(2)}) collective-permute-start(f32[384,128]{1,0:T(8,128)} %get-tuple-element.32), channel_id=1, source_target_pairs={{0,64},{64,0},{128,192},{192,128},{1,65},{65,1},{129,193},{193,129... | collective-permute-start | bytes 589832 | tf_op jit(solution)/shard_map/ppermute | solution.py:170
  245.7 7.8 %collective-permute-start.20 = (f32[384,128]{1,0:T(8,128)}, f32[384,128]{1,0:T(8,128)S(1)}, u32[]{:S(2)}, u32[]{:S(2)}) collective-permute-start(f32[384,128]{1,0:T(8,128)} %get-tuple-element.33), channel_id=1, source_target_pairs={{0,128},{64,192},{128,0},{192,64},{1,129},{65,193},{129,1},{193,65... | collective-permute-start | bytes 589832 | tf_op jit(solution)/shard_map/ppermute | solution.py:170
  253.6 11.9 %collective-permute-start.22 = (f32[384,128]{1,0:T(8,128)S(1)}, f32[384,128]{1,0:T(8,128)S(1)}, u32[]{:S(2)}, u32[]{:S(2)}) collective-permute-start(f32[384,128]{1,0:T(8,128)S(1)} %add_add_fusion), channel_id=1, source_target_pairs={{0,16},{16,0},{32,48},{48,32},{1,17},{17,1},{33,49},{49,33},{2,18}... | collective-permute-start | bytes 589832 | tf_op jit(solution)/shard_map/ppermute | solution.py:170
  264.4 4.7 %collective-permute-start.16 = (f32[384,128]{1,0:T(8,128)}, f32[384,128]{1,0:T(8,128)S(1)}, u32[]{:S(2)}, u32[]{:S(2)}) collective-permute-start(f32[384,128]{1,0:T(8,128)} %get-tuple-element.30), channel_id=1, source_target_pairs={{0,64},{64,0},{128,192},{192,128},{1,65},{65,1},{129,193},{193,129... | collective-permute-start | bytes 589832 | tf_op jit(solution)/shard_map/ppermute | solution.py:170
  265.5 10.3 %collective-permute-start.23 = (f32[384,128]{1,0:T(8,128)S(1)}, f32[384,128]{1,0:T(8,128)S(1)}, u32[]{:S(2)}, u32[]{:S(2)}) collective-permute-start(f32[384,128]{1,0:T(8,128)S(1)} %add.90), channel_id=1, source_target_pairs={{0,32},{16,48},{32,0},{48,16},{1,33},{17,49},{33,1},{49,17},{2,34}... | collective-permute-start | bytes 589832 | tf_op jit(solution)/shard_map/ppermute | solution.py:170
  270.1 6.7 %collective-permute-start.17 = (f32[384,128]{1,0:T(8,128)S(1)}, f32[384,128]{1,0:T(8,128)S(1)}, u32[]{:S(2)}, u32[]{:S(2)}) collective-permute-start(f32[384,128]{1,0:T(8,128)S(1)} %add.84), channel_id=1, source_target_pairs={{0,16},{16,0},{32,48},{48,32},{1,17},{17,1},{33,49},{49,33},{2,18}... | collective-permute-start | bytes 589832 | tf_op jit(solution)/shard_map/ppermute | solution.py:170
  276.9 6.2 %collective-permute-start.18 = (f32[384,128]{1,0:T(8,128)S(1)}, f32[384,128]{1,0:T(8,128)S(1)}, u32[]{:S(2)}, u32[]{:S(2)}) collective-permute-start(f32[384,128]{1,0:T(8,128)S(1)} %add.85), channel_id=1, source_target_pairs={{0,32},{16,48},{32,0},{48,16},{1,33},{17,49},{33,1},{49,17},{2,34}... | collective-permute-start | bytes 589832 | tf_op jit(solution)/shard_map/ppermute | solution.py:170
  331.6 3.9 %collective-permute-start.24 = (f32[256,128]{1,0:T(8,128)}, f32[256,128]{1,0:T(8,128)S(1)}, u32[]{:S(2)}, u32[]{:S(2)}) collective-permute-start(f32[256,128]{1,0:T(8,128)} %backward0.1), channel_id=1, source_target_pairs={{0,16},{16,0},{32,48},{48,32},{1,17},{17,1},{33,49},{49,33},{2,18}... | collective-permute-start | bytes 393224 | tf_op jit(solution)/shard_map/ppermute | solution.py:170
  336.3 4.8 %collective-permute-start.25 = (f32[256,128]{1,0:T(8,128)S(1)}, f32[256,128]{1,0:T(8,128)S(1)}, u32[]{:S(2)}, u32[]{:S(2)}) collective-permute-start(f32[256,128]{1,0:T(8,128)S(1)} %add.94), channel_id=1, source_target_pairs={{0,32},{16,48},{32,0},{48,16},{1,33},{17,49},{33,1},{49,17},{2,34}... | collective-permute-start | bytes 393224 | tf_op jit(solution)/shard_map/ppermute | solution.py:170

commit v3 on v1

v3 whole, which is shorter than its diff:
```python
import functools

import jax
import jax.numpy as jnp
from jax import lax
from jax.experimental import pallas as pl
from jax.experimental.pallas import tpu as pltpu
from jax.sharding import PartitionSpec as P

S = 4096
N = 128
C = 256
R = 1024
K = 128
STEP = 256
LEVELS = 3
VMEM_LIMIT = 46 * 2**20
FIRST_LIMIT = 58 * 2**20
LIST_AT = 2 * C
PACKED = 2 * C + 8
mode = lax.Precision.HIGH


def halves(value):
    high = value.astype(jnp.bfloat16)
    low = (value - high.astype(jnp.float32)).astype(jnp.bfloat16)
    return high, low


def mm(a, b):
    return jnp.dot(a, b, preferred_element_type=jnp.float32)


def hits(seen_ref, place, slots, panels):
    targets = jnp.concatenate(
        [seen_ref[place, LIST_AT + t : LIST_AT + t + 1, :] for t in slots], axis=1
    ).astype(jnp.int32)
    shape = (panels * C, K * len(slots))
    rows = lax.broadcasted_iota(jnp.int32, shape, 0)
    return jnp.where(rows == targets, 1.0, 0.0).astype(jnp.bfloat16)


SLOTS_OF = {1: (0,), 2: (1, 2)}


def piece(spans, step, diag_ref, buffer_ref, sems):
    rows = pl.ds(pl.multiple_of(step * STEP, STEP), STEP)
    source = diag_ref.at[pl.ds(spans - 1, spans), rows, :]
    return pltpu.make_async_copy(source, buffer_ref.at[:, rows, :], sems.at[step])


def fetch(*refs):
    for step in range(R // STEP):
        piece(refs[0], step, *refs[1:]).start()


def forward_kernel(level, sub_ref, seen_ref, *refs):
    spans = 2**level
    update_refs, (diag_ref, out_ref, right_ref, buffer_ref, sems) = refs[:-5], refs[-5:]
    fetch(spans, diag_ref, buffer_ref, sems)
    if level == 0:
        high, low = halves(seen_ref[0])
        right_ref[0] = jnp.concatenate([high, low], axis=1)
    else:
        sub = sub_ref[0] % spans
        count = len(SLOTS_OF[level])
        total = None
        for m in range(spans):
            own = [update_refs[t * spans + m][...] for t in range(count)]
            high, low = halves(jnp.concatenate(own, axis=0))
            pair = jnp.concatenate([high, low], axis=1)
            term = mm(hits(seen_ref, m, SLOTS_OF[level], spans), pair)
            total = term if total is None else total + term
        total = total[:, :N] + total[:, N:]
        for a in range(spans):
            rhs = seen_ref[a ^ sub, (level - 1) * C : level * C, :]
            high, low = halves(rhs - total[a * C : (a + 1) * C])
            right_ref[a] = jnp.concatenate([high, low], axis=1)

    @pl.loop(0, R // STEP)
    def _(step):
        piece(spans, step, diag_ref, buffer_ref, sems).wait()
        rows = pl.ds(pl.multiple_of(step * STEP, STEP), STEP)
        wide, thin = None, None
        for a in range(spans):
            high, low = halves(buffer_ref[a, rows, :])
            one, two = mm(high, right_ref[a]), mm(low, right_ref[a, :, :N])
            wide = one if wide is None else wide + one
            thin = two if thin is None else thin + two
        out_ref[rows, :] = wide[:, :N] + wide[:, N:] + thin


def backward_kernel(level, sub_ref, seen_ref, base_ref, *refs):
    spans = 2**level
    minus = level < LEVELS - 1
    if minus:
        minus_ref, refs = refs[0], refs[1:]
    diag_ref, out_refs, (total_ref, buffer_ref, sems) = refs[0], refs[1:-3], refs[-3:]
    fetch(spans, diag_ref, buffer_ref, sems)
    total_ref[...] = jnp.zeros_like(total_ref)

    @pl.loop(0, R // STEP)
    def _(step):
        rows = pl.ds(pl.multiple_of(step * STEP, STEP), STEP)
        residue = base_ref[rows, :]
        if minus:
            residue = residue - minus_ref[rows, :]
        high, low = halves(residue.T)
        both = jnp.concatenate([high, low], axis=0)
        piece(spans, step, diag_ref, buffer_ref, sems).wait()
        for a in range(spans):
            diag_high, diag_low = halves(buffer_ref[a, rows, :])
            one = mm(both, diag_high)
            total_ref[a] += one[:N] + one[N:] + mm(high, diag_low)

    if level == 0:
        out_refs[0][...] = total_ref[0].T
        return
    sub = sub_ref[0] % spans
    pieces = jnp.concatenate([total_ref[a] for a in range(spans)], axis=1)
    high, low = halves(pieces)
    both = jnp.concatenate([high, low], axis=0)
    for m in range(spans):
        picked = mm(both, hits(seen_ref, m, SLOTS_OF[level], spans))
        picked = (picked[:N] + picked[N:]).T
        own = total_ref[m ^ sub].T
        soon_ref, later_ref = out_refs[2 * m], out_refs[2 * m + 1]
        if level == 2:
            soon_ref[...] = picked[K:]
            later_ref[:K, :] = picked[:K]
            later_ref[K:, :] = own
        else:
            soon_ref[...] = picked
            later_ref[...] = own


def call(kernel, level, heights, scratch, sub, *arrays):
    spans = 2**level
    vmem = pl.BlockSpec(memory_space=pltpu.VMEM)
    limit = FIRST_LIMIT if len(arrays) == 2 else VMEM_LIMIT
    specs = [vmem] * (len(arrays) - 1) + [pl.BlockSpec(memory_space=pltpu.HBM)]
    return pl.pallas_call(
        functools.partial(kernel, level),
        in_specs=[pl.BlockSpec(memory_space=pltpu.SMEM)] + specs,
        out_specs=[vmem] * len(heights),
        scratch_shapes=[
            scratch,
            pltpu.VMEM((spans, R, C), jnp.float32),
            pltpu.SemaphoreType.DMA((R // STEP,)),
        ],
        out_shape=[jax.ShapeDtypeStruct((h, N), jnp.float32) for h in heights],
        compiler_params=pltpu.CompilerParams(vmem_limit_bytes=limit),
        cost_estimate=pl.CostEstimate(
            flops=6 * R * spans * C * N, bytes_accessed=4 * R * spans * C, transcendentals=0
        ),
        name=f"{kernel.__name__}{level}",
    )(sub, *arrays)


def forward(level, sub, seen, updates, diag):
    scratch = pltpu.VMEM((2**level, C, 2 * N), jnp.bfloat16)
    return call(forward_kernel, level, [R], scratch, sub, seen, *updates, diag)[0]


def backward(level, sub, seen, residue, diag):
    heights = {0: [C], 1: [K, C] * 2, 2: [K, K + C] * 4}[level]
    scratch = pltpu.VMEM((2**level, N, C), jnp.float32)
    return call(backward_kernel, level, heights, scratch, sub, seen, *residue, diag)


def correct_kernel(slots, *refs):
    picked_refs, factor_ref, out_ref = refs[:-2], refs[-2], refs[-1]
    pairs = []
    for index in range(len(slots)):
        own, core, chip, both = (ref[...] for ref in picked_refs[4 * index : 4 * index + 4])
        pairs.append(halves((own + core) + (chip + both)))
    @pl.loop(0, R // STEP)
    def _(step):
        cols = pl.ds(pl.multiple_of(step * STEP, STEP), STEP)
        total = None
        for slot, (picked_high, picked_low) in zip(slots, pairs):
            high, low = halves(factor_ref[slot, :, cols].T)
            wide = mm(high, jnp.concatenate([picked_high, picked_low], axis=1))
            term = wide[:, :N] + wide[:, N:] + mm(low, picked_high)
            total = term if total is None else total + term
        out_ref[cols, :] = total


def correct(slots, picked, factor):
    vmem = pl.BlockSpec(memory_space=pltpu.VMEM)
    return pl.pallas_call(
        functools.partial(correct_kernel, slots),
        in_specs=[vmem] * (len(picked) + 1),
        out_specs=vmem,
        out_shape=jax.ShapeDtypeStruct((R, N), jnp.float32),
        compiler_params=pltpu.CompilerParams(vmem_limit_bytes=8 * 2**20),
        cost_estimate=pl.CostEstimate(
            flops=6 * R * K * N * len(slots), bytes_accessed=4 * R * K, transcendentals=0
        ),
        name=f"correct{len(slots)}",
    )(*picked, factor)


def swapped(value, axis, mask):
    pairs = [(source, source ^ mask) for source in range(lax.axis_size(axis))]
    return lax.ppermute(value, axis, pairs)


def col_sum(part, held=None):
    blocks = part.reshape(lax.axis_size("col"), -1, N)
    own = lax.all_to_all(blocks, "col", 0, 0).sum(0)
    if held is not None:
        own, held = lax.optimization_barrier((own, held))
    full = lax.all_to_all(jnp.broadcast_to(own, blocks.shape), "col", 0, 0)
    full = full.reshape(part.shape)
    return full if held is None else (full, held)


def row_parts(part):
    return [part] + [swapped(part, "row", m) for m in (1, 2, 3)]


def row_sum(part):
    own, core, chip, both = row_parts(part)
    return (own + core) + (chip + both)


def sub_parts(part):
    return [part] + [swapped(part, "sub", m) for m in (1, 2, 3)]


def sub_sum(parts):
    return parts[0] + sum(swapped(parts[m], "sub", m) for m in range(1, len(parts)))


def on_device(pressure_rhs, diag_inverse, factor_blocks, row_lists):
    sub = lax.axis_index("sub").astype(jnp.int32).reshape(1)
    rhs = pressure_rhs[:, 0]
    diag = diag_inverse[0].transpose(1, 0, 2)
    factor = factor_blocks[:, 0]
    lists = row_lists[:, 0]
    targets = lists // S * C + lists % S - lax.axis_index("col") * C

    packed = jnp.concatenate(
        [
            rhs[1:].reshape(-1, N),
            targets.astype(jnp.float32),
            jnp.zeros((PACKED - LIST_AT - 3, N), jnp.float32),
        ]
    )
    def update(slot, solved):
        return jnp.dot(factor[slot], solved, precision=mode)

    y0, packed = col_sum(forward(0, sub, rhs, [], diag), packed)
    seen = jnp.stack(sub_parts(packed))
    u01 = row_sum(update(0, y0))
    part1 = forward(1, sub, seen, [u01, swapped(u01, "sub", 1)], diag)
    part1, u02 = lax.optimization_barrier((part1, update(1, y0)))
    u02 = sub_parts(row_sum(u02))
    y1 = col_sum(part1)
    u12 = sub_parts(row_sum(update(2, y1)))
    y2 = col_sum(forward(2, sub, seen, u02 + u12, diag))

    out2 = backward(2, sub, seen, [y2], diag)
    pick12 = row_parts(sub_sum(out2[0::2]))
    part1, *later = lax.optimization_barrier([correct((2,), pick12, factor)] + list(out2[1::2]))
    later = row_sum(sub_sum(later))
    pick02, x2 = later[:K], later[K:]
    out1 = backward(1, sub, seen, [y1, col_sum(part1)], diag)
    pick01 = row_parts(sub_sum(out1[0::2]))
    zero = jnp.zeros_like(pick02)
    part0, *later = lax.optimization_barrier(
        [correct((0, 1), pick01 + [pick02, zero, zero, zero], factor)] + list(out1[1::2])
    )
    x1 = row_sum(sub_sum(later))
    (x0,) = backward(0, sub, rhs, [y0, col_sum(part0)], diag)
    x0 = row_sum(x0)
    return jnp.stack([x0, x1, x2])[:, None]


def solution(mesh):
    in_specs = (
        P(None, "sub", "col", None),
        P("sub", "row", None, "col"),
        P(None, "sub", "col", "row"),
        P(None, "sub", "col"),
    )
    out_specs = P(None, "sub", "col", None)
    return jax.shard_map(
        on_device, mesh=mesh, in_specs=in_specs, out_specs=out_specs, check_vma=False
    )
```

time: 378 us -> 327 us (0.87)
  local copies, waits for them, and re-layouts: 62.8 us -> 7.4 us
  waiting for transfers between devices: 116 us -> 84.5 us
  blocking collectives: 75.4 us -> 103 us
  starting transfers between devices: 71 us -> 93.8 us
  Pallas kernels: 0 us -> 21.9 us
  matrix products: 23 us -> 2.78 us
  other arithmetic: 25.3 us -> 11.3 us
    all_to_all x2 -> x4, blocking collectives: 41.1 us -> 84.2 us  [col_sum(): own = lax.all_to_all(blocks, 'col', 0, 0).sum(0)]
    ppermute x18 -> x42, starting transfers between devices: 35.8 us -> 64 us  [swapped(): return lax.ppermute(value, axis, pairs)]
    pallas_call x0 -> x8, Pallas kernels: none -> 21.9 us  [the longest x6 19.5 us: call(): pl.pallas_call(functools.partial(kernel, level), in_specs=[pl.BlockSpec(m...]
    dot_general x9 -> x0, matrix products: 21.7 us -> none  [the longest x3 10.9 us: forward(): part = jnp.einsum('ias,asn->in', blocks, right, precision=mode)]
    broadcast_in_dim x20 -> x2, local copies, waits for them, and re-layouts: 19.7 us -> 0.01 us  [the longest x1 0.01 us: on_device(): zero = jnp.zeros_like(pick02)]
    all_to_all x4, waiting for transfers between devices: 51.5 us -> 33.2 us  [col_sum(): full = lax.all_to_all(jnp.broadcast_to(own, blocks.shape), 'col', 0, 0)]
    reduce_sum x20 -> x0, local copies, waits for them, and re-layouts: 15.9 us -> none  [pick(): return jnp.where(keep[..., None], parts, 0.0).sum((0, 2))]
    all_to_all x3 -> x1, waiting for transfers between devices: 30.6 us -> 16.9 us  [col_sum(): own = lax.all_to_all(blocks, 'col', 0, 0).sum(0)]
  transfers between devices with their start and end apart: 25 -> 47, of which waited for: 19 -> 22; matrix products, arithmetic and copies ran while one was open for 13% -> 3% of each run, Pallas kernels for 0% -> 2%
where the time goes in v3:
time: 327 us; the launch traced here: 326 us
  blocking collectives  103 us (31%)
  starting transfers between devices  93.8 us (29%)
  waiting for transfers between devices  84.5 us (26%)
  Pallas kernels  21.9 us (7%)
  other arithmetic  11.3 us (3%)
  local copies, waits for them, and re-layouts  7.4 us (2%)
    all_to_all x4, blocking collectives, col_sum(): own = lax.all_to_all(blocks, 'col', 0, 0).sum(0)  84.2 us
    ppermute x42, starting transfers between devices, swapped(): return lax.ppermute(value, axis, pairs)  64 us
    ppermute x42, waiting for transfers between devices, swapped(): return lax.ppermute(value, axis, pairs)  34.4 us
    all_to_all x4, waiting for transfers between devices, col_sum(): full = lax.all_to_all(jnp.broadcast_to(own, blocks.shape), 'col', 0, 0)  33.2 us
    pallas_call x6, Pallas kernels, call(): pl.pallas_call(functools.partial(kernel, level), in_specs=[pl.BlockSpec(m...  19.5 us
    all_to_all x1, blocking collectives, col_sum(): full = lax.all_to_all(jnp.broadcast_to(own, blocks.shape), 'col', 0, 0)  19.2 us
    all_to_all x4, starting transfers between devices, col_sum(): full = lax.all_to_all(jnp.broadcast_to(own, blocks.shape), 'col', 0, 0)  18.2 us
    all_to_all x1, waiting for transfers between devices, col_sum(): own = lax.all_to_all(blocks, 'col', 0, 0).sum(0)  16.9 us
  transfers between devices with their start and end apart: 47, of which 22 were waited for; matrix products, arithmetic and copies ran while one was open for 3% of the time, Pallas kernels for 2%

profile of v3, /device:TPU:1, one launch (start us, length us, event | category | flops | bytes accessed | tf_op | source)
XLA Modules:
  0.0 325.6 jit_solution(5109780416833406305)
XLA Ops:
  0.0 3.8 %forward_kernel0.1 = f32[1024,128]{1,0:T(8,128)} custom-call(s32[1]{0:T(128)} %bitcast.sub_ref, f32[3,256,128]{2,1,0:T(8,128)} %bitcast.70, f32[7,1024,256]{2,1,0:T(8,128)} %bitcast.78), custom_call_target="tpu_custom_call" | custom-call | flops 201326592 | bytes 1048576 | tf_op jit(solution)/shard_map/forward_kernel0/pallas_call | solution.py:142
  3.8 11.6 %all-to-all-start = ((f32[16,64,128]{2,1,0:T(8,128)}), f32[16,64,128]{2,1,0:T(8,128)S(1)}, u32[]{:S(2)}, u32[]{:S(2)}) async-start(f32[16,64,128]{2,1,0:T(8,128)} %bitcast.84), calls=%async_computation | async-start | bytes 1048576 | tf_op jit(solution)/shard_map/all_to_all | solution.py:211
  15.7 16.9 %all-to-all-done = f32[16,64,128]{2,1,0:T(8,128)S(1)} async-done(((f32[16,64,128]{2,1,0:T(8,128)}), f32[16,64,128]{2,1,0:T(8,128)S(1)}, u32[]{:S(2)}, u32[]{:S(2)}) %all-to-all-start) | async-done | bytes 524320 | tf_op jit(solution)/shard_map/all_to_all | solution.py:211
  33.5 4.7 %all-to-all-start.1 = ((f32[16,64,128]{2,1,0:T(8,128)}), f32[16,64,128]{2,1,0:T(8,128)S(1)}, u32[]{:S(2)}, u32[]{:S(2)}) async-start(f32[16,64,128]{2,1,0:T(8,128)} %broadcast_in_dim.25), calls=%async_computation.1 | async-start | bytes 1048576 | tf_op jit(solution)/shard_map/all_to_all | solution.py:214
  38.2 2.8 collective-permute-start.2
  41.7 13.8 %all-to-all-done.1 = f32[16,64,128]{2,1,0:T(8,128)S(1)} async-done(((f32[16,64,128]{2,1,0:T(8,128)}), f32[16,64,128]{2,1,0:T(8,128)S(1)}, u32[]{:S(2)}, u32[]{:S(2)}) %all-to-all-start.1) | async-done | bytes 524320 | tf_op jit(solution)/shard_map/all_to_all | solution.py:214
  56.3 3.7 %collective-permute-start.5 = (f32[128,128]{1,0:T(8,128)S(1)}, f32[128,128]{1,0:T(8,128)S(1)}, u32[]{:S(2)}, u32[]{:S(2)}) collective-permute-start(f32[128,128]{1,0:T(8,128)S(1)} %convolution_bitcast_fusion.2), channel_id=1, source_target_pairs={{0,48},{16,32},{32,16},{48,0},{1,49},{17,33},{33,17},{49,1},{2,50}... | collective-permute-start | bytes 196616 | tf_op jit(solution)/shard_map/ppermute | solution.py:206
  60.9 1.3 pad_maximum_fusion.seen_ref
  62.1 1.2 collective-permute-done.5
  63.4 1.4 collective-permute-start.6
  65.8 1.3 collective-permute-done.6.refs_1_
  67.1 2.3 forward_kernel1.1
  69.4 20.4 %all_to_all.50 = f32[16,64,128]{2,1,0:T(8,128)} all-to-all(f32[16,64,128]{2,1,0:T(8,128)S(1)} %bitcast.76), channel_id=1, replica_groups=mesh['sub'=4,'row'=4,'col'=16] {'col'}, dimensions={0} | all-to-all | bytes 1048576 | tf_op jit(solution)/shard_map/all_to_all | solution.py:211
  89.8 1.7 reduce_sum.46
  91.5 1.6 broadcast_in_dim.26
  93.1 4.8 %all-to-all-start.3 = ((f32[16,64,128]{2,1,0:T(8,128)}), f32[16,64,128]{2,1,0:T(8,128)}, u32[]{:S(2)}, u32[]{:S(2)}) async-start(f32[16,64,128]{2,1,0:T(8,128)} %broadcast_in_dim.26), calls=%async_computation.3 | async-start | bytes 1048576 | tf_op jit(solution)/shard_map/all_to_all | solution.py:214
  98.0 4.3 %collective-permute-start.9 = (f32[128,128]{1,0:T(8,128)}, f32[128,128]{1,0:T(8,128)}, u32[]{:S(2)}, u32[]{:S(2)}) collective-permute-start(f32[128,128]{1,0:T(8,128)} %convolution_bitcast_fusion.1), channel_id=1, source_target_pairs={{0,48},{16,32},{32,16},{48,0},{1,49},{17,33},{33,17},{49,1},{2,50}... | collective-permute-start | bytes 196616 | tf_op jit(solution)/shard_map/ppermute | solution.py:206
  102.3 11.2 %all-to-all-done.3 = f32[16,64,128]{2,1,0:T(8,128)} async-done(((f32[16,64,128]{2,1,0:T(8,128)}), f32[16,64,128]{2,1,0:T(8,128)}, u32[]{:S(2)}, u32[]{:S(2)}) %all-to-all-start.3) | async-done | bytes 524320 | tf_op jit(solution)/shard_map/all_to_all | solution.py:214
  113.5 1.4 convolution_bitcast_fusion
  115.0 5.9 %collective-permute-start.15 = (f32[128,128]{1,0:T(8,128)S(1)}, f32[128,128]{1,0:T(8,128)S(1)}, u32[]{:S(2)}, u32[]{:S(2)}) collective-permute-start(f32[128,128]{1,0:T(8,128)S(1)} %convolution_bitcast_fusion), channel_id=1, source_target_pairs={{0,48},{16,32},{32,16},{48,0},{1,49},{17,33},{33,17},{49,1},{2,50}... | collective-permute-start | bytes 196616 | tf_op jit(solution)/shard_map/ppermute | solution.py:206
  121.9 1.4 collective-permute-start.10
  123.3 2.6 collective-permute-start.11
  126.1 3.8 %collective-permute-start.17 = (f32[128,128]{1,0:T(8,128)S(1)}, f32[128,128]{1,0:T(8,128)S(1)}, u32[]{:S(2)}, u32[]{:S(2)}) collective-permute-start(f32[128,128]{1,0:T(8,128)S(1)} %add_add_fusion.3.refs_4_), channel_id=1, source_target_pairs={{0,128},{64,192},{128,0},{192,64},{1,129},{65,193},{129,1},{193,65... | collective-permute-start | bytes 196616 | tf_op jit(solution)/shard_map/ppermute | solution.py:206
  130.4 2.0 collective-permute-done.17.refs_6_
  132.4 2.4 collective-permute-done.18.refs_7_
  134.8 3.1 forward_kernel2.1
  137.8 18.8 %all_to_all.51 = f32[16,64,128]{2,1,0:T(8,128)} all-to-all(f32[16,64,128]{2,1,0:T(8,128)S(1)} %bitcast.74), channel_id=1, replica_groups=mesh['sub'=4,'row'=4,'col'=16] {'col'}, dimensions={0} | all-to-all | bytes 1048576 | tf_op jit(solution)/shard_map/all_to_all | solution.py:211
  156.6 1.7 reduce_sum.47
  159.1 19.2 %all_to_all.52 = f32[16,64,128]{2,1,0:T(8,128)S(1)} all-to-all(f32[16,64,128]{2,1,0:T(8,128)S(1)} %broadcast_in_dim.27), channel_id=1, replica_groups=mesh['sub'=4,'row'=4,'col'=16] {'col'}, dimensions={0} | all-to-all | bytes 1048576 | tf_op jit(solution)/shard_map/all_to_all | solution.py:214
  178.3 4.0 %backward_kernel2.1 = (f32[128,128]{1,0:T(8,128)S(1)}, f32[384,128]{1,0:T(8,128)S(1)}, f32[128,128]{1,0:T(8,128)S(1)}, f32[384,128]{1,0:T(8,128)S(1)}, f32[128,1...) custom-call(s32[1]{0:T(128)} %bitcast.sub_ref, ...), custom_call_target="tpu_custom_call" | custom-call | flops 805306368 | bytes 4194304 | tf_op jit(solution)/shard_map/backward_kernel2/pallas_call | solution.py:142
  183.0 3.0 collective-permute-start.21
  186.0 1.3 collective-permute-start.20
  187.6 1.5 collective-permute-done.19
  189.1 1.5 collective-permute-done.20
  190.6 5.2 %collective-permute-start.22 = (f32[128,128]{1,0:T(8,128)S(1)}, f32[128,128]{1,0:T(8,128)S(1)}, u32[]{:S(2)}, u32[]{:S(2)}) collective-permute-start(f32[128,128]{1,0:T(8,128)S(1)} %add_add_fusion.2.refs_0_), channel_id=1, source_target_pairs={{0,16},{16,0},{32,48},{48,32},{1,17},{17,1},{33,49},{49,33},{2,18}... | collective-permute-start | bytes 196616 | tf_op jit(solution)/shard_map/ppermute | solution.py:206
  195.8 1.7 collective-permute-start.24
  197.6 1.8 collective-permute-done.23.refs_2_
  199.4 1.7 collective-permute-done.24.refs_3_
  201.0 1.1 correct1.1
  202.2 21.1 %all_to_all.53 = f32[16,64,128]{2,1,0:T(8,128)} all-to-all(f32[16,64,128]{2,1,0:T(8,128)S(1)} %bitcast.77), channel_id=1, replica_groups=mesh['sub'=4,'row'=4,'col'=16] {'col'}, dimensions={0} | all-to-all | bytes 1048576 | tf_op jit(solution)/shard_map/all_to_all | solution.py:211
  223.2 1.7 reduce_sum.48
  224.9 1.6 broadcast_in_dim.28
  226.5 4.2 %all-to-all-start.7 = ((f32[16,64,128]{2,1,0:T(8,128)}), f32[16,64,128]{2,1,0:T(8,128)}, u32[]{:S(2)}, u32[]{:S(2)}) async-start(f32[16,64,128]{2,1,0:T(8,128)} %broadcast_in_dim.28), calls=%async_computation.7 | async-start | bytes 1048576 | tf_op jit(solution)/shard_map/all_to_all | solution.py:214
  230.8 1.7 collective-permute-start.31
  232.8 1.9 collective-permute-start.30
  234.7 2.1 collective-permute-done.31
  237.6 3.9 %collective-permute-done.30 = f32[384,128]{1,0:T(8,128)S(1)} collective-permute-done((f32[384,128]{1,0:T(8,128)}, f32[384,128]{1,0:T(8,128)S(1)}, u32[]{:S(2)}, u32[]{:S(2)}) %collective-permute-start.30) | collective-permute-done | bytes 196640 | tf_op jit(solution)/shard_map/ppermute | solution.py:206
  241.5 1.6 add_add_fusion.1
  243.1 5.2 %collective-permute-start.34 = (f32[384,128]{1,0:T(8,128)}, f32[384,128]{1,0:T(8,128)}, u32[]{:S(2)}, u32[]{:S(2)}) collective-permute-start(f32[384,128]{1,0:T(8,128)} %add_add_fusion.1), channel_id=1, source_target_pairs={{0,48},{16,32},{32,16},{48,0},{1,49},{17,33},{33,17},{49,1},{2,50}... | collective-permute-start | bytes 589832 | tf_op jit(solution)/shard_map/ppermute | solution.py:206
  248.3 4.1 %backward_kernel1.1 = (f32[128,128]{1,0:T(8,128)S(1)}, f32[256,128]{1,0:T(8,128)S(1)}, f32[128,128]{1,0:T(8,128)S(1)}, f32[256,128]{1,0:T(8,128)S(1)}) custom-call(s32[1]{0:T(128)} %bitcast.sub_ref, f32[4,520,128]{2,1,0:T(8,128)S(1)} %pad_maximum_fusion.seen_ref, f32[1024,128]{1,0:T(8,128)} %bitcast.17.base_ref, f32[1024,128]{1,0:T(8,128)} %bitcast.24.refs_0_, ...), custom_call_target="tpu_custom_call" | custom-call | flops 402653184 | bytes 2097152 | tf_op jit(solution)/shard_map/backward_kernel1/pallas_call | solution.py:142
  253.1 2.6 collective-permute-done.25
  255.6 4.1 %collective-permute-start.26 = (f32[128,128]{1,0:T(8,128)S(1)}, f32[128,128]{1,0:T(8,128)S(1)}, u32[]{:S(2)}, u32[]{:S(2)}) collective-permute-start(f32[128,128]{1,0:T(8,128)S(1)} %add.102.refs_0_), channel_id=1, source_target_pairs={{0,16},{16,0},{32,48},{48,32},{1,17},{17,1},{33,49},{49,33},{2,18}... | collective-permute-start | bytes 196616 | tf_op jit(solution)/shard_map/ppermute | solution.py:206
  259.7 1.7 collective-permute-start.28
  261.5 1.3 add_add_fusion
  263.3 1.7 collective-permute-done.28.refs_3_
  265.0 1.3 correct2.1
  266.3 23.9 %all_to_all.54 = f32[16,64,128]{2,1,0:T(8,128)S(1)} all-to-all(f32[16,64,128]{2,1,0:T(8,128)S(1)} %bitcast.75), channel_id=1, replica_groups=mesh['sub'=4,'row'=4,'col'=16] {'col'}, dimensions={0} | all-to-all | bytes 1048576 | tf_op jit(solution)/shard_map/all_to_all | solution.py:211
  291.1 4.5 %all-to-all-start.9 = ((f32[16,64,128]{2,1,0:T(8,128)}), f32[16,64,128]{2,1,0:T(8,128)S(1)}, u32[]{:S(2)}, u32[]{:S(2)}) async-start(f32[16,64,128]{2,1,0:T(8,128)} %broadcast_in_dim.30), calls=%async_computation.9 | async-start | bytes 1048576 | tf_op jit(solution)/shard_map/all_to_all | solution.py:214
  296.2 3.3 %collective-permute-done.38 = f32[256,128]{1,0:T(8,128)S(1)} collective-permute-done((f32[256,128]{1,0:T(8,128)S(1)}, f32[256,128]{1,0:T(8,128)S(1)}, u32[]{:S(2)}, u32[]{:S(2)}) %collective-permute-start.38) | collective-permute-done | bytes 131104 | tf_op jit(solution)/shard_map/ppermute | solution.py:206
  299.9 4.3 %collective-permute-start.41 = (f32[256,128]{1,0:T(8,128)S(1)}, f32[256,128]{1,0:T(8,128)S(1)}, u32[]{:S(2)}, u32[]{:S(2)}) collective-permute-start(f32[256,128]{1,0:T(8,128)S(1)} %add.112), channel_id=1, source_target_pairs={{0,48},{16,32},{32,16},{48,0},{1,49},{17,33},{33,17},{49,1},{2,50}... | collective-permute-start | bytes 393224 | tf_op jit(solution)/shard_map/ppermute | solution.py:206
  304.2 8.2 %all-to-all-done.9 = f32[16,64,128]{2,1,0:T(8,128)S(1)} async-done(((f32[16,64,128]{2,1,0:T(8,128)}), f32[16,64,128]{2,1,0:T(8,128)S(1)}, u32[]{:S(2)}, u32[]{:S(2)}) %all-to-all-start.9) | async-done | bytes 524320 | tf_op jit(solution)/shard_map/all_to_all | solution.py:214
  312.3 2.3 backward_kernel0.1
  314.9 4.4 %collective-permute-start.37 = (f32[256,128]{1,0:T(8,128)S(1)}, f32[256,128]{1,0:T(8,128)S(1)}, u32[]{:S(2)}, u32[]{:S(2)}) collective-permute-start(f32[256,128]{1,0:T(8,128)S(1)} %backward_kernel0.1), channel_id=1, source_target_pairs={{0,48},{16,32},{32,16},{48,0},{1,49},{17,33},{33,17},{49,1},{2,50}... | collective-permute-start | bytes 393224 | tf_op jit(solution)/shard_map/ppermute | solution.py:206
  319.4 5.3 %collective-permute-done.37 = f32[256,128]{1,0:T(8,128)S(1)} collective-permute-done((f32[256,128]{1,0:T(8,128)S(1)}, f32[256,128]{1,0:T(8,128)S(1)}, u32[]{:S(2)}, u32[]{:S(2)}) %collective-permute-start.37) | collective-permute-done | bytes 131104 | tf_op jit(solution)/shard_map/ppermute | solution.py:206
  (106 shorter events, 13.5 us)
Async XLA Ops:
  0.0 15.4 %copy-start.1 = (f32[3,1,256,128]{3,2,1,0:T(8,128)S(1)}, f32[3,1,256,128]{3,2,1,0:T(8,128)}, u32[]{:S(2)}) copy-start(f32[3,1,256,128]{3,2,1,0:T(8,128)} %param.4) | copy-start | bytes 1179652
  3.8 11.7 %copy-start.14 = (s32[3,1,128]{2,1,0:T(1,128)S(1)}, s32[3,1,128]{2,1,0:T(1,128)}, u32[]{:S(2)}) copy-start(s32[3,1,128]{2,1,0:T(1,128)} %param.7) | copy-start | bytes 4612
  3.8 28.8 %all-to-all-start = ((f32[16,64,128]{2,1,0:T(8,128)}), f32[16,64,128]{2,1,0:T(8,128)S(1)}, u32[]{:S(2)}, u32[]{:S(2)}) async-start(f32[16,64,128]{2,1,0:T(8,128)} %bitcast.84), calls=%async_computation | async-start | bytes 1048576 | tf_op jit(solution)/shard_map/all_to_all | solution.py:211
  15.4 40.1 %copy-start = (f32[3,1,128,1024]{3,2,1,0:T(8,128)S(1)}, f32[3,1,128,1024]{3,2,1,0:T(8,128)}, u32[]{:S(2)}) copy-start(f32[3,1,128,1024]{3,2,1,0:T(8,128)} %param.6) | copy-start | bytes 4718596
  15.7 40.2 %copy-start.10 = (f32[520,128]{1,0:T(8,128)}, f32[520,128]{1,0:T(8,128)S(1)}, u32[]{:S(2)}) copy-start(f32[520,128]{1,0:T(8,128)S(1)} %maximum_maximum_fusion) | copy-start | bytes 798724
  33.5 22.0 %all-to-all-start.1 = ((f32[16,64,128]{2,1,0:T(8,128)}), f32[16,64,128]{2,1,0:T(8,128)S(1)}, u32[]{:S(2)}, u32[]{:S(2)}) async-start(f32[16,64,128]{2,1,0:T(8,128)} %broadcast_in_dim.25), calls=%async_computation.1 | async-start | bytes 1048576 | tf_op jit(solution)/shard_map/all_to_all | solution.py:214
  38.2 21.8 %collective-permute-start.2 = (f32[520,128]{1,0:T(8,128)S(1)}, f32[520,128]{1,0:T(8,128)S(1)}, u32[]{:S(2)}, u32[]{:S(2)}) collective-permute-start(f32[520,128]{1,0:T(8,128)S(1)} %maximum_maximum_fusion), channel_id=1, source_target_pairs={{0,192},{64,128},{128,64},{192,0},{1,193},{65,129},{129,65},{193,1... | collective-permute-start | bytes 798728 | tf_op jit(solution)/shard_map/ppermute | solution.py:206
  41.0 19.0 %collective-permute-start.1 = (f32[520,128]{1,0:T(8,128)S(1)}, f32[520,128]{1,0:T(8,128)S(1)}, u32[]{:S(2)}, u32[]{:S(2)}) collective-permute-start(f32[520,128]{1,0:T(8,128)S(1)} %maximum_maximum_fusion), channel_id=1, source_target_pairs={{0,128},{64,192},{128,0},{192,64},{1,129},{65,193},{129,1},{193,65... | collective-permute-start | bytes 798728 | tf_op jit(solution)/shard_map/ppermute | solution.py:206
  41.4 18.7 %collective-permute-start = (f32[520,128]{1,0:T(8,128)S(1)}, f32[520,128]{1,0:T(8,128)S(1)}, u32[]{:S(2)}, u32[]{:S(2)}) collective-permute-start(f32[520,128]{1,0:T(8,128)S(1)} %maximum_maximum_fusion), channel_id=1, source_target_pairs={{0,64},{64,0},{128,192},{192,128},{1,65},{65,1},{129,193},{193,129... | collective-permute-start | bytes 798728 | tf_op jit(solution)/shard_map/ppermute | solution.py:206
  55.9 6.2 %collective-permute-start.4 = (f32[128,128]{1,0:T(8,128)S(1)}, f32[128,128]{1,0:T(8,128)S(1)}, u32[]{:S(2)}, u32[]{:S(2)}) collective-permute-start(f32[128,128]{1,0:T(8,128)S(1)} %convolution_bitcast_fusion.2), channel_id=1, source_target_pairs={{0,32},{16,48},{32,0},{48,16},{1,33},{17,49},{33,1},{49,17},{2,34}... | collective-permute-start | bytes 196616 | tf_op jit(solution)/shard_map/ppermute | solution.py:206
  56.3 7.0 %collective-permute-start.5 = (f32[128,128]{1,0:T(8,128)S(1)}, f32[128,128]{1,0:T(8,128)S(1)}, u32[]{:S(2)}, u32[]{:S(2)}) collective-permute-start(f32[128,128]{1,0:T(8,128)S(1)} %convolution_bitcast_fusion.2), channel_id=1, source_target_pairs={{0,48},{16,32},{32,16},{48,0},{1,49},{17,33},{33,17},{49,1},{2,50}... | collective-permute-start | bytes 196616 | tf_op jit(solution)/shard_map/ppermute | solution.py:206
  60.0 0.7 copy-start.11
  60.0 3.3 %collective-permute-start.3 = (f32[128,128]{1,0:T(8,128)S(1)}, f32[128,128]{1,0:T(8,128)S(1)}, u32[]{:S(2)}, u32[]{:S(2)}) collective-permute-start(f32[128,128]{1,0:T(8,128)S(1)} %convolution_bitcast_fusion.2), channel_id=1, source_target_pairs={{0,16},{16,0},{32,48},{48,32},{1,17},{17,1},{33,49},{49,33},{2,18}... | collective-permute-start | bytes 196616 | tf_op jit(solution)/shard_map/ppermute | solution.py:206
  60.0 0.8 copy-start.12
  60.0 0.8 copy-start.13
  63.4 3.7 %collective-permute-start.6 = (f32[128,128]{1,0:T(8,128)S(1)}, f32[128,128]{1,0:T(8,128)S(1)}, u32[]{:S(2)}, u32[]{:S(2)}) collective-permute-start(f32[128,128]{1,0:T(8,128)S(1)} %add_add_fusion.5.refs_0_), channel_id=1, source_target_pairs={{0,64},{64,0},{128,192},{192,128},{1,65},{65,1},{129,193},{193,129... | collective-permute-start | bytes 196616 | tf_op jit(solution)/shard_map/ppermute | solution.py:206
  93.1 20.4 %all-to-all-start.3 = ((f32[16,64,128]{2,1,0:T(8,128)}), f32[16,64,128]{2,1,0:T(8,128)}, u32[]{:S(2)}, u32[]{:S(2)}) async-start(f32[16,64,128]{2,1,0:T(8,128)} %broadcast_in_dim.26), calls=%async_computation.3 | async-start | bytes 1048576 | tf_op jit(solution)/shard_map/all_to_all | solution.py:214
  97.9 23.1 %collective-permute-start.8 = (f32[128,128]{1,0:T(8,128)}, f32[128,128]{1,0:T(8,128)}, u32[]{:S(2)}, u32[]{:S(2)}) collective-permute-start(f32[128,128]{1,0:T(8,128)} %convolution_bitcast_fusion.1), channel_id=1, source_target_pairs={{0,32},{16,48},{32,0},{48,16},{1,33},{17,49},{33,1},{49,17},{2,34}... | collective-permute-start | bytes 196616 | tf_op jit(solution)/shard_map/ppermute | solution.py:206
  98.0 23.0 %collective-permute-start.9 = (f32[128,128]{1,0:T(8,128)}, f32[128,128]{1,0:T(8,128)}, u32[]{:S(2)}, u32[]{:S(2)}) collective-permute-start(f32[128,128]{1,0:T(8,128)} %convolution_bitcast_fusion.1), channel_id=1, source_target_pairs={{0,48},{16,32},{32,16},{48,0},{1,49},{17,33},{33,17},{49,1},{2,50}... | collective-permute-start | bytes 196616 | tf_op jit(solution)/shard_map/ppermute | solution.py:206
  102.3 18.7 %collective-permute-start.7 = (f32[128,128]{1,0:T(8,128)}, f32[128,128]{1,0:T(8,128)}, u32[]{:S(2)}, u32[]{:S(2)}) collective-permute-start(f32[128,128]{1,0:T(8,128)} %convolution_bitcast_fusion.1), channel_id=1, source_target_pairs={{0,16},{16,0},{32,48},{48,32},{1,17},{17,1},{33,49},{49,33},{2,18}... | collective-permute-start | bytes 196616 | tf_op jit(solution)/shard_map/ppermute | solution.py:206
  114.9 11.0 %collective-permute-start.14 = (f32[128,128]{1,0:T(8,128)S(1)}, f32[128,128]{1,0:T(8,128)S(1)}, u32[]{:S(2)}, u32[]{:S(2)}) collective-permute-start(f32[128,128]{1,0:T(8,128)S(1)} %convolution_bitcast_fusion), channel_id=1, source_target_pairs={{0,32},{16,48},{32,0},{48,16},{1,33},{17,49},{33,1},{49,17},{2,34}... | collective-permute-start | bytes 196616 | tf_op jit(solution)/shard_map/ppermute | solution.py:206
  115.0 10.9 %collective-permute-start.15 = (f32[128,128]{1,0:T(8,128)S(1)}, f32[128,128]{1,0:T(8,128)S(1)}, u32[]{:S(2)}, u32[]{:S(2)}) collective-permute-start(f32[128,128]{1,0:T(8,128)S(1)} %convolution_bitcast_fusion), channel_id=1, source_target_pairs={{0,48},{16,32},{32,16},{48,0},{1,49},{17,33},{33,17},{49,1},{2,50}... | collective-permute-start | bytes 196616 | tf_op jit(solution)/shard_map/ppermute | solution.py:206
  121.0 5.0 %collective-permute-start.13 = (f32[128,128]{1,0:T(8,128)S(1)}, f32[128,128]{1,0:T(8,128)S(1)}, u32[]{:S(2)}, u32[]{:S(2)}) collective-permute-start(f32[128,128]{1,0:T(8,128)S(1)} %convolution_bitcast_fusion), channel_id=1, source_target_pairs={{0,16},{16,0},{32,48},{48,32},{1,17},{17,1},{33,49},{49,33},{2,18}... | collective-permute-start | bytes 196616 | tf_op jit(solution)/shard_map/ppermute | solution.py:206
  121.9 8.0 %collective-permute-start.10 = (f32[128,128]{1,0:T(8,128)S(1)}, f32[128,128]{1,0:T(8,128)S(1)}, u32[]{:S(2)}, u32[]{:S(2)}) collective-permute-start(f32[128,128]{1,0:T(8,128)S(1)} %add_add_fusion.4.refs_0_), channel_id=1, source_target_pairs={{0,64},{64,0},{128,192},{192,128},{1,65},{65,1},{129,193},{193,129... | collective-permute-start | bytes 196616 | tf_op jit(solution)/shard_map/ppermute | solution.py:206
  123.3 6.6 %collective-permute-start.11 = (f32[128,128]{1,0:T(8,128)S(1)}, f32[128,128]{1,0:T(8,128)S(1)}, u32[]{:S(2)}, u32[]{:S(2)}) collective-permute-start(f32[128,128]{1,0:T(8,128)S(1)} %add_add_fusion.4.refs_0_), channel_id=1, source_target_pairs={{0,128},{64,192},{128,0},{192,64},{1,129},{65,193},{129,1},{193,65... | collective-permute-start | bytes 196616 | tf_op jit(solution)/shard_map/ppermute | solution.py:206
  125.9 4.5 %collective-permute-start.12 = (f32[128,128]{1,0:T(8,128)S(1)}, f32[128,128]{1,0:T(8,128)S(1)}, u32[]{:S(2)}, u32[]{:S(2)}) collective-permute-start(f32[128,128]{1,0:T(8,128)S(1)} %add_add_fusion.4.refs_0_), channel_id=1, source_target_pairs={{0,192},{64,128},{128,64},{192,0},{1,193},{65,129},{129,65},{193,1... | collective-permute-start | bytes 196616 | tf_op jit(solution)/shard_map/ppermute | solution.py:206
  126.0 4.4 %collective-permute-start.16 = (f32[128,128]{1,0:T(8,128)S(1)}, f32[128,128]{1,0:T(8,128)S(1)}, u32[]{:S(2)}, u32[]{:S(2)}) collective-permute-start(f32[128,128]{1,0:T(8,128)S(1)} %add_add_fusion.3.refs_4_), channel_id=1, source_target_pairs={{0,64},{64,0},{128,192},{192,128},{1,65},{65,1},{129,193},{193,129... | collective-permute-start | bytes 196616 | tf_op jit(solution)/shard_map/ppermute | solution.py:206
  126.1 6.3 %collective-permute-start.17 = (f32[128,128]{1,0:T(8,128)S(1)}, f32[128,128]{1,0:T(8,128)S(1)}, u32[]{:S(2)}, u32[]{:S(2)}) collective-permute-start(f32[128,128]{1,0:T(8,128)S(1)} %add_add_fusion.3.refs_4_), channel_id=1, source_target_pairs={{0,128},{64,192},{128,0},{192,64},{1,129},{65,193},{129,1},{193,65... | collective-permute-start | bytes 196616 | tf_op jit(solution)/shard_map/ppermute | solution.py:206
  129.9 4.8 %collective-permute-start.18 = (f32[128,128]{1,0:T(8,128)S(1)}, f32[128,128]{1,0:T(8,128)S(1)}, u32[]{:S(2)}, u32[]{:S(2)}) collective-permute-start(f32[128,128]{1,0:T(8,128)S(1)} %add_add_fusion.3.refs_4_), channel_id=1, source_target_pairs={{0,192},{64,128},{128,64},{192,0},{1,193},{65,129},{129,65},{193,1... | collective-permute-start | bytes 196616 | tf_op jit(solution)/shard_map/ppermute | solution.py:206
  182.3 0.7 copy-start.7
  183.0 19.1 %copy-start.2 = (f32[384,128]{1,0:T(8,128)}, f32[384,128]{1,0:T(8,128)S(1)}, u32[]{:S(2)}) copy-start(f32[384,128]{1,0:T(8,128)S(1)} %get-tuple-element.44) | copy-start | bytes 589828
  183.0 19.1 %copy-start.5 = (f32[384,128]{1,0:T(8,128)}, f32[384,128]{1,0:T(8,128)S(1)}, u32[]{:S(2)}) copy-start(f32[384,128]{1,0:T(8,128)S(1)} %get-tuple-element.46) | copy-start | bytes 589828
  183.0 19.2 %copy-start.6 = (f32[384,128]{1,0:T(8,128)}, f32[384,128]{1,0:T(8,128)S(1)}, u32[]{:S(2)}) copy-start(f32[384,128]{1,0:T(8,128)S(1)} %get-tuple-element.45) | copy-start | bytes 589828
  183.0 4.6 %collective-permute-start.21 = (f32[128,128]{1,0:T(8,128)S(1)}, f32[128,128]{1,0:T(8,128)S(1)}, u32[]{:S(2)}, u32[]{:S(2)}) collective-permute-start(f32[128,128]{1,0:T(8,128)S(1)} %get-tuple-element.36), channel_id=1, source_target_pairs={{0,192},{64,128},{128,64},{192,0},{1,193},{65,129},{129,65},{193,1... | collective-permute-start | bytes 196616 | tf_op jit(solution)/shard_map/ppermute | solution.py:206
  186.0 3.1 collective-permute-start.19
  186.0 4.6 %collective-permute-start.20 = (f32[128,128]{1,0:T(8,128)S(1)}, f32[128,128]{1,0:T(8,128)S(1)}, u32[]{:S(2)}, u32[]{:S(2)}) collective-permute-start(f32[128,128]{1,0:T(8,128)S(1)} %get-tuple-element.35), channel_id=1, source_target_pairs={{0,128},{64,192},{128,0},{192,64},{1,129},{65,193},{129,1},{193,65... | collective-permute-start | bytes 196616 | tf_op jit(solution)/shard_map/ppermute | solution.py:206
  190.6 6.9 %collective-permute-start.22 = (f32[128,128]{1,0:T(8,128)S(1)}, f32[128,128]{1,0:T(8,128)S(1)}, u32[]{:S(2)}, u32[]{:S(2)}) collective-permute-start(f32[128,128]{1,0:T(8,128)S(1)} %add_add_fusion.2.refs_0_), channel_id=1, source_target_pairs={{0,16},{16,0},{32,48},{48,32},{1,17},{17,1},{33,49},{49,33},{2,18}... | collective-permute-start | bytes 196616 | tf_op jit(solution)/shard_map/ppermute | solution.py:206
  195.8 3.5 %collective-permute-start.23 = (f32[128,128]{1,0:T(8,128)S(1)}, f32[128,128]{1,0:T(8,128)S(1)}, u32[]{:S(2)}, u32[]{:S(2)}) collective-permute-start(f32[128,128]{1,0:T(8,128)S(1)} %add_add_fusion.2.refs_0_), channel_id=1, source_target_pairs={{0,32},{16,48},{32,0},{48,16},{1,33},{17,49},{33,1},{49,17},{2,34}... | collective-permute-start | bytes 196616 | tf_op jit(solution)/shard_map/ppermute | solution.py:206
  195.8 5.2 %collective-permute-start.24 = (f32[128,128]{1,0:T(8,128)S(1)}, f32[128,128]{1,0:T(8,128)S(1)}, u32[]{:S(2)}, u32[]{:S(2)}) collective-permute-start(f32[128,128]{1,0:T(8,128)S(1)} %add_add_fusion.2.refs_0_), channel_id=1, source_target_pairs={{0,48},{16,32},{32,16},{48,0},{1,49},{17,33},{33,17},{49,1},{2,50}... | collective-permute-start | bytes 196616 | tf_op jit(solution)/shard_map/ppermute | solution.py:206
  226.5 21.8 %all-to-all-start.7 = ((f32[16,64,128]{2,1,0:T(8,128)}), f32[16,64,128]{2,1,0:T(8,128)}, u32[]{:S(2)}, u32[]{:S(2)}) async-start(f32[16,64,128]{2,1,0:T(8,128)} %broadcast_in_dim.28), calls=%async_computation.7 | async-start | bytes 1048576 | tf_op jit(solution)/shard_map/all_to_all | solution.py:214
  230.8 6.0 %collective-permute-start.31 = (f32[384,128]{1,0:T(8,128)}, f32[384,128]{1,0:T(8,128)S(1)}, u32[]{:S(2)}, u32[]{:S(2)}) collective-permute-start(f32[384,128]{1,0:T(8,128)} %copy-done.7), channel_id=1, source_target_pairs={{0,192},{64,128},{128,64},{192,0},{1,193},{65,129},{129,65},{193,1... | collective-permute-start | bytes 589832 | tf_op jit(solution)/shard_map/ppermute | solution.py:206
  232.5 5.1 %collective-permute-start.29 = (f32[384,128]{1,0:T(8,128)}, f32[384,128]{1,0:T(8,128)S(1)}, u32[]{:S(2)}, u32[]{:S(2)}) collective-permute-start(f32[384,128]{1,0:T(8,128)} %copy-done.6), channel_id=1, source_target_pairs={{0,64},{64,0},{128,192},{192,128},{1,65},{65,1},{129,193},{193,129... | collective-permute-start | bytes 589832 | tf_op jit(solution)/shard_map/ppermute | solution.py:206
  232.8 8.7 %collective-permute-start.30 = (f32[384,128]{1,0:T(8,128)}, f32[384,128]{1,0:T(8,128)S(1)}, u32[]{:S(2)}, u32[]{:S(2)}) collective-permute-start(f32[384,128]{1,0:T(8,128)} %copy-done.5), channel_id=1, source_target_pairs={{0,128},{64,192},{128,0},{192,64},{1,129},{65,193},{129,1},{193,65... | collective-permute-start | bytes 589832 | tf_op jit(solution)/shard_map/ppermute | solution.py:206
  243.1 16.6 %collective-permute-start.33 = (f32[384,128]{1,0:T(8,128)}, f32[384,128]{1,0:T(8,128)}, u32[]{:S(2)}, u32[]{:S(2)}) collective-permute-start(f32[384,128]{1,0:T(8,128)} %add_add_fusion.1), channel_id=1, source_target_pairs={{0,32},{16,48},{32,0},{48,16},{1,33},{17,49},{33,1},{49,17},{2,34}... | collective-permute-start | bytes 589832 | tf_op jit(solution)/shard_map/ppermute | solution.py:206
  243.1 18.3 %collective-permute-start.34 = (f32[384,128]{1,0:T(8,128)}, f32[384,128]{1,0:T(8,128)}, u32[]{:S(2)}, u32[]{:S(2)}) collective-permute-start(f32[384,128]{1,0:T(8,128)} %add_add_fusion.1), channel_id=1, source_target_pairs={{0,48},{16,32},{32,16},{48,0},{1,49},{17,33},{33,17},{49,1},{2,50}... | collective-permute-start | bytes 589832 | tf_op jit(solution)/shard_map/ppermute | solution.py:206
  248.3 13.2 %collective-permute-start.32 = (f32[384,128]{1,0:T(8,128)}, f32[384,128]{1,0:T(8,128)}, u32[]{:S(2)}, u32[]{:S(2)}) collective-permute-start(f32[384,128]{1,0:T(8,128)} %add_add_fusion.1), channel_id=1, source_target_pairs={{0,16},{16,0},{32,48},{48,32},{1,17},{17,1},{33,49},{49,33},{2,18}... | collective-permute-start | bytes 589832 | tf_op jit(solution)/shard_map/ppermute | solution.py:206
  252.4 13.9 %copy-start.3 = (f32[256,128]{1,0:T(8,128)}, f32[256,128]{1,0:T(8,128)S(1)}, u32[]{:S(2)}) copy-start(f32[256,128]{1,0:T(8,128)S(1)} %get-tuple-element.51) | copy-start | bytes 393220
  252.4 13.9 %copy-start.8 = (f32[256,128]{1,0:T(8,128)}, f32[256,128]{1,0:T(8,128)S(1)}, u32[]{:S(2)}) copy-start(f32[256,128]{1,0:T(8,128)S(1)} %get-tuple-element.52) | copy-start | bytes 393220
  252.4 3.2 collective-permute-start.25
  255.6 7.1 %collective-permute-start.26 = (f32[128,128]{1,0:T(8,128)S(1)}, f32[128,128]{1,0:T(8,128)S(1)}, u32[]{:S(2)}, u32[]{:S(2)}) collective-permute-start(f32[128,128]{1,0:T(8,128)S(1)} %add.102.refs_0_), channel_id=1, source_target_pairs={{0,16},{16,0},{32,48},{48,32},{1,17},{17,1},{33,49},{49,33},{2,18}... | collective-permute-start | bytes 196616 | tf_op jit(solution)/shard_map/ppermute | solution.py:206
  259.7 3.5 %collective-permute-start.27 = (f32[128,128]{1,0:T(8,128)S(1)}, f32[128,128]{1,0:T(8,128)S(1)}, u32[]{:S(2)}, u32[]{:S(2)}) collective-permute-start(f32[128,128]{1,0:T(8,128)S(1)} %add.102.refs_0_), channel_id=1, source_target_pairs={{0,32},{16,48},{32,0},{48,16},{1,33},{17,49},{33,1},{49,17},{2,34}... | collective-permute-start | bytes 196616 | tf_op jit(solution)/shard_map/ppermute | solution.py:206
  259.7 5.2 %collective-permute-start.28 = (f32[128,128]{1,0:T(8,128)S(1)}, f32[128,128]{1,0:T(8,128)S(1)}, u32[]{:S(2)}, u32[]{:S(2)}) collective-permute-start(f32[128,128]{1,0:T(8,128)S(1)} %add.102.refs_0_), channel_id=1, source_target_pairs={{0,48},{16,32},{32,16},{48,0},{1,49},{17,33},{33,17},{49,1},{2,50}... | collective-permute-start | bytes 196616 | tf_op jit(solution)/shard_map/ppermute | solution.py:206
  266.3 29.3 %copy-start.9 = (f32[256,128]{1,0:T(8,128)S(1)}, f32[256,128]{1,0:T(8,128)}, u32[]{:S(2)}) copy-start(f32[256,128]{1,0:T(8,128)} %copy-done.8) | copy-start | bytes 393220
  266.3 33.2 %copy-start.4 = (f32[256,128]{1,0:T(8,128)S(1)}, f32[256,128]{1,0:T(8,128)}, u32[]{:S(2)}) copy-start(f32[256,128]{1,0:T(8,128)} %copy-done.3) | copy-start | bytes 393220
  291.1 21.2 %all-to-all-start.9 = ((f32[16,64,128]{2,1,0:T(8,128)}), f32[16,64,128]{2,1,0:T(8,128)S(1)}, u32[]{:S(2)}, u32[]{:S(2)}) async-start(f32[16,64,128]{2,1,0:T(8,128)} %broadcast_in_dim.30), calls=%async_computation.9 | async-start | bytes 1048576 | tf_op jit(solution)/shard_map/all_to_all | solution.py:214
  295.6 3.9 %collective-permute-start.38 = (f32[256,128]{1,0:T(8,128)S(1)}, f32[256,128]{1,0:T(8,128)S(1)}, u32[]{:S(2)}, u32[]{:S(2)}) collective-permute-start(f32[256,128]{1,0:T(8,128)S(1)} %copy-done.9), channel_id=1, source_target_pairs={{0,64},{64,0},{128,192},{192,128},{1,65},{65,1},{129,193},{193,129... | collective-permute-start | bytes 393224 | tf_op jit(solution)/shard_map/ppermute | solution.py:206
  299.5 19.8 %collective-permute-start.40 = (f32[256,128]{1,0:T(8,128)S(1)}, f32[256,128]{1,0:T(8,128)S(1)}, u32[]{:S(2)}, u32[]{:S(2)}) collective-permute-start(f32[256,128]{1,0:T(8,128)S(1)} %add.112), channel_id=1, source_target_pairs={{0,32},{16,48},{32,0},{48,16},{1,33},{17,49},{33,1},{49,17},{2,34}... | collective-permute-start | bytes 393224 | tf_op jit(solution)/shard_map/ppermute | solution.py:206
  299.9 19.5 %collective-permute-start.41 = (f32[256,128]{1,0:T(8,128)S(1)}, f32[256,128]{1,0:T(8,128)S(1)}, u32[]{:S(2)}, u32[]{:S(2)}) collective-permute-start(f32[256,128]{1,0:T(8,128)S(1)} %add.112), channel_id=1, source_target_pairs={{0,48},{16,32},{32,16},{48,0},{1,49},{17,33},{33,17},{49,1},{2,50}... | collective-permute-start | bytes 393224 | tf_op jit(solution)/shard_map/ppermute | solution.py:206
  304.1 15.2 %collective-permute-start.39 = (f32[256,128]{1,0:T(8,128)S(1)}, f32[256,128]{1,0:T(8,128)S(1)}, u32[]{:S(2)}, u32[]{:S(2)}) collective-permute-start(f32[256,128]{1,0:T(8,128)S(1)} %add.112), channel_id=1, source_target_pairs={{0,16},{16,0},{32,48},{48,32},{1,17},{17,1},{33,49},{49,33},{2,18}... | collective-permute-start | bytes 393224 | tf_op jit(solution)/shard_map/ppermute | solution.py:206
  314.7 4.7 %collective-permute-start.36 = (f32[256,128]{1,0:T(8,128)S(1)}, f32[256,128]{1,0:T(8,128)S(1)}, u32[]{:S(2)}, u32[]{:S(2)}) collective-permute-start(f32[256,128]{1,0:T(8,128)S(1)} %backward_kernel0.1), channel_id=1, source_target_pairs={{0,32},{16,48},{32,0},{48,16},{1,33},{17,49},{33,1},{49,17},{2,34}... | collective-permute-start | bytes 393224 | tf_op jit(solution)/shard_map/ppermute | solution.py:206
  314.9 9.8 %collective-permute-start.37 = (f32[256,128]{1,0:T(8,128)S(1)}, f32[256,128]{1,0:T(8,128)S(1)}, u32[]{:S(2)}, u32[]{:S(2)}) collective-permute-start(f32[256,128]{1,0:T(8,128)S(1)} %backward_kernel0.1), channel_id=1, source_target_pairs={{0,48},{16,32},{32,16},{48,0},{1,49},{17,33},{33,17},{49,1},{2,50}... | collective-permute-start | bytes 393224 | tf_op jit(solution)/shard_map/ppermute | solution.py:206
  319.3 5.4 %collective-permute-start.35 = (f32[256,128]{1,0:T(8,128)S(1)}, f32[256,128]{1,0:T(8,128)S(1)}, u32[]{:S(2)}, u32[]{:S(2)}) collective-permute-start(f32[256,128]{1,0:T(8,128)S(1)} %backward_kernel0.1), channel_id=1, source_target_pairs={{0,16},{16,0},{32,48},{48,32},{1,17},{17,1},{33,49},{49,33},{2,18}... | collective-permute-start | bytes 393224 | tf_op jit(solution)/shard_map/ppermute | solution.py:206

commit v4 on v3

--- a/solution.py
+++ b/solution.py
@@ -15,7 +15,7 @@
 STEP = 256
 LEVELS = 3
 VMEM_LIMIT = 46 * 2**20
-FIRST_LIMIT = 58 * 2**20
+FIRST_LIMIT = 48 * 2**20
 LIST_AT = 2 * C
 PACKED = 2 * C + 8
 mode = lax.Precision.HIGH
@@ -63,11 +63,14 @@
         right_ref[0] = jnp.concatenate([high, low], axis=1)
     else:
         sub = sub_ref[0] % spans
-        count = len(SLOTS_OF[level])
         total = None
         for m in range(spans):
-            own = [update_refs[t * spans + m][...] for t in range(count)]
-            high, low = halves(jnp.concatenate(own, axis=0))
+            if level == 1:
+                own = update_refs[m][...]
+            else:
+                early = update_refs[0][m * K : (m + 1) * K, :]
+                own = jnp.concatenate([early, update_refs[m + 1][...]], axis=0)
+            high, low = halves(own)
             pair = jnp.concatenate([high, low], axis=1)
             term = mm(hits(seen_ref, m, SLOTS_OF[level], spans), pair)
             total = term if total is None else total + term
@@ -206,14 +209,31 @@
     return lax.ppermute(value, axis, pairs)
 
 
-def col_sum(part, held=None):
+def fold_kernel(parts_ref, out_ref):
+    total = parts_ref[0]
+    for place in range(1, parts_ref.shape[0]):
+        total = total + parts_ref[place]
+    for place in range(parts_ref.shape[0]):
+        out_ref[place] = total
+
+
+def fold(parts):
+    vmem = pl.BlockSpec(memory_space=pltpu.VMEM)
+    return pl.pallas_call(
+        fold_kernel,
+        in_specs=[vmem],
+        out_specs=vmem,
+        out_shape=jax.ShapeDtypeStruct(parts.shape, jnp.float32),
+        compiler_params=pltpu.CompilerParams(vmem_limit_bytes=4 * 2**20),
+        name="fold",
+    )(parts)
+
+
+def col_sum(part, *held):
     blocks = part.reshape(lax.axis_size("col"), -1, N)
-    own = lax.all_to_all(blocks, "col", 0, 0).sum(0)
-    if held is not None:
-        own, held = lax.optimization_barrier((own, held))
-    full = lax.all_to_all(jnp.broadcast_to(own, blocks.shape), "col", 0, 0)
-    full = full.reshape(part.shape)
-    return full if held is None else (full, held)
+    own, *held = lax.optimization_barrier((fold(lax.all_to_all(blocks, "col", 0, 0)), *held))
+    full = lax.all_to_all(own, "col", 0, 0).reshape(part.shape)
+    return (full, *held)
 
 
 def row_parts(part):
@@ -256,24 +276,24 @@
     u01 = row_sum(update(0, y0))
     part1 = forward(1, sub, seen, [u01, swapped(u01, "sub", 1)], diag)
     part1, u02 = lax.optimization_barrier((part1, update(1, y0)))
-    u02 = sub_parts(row_sum(u02))
-    y1 = col_sum(part1)
+    y1, u02 = col_sum(part1, row_sum(u02))
+    y1, u02 = lax.optimization_barrier((y1, jnp.concatenate(sub_parts(u02))))
     u12 = sub_parts(row_sum(update(2, y1)))
-    y2 = col_sum(forward(2, sub, seen, u02 + u12, diag))
+    (y2,) = col_sum(forward(2, sub, seen, [u02] + u12, diag))
 
     out2 = backward(2, sub, seen, [y2], diag)
     pick12 = row_parts(sub_sum(out2[0::2]))
     part1, *later = lax.optimization_barrier([correct((2,), pick12, factor)] + list(out2[1::2]))
     later = row_sum(sub_sum(later))
     pick02, x2 = later[:K], later[K:]
-    out1 = backward(1, sub, seen, [y1, col_sum(part1)], diag)
+    out1 = backward(1, sub, seen, [y1, *col_sum(part1)], diag)
     pick01 = row_parts(sub_sum(out1[0::2]))
     zero = jnp.zeros_like(pick02)
     part0, *later = lax.optimization_barrier(
         [correct((0, 1), pick01 + [pick02, zero, zero, zero], factor)] + list(out1[1::2])
     )
     x1 = row_sum(sub_sum(later))
-    (x0,) = backward(0, sub, rhs, [y0, col_sum(part0)], diag)
+    (x0,) = backward(0, sub, rhs, [y0, *col_sum(part0)], diag)
     x0 = row_sum(x0)
     return jnp.stack([x0, x1, x2])[:, None]
 

time: 327 us -> 320 us (0.979)
  blocking collectives: 103 us -> 84.6 us
  waiting for transfers between devices: 84.5 us -> 99.6 us
    all_to_all x5 -> x4, blocking collectives: 103 us -> 84.6 us  [the longest x3 63.9 us: col_sum(): lax.all_to_all(blocks, 'col', 0, 0)]
    ppermute x42, waiting for transfers between devices: 34.4 us -> 46.1 us  [swapped(): return lax.ppermute(value, axis, pairs)]
    broadcast_in_dim x5 -> x0, local copies, waits for them, and re-layouts: 5.74 us -> none  [col_sum(): full = lax.all_to_all(jnp.broadcast_to(own, blocks.shape), 'col', 0, 0)]
    reduce_sum x5 -> x0, other arithmetic: 5.11 us -> none  [col_sum(): own = lax.all_to_all(blocks, 'col', 0, 0).sum(0)]
    all_to_all x5 -> x6, starting transfers between devices: 29.8 us -> 34 us  [the longest x4 18.2 us: col_sum(): full = lax.all_to_all(own, 'col', 0, 0).reshape(part.shape)]
    ppermute x42, starting transfers between devices: 64 us -> 60.4 us  [swapped(): return lax.ppermute(value, axis, pairs)]
    all_to_all x5 -> x6, waiting for transfers between devices: 50.1 us -> 53.5 us  [the longest x4 28.3 us: col_sum(): full = lax.all_to_all(own, 'col', 0, 0).reshape(part.shape)]
  transfers between devices with their start and end apart: 47 -> 48, of which waited for: 22 -> 27; matrix products, arithmetic and copies ran while one was open for 3% -> 3% of each run, Pallas kernels for 2% -> 2%
where the time goes in v4:
time: 320 us; the launch traced here: 319 us
  waiting for transfers between devices  99.6 us (31%)
  starting transfers between devices  94.5 us (30%)
  blocking collectives  84.6 us (26%)
  Pallas kernels  23.9 us (7%)
  other arithmetic  8.27 us (3%)
  local copies, waits for them, and re-layouts  4.4 us (1%)
    all_to_all x3, blocking collectives, col_sum(): lax.all_to_all(blocks, 'col', 0, 0)  63.9 us
    ppermute x42, starting transfers between devices, swapped(): return lax.ppermute(value, axis, pairs)  60.4 us
    ppermute x42, waiting for transfers between devices, swapped(): return lax.ppermute(value, axis, pairs)  46.1 us
    all_to_all x4, waiting for transfers between devices, col_sum(): full = lax.all_to_all(own, 'col', 0, 0).reshape(part.shape)  28.3 us
    all_to_all x2, waiting for transfers between devices, col_sum(): lax.all_to_all(blocks, 'col', 0, 0)  25.3 us
    all_to_all x1, blocking collectives, col_sum(): full = lax.all_to_all(own, 'col', 0, 0).reshape(part.shape)  20.7 us
    pallas_call x6, Pallas kernels, call(): pl.pallas_call(functools.partial(kernel, level), in_specs=[pl.BlockSpec(m...  18.5 us
    all_to_all x4, starting transfers between devices, col_sum(): full = lax.all_to_all(own, 'col', 0, 0).reshape(part.shape)  18.2 us
  transfers between devices with their start and end apart: 48, of which 27 were waited for; matrix products, arithmetic and copies ran while one was open for 3% of the time, Pallas kernels for 2%

profile of v4, /device:TPU:1, one launch (start us, length us, event | category | flops | bytes accessed | tf_op | source)
XLA Modules:
  0.0 318.6 jit_solution(11920472837125752929)
XLA Ops:
  1.0 2.8 forward_kernel0.1
  3.8 11.6 %all-to-all-start = ((f32[16,64,128]{2,1,0:T(8,128)}), f32[16,64,128]{2,1,0:T(8,128)S(1)}, u32[]{:S(2)}, u32[]{:S(2)}) async-start(f32[16,64,128]{2,1,0:T(8,128)} %bitcast.4), calls=%async_computation | async-start | bytes 1048576 | tf_op jit(solution)/shard_map/all_to_all | solution.py:234
  15.7 16.9 %all-to-all-done.parts_ref = f32[16,64,128]{2,1,0:T(8,128)S(1)} async-done(((f32[16,64,128]{2,1,0:T(8,128)}), f32[16,64,128]{2,1,0:T(8,128)S(1)}, u32[]{:S(2)}, u32[]{:S(2)}) %all-to-all-start) | async-done | bytes 524320 | tf_op jit(solution)/shard_map/all_to_all | solution.py:234
  33.5 4.7 %all-to-all-start.1 = ((f32[16,64,128]{2,1,0:T(8,128)}), f32[16,64,128]{2,1,0:T(8,128)S(1)}, u32[]{:S(2)}, u32[]{:S(2)}) async-start(f32[16,64,128]{2,1,0:T(8,128)} %fold.5), calls=%async_computation.1 | async-start | bytes 1048576 | tf_op jit(solution)/shard_map/all_to_all | solution.py:235
  38.2 2.8 collective-permute-start.2
  41.7 13.8 %all-to-all-done.1 = f32[16,64,128]{2,1,0:T(8,128)S(1)} async-done(((f32[16,64,128]{2,1,0:T(8,128)}), f32[16,64,128]{2,1,0:T(8,128)S(1)}, u32[]{:S(2)}, u32[]{:S(2)}) %all-to-all-start.1) | async-done | bytes 524320 | tf_op jit(solution)/shard_map/all_to_all | solution.py:235
  56.3 3.7 %collective-permute-start.5 = (f32[128,128]{1,0:T(8,128)S(1)}, f32[128,128]{1,0:T(8,128)S(1)}, u32[]{:S(2)}, u32[]{:S(2)}) collective-permute-start(f32[128,128]{1,0:T(8,128)S(1)} %convolution_bitcast_fusion.2), channel_id=1, source_target_pairs={{0,48},{16,32},{32,16},{48,0},{1,49},{17,33},{33,17},{49,1},{2,50}... | collective-permute-start | bytes 196616 | tf_op jit(solution)/shard_map/ppermute | solution.py:209
  60.9 1.3 pad_maximum_fusion.seen_ref
  63.4 1.4 collective-permute-start.6
  65.8 1.3 collective-permute-done.6.refs_1_
  67.1 2.3 forward_kernel1.1
  70.2 4.2 %all-to-all-start.2 = ((f32[16,64,128]{2,1,0:T(8,128)}), f32[16,64,128]{2,1,0:T(8,128)}, u32[]{:S(2)}, u32[]{:S(2)}) async-start(f32[16,64,128]{2,1,0:T(8,128)} %bitcast.73), calls=%async_computation.2 | async-start | bytes 1048576 | tf_op jit(solution)/shard_map/all_to_all | solution.py:234
  74.5 2.5 collective-permute-start.9
  77.0 1.2 collective-permute-done.8
  78.2 3.6 %collective-permute-done.9 = f32[128,128]{1,0:T(8,128)S(1)} collective-permute-done((f32[128,128]{1,0:T(8,128)}, f32[128,128]{1,0:T(8,128)S(1)}, u32[]{:S(2)}, u32[]{:S(2)}) %collective-permute-start.9) | collective-permute-done | bytes 65568 | tf_op jit(solution)/shard_map/ppermute | solution.py:209
  81.8 1.5 add_add_fusion.4
  83.2 8.4 %all-to-all-done.2.parts_ref = f32[16,64,128]{2,1,0:T(8,128)} async-done(((f32[16,64,128]{2,1,0:T(8,128)}), f32[16,64,128]{2,1,0:T(8,128)}, u32[]{:S(2)}, u32[]{:S(2)}) %all-to-all-start.2) | async-done | bytes 524320 | tf_op jit(solution)/shard_map/all_to_all | solution.py:234
  93.5 4.7 %all-to-all-start.3 = ((f32[16,64,128]{2,1,0:T(8,128)}), f32[16,64,128]{2,1,0:T(8,128)}, u32[]{:S(2)}, u32[]{:S(2)}) async-start(f32[16,64,128]{2,1,0:T(8,128)} %copy-done.5), calls=%async_computation.3 | async-start | bytes 1048576 | tf_op jit(solution)/shard_map/all_to_all | solution.py:235
  98.3 2.8 collective-permute-start.12
  101.8 1.6 collective-permute-done.12
  103.3 2.7 collective-permute-done.11
  106.1 1.6 pad_maximum_fusion.1.refs_0_
  107.7 6.3 %all-to-all-done.3 = f32[16,64,128]{2,1,0:T(8,128)} async-done(((f32[16,64,128]{2,1,0:T(8,128)}), f32[16,64,128]{2,1,0:T(8,128)}, u32[]{:S(2)}, u32[]{:S(2)}) %all-to-all-start.3) | async-done | bytes 524320 | tf_op jit(solution)/shard_map/all_to_all | solution.py:235
  113.9 1.5 convolution_bitcast_fusion
  115.5 5.9 %collective-permute-start.15 = (f32[128,128]{1,0:T(8,128)S(1)}, f32[128,128]{1,0:T(8,128)S(1)}, u32[]{:S(2)}, u32[]{:S(2)}) collective-permute-start(f32[128,128]{1,0:T(8,128)S(1)} %convolution_bitcast_fusion), channel_id=1, source_target_pairs={{0,48},{16,32},{32,16},{48,0},{1,49},{17,33},{33,17},{49,1},{2,50}... | collective-permute-start | bytes 196616 | tf_op jit(solution)/shard_map/ppermute | solution.py:209
  121.4 2.9 collective-permute-done.15
  124.3 1.4 collective-permute-start.16
  125.7 2.6 collective-permute-start.17
  128.3 3.6 %collective-permute-done.17.refs_3_ = f32[128,128]{1,0:T(8,128)S(1)} collective-permute-done((f32[128,128]{1,0:T(8,128)S(1)}, f32[128,128]{1,0:T(8,128)S(1)}, u32[]{:S(2)}, u32[]{:S(2)}) %collective-permute-start.17) | collective-permute-done | bytes 65568 | tf_op jit(solution)/shard_map/ppermute | solution.py:209
  132.8 3.1 forward_kernel2.1
  135.9 19.3 %all_to_all.50.parts_ref = f32[16,64,128]{2,1,0:T(8,128)S(1)} all-to-all(f32[16,64,128]{2,1,0:T(8,128)S(1)} %bitcast.76), channel_id=1, replica_groups=mesh['sub'=4,'row'=4,'col'=16] {'col'}, dimensions={0} | all-to-all | bytes 1048576 | tf_op jit(solution)/shard_map/all_to_all | solution.py:234
  155.3 20.7 %all_to_all.51 = f32[16,64,128]{2,1,0:T(8,128)S(1)} all-to-all(f32[16,64,128]{2,1,0:T(8,128)S(1)} %fold.7), channel_id=1, replica_groups=mesh['sub'=4,'row'=4,'col'=16] {'col'}, dimensions={0} | all-to-all | bytes 1048576 | tf_op jit(solution)/shard_map/all_to_all | solution.py:235
  175.9 4.0 %backward_kernel2.1 = (f32[128,128]{1,0:T(8,128)S(1)}, f32[384,128]{1,0:T(8,128)S(1)}, f32[128,128]{1,0:T(8,128)S(1)}, f32[384,128]{1,0:T(8,128)S(1)}, f32[128,1...) custom-call(s32[1]{0:T(128)} %bitcast.sub_ref, ...), custom_call_target="tpu_custom_call" | custom-call | flops 805306368 | bytes 4194304 | tf_op jit(solution)/shard_map/backward_kernel2/pallas_call | solution.py:145
  179.9 3.4 %collective-permute-start.21 = (f32[128,128]{1,0:T(8,128)S(1)}, f32[128,128]{1,0:T(8,128)S(1)}, u32[]{:S(2)}, u32[]{:S(2)}) collective-permute-start(f32[128,128]{1,0:T(8,128)S(1)} %get-tuple-element.44), channel_id=1, source_target_pairs={{0,192},{64,128},{128,64},{192,0},{1,193},{65,129},{129,65},{193,1... | collective-permute-start | bytes 196616 | tf_op jit(solution)/shard_map/ppermute | solution.py:209
  183.4 1.3 collective-permute-start.20
  185.0 1.5 collective-permute-done.19
  186.5 1.5 collective-permute-done.20
  188.0 3.8 %collective-permute-start.22 = (f32[128,128]{1,0:T(8,128)S(1)}, f32[128,128]{1,0:T(8,128)S(1)}, u32[]{:S(2)}, u32[]{:S(2)}) collective-permute-start(f32[128,128]{1,0:T(8,128)S(1)} %add_add_fusion.2.refs_0_), channel_id=1, source_target_pairs={{0,16},{16,0},{32,48},{48,32},{1,17},{17,1},{33,49},{49,33},{2,18}... | collective-permute-start | bytes 196616 | tf_op jit(solution)/shard_map/ppermute | solution.py:209
  191.9 1.7 collective-permute-start.24
  193.6 1.8 collective-permute-done.23.refs_2_
  195.4 1.7 collective-permute-done.24.refs_3_
  198.2 20.3 %all_to_all.52.parts_ref = f32[16,64,128]{2,1,0:T(8,128)S(1)} all-to-all(f32[16,64,128]{2,1,0:T(8,128)S(1)} %bitcast.77), channel_id=1, replica_groups=mesh['sub'=4,'row'=4,'col'=16] {'col'}, dimensions={0} | all-to-all | bytes 1048576 | tf_op jit(solution)/shard_map/all_to_all | solution.py:234
  219.3 4.3 %all-to-all-start.7 = ((f32[16,64,128]{2,1,0:T(8,128)}), f32[16,64,128]{2,1,0:T(8,128)}, u32[]{:S(2)}, u32[]{:S(2)}) async-start(f32[16,64,128]{2,1,0:T(8,128)} %copy-done.4), calls=%async_computation.7 | async-start | bytes 1048576 | tf_op jit(solution)/shard_map/all_to_all | solution.py:235
  223.6 1.7 collective-permute-start.31
  225.7 1.9 collective-permute-start.30
  227.6 2.1 collective-permute-done.31
  230.5 4.0 %collective-permute-done.30 = f32[384,128]{1,0:T(8,128)S(1)} collective-permute-done((f32[384,128]{1,0:T(8,128)}, f32[384,128]{1,0:T(8,128)S(1)}, u32[]{:S(2)}, u32[]{:S(2)}) %collective-permute-start.30) | collective-permute-done | bytes 196640 | tf_op jit(solution)/shard_map/ppermute | solution.py:209
  234.5 1.6 add_add_fusion.1
  236.5 4.7 %collective-permute-start.34 = (f32[384,128]{1,0:T(8,128)}, f32[384,128]{1,0:T(8,128)}, u32[]{:S(2)}, u32[]{:S(2)}) collective-permute-start(f32[384,128]{1,0:T(8,128)} %add_add_fusion.1), channel_id=1, source_target_pairs={{0,48},{16,32},{32,16},{48,0},{1,49},{17,33},{33,17},{49,1},{2,50}... | collective-permute-start | bytes 589832 | tf_op jit(solution)/shard_map/ppermute | solution.py:209
  241.2 4.1 %backward_kernel1.1 = (f32[128,128]{1,0:T(8,128)S(1)}, f32[256,128]{1,0:T(8,128)S(1)}, f32[128,128]{1,0:T(8,128)S(1)}, f32[256,128]{1,0:T(8,128)S(1)}) custom-call(s32[1]{0:T(128)} %bitcast.sub_ref, f32[4,520,128]{2,1,0:T(8,128)S(1)} %pad_maximum_fusion.seen_ref, f32[1024,128]{1,0:T(8,128)} %bitcast.17.base_ref, f32[1024,128]{1,0:T(8,128)} %bitcast.24.refs_0_, ...), custom_call_target="tpu_custom_call" | custom-call | flops 402653184 | bytes 2097152 | tf_op jit(solution)/shard_map/backward_kernel1/pallas_call | solution.py:145
  245.9 2.6 collective-permute-done.25
  248.5 3.8 %collective-permute-start.26 = (f32[128,128]{1,0:T(8,128)S(1)}, f32[128,128]{1,0:T(8,128)S(1)}, u32[]{:S(2)}, u32[]{:S(2)}) collective-permute-start(f32[128,128]{1,0:T(8,128)S(1)} %add.102.refs_0_), channel_id=1, source_target_pairs={{0,16},{16,0},{32,48},{48,32},{1,17},{17,1},{33,49},{49,33},{2,18}... | collective-permute-start | bytes 196616 | tf_op jit(solution)/shard_map/ppermute | solution.py:209
  252.7 1.4 collective-permute-start.28
  254.1 1.3 add_add_fusion
  255.9 1.7 collective-permute-done.28.refs_3_
  257.6 1.3 correct2.1
  258.9 24.3 %all_to_all.53.parts_ref = f32[16,64,128]{2,1,0:T(8,128)S(1)} all-to-all(f32[16,64,128]{2,1,0:T(8,128)S(1)} %bitcast.75), channel_id=1, replica_groups=mesh['sub'=4,'row'=4,'col'=16] {'col'}, dimensions={0} | all-to-all | bytes 1048576 | tf_op jit(solution)/shard_map/all_to_all | solution.py:234
  284.1 4.5 %all-to-all-start.9 = ((f32[16,64,128]{2,1,0:T(8,128)}), f32[16,64,128]{2,1,0:T(8,128)S(1)}, u32[]{:S(2)}, u32[]{:S(2)}) async-start(f32[16,64,128]{2,1,0:T(8,128)} %fold.9), calls=%async_computation.9 | async-start | bytes 1048576 | tf_op jit(solution)/shard_map/all_to_all | solution.py:235
  289.2 3.3 %collective-permute-done.38 = f32[256,128]{1,0:T(8,128)S(1)} collective-permute-done((f32[256,128]{1,0:T(8,128)S(1)}, f32[256,128]{1,0:T(8,128)S(1)}, u32[]{:S(2)}, u32[]{:S(2)}) %collective-permute-start.38) | collective-permute-done | bytes 131104 | tf_op jit(solution)/shard_map/ppermute | solution.py:209
  292.9 4.3 %collective-permute-start.41 = (f32[256,128]{1,0:T(8,128)S(1)}, f32[256,128]{1,0:T(8,128)S(1)}, u32[]{:S(2)}, u32[]{:S(2)}) collective-permute-start(f32[256,128]{1,0:T(8,128)S(1)} %add.112), channel_id=1, source_target_pairs={{0,48},{16,32},{32,16},{48,0},{1,49},{17,33},{33,17},{49,1},{2,50}... | collective-permute-start | bytes 393224 | tf_op jit(solution)/shard_map/ppermute | solution.py:209
  297.2 8.2 %all-to-all-done.9 = f32[16,64,128]{2,1,0:T(8,128)S(1)} async-done(((f32[16,64,128]{2,1,0:T(8,128)}), f32[16,64,128]{2,1,0:T(8,128)S(1)}, u32[]{:S(2)}, u32[]{:S(2)}) %all-to-all-start.9) | async-done | bytes 524320 | tf_op jit(solution)/shard_map/all_to_all | solution.py:235
  305.4 2.3 backward_kernel0.1
  308.0 4.4 %collective-permute-start.37 = (f32[256,128]{1,0:T(8,128)S(1)}, f32[256,128]{1,0:T(8,128)S(1)}, u32[]{:S(2)}, u32[]{:S(2)}) collective-permute-start(f32[256,128]{1,0:T(8,128)S(1)} %backward_kernel0.1), channel_id=1, source_target_pairs={{0,48},{16,32},{32,16},{48,0},{1,49},{17,33},{33,17},{49,1},{2,50}... | collective-permute-start | bytes 393224 | tf_op jit(solution)/shard_map/ppermute | solution.py:209
  312.4 5.3 %collective-permute-done.37 = f32[256,128]{1,0:T(8,128)S(1)} collective-permute-done((f32[256,128]{1,0:T(8,128)S(1)}, f32[256,128]{1,0:T(8,128)S(1)}, u32[]{:S(2)}, u32[]{:S(2)}) %collective-permute-start.37) | collective-permute-done | bytes 131104 | tf_op jit(solution)/shard_map/ppermute | solution.py:209
  (113 shorter events, 19.5 us)
Async XLA Ops:
  0.0 1.0 copy-start.1
  1.0 14.4 %copy-start.2 = (f32[3,1,256,128]{3,2,1,0:T(8,128)S(1)}, f32[3,1,256,128]{3,2,1,0:T(8,128)}, u32[]{:S(2)}) copy-start(f32[3,1,256,128]{3,2,1,0:T(8,128)} %param.4) | copy-start | bytes 1179652
  3.8 11.7 %copy-start.19 = (s32[3,1,128]{2,1,0:T(1,128)S(1)}, s32[3,1,128]{2,1,0:T(1,128)}, u32[]{:S(2)}) copy-start(s32[3,1,128]{2,1,0:T(1,128)} %param.7) | copy-start | bytes 4612
  3.8 28.8 %all-to-all-start = ((f32[16,64,128]{2,1,0:T(8,128)}), f32[16,64,128]{2,1,0:T(8,128)S(1)}, u32[]{:S(2)}, u32[]{:S(2)}) async-start(f32[16,64,128]{2,1,0:T(8,128)} %bitcast.4), calls=%async_computation | async-start | bytes 1048576 | tf_op jit(solution)/shard_map/all_to_all | solution.py:234
  15.4 40.1 %copy-start = (f32[3,1,128,1024]{3,2,1,0:T(8,128)S(1)}, f32[3,1,128,1024]{3,2,1,0:T(8,128)}, u32[]{:S(2)}) copy-start(f32[3,1,128,1024]{3,2,1,0:T(8,128)} %param.6) | copy-start | bytes 4718596
  15.7 40.2 %copy-start.15 = (f32[520,128]{1,0:T(8,128)}, f32[520,128]{1,0:T(8,128)S(1)}, u32[]{:S(2)}) copy-start(f32[520,128]{1,0:T(8,128)S(1)} %maximum_maximum_fusion) | copy-start | bytes 798724
  33.5 22.0 %all-to-all-start.1 = ((f32[16,64,128]{2,1,0:T(8,128)}), f32[16,64,128]{2,1,0:T(8,128)S(1)}, u32[]{:S(2)}, u32[]{:S(2)}) async-start(f32[16,64,128]{2,1,0:T(8,128)} %fold.5), calls=%async_computation.1 | async-start | bytes 1048576 | tf_op jit(solution)/shard_map/all_to_all | solution.py:235
  38.2 21.8 %collective-permute-start.2 = (f32[520,128]{1,0:T(8,128)S(1)}, f32[520,128]{1,0:T(8,128)S(1)}, u32[]{:S(2)}, u32[]{:S(2)}) collective-permute-start(f32[520,128]{1,0:T(8,128)S(1)} %maximum_maximum_fusion), channel_id=1, source_target_pairs={{0,192},{64,128},{128,64},{192,0},{1,193},{65,129},{129,65},{193,1... | collective-permute-start | bytes 798728 | tf_op jit(solution)/shard_map/ppermute | solution.py:209
  41.0 19.0 %collective-permute-start.1 = (f32[520,128]{1,0:T(8,128)S(1)}, f32[520,128]{1,0:T(8,128)S(1)}, u32[]{:S(2)}, u32[]{:S(2)}) collective-permute-start(f32[520,128]{1,0:T(8,128)S(1)} %maximum_maximum_fusion), channel_id=1, source_target_pairs={{0,128},{64,192},{128,0},{192,64},{1,129},{65,193},{129,1},{193,65... | collective-permute-start | bytes 798728 | tf_op jit(solution)/shard_map/ppermute | solution.py:209
  41.4 18.6 %collective-permute-start = (f32[520,128]{1,0:T(8,128)S(1)}, f32[520,128]{1,0:T(8,128)S(1)}, u32[]{:S(2)}, u32[]{:S(2)}) collective-permute-start(f32[520,128]{1,0:T(8,128)S(1)} %maximum_maximum_fusion), channel_id=1, source_target_pairs={{0,64},{64,0},{128,192},{192,128},{1,65},{65,1},{129,193},{193,129... | collective-permute-start | bytes 798728 | tf_op jit(solution)/shard_map/ppermute | solution.py:209
  55.9 6.3 %collective-permute-start.4 = (f32[128,128]{1,0:T(8,128)S(1)}, f32[128,128]{1,0:T(8,128)S(1)}, u32[]{:S(2)}, u32[]{:S(2)}) collective-permute-start(f32[128,128]{1,0:T(8,128)S(1)} %convolution_bitcast_fusion.2), channel_id=1, source_target_pairs={{0,32},{16,48},{32,0},{48,16},{1,33},{17,49},{33,1},{49,17},{2,34}... | collective-permute-start | bytes 196616 | tf_op jit(solution)/shard_map/ppermute | solution.py:209
  56.3 7.0 %collective-permute-start.5 = (f32[128,128]{1,0:T(8,128)S(1)}, f32[128,128]{1,0:T(8,128)S(1)}, u32[]{:S(2)}, u32[]{:S(2)}) collective-permute-start(f32[128,128]{1,0:T(8,128)S(1)} %convolution_bitcast_fusion.2), channel_id=1, source_target_pairs={{0,48},{16,32},{32,16},{48,0},{1,49},{17,33},{33,17},{49,1},{2,50}... | collective-permute-start | bytes 196616 | tf_op jit(solution)/shard_map/ppermute | solution.py:209
  60.0 3.3 %collective-permute-start.3 = (f32[128,128]{1,0:T(8,128)S(1)}, f32[128,128]{1,0:T(8,128)S(1)}, u32[]{:S(2)}, u32[]{:S(2)}) collective-permute-start(f32[128,128]{1,0:T(8,128)S(1)} %convolution_bitcast_fusion.2), channel_id=1, source_target_pairs={{0,16},{16,0},{32,48},{48,32},{1,17},{17,1},{33,49},{49,33},{2,18}... | collective-permute-start | bytes 196616 | tf_op jit(solution)/shard_map/ppermute | solution.py:209
  60.0 0.9 copy-start.18
  63.4 3.7 %collective-permute-start.6 = (f32[128,128]{1,0:T(8,128)S(1)}, f32[128,128]{1,0:T(8,128)S(1)}, u32[]{:S(2)}, u32[]{:S(2)}) collective-permute-start(f32[128,128]{1,0:T(8,128)S(1)} %add_add_fusion.5.refs_0_), channel_id=1, source_target_pairs={{0,64},{64,0},{128,192},{192,128},{1,65},{65,1},{129,193},{193,129... | collective-permute-start | bytes 196616 | tf_op jit(solution)/shard_map/ppermute | solution.py:209
  70.2 21.4 %all-to-all-start.2 = ((f32[16,64,128]{2,1,0:T(8,128)}), f32[16,64,128]{2,1,0:T(8,128)}, u32[]{:S(2)}, u32[]{:S(2)}) async-start(f32[16,64,128]{2,1,0:T(8,128)} %bitcast.73), calls=%async_computation.2 | async-start | bytes 1048576 | tf_op jit(solution)/shard_map/all_to_all | solution.py:234
  74.4 3.8 %collective-permute-start.8 = (f32[128,128]{1,0:T(8,128)}, f32[128,128]{1,0:T(8,128)S(1)}, u32[]{:S(2)}, u32[]{:S(2)}) collective-permute-start(f32[128,128]{1,0:T(8,128)} %convolution_bitcast_fusion.1), channel_id=1, source_target_pairs={{0,32},{16,48},{32,0},{48,16},{1,33},{17,49},{33,1},{49,17},{2,34}... | collective-permute-start | bytes 196616 | tf_op jit(solution)/shard_map/ppermute | solution.py:209
  74.5 7.2 %collective-permute-start.9 = (f32[128,128]{1,0:T(8,128)}, f32[128,128]{1,0:T(8,128)S(1)}, u32[]{:S(2)}, u32[]{:S(2)}) collective-permute-start(f32[128,128]{1,0:T(8,128)} %convolution_bitcast_fusion.1), channel_id=1, source_target_pairs={{0,48},{16,32},{32,16},{48,0},{1,49},{17,33},{33,17},{49,1},{2,50}... | collective-permute-start | bytes 196616 | tf_op jit(solution)/shard_map/ppermute | solution.py:209
  77.0 4.8 %collective-permute-start.7 = (f32[128,128]{1,0:T(8,128)}, f32[128,128]{1,0:T(8,128)S(1)}, u32[]{:S(2)}, u32[]{:S(2)}) collective-permute-start(f32[128,128]{1,0:T(8,128)} %convolution_bitcast_fusion.1), channel_id=1, source_target_pairs={{0,16},{16,0},{32,48},{48,32},{1,17},{17,1},{33,49},{49,33},{2,18}... | collective-permute-start | bytes 196616 | tf_op jit(solution)/shard_map/ppermute | solution.py:209
  92.7 0.8 copy-start.5
  93.5 20.4 %all-to-all-start.3 = ((f32[16,64,128]{2,1,0:T(8,128)}), f32[16,64,128]{2,1,0:T(8,128)}, u32[]{:S(2)}, u32[]{:S(2)}) async-start(f32[16,64,128]{2,1,0:T(8,128)} %copy-done.5), calls=%async_computation.3 | async-start | bytes 1048576 | tf_op jit(solution)/shard_map/all_to_all | solution.py:235
  98.3 5.1 %collective-permute-start.12 = (f32[128,128]{1,0:T(8,128)}, f32[128,128]{1,0:T(8,128)S(1)}, u32[]{:S(2)}, u32[]{:S(2)}) collective-permute-start(f32[128,128]{1,0:T(8,128)} %add_add_fusion.4), channel_id=1, source_target_pairs={{0,192},{64,128},{128,64},{192,0},{1,193},{65,129},{129,65},{193,1... | collective-permute-start | bytes 196616 | tf_op jit(solution)/shard_map/ppermute | solution.py:209
  101.1 5.0 %collective-permute-start.11 = (f32[128,128]{1,0:T(8,128)}, f32[128,128]{1,0:T(8,128)S(1)}, u32[]{:S(2)}, u32[]{:S(2)}) collective-permute-start(f32[128,128]{1,0:T(8,128)} %add_add_fusion.4), channel_id=1, source_target_pairs={{0,128},{64,192},{128,0},{192,64},{1,129},{65,193},{129,1},{193,65... | collective-permute-start | bytes 196616 | tf_op jit(solution)/shard_map/ppermute | solution.py:209
  101.5 4.6 %collective-permute-start.10 = (f32[128,128]{1,0:T(8,128)}, f32[128,128]{1,0:T(8,128)S(1)}, u32[]{:S(2)}, u32[]{:S(2)}) collective-permute-start(f32[128,128]{1,0:T(8,128)} %add_add_fusion.4), channel_id=1, source_target_pairs={{0,64},{64,0},{128,192},{192,128},{1,65},{65,1},{129,193},{193,129... | collective-permute-start | bytes 196616 | tf_op jit(solution)/shard_map/ppermute | solution.py:209
  113.9 18.9 %copy-start.6 = (f32[512,128]{1,0:T(8,128)S(1)}, f32[512,128]{1,0:T(8,128)}, u32[]{:S(2)}) copy-start(f32[512,128]{1,0:T(8,128)} %pad_maximum_fusion.1.refs_0_) | copy-start | bytes 786436
  115.4 6.1 %collective-permute-start.14 = (f32[128,128]{1,0:T(8,128)S(1)}, f32[128,128]{1,0:T(8,128)S(1)}, u32[]{:S(2)}, u32[]{:S(2)}) collective-permute-start(f32[128,128]{1,0:T(8,128)S(1)} %convolution_bitcast_fusion), channel_id=1, source_target_pairs={{0,32},{16,48},{32,0},{48,16},{1,33},{17,49},{33,1},{49,17},{2,34}... | collective-permute-start | bytes 196616 | tf_op jit(solution)/shard_map/ppermute | solution.py:209
  115.5 8.8 %collective-permute-start.15 = (f32[128,128]{1,0:T(8,128)S(1)}, f32[128,128]{1,0:T(8,128)S(1)}, u32[]{:S(2)}, u32[]{:S(2)}) collective-permute-start(f32[128,128]{1,0:T(8,128)S(1)} %convolution_bitcast_fusion), channel_id=1, source_target_pairs={{0,48},{16,32},{32,16},{48,0},{1,49},{17,33},{33,17},{49,1},{2,50}... | collective-permute-start | bytes 196616 | tf_op jit(solution)/shard_map/ppermute | solution.py:209
  121.4 2.9 collective-permute-start.13
  124.3 4.0 %collective-permute-start.16 = (f32[128,128]{1,0:T(8,128)S(1)}, f32[128,128]{1,0:T(8,128)S(1)}, u32[]{:S(2)}, u32[]{:S(2)}) collective-permute-start(f32[128,128]{1,0:T(8,128)S(1)} %add_add_fusion.3.refs_1_), channel_id=1, source_target_pairs={{0,64},{64,0},{128,192},{192,128},{1,65},{65,1},{129,193},{193,129... | collective-permute-start | bytes 196616 | tf_op jit(solution)/shard_map/ppermute | solution.py:209
  125.7 6.2 %collective-permute-start.17 = (f32[128,128]{1,0:T(8,128)S(1)}, f32[128,128]{1,0:T(8,128)S(1)}, u32[]{:S(2)}, u32[]{:S(2)}) collective-permute-start(f32[128,128]{1,0:T(8,128)S(1)} %add_add_fusion.3.refs_1_), channel_id=1, source_target_pairs={{0,128},{64,192},{128,0},{192,64},{1,129},{65,193},{129,1},{193,65... | collective-permute-start | bytes 196616 | tf_op jit(solution)/shard_map/ppermute | solution.py:209
  128.3 4.5 %collective-permute-start.18 = (f32[128,128]{1,0:T(8,128)S(1)}, f32[128,128]{1,0:T(8,128)S(1)}, u32[]{:S(2)}, u32[]{:S(2)}) collective-permute-start(f32[128,128]{1,0:T(8,128)S(1)} %add_add_fusion.3.refs_1_), channel_id=1, source_target_pairs={{0,192},{64,128},{128,64},{192,0},{1,193},{65,129},{129,65},{193,1... | collective-permute-start | bytes 196616 | tf_op jit(solution)/shard_map/ppermute | solution.py:209
  179.9 38.5 %copy-start.7 = (f32[384,128]{1,0:T(8,128)}, f32[384,128]{1,0:T(8,128)S(1)}, u32[]{:S(2)}) copy-start(f32[384,128]{1,0:T(8,128)S(1)} %get-tuple-element.52) | copy-start | bytes 589828
  179.9 38.5 %copy-start.10 = (f32[384,128]{1,0:T(8,128)}, f32[384,128]{1,0:T(8,128)S(1)}, u32[]{:S(2)}) copy-start(f32[384,128]{1,0:T(8,128)S(1)} %get-tuple-element.54) | copy-start | bytes 589828
  179.9 38.5 %copy-start.11 = (f32[384,128]{1,0:T(8,128)}, f32[384,128]{1,0:T(8,128)S(1)}, u32[]{:S(2)}) copy-start(f32[384,128]{1,0:T(8,128)S(1)} %get-tuple-element.53) | copy-start | bytes 589828
  179.9 38.5 %copy-start.12 = (f32[384,128]{1,0:T(8,128)}, f32[384,128]{1,0:T(8,128)S(1)}, u32[]{:S(2)}) copy-start(f32[384,128]{1,0:T(8,128)S(1)} %get-tuple-element.55) | copy-start | bytes 589828
  179.9 5.1 %collective-permute-start.21 = (f32[128,128]{1,0:T(8,128)S(1)}, f32[128,128]{1,0:T(8,128)S(1)}, u32[]{:S(2)}, u32[]{:S(2)}) collective-permute-start(f32[128,128]{1,0:T(8,128)S(1)} %get-tuple-element.44), channel_id=1, source_target_pairs={{0,192},{64,128},{128,64},{192,0},{1,193},{65,129},{129,65},{193,1... | collective-permute-start | bytes 196616 | tf_op jit(solution)/shard_map/ppermute | solution.py:209
  183.4 3.1 collective-permute-start.19
  183.4 4.6 %collective-permute-start.20 = (f32[128,128]{1,0:T(8,128)S(1)}, f32[128,128]{1,0:T(8,128)S(1)}, u32[]{:S(2)}, u32[]{:S(2)}) collective-permute-start(f32[128,128]{1,0:T(8,128)S(1)} %get-tuple-element.43), channel_id=1, source_target_pairs={{0,128},{64,192},{128,0},{192,64},{1,129},{65,193},{129,1},{193,65... | collective-permute-start | bytes 196616 | tf_op jit(solution)/shard_map/ppermute | solution.py:209
  188.0 5.5 %collective-permute-start.22 = (f32[128,128]{1,0:T(8,128)S(1)}, f32[128,128]{1,0:T(8,128)S(1)}, u32[]{:S(2)}, u32[]{:S(2)}) collective-permute-start(f32[128,128]{1,0:T(8,128)S(1)} %add_add_fusion.2.refs_0_), channel_id=1, source_target_pairs={{0,16},{16,0},{32,48},{48,32},{1,17},{17,1},{33,49},{49,33},{2,18}... | collective-permute-start | bytes 196616 | tf_op jit(solution)/shard_map/ppermute | solution.py:209
  191.9 3.5 %collective-permute-start.23 = (f32[128,128]{1,0:T(8,128)S(1)}, f32[128,128]{1,0:T(8,128)S(1)}, u32[]{:S(2)}, u32[]{:S(2)}) collective-permute-start(f32[128,128]{1,0:T(8,128)S(1)} %add_add_fusion.2.refs_0_), channel_id=1, source_target_pairs={{0,32},{16,48},{32,0},{48,16},{1,33},{17,49},{33,1},{49,17},{2,34}... | collective-permute-start | bytes 196616 | tf_op jit(solution)/shard_map/ppermute | solution.py:209
  191.9 5.2 %collective-permute-start.24 = (f32[128,128]{1,0:T(8,128)S(1)}, f32[128,128]{1,0:T(8,128)S(1)}, u32[]{:S(2)}, u32[]{:S(2)}) collective-permute-start(f32[128,128]{1,0:T(8,128)S(1)} %add_add_fusion.2.refs_0_), channel_id=1, source_target_pairs={{0,48},{16,32},{32,16},{48,0},{1,49},{17,33},{33,17},{49,1},{2,50}... | collective-permute-start | bytes 196616 | tf_op jit(solution)/shard_map/ppermute | solution.py:209
  219.3 21.9 %all-to-all-start.7 = ((f32[16,64,128]{2,1,0:T(8,128)}), f32[16,64,128]{2,1,0:T(8,128)}, u32[]{:S(2)}, u32[]{:S(2)}) async-start(f32[16,64,128]{2,1,0:T(8,128)} %copy-done.4), calls=%async_computation.7 | async-start | bytes 1048576 | tf_op jit(solution)/shard_map/all_to_all | solution.py:235
  223.6 6.0 %collective-permute-start.31 = (f32[384,128]{1,0:T(8,128)}, f32[384,128]{1,0:T(8,128)S(1)}, u32[]{:S(2)}, u32[]{:S(2)}) collective-permute-start(f32[384,128]{1,0:T(8,128)} %copy-done.12), channel_id=1, source_target_pairs={{0,192},{64,128},{128,64},{192,0},{1,193},{65,129},{129,65},{193,1... | collective-permute-start | bytes 589832 | tf_op jit(solution)/shard_map/ppermute | solution.py:209
  225.3 5.1 %collective-permute-start.29 = (f32[384,128]{1,0:T(8,128)}, f32[384,128]{1,0:T(8,128)S(1)}, u32[]{:S(2)}, u32[]{:S(2)}) collective-permute-start(f32[384,128]{1,0:T(8,128)} %copy-done.11), channel_id=1, source_target_pairs={{0,64},{64,0},{128,192},{192,128},{1,65},{65,1},{129,193},{193,129... | collective-permute-start | bytes 589832 | tf_op jit(solution)/shard_map/ppermute | solution.py:209
  225.7 8.8 %collective-permute-start.30 = (f32[384,128]{1,0:T(8,128)}, f32[384,128]{1,0:T(8,128)S(1)}, u32[]{:S(2)}, u32[]{:S(2)}) collective-permute-start(f32[384,128]{1,0:T(8,128)} %copy-done.10), channel_id=1, source_target_pairs={{0,128},{64,192},{128,0},{192,64},{1,129},{65,193},{129,1},{193,65... | collective-permute-start | bytes 589832 | tf_op jit(solution)/shard_map/ppermute | solution.py:209
  236.1 16.5 %collective-permute-start.33 = (f32[384,128]{1,0:T(8,128)}, f32[384,128]{1,0:T(8,128)}, u32[]{:S(2)}, u32[]{:S(2)}) collective-permute-start(f32[384,128]{1,0:T(8,128)} %add_add_fusion.1), channel_id=1, source_target_pairs={{0,32},{16,48},{32,0},{48,16},{1,33},{17,49},{33,1},{49,17},{2,34}... | collective-permute-start | bytes 589832 | tf_op jit(solution)/shard_map/ppermute | solution.py:209
  236.5 17.6 %collective-permute-start.34 = (f32[384,128]{1,0:T(8,128)}, f32[384,128]{1,0:T(8,128)}, u32[]{:S(2)}, u32[]{:S(2)}) collective-permute-start(f32[384,128]{1,0:T(8,128)} %add_add_fusion.1), channel_id=1, source_target_pairs={{0,48},{16,32},{32,16},{48,0},{1,49},{17,33},{33,17},{49,1},{2,50}... | collective-permute-start | bytes 589832 | tf_op jit(solution)/shard_map/ppermute | solution.py:209
  241.2 12.9 %collective-permute-start.32 = (f32[384,128]{1,0:T(8,128)}, f32[384,128]{1,0:T(8,128)}, u32[]{:S(2)}, u32[]{:S(2)}) collective-permute-start(f32[384,128]{1,0:T(8,128)} %add_add_fusion.1), channel_id=1, source_target_pairs={{0,16},{16,0},{32,48},{48,32},{1,17},{17,1},{33,49},{49,33},{2,18}... | collective-permute-start | bytes 589832 | tf_op jit(solution)/shard_map/ppermute | solution.py:209
  245.3 13.6 %copy-start.8 = (f32[256,128]{1,0:T(8,128)}, f32[256,128]{1,0:T(8,128)S(1)}, u32[]{:S(2)}) copy-start(f32[256,128]{1,0:T(8,128)S(1)} %get-tuple-element.59) | copy-start | bytes 393220
  245.3 13.6 %copy-start.13 = (f32[256,128]{1,0:T(8,128)}, f32[256,128]{1,0:T(8,128)S(1)}, u32[]{:S(2)}) copy-start(f32[256,128]{1,0:T(8,128)S(1)} %get-tuple-element.60) | copy-start | bytes 393220
  245.3 3.2 %collective-permute-start.25 = (f32[128,128]{1,0:T(8,128)S(1)}, f32[128,128]{1,0:T(8,128)S(1)}, u32[]{:S(2)}, u32[]{:S(2)}) collective-permute-start(f32[128,128]{1,0:T(8,128)S(1)} %get-tuple-element.51), channel_id=1, source_target_pairs={{0,64},{64,0},{128,192},{192,128},{1,65},{65,1},{129,193},{193,129... | collective-permute-start | bytes 196616 | tf_op jit(solution)/shard_map/ppermute | solution.py:209
  248.5 6.8 %collective-permute-start.26 = (f32[128,128]{1,0:T(8,128)S(1)}, f32[128,128]{1,0:T(8,128)S(1)}, u32[]{:S(2)}, u32[]{:S(2)}) collective-permute-start(f32[128,128]{1,0:T(8,128)S(1)} %add.102.refs_0_), channel_id=1, source_target_pairs={{0,16},{16,0},{32,48},{48,32},{1,17},{17,1},{33,49},{49,33},{2,18}... | collective-permute-start | bytes 196616 | tf_op jit(solution)/shard_map/ppermute | solution.py:209
  252.3 3.5 %collective-permute-start.27 = (f32[128,128]{1,0:T(8,128)S(1)}, f32[128,128]{1,0:T(8,128)S(1)}, u32[]{:S(2)}, u32[]{:S(2)}) collective-permute-start(f32[128,128]{1,0:T(8,128)S(1)} %add.102.refs_0_), channel_id=1, source_target_pairs={{0,32},{16,48},{32,0},{48,16},{1,33},{17,49},{33,1},{49,17},{2,34}... | collective-permute-start | bytes 196616 | tf_op jit(solution)/shard_map/ppermute | solution.py:209
  252.7 4.9 %collective-permute-start.28 = (f32[128,128]{1,0:T(8,128)S(1)}, f32[128,128]{1,0:T(8,128)S(1)}, u32[]{:S(2)}, u32[]{:S(2)}) collective-permute-start(f32[128,128]{1,0:T(8,128)S(1)} %add.102.refs_0_), channel_id=1, source_target_pairs={{0,48},{16,32},{32,16},{48,0},{1,49},{17,33},{33,17},{49,1},{2,50}... | collective-permute-start | bytes 196616 | tf_op jit(solution)/shard_map/ppermute | solution.py:209
  258.9 29.7 %copy-start.14 = (f32[256,128]{1,0:T(8,128)S(1)}, f32[256,128]{1,0:T(8,128)}, u32[]{:S(2)}) copy-start(f32[256,128]{1,0:T(8,128)} %copy-done.13) | copy-start | bytes 393220
  258.9 33.6 %copy-start.9 = (f32[256,128]{1,0:T(8,128)S(1)}, f32[256,128]{1,0:T(8,128)}, u32[]{:S(2)}) copy-start(f32[256,128]{1,0:T(8,128)} %copy-done.8) | copy-start | bytes 393220
  284.1 21.2 %all-to-all-start.9 = ((f32[16,64,128]{2,1,0:T(8,128)}), f32[16,64,128]{2,1,0:T(8,128)S(1)}, u32[]{:S(2)}, u32[]{:S(2)}) async-start(f32[16,64,128]{2,1,0:T(8,128)} %fold.9), calls=%async_computation.9 | async-start | bytes 1048576 | tf_op jit(solution)/shard_map/all_to_all | solution.py:235
  288.6 3.9 %collective-permute-start.38 = (f32[256,128]{1,0:T(8,128)S(1)}, f32[256,128]{1,0:T(8,128)S(1)}, u32[]{:S(2)}, u32[]{:S(2)}) collective-permute-start(f32[256,128]{1,0:T(8,128)S(1)} %copy-done.14), channel_id=1, source_target_pairs={{0,64},{64,0},{128,192},{192,128},{1,65},{65,1},{129,193},{193,129... | collective-permute-start | bytes 393224 | tf_op jit(solution)/shard_map/ppermute | solution.py:209
  292.5 19.8 %collective-permute-start.40 = (f32[256,128]{1,0:T(8,128)S(1)}, f32[256,128]{1,0:T(8,128)S(1)}, u32[]{:S(2)}, u32[]{:S(2)}) collective-permute-start(f32[256,128]{1,0:T(8,128)S(1)} %add.112), channel_id=1, source_target_pairs={{0,32},{16,48},{32,0},{48,16},{1,33},{17,49},{33,1},{49,17},{2,34}... | collective-permute-start | bytes 393224 | tf_op jit(solution)/shard_map/ppermute | solution.py:209
  292.9 19.5 %collective-permute-start.41 = (f32[256,128]{1,0:T(8,128)S(1)}, f32[256,128]{1,0:T(8,128)S(1)}, u32[]{:S(2)}, u32[]{:S(2)}) collective-permute-start(f32[256,128]{1,0:T(8,128)S(1)} %add.112), channel_id=1, source_target_pairs={{0,48},{16,32},{32,16},{48,0},{1,49},{17,33},{33,17},{49,1},{2,50}... | collective-permute-start | bytes 393224 | tf_op jit(solution)/shard_map/ppermute | solution.py:209
  297.2 15.2 %collective-permute-start.39 = (f32[256,128]{1,0:T(8,128)S(1)}, f32[256,128]{1,0:T(8,128)S(1)}, u32[]{:S(2)}, u32[]{:S(2)}) collective-permute-start(f32[256,128]{1,0:T(8,128)S(1)} %add.112), channel_id=1, source_target_pairs={{0,16},{16,0},{32,48},{48,32},{1,17},{17,1},{33,49},{49,33},{2,18}... | collective-permute-start | bytes 393224 | tf_op jit(solution)/shard_map/ppermute | solution.py:209
  307.7 4.7 %collective-permute-start.36 = (f32[256,128]{1,0:T(8,128)S(1)}, f32[256,128]{1,0:T(8,128)S(1)}, u32[]{:S(2)}, u32[]{:S(2)}) collective-permute-start(f32[256,128]{1,0:T(8,128)S(1)} %backward_kernel0.1), channel_id=1, source_target_pairs={{0,32},{16,48},{32,0},{48,16},{1,33},{17,49},{33,1},{49,17},{2,34}... | collective-permute-start | bytes 393224 | tf_op jit(solution)/shard_map/ppermute | solution.py:209
  308.0 9.8 %collective-permute-start.37 = (f32[256,128]{1,0:T(8,128)S(1)}, f32[256,128]{1,0:T(8,128)S(1)}, u32[]{:S(2)}, u32[]{:S(2)}) collective-permute-start(f32[256,128]{1,0:T(8,128)S(1)} %backward_kernel0.1), channel_id=1, source_target_pairs={{0,48},{16,32},{32,16},{48,0},{1,49},{17,33},{33,17},{49,1},{2,50}... | collective-permute-start | bytes 393224 | tf_op jit(solution)/shard_map/ppermute | solution.py:209
  312.4 5.4 %collective-permute-start.35 = (f32[256,128]{1,0:T(8,128)S(1)}, f32[256,128]{1,0:T(8,128)S(1)}, u32[]{:S(2)}, u32[]{:S(2)}) collective-permute-start(f32[256,128]{1,0:T(8,128)S(1)} %backward_kernel0.1), channel_id=1, source_target_pairs={{0,16},{16,0},{32,48},{48,32},{1,17},{17,1},{33,49},{49,33},{2,18}... | collective-permute-start | bytes 393224 | tf_op jit(solution)/shard_map/ppermute | solution.py:209
  (4 other events, 3.1 us)

commit v5 on v4

--- a/solution.py
+++ b/solution.py
@@ -65,12 +65,7 @@
         sub = sub_ref[0] % spans
         total = None
         for m in range(spans):
-            if level == 1:
-                own = update_refs[m][...]
-            else:
-                early = update_refs[0][m * K : (m + 1) * K, :]
-                own = jnp.concatenate([early, update_refs[m + 1][...]], axis=0)
-            high, low = halves(own)
+            high, low = halves(update_refs[m][...])
             pair = jnp.concatenate([high, low], axis=1)
             term = mm(hits(seen_ref, m, SLOTS_OF[level], spans), pair)
             total = term if total is None else total + term
@@ -130,8 +125,9 @@
         soon_ref, later_ref = out_refs[2 * m], out_refs[2 * m + 1]
         if level == 2:
             soon_ref[...] = picked[K:]
-            later_ref[:K, :] = picked[:K]
-            later_ref[K:, :] = own
+            early_ref = out_refs[2 * spans + m]
+            early_ref[...] = picked[:K]
+            later_ref[...] = own
         else:
             soon_ref[...] = picked
             later_ref[...] = own
@@ -166,9 +162,29 @@
 
 
 def backward(level, sub, seen, residue, diag):
-    heights = {0: [C], 1: [K, C] * 2, 2: [K, K + C] * 4}[level]
+    heights = {0: [C], 1: [K, C] * 2, 2: [K, C] * 4 + [K] * 4}[level]
     scratch = pltpu.VMEM((2**level, N, C), jnp.float32)
     return call(backward_kernel, level, heights, scratch, sub, seen, *residue, diag)
+
+
+def join_kernel(early_ref, solved_ref, factor_ref, out_ref):
+    out_ref[:K, :] = early_ref[...]
+    solved_high, solved_low = halves(solved_ref[...])
+    high, low = halves(factor_ref[2])
+    wide = mm(high, jnp.concatenate([solved_high, solved_low], axis=1))
+    out_ref[K:, :] = wide[:, :N] + wide[:, N:] + mm(low, solved_high)
+
+
+def join(early, solved, factor):
+    vmem = pl.BlockSpec(memory_space=pltpu.VMEM)
+    return pl.pallas_call(
+        join_kernel,
+        in_specs=[vmem] * 3,
+        out_specs=vmem,
+        out_shape=jax.ShapeDtypeStruct((2 * K, N), jnp.float32),
+        compiler_params=pltpu.CompilerParams(vmem_limit_bytes=8 * 2**20),
+        name="join",
+    )(early, solved, factor)
 
 
 def correct_kernel(slots, *refs):
@@ -268,6 +284,7 @@
             jnp.zeros((PACKED - LIST_AT - 3, N), jnp.float32),
         ]
     )
+
     def update(slot, solved):
         return jnp.dot(factor[slot], solved, precision=mode)
 
@@ -276,26 +293,24 @@
     u01 = row_sum(update(0, y0))
     part1 = forward(1, sub, seen, [u01, swapped(u01, "sub", 1)], diag)
     part1, u02 = lax.optimization_barrier((part1, update(1, y0)))
-    y1, u02 = col_sum(part1, row_sum(u02))
-    y1, u02 = lax.optimization_barrier((y1, jnp.concatenate(sub_parts(u02))))
-    u12 = sub_parts(row_sum(update(2, y1)))
-    (y2,) = col_sum(forward(2, sub, seen, [u02] + u12, diag))
+    (y1,) = col_sum(part1)
+    u2 = sub_parts(row_sum(join(u02, y1, factor)))
+    (y2,) = col_sum(forward(2, sub, seen, u2, diag))
 
     out2 = backward(2, sub, seen, [y2], diag)
-    pick12 = row_parts(sub_sum(out2[0::2]))
-    part1, *later = lax.optimization_barrier([correct((2,), pick12, factor)] + list(out2[1::2]))
-    later = row_sum(sub_sum(later))
-    pick02, x2 = later[:K], later[K:]
-    out1 = backward(1, sub, seen, [y1, *col_sum(part1)], diag)
+    soon, later, early = out2[0:8:2], out2[1:8:2], out2[8:]
+    pick12 = row_parts(sub_sum(soon))
+    (part1, *early) = col_sum(correct((2,), pick12, factor), *early)
+    part1, pick02 = lax.optimization_barrier((part1, row_sum(sub_sum(early))))
+    out1 = backward(1, sub, seen, [y1, part1], diag)
     pick01 = row_parts(sub_sum(out1[0::2]))
     zero = jnp.zeros_like(pick02)
-    part0, *later = lax.optimization_barrier(
-        [correct((0, 1), pick01 + [pick02, zero, zero, zero], factor)] + list(out1[1::2])
-    )
-    x1 = row_sum(sub_sum(later))
-    (x0,) = backward(0, sub, rhs, [y0, *col_sum(part0)], diag)
+    part0 = correct((0, 1), pick01 + [pick02, zero, zero, zero], factor)
+    (part0, *later) = col_sum(part0, *later, *out1[1::2])
+    x12 = row_sum(jnp.concatenate([sub_sum(later[4:]), sub_sum(later[:4])]))
+    (x0,) = backward(0, sub, rhs, [y0, part0], diag)
     x0 = row_sum(x0)
-    return jnp.stack([x0, x1, x2])[:, None]
+    return jnp.concatenate([x0, x12]).reshape(LEVELS, 1, C, N)
 
 
 def solution(mesh):

time: 320 us -> 328 us (1.025)
  blocking collectives: 84.6 us -> 128 us
  starting transfers between devices: 94.5 us -> 80.3 us
  waiting for transfers between devices: 99.6 us -> 85.5 us
  other arithmetic: 8.27 us -> 3.91 us
    all_to_all x3 -> x4, blocking collectives: 63.9 us -> 85.6 us  [col_sum(): lax.all_to_all(blocks, 'col', 0, 0)]
    all_to_all x1 -> x2, blocking collectives: 20.7 us -> 42.1 us  [col_sum(): full = lax.all_to_all(own, 'col', 0, 0).reshape(part.shape)]
    all_to_all x4 -> x3, waiting for transfers between devices: 28.3 us -> 15.8 us  [col_sum(): full = lax.all_to_all(own, 'col', 0, 0).reshape(part.shape)]
    all_to_all x2 -> x1, waiting for transfers between devices: 25.3 us -> 16.9 us  [col_sum(): lax.all_to_all(blocks, 'col', 0, 0)]
    ppermute x42 -> x39, waiting for transfers between devices: 46.1 us -> 52.8 us  [swapped(): return lax.ppermute(value, axis, pairs)]
    ppermute x42 -> x39, starting transfers between devices: 60.4 us -> 55 us  [swapped(): return lax.ppermute(value, axis, pairs)]
    all_to_all x4 -> x3, starting transfers between devices: 18.2 us -> 13.6 us  [col_sum(): full = lax.all_to_all(own, 'col', 0, 0).reshape(part.shape)]
    all_to_all x2 -> x1, starting transfers between devices: 15.8 us -> 11.7 us  [col_sum(): lax.all_to_all(blocks, 'col', 0, 0)]
  transfers between devices with their start and end apart: 48 -> 43, of which waited for: 27 -> 26; matrix products, arithmetic and copies ran while one was open for 3% -> 1% of each run, Pallas kernels for 2% -> 1%
where the time goes in v5:
time: 328 us; the launch traced here: 327 us
  blocking collectives  128 us (39%)
  waiting for transfers between devices  85.5 us (26%)
  starting transfers between devices  80.3 us (24%)
  Pallas kernels  22.9 us (7%)
  local copies, waits for them, and re-layouts  5.62 us (2%)
  other arithmetic  3.91 us (1%)
    all_to_all x4, blocking collectives, col_sum(): lax.all_to_all(blocks, 'col', 0, 0)  85.6 us
    ppermute x39, starting transfers between devices, swapped(): return lax.ppermute(value, axis, pairs)  55 us
    ppermute x39, waiting for transfers between devices, swapped(): return lax.ppermute(value, axis, pairs)  52.8 us
    all_to_all x2, blocking collectives, col_sum(): full = lax.all_to_all(own, 'col', 0, 0).reshape(part.shape)  42.1 us
    pallas_call x6, Pallas kernels, call(): pl.pallas_call(functools.partial(kernel, level), in_specs=[pl.BlockSpec(m...  18.2 us
    all_to_all x1, waiting for transfers between devices, col_sum(): lax.all_to_all(blocks, 'col', 0, 0)  16.9 us
    all_to_all x3, waiting for transfers between devices, col_sum(): full = lax.all_to_all(own, 'col', 0, 0).reshape(part.shape)  15.8 us
    all_to_all x3, starting transfers between devices, col_sum(): full = lax.all_to_all(own, 'col', 0, 0).reshape(part.shape)  13.6 us
  transfers between devices with their start and end apart: 43, of which 26 were waited for; matrix products, arithmetic and copies ran while one was open for 1% of the time, Pallas kernels for 1%

profile of v5, /device:TPU:1, one launch (start us, length us, event | category | flops | bytes accessed | tf_op | source)
XLA Modules:
  0.0 327.2 jit_solution(4210976247066455468)
XLA Ops:
  1.0 2.7 forward_kernel0.1
  3.7 11.7 %all-to-all-start = ((f32[16,64,128]{2,1,0:T(8,128)}), f32[16,64,128]{2,1,0:T(8,128)S(1)}, u32[]{:S(2)}, u32[]{:S(2)}) async-start(f32[16,64,128]{2,1,0:T(8,128)} %bitcast.4), calls=%async_computation | async-start | bytes 1048576 | tf_op jit(solution)/shard_map/all_to_all | solution.py:250
  15.8 16.9 %all-to-all-done.parts_ref = f32[16,64,128]{2,1,0:T(8,128)S(1)} async-done(((f32[16,64,128]{2,1,0:T(8,128)}), f32[16,64,128]{2,1,0:T(8,128)S(1)}, u32[]{:S(2)}, u32[]{:S(2)}) %all-to-all-start) | async-done | bytes 524320 | tf_op jit(solution)/shard_map/all_to_all | solution.py:250
  33.5 4.7 %all-to-all-start.1 = ((f32[16,64,128]{2,1,0:T(8,128)}), f32[16,64,128]{2,1,0:T(8,128)S(1)}, u32[]{:S(2)}, u32[]{:S(2)}) async-start(f32[16,64,128]{2,1,0:T(8,128)} %fold.5), calls=%async_computation.1 | async-start | bytes 1048576 | tf_op jit(solution)/shard_map/all_to_all | solution.py:251
  38.3 2.8 collective-permute-start.2
  41.1 1.3 collective-permute-start.1
  42.4 13.2 %all-to-all-done.1 = f32[16,64,128]{2,1,0:T(8,128)S(1)} async-done(((f32[16,64,128]{2,1,0:T(8,128)}), f32[16,64,128]{2,1,0:T(8,128)S(1)}, u32[]{:S(2)}, u32[]{:S(2)}) %all-to-all-start.1) | async-done | bytes 524320 | tf_op jit(solution)/shard_map/all_to_all | solution.py:251
  56.0 2.4 collective-permute-start.3
  58.7 1.4 collective-permute-start.5
  61.0 1.3 pad_maximum_fusion.seen_ref
  62.3 1.4 collective-permute-done.5
  63.7 1.4 collective-permute-start.6
  65.4 1.9 collective-permute-done.6.refs_1_
  67.3 2.3 forward_kernel1.1
  69.6 19.7 %all_to_all.50.parts_ref = f32[16,64,128]{2,1,0:T(8,128)S(1)} all-to-all(f32[16,64,128]{2,1,0:T(8,128)S(1)} %bitcast.66), channel_id=1, replica_groups=mesh['sub'=4,'row'=4,'col'=16] {'col'}, dimensions={0} | all-to-all | bytes 1048576 | tf_op jit(solution)/shard_map/all_to_all | solution.py:250
  89.3 20.3 %all_to_all.51 = f32[16,64,128]{2,1,0:T(8,128)S(1)} all-to-all(f32[16,64,128]{2,1,0:T(8,128)S(1)} %fold.6), channel_id=1, replica_groups=mesh['sub'=4,'row'=4,'col'=16] {'col'}, dimensions={0} | all-to-all | bytes 1048576 | tf_op jit(solution)/shard_map/all_to_all | solution.py:251
  110.4 3.7 %collective-permute-start.7 = (f32[256,128]{1,0:T(8,128)S(1)}, f32[256,128]{1,0:T(8,128)S(1)}, u32[]{:S(2)}, u32[]{:S(2)}) collective-permute-start(f32[256,128]{1,0:T(8,128)S(1)} %join.1), channel_id=1, source_target_pairs={{0,16},{16,0},{32,48},{48,32},{1,17},{17,1},{33,49},{49,33},{2,18}... | collective-permute-start | bytes 393224 | tf_op jit(solution)/shard_map/ppermute | solution.py:225
  114.2 1.6 collective-permute-start.9
  115.8 3.4 %collective-permute-done.8 = f32[256,128]{1,0:T(8,128)S(1)} collective-permute-done((f32[256,128]{1,0:T(8,128)S(1)}, f32[256,128]{1,0:T(8,128)S(1)}, u32[]{:S(2)}, u32[]{:S(2)}) %collective-permute-start.8) | collective-permute-done | bytes 131104 | tf_op jit(solution)/shard_map/ppermute | solution.py:225
  119.2 3.0 collective-permute-done.9
  122.2 1.4 collective-permute-start.10
  123.6 2.6 collective-permute-start.11
  127.1 5.3 %collective-permute-done.11.refs_2_ = f32[256,128]{1,0:T(8,128)S(1)} collective-permute-done((f32[256,128]{1,0:T(8,128)S(1)}, f32[256,128]{1,0:T(8,128)S(1)}, u32[]{:S(2)}, u32[]{:S(2)}) %collective-permute-start.11) | collective-permute-done | bytes 131104 | tf_op jit(solution)/shard_map/ppermute | solution.py:225
  132.4 2.5 collective-permute-done.12.refs_3_
  134.9 3.0 forward_kernel2.1
  138.0 19.8 %all_to_all.52.parts_ref = f32[16,64,128]{2,1,0:T(8,128)S(1)} all-to-all(f32[16,64,128]{2,1,0:T(8,128)S(1)} %bitcast.65), channel_id=1, replica_groups=mesh['sub'=4,'row'=4,'col'=16] {'col'}, dimensions={0} | all-to-all | bytes 1048576 | tf_op jit(solution)/shard_map/all_to_all | solution.py:250
  157.8 21.8 %all_to_all.53 = f32[16,64,128]{2,1,0:T(8,128)S(1)} all-to-all(f32[16,64,128]{2,1,0:T(8,128)S(1)} %fold.7), channel_id=1, replica_groups=mesh['sub'=4,'row'=4,'col'=16] {'col'}, dimensions={0} | all-to-all | bytes 1048576 | tf_op jit(solution)/shard_map/all_to_all | solution.py:251
  179.6 4.0 %backward_kernel2.1 = (f32[128,128]{1,0:T(8,128)S(1)}, f32[256,128]{1,0:T(8,128)S(1)}, f32[128,128]{1,0:T(8,128)S(1)}, f32[256,128]{1,0:T(8,128)S(1)}, f32[128,1...) custom-call(s32[1]{0:T(128)} %bitcast.sub_ref, ...), custom_call_target="tpu_custom_call" | custom-call | flops 805306368 | bytes 4194304 | tf_op jit(solution)/shard_map/backward_kernel2/pallas_call | solution.py:141
  185.0 1.4 collective-permute-start.14
  186.4 2.5 collective-permute-start.15
  190.7 4.1 %collective-permute-start.16 = (f32[128,128]{1,0:T(8,128)S(1)}, f32[128,128]{1,0:T(8,128)S(1)}, u32[]{:S(2)}, u32[]{:S(2)}) collective-permute-start(f32[128,128]{1,0:T(8,128)S(1)} %add_add_fusion.6.refs_0_), channel_id=1, source_target_pairs={{0,16},{16,0},{32,48},{48,32},{1,17},{17,1},{33,49},{49,33},{2,18}... | collective-permute-start | bytes 196616 | tf_op jit(solution)/shard_map/ppermute | solution.py:225
  195.5 1.1 collective-permute-start.18
  196.6 1.8 collective-permute-done.17.refs_2_
  198.4 1.7 collective-permute-done.18.refs_3_
  201.2 20.1 %all_to_all.54.parts_ref = f32[16,64,128]{2,1,0:T(8,128)S(1)} all-to-all(f32[16,64,128]{2,1,0:T(8,128)S(1)} %bitcast.67), channel_id=1, replica_groups=mesh['sub'=4,'row'=4,'col'=16] {'col'}, dimensions={0} | all-to-all | bytes 1048576 | tf_op jit(solution)/shard_map/all_to_all | solution.py:250
  222.2 4.4 %all-to-all-start.7 = ((f32[16,64,128]{2,1,0:T(8,128)}), f32[16,64,128]{2,1,0:T(8,128)}, u32[]{:S(2)}, u32[]{:S(2)}) async-start(f32[16,64,128]{2,1,0:T(8,128)} %copy-done.5), calls=%async_computation.7 | async-start | bytes 1048576 | tf_op jit(solution)/shard_map/all_to_all | solution.py:251
  226.9 3.6 %collective-permute-start.20 = (f32[128,128]{1,0:T(8,128)}, f32[128,128]{1,0:T(8,128)S(1)}, u32[]{:S(2)}, u32[]{:S(2)}) collective-permute-start(f32[128,128]{1,0:T(8,128)} %copy-done.21), channel_id=1, source_target_pairs={{0,128},{64,192},{128,0},{192,64},{1,129},{65,193},{129,1},{193,65... | collective-permute-start | bytes 196616 | tf_op jit(solution)/shard_map/ppermute | solution.py:225
  230.6 2.4 collective-permute-done.20
  233.0 2.4 collective-permute-done.21
  236.2 3.8 %collective-permute-start.22 = (f32[128,128]{1,0:T(8,128)S(1)}, f32[128,128]{1,0:T(8,128)S(1)}, u32[]{:S(2)}, u32[]{:S(2)}) collective-permute-start(f32[128,128]{1,0:T(8,128)S(1)} %add_add_fusion.5), channel_id=1, source_target_pairs={{0,16},{16,0},{32,48},{48,32},{1,17},{17,1},{33,49},{49,33},{2,18}... | collective-permute-start | bytes 196616 | tf_op jit(solution)/shard_map/ppermute | solution.py:225
  241.8 2.3 collective-permute-done.23
  244.1 2.0 collective-permute-done.24
  247.7 4.0 %backward_kernel1.1 = (f32[128,128]{1,0:T(8,128)S(1)}, f32[256,128]{1,0:T(8,128)S(1)}, f32[128,128]{1,0:T(8,128)S(1)}, f32[256,128]{1,0:T(8,128)S(1)}) custom-call(s32[1]{0:T(128)} %bitcast.sub_ref, f32[4,520,128]{2,1,0:T(8,128)S(1)} %pad_maximum_fusion.seen_ref, f32[1024,128]{1,0:T(8,128)S(1)} %bitcast.59, f32[1024,128]{1,0:T(8,128)} %bitcast.22.refs_0_, ...), custom_call_target="tpu_custom_call" | custom-call | flops 402653184 | bytes 2097152 | tf_op jit(solution)/shard_map/backward_kernel1/pallas_call | solution.py:141
  251.8 3.5 %collective-permute-done.25 = f32[128,128]{1,0:T(8,128)S(1)} collective-permute-done((f32[128,128]{1,0:T(8,128)S(1)}, f32[128,128]{1,0:T(8,128)S(1)}, u32[]{:S(2)}, u32[]{:S(2)}) %collective-permute-start.25) | collective-permute-done | bytes 65568 | tf_op jit(solution)/shard_map/ppermute | solution.py:225
  255.3 1.1 collective-permute-start.26
  257.0 1.1 collective-permute-start.28
  258.1 1.8 collective-permute-done.27.refs_2_
  259.9 1.7 collective-permute-done.28.refs_3_
  261.6 1.3 correct2.1
  263.0 26.0 %all_to_all.55.parts_ref = f32[16,64,128]{2,1,0:T(8,128)S(1)} all-to-all(f32[16,64,128]{2,1,0:T(8,128)S(1)} %bitcast.64), channel_id=1, replica_groups=mesh['sub'=4,'row'=4,'col'=16] {'col'}, dimensions={0} | all-to-all | bytes 1048576 | tf_op jit(solution)/shard_map/all_to_all | solution.py:250
  289.9 4.5 %all-to-all-start.9 = ((f32[16,64,128]{2,1,0:T(8,128)}), f32[16,64,128]{2,1,0:T(8,128)S(1)}, u32[]{:S(2)}, u32[]{:S(2)}) async-start(f32[16,64,128]{2,1,0:T(8,128)} %fold.9), calls=%async_computation.9 | async-start | bytes 1048576 | tf_op jit(solution)/shard_map/all_to_all | solution.py:251
  294.7 1.4 collective-permute-start.33
  296.4 2.3 collective-permute-start.35
  298.7 2.1 collective-permute-done.33
  300.8 2.9 collective-permute-done.34
  303.8 3.0 collective-permute-start.36
  307.1 1.4 collective-permute-start.38
  308.5 2.6 all-to-all-done.9
  311.1 2.3 backward_kernel0.1
  313.5 3.0 collective-permute-start.29
  316.8 1.4 collective-permute-start.31
  318.2 3.1 collective-permute-done.38
  321.4 1.9 collective-permute-done.30
  323.3 3.1 collective-permute-done.31
  (119 shorter events, 20.3 us)
Async XLA Ops:
  3.7 11.7 %copy-start.4 = (f32[3,1,256,128]{3,2,1,0:T(8,128)S(1)}, f32[3,1,256,128]{3,2,1,0:T(8,128)}, u32[]{:S(2)}) copy-start(f32[3,1,256,128]{3,2,1,0:T(8,128)} %param.4) | copy-start | bytes 1179652
  3.7 11.9 %copy-start.27 = (s32[3,1,128]{2,1,0:T(1,128)S(1)}, s32[3,1,128]{2,1,0:T(1,128)}, u32[]{:S(2)}) copy-start(s32[3,1,128]{2,1,0:T(1,128)} %param.7) | copy-start | bytes 4612
  3.7 28.9 %all-to-all-start = ((f32[16,64,128]{2,1,0:T(8,128)}), f32[16,64,128]{2,1,0:T(8,128)S(1)}, u32[]{:S(2)}, u32[]{:S(2)}) async-start(f32[16,64,128]{2,1,0:T(8,128)} %bitcast.4), calls=%async_computation | async-start | bytes 1048576 | tf_op jit(solution)/shard_map/all_to_all | solution.py:250
  15.7 40.2 %copy-start.23 = (f32[520,128]{1,0:T(8,128)}, f32[520,128]{1,0:T(8,128)S(1)}, u32[]{:S(2)}) copy-start(f32[520,128]{1,0:T(8,128)S(1)} %maximum_maximum_fusion) | copy-start | bytes 798724
  15.7 39.8 %copy-start = (f32[3,1,128,1024]{3,2,1,0:T(8,128)S(1)}, f32[3,1,128,1024]{3,2,1,0:T(8,128)}, u32[]{:S(2)}) copy-start(f32[3,1,128,1024]{3,2,1,0:T(8,128)} %param.6) | copy-start | bytes 4718596
  33.5 22.0 %all-to-all-start.1 = ((f32[16,64,128]{2,1,0:T(8,128)}), f32[16,64,128]{2,1,0:T(8,128)S(1)}, u32[]{:S(2)}, u32[]{:S(2)}) async-start(f32[16,64,128]{2,1,0:T(8,128)} %fold.5), calls=%async_computation.1 | async-start | bytes 1048576 | tf_op jit(solution)/shard_map/all_to_all | solution.py:251
  38.3 20.5 %collective-permute-start.2 = (f32[520,128]{1,0:T(8,128)S(1)}, f32[520,128]{1,0:T(8,128)S(1)}, u32[]{:S(2)}, u32[]{:S(2)}) collective-permute-start(f32[520,128]{1,0:T(8,128)S(1)} %maximum_maximum_fusion), channel_id=1, source_target_pairs={{0,192},{64,128},{128,64},{192,0},{1,193},{65,129},{129,65},{193,1... | collective-permute-start | bytes 798728 | tf_op jit(solution)/shard_map/ppermute | solution.py:225
  41.1 19.1 %collective-permute-start = (f32[520,128]{1,0:T(8,128)S(1)}, f32[520,128]{1,0:T(8,128)S(1)}, u32[]{:S(2)}, u32[]{:S(2)}) collective-permute-start(f32[520,128]{1,0:T(8,128)S(1)} %maximum_maximum_fusion), channel_id=1, source_target_pairs={{0,64},{64,0},{128,192},{192,128},{1,65},{65,1},{129,193},{193,129... | collective-permute-start | bytes 798728 | tf_op jit(solution)/shard_map/ppermute | solution.py:225
  41.1 19.1 %collective-permute-start.1 = (f32[520,128]{1,0:T(8,128)S(1)}, f32[520,128]{1,0:T(8,128)S(1)}, u32[]{:S(2)}, u32[]{:S(2)}) collective-permute-start(f32[520,128]{1,0:T(8,128)S(1)} %maximum_maximum_fusion), channel_id=1, source_target_pairs={{0,128},{64,192},{128,0},{192,64},{1,129},{65,193},{129,1},{193,65... | collective-permute-start | bytes 798728 | tf_op jit(solution)/shard_map/ppermute | solution.py:225
  56.0 6.3 %collective-permute-start.3 = (f32[128,128]{1,0:T(8,128)S(1)}, f32[128,128]{1,0:T(8,128)S(1)}, u32[]{:S(2)}, u32[]{:S(2)}) collective-permute-start(f32[128,128]{1,0:T(8,128)S(1)} %convolution_bitcast_fusion.1), channel_id=1, source_target_pairs={{0,16},{16,0},{32,48},{48,32},{1,17},{17,1},{33,49},{49,33},{2,18}... | collective-permute-start | bytes 196616 | tf_op jit(solution)/shard_map/ppermute | solution.py:225
  58.4 3.8 %collective-permute-start.4 = (f32[128,128]{1,0:T(8,128)S(1)}, f32[128,128]{1,0:T(8,128)S(1)}, u32[]{:S(2)}, u32[]{:S(2)}) collective-permute-start(f32[128,128]{1,0:T(8,128)S(1)} %convolution_bitcast_fusion.1), channel_id=1, source_target_pairs={{0,32},{16,48},{32,0},{48,16},{1,33},{17,49},{33,1},{49,17},{2,34}... | collective-permute-start | bytes 196616 | tf_op jit(solution)/shard_map/ppermute | solution.py:225
  58.7 1.4 copy-start.24
  58.7 4.9 %collective-permute-start.5 = (f32[128,128]{1,0:T(8,128)S(1)}, f32[128,128]{1,0:T(8,128)S(1)}, u32[]{:S(2)}, u32[]{:S(2)}) collective-permute-start(f32[128,128]{1,0:T(8,128)S(1)} %convolution_bitcast_fusion.1), channel_id=1, source_target_pairs={{0,48},{16,32},{32,16},{48,0},{1,49},{17,33},{33,17},{49,1},{2,50}... | collective-permute-start | bytes 196616 | tf_op jit(solution)/shard_map/ppermute | solution.py:225
  63.7 3.6 %collective-permute-start.6 = (f32[128,128]{1,0:T(8,128)S(1)}, f32[128,128]{1,0:T(8,128)S(1)}, u32[]{:S(2)}, u32[]{:S(2)}) collective-permute-start(f32[128,128]{1,0:T(8,128)S(1)} %add_add_fusion.7.refs_0_), channel_id=1, source_target_pairs={{0,64},{64,0},{128,192},{192,128},{1,65},{65,1},{129,193},{193,129... | collective-permute-start | bytes 196616 | tf_op jit(solution)/shard_map/ppermute | solution.py:225
  110.4 5.4 %collective-permute-start.7 = (f32[256,128]{1,0:T(8,128)S(1)}, f32[256,128]{1,0:T(8,128)S(1)}, u32[]{:S(2)}, u32[]{:S(2)}) collective-permute-start(f32[256,128]{1,0:T(8,128)S(1)} %join.1), channel_id=1, source_target_pairs={{0,16},{16,0},{32,48},{48,32},{1,17},{17,1},{33,49},{49,33},{2,18}... | collective-permute-start | bytes 393224 | tf_op jit(solution)/shard_map/ppermute | solution.py:225
  114.1 5.1 %collective-permute-start.8 = (f32[256,128]{1,0:T(8,128)S(1)}, f32[256,128]{1,0:T(8,128)S(1)}, u32[]{:S(2)}, u32[]{:S(2)}) collective-permute-start(f32[256,128]{1,0:T(8,128)S(1)} %join.1), channel_id=1, source_target_pairs={{0,32},{16,48},{32,0},{48,16},{1,33},{17,49},{33,1},{49,17},{2,34}... | collective-permute-start | bytes 393224 | tf_op jit(solution)/shard_map/ppermute | solution.py:225
  114.2 8.0 %collective-permute-start.9 = (f32[256,128]{1,0:T(8,128)S(1)}, f32[256,128]{1,0:T(8,128)S(1)}, u32[]{:S(2)}, u32[]{:S(2)}) collective-permute-start(f32[256,128]{1,0:T(8,128)S(1)} %join.1), channel_id=1, source_target_pairs={{0,48},{16,32},{32,16},{48,0},{1,49},{17,33},{33,17},{49,1},{2,50}... | collective-permute-start | bytes 393224 | tf_op jit(solution)/shard_map/ppermute | solution.py:225
  122.2 4.9 %collective-permute-start.10 = (f32[256,128]{1,0:T(8,128)S(1)}, f32[256,128]{1,0:T(8,128)S(1)}, u32[]{:S(2)}, u32[]{:S(2)}) collective-permute-start(f32[256,128]{1,0:T(8,128)S(1)} %add_add_fusion.3.refs_0_), channel_id=1, source_target_pairs={{0,64},{64,0},{128,192},{192,128},{1,65},{65,1},{129,193},{193,129... | collective-permute-start | bytes 393224 | tf_op jit(solution)/shard_map/ppermute | solution.py:225
  123.6 8.8 %collective-permute-start.11 = (f32[256,128]{1,0:T(8,128)S(1)}, f32[256,128]{1,0:T(8,128)S(1)}, u32[]{:S(2)}, u32[]{:S(2)}) collective-permute-start(f32[256,128]{1,0:T(8,128)S(1)} %add_add_fusion.3.refs_0_), channel_id=1, source_target_pairs={{0,128},{64,192},{128,0},{192,64},{1,129},{65,193},{129,1},{193,65... | collective-permute-start | bytes 393224 | tf_op jit(solution)/shard_map/ppermute | solution.py:225
  126.2 8.8 %collective-permute-start.12 = (f32[256,128]{1,0:T(8,128)S(1)}, f32[256,128]{1,0:T(8,128)S(1)}, u32[]{:S(2)}, u32[]{:S(2)}) collective-permute-start(f32[256,128]{1,0:T(8,128)S(1)} %add_add_fusion.3.refs_0_), channel_id=1, source_target_pairs={{0,192},{64,128},{128,64},{192,0},{1,193},{65,129},{129,65},{193,1... | collective-permute-start | bytes 393224 | tf_op jit(solution)/shard_map/ppermute | solution.py:225
  184.9 9.9 %copy-start.14 = (f32[256,128]{1,0:T(8,128)}, f32[256,128]{1,0:T(8,128)S(1)}, u32[]{:S(2)}) copy-start(f32[256,128]{1,0:T(8,128)S(1)} %get-tuple-element.71) | copy-start | bytes 393220
  184.9 16.2 %copy-start.7 = (f32[256,128]{1,0:T(8,128)}, f32[256,128]{1,0:T(8,128)S(1)}, u32[]{:S(2)}) copy-start(f32[256,128]{1,0:T(8,128)S(1)} %get-tuple-element.69) | copy-start | bytes 393220
  184.9 16.3 %copy-start.11 = (f32[128,128]{1,0:T(8,128)}, f32[128,128]{1,0:T(8,128)S(1)}, u32[]{:S(2)}) copy-start(f32[128,128]{1,0:T(8,128)S(1)} %get-tuple-element.52) | copy-start | bytes 196612
  184.9 16.3 %copy-start.20 = (f32[128,128]{1,0:T(8,128)}, f32[128,128]{1,0:T(8,128)S(1)}, u32[]{:S(2)}) copy-start(f32[128,128]{1,0:T(8,128)S(1)} %get-tuple-element.55) | copy-start | bytes 196612
  184.9 16.3 %copy-start.21 = (f32[128,128]{1,0:T(8,128)}, f32[128,128]{1,0:T(8,128)S(1)}, u32[]{:S(2)}) copy-start(f32[128,128]{1,0:T(8,128)S(1)} %get-tuple-element.54) | copy-start | bytes 196612
  184.9 16.3 %copy-start.22 = (f32[128,128]{1,0:T(8,128)}, f32[128,128]{1,0:T(8,128)S(1)}, u32[]{:S(2)}) copy-start(f32[128,128]{1,0:T(8,128)S(1)} %get-tuple-element.53) | copy-start | bytes 196612
  184.9 3.9 %collective-permute-start.13 = (f32[128,128]{1,0:T(8,128)S(1)}, f32[128,128]{1,0:T(8,128)S(1)}, u32[]{:S(2)}, u32[]{:S(2)}) collective-permute-start(f32[128,128]{1,0:T(8,128)S(1)} %get-tuple-element.44), channel_id=1, source_target_pairs={{0,64},{64,0},{128,192},{192,128},{1,65},{65,1},{129,193},{193,129... | collective-permute-start | bytes 196616 | tf_op jit(solution)/shard_map/ppermute | solution.py:225
  185.0 4.7 %collective-permute-start.14 = (f32[128,128]{1,0:T(8,128)S(1)}, f32[128,128]{1,0:T(8,128)S(1)}, u32[]{:S(2)}, u32[]{:S(2)}) collective-permute-start(f32[128,128]{1,0:T(8,128)S(1)} %get-tuple-element.45), channel_id=1, source_target_pairs={{0,128},{64,192},{128,0},{192,64},{1,129},{65,193},{129,1},{193,65... | collective-permute-start | bytes 196616 | tf_op jit(solution)/shard_map/ppermute | solution.py:225
  186.4 4.3 %collective-permute-start.15 = (f32[128,128]{1,0:T(8,128)S(1)}, f32[128,128]{1,0:T(8,128)S(1)}, u32[]{:S(2)}, u32[]{:S(2)}) collective-permute-start(f32[128,128]{1,0:T(8,128)S(1)} %get-tuple-element.46), channel_id=1, source_target_pairs={{0,192},{64,128},{128,64},{192,0},{1,193},{65,129},{129,65},{193,1... | collective-permute-start | bytes 196616 | tf_op jit(solution)/shard_map/ppermute | solution.py:225
  190.7 5.9 %collective-permute-start.16 = (f32[128,128]{1,0:T(8,128)S(1)}, f32[128,128]{1,0:T(8,128)S(1)}, u32[]{:S(2)}, u32[]{:S(2)}) collective-permute-start(f32[128,128]{1,0:T(8,128)S(1)} %add_add_fusion.6.refs_0_), channel_id=1, source_target_pairs={{0,16},{16,0},{32,48},{48,32},{1,17},{17,1},{33,49},{49,33},{2,18}... | collective-permute-start | bytes 196616 | tf_op jit(solution)/shard_map/ppermute | solution.py:225
  194.8 3.5 %collective-permute-start.17 = (f32[128,128]{1,0:T(8,128)S(1)}, f32[128,128]{1,0:T(8,128)S(1)}, u32[]{:S(2)}, u32[]{:S(2)}) collective-permute-start(f32[128,128]{1,0:T(8,128)S(1)} %add_add_fusion.6.refs_0_), channel_id=1, source_target_pairs={{0,32},{16,48},{32,0},{48,16},{1,33},{17,49},{33,1},{49,17},{2,34}... | collective-permute-start | bytes 196616 | tf_op jit(solution)/shard_map/ppermute | solution.py:225
  195.5 4.6 %collective-permute-start.18 = (f32[128,128]{1,0:T(8,128)S(1)}, f32[128,128]{1,0:T(8,128)S(1)}, u32[]{:S(2)}, u32[]{:S(2)}) collective-permute-start(f32[128,128]{1,0:T(8,128)S(1)} %add_add_fusion.6.refs_0_), channel_id=1, source_target_pairs={{0,48},{16,32},{32,16},{48,0},{1,49},{17,33},{33,17},{49,1},{2,50}... | collective-permute-start | bytes 196616 | tf_op jit(solution)/shard_map/ppermute | solution.py:225
  222.2 24.4 %all-to-all-start.7 = ((f32[16,64,128]{2,1,0:T(8,128)}), f32[16,64,128]{2,1,0:T(8,128)}, u32[]{:S(2)}, u32[]{:S(2)}) async-start(f32[16,64,128]{2,1,0:T(8,128)} %copy-done.5), calls=%async_computation.7 | async-start | bytes 1048576 | tf_op jit(solution)/shard_map/all_to_all | solution.py:251
  226.7 3.9 %collective-permute-start.19 = (f32[128,128]{1,0:T(8,128)}, f32[128,128]{1,0:T(8,128)S(1)}, u32[]{:S(2)}, u32[]{:S(2)}) collective-permute-start(f32[128,128]{1,0:T(8,128)} %copy-done.22), channel_id=1, source_target_pairs={{0,64},{64,0},{128,192},{192,128},{1,65},{65,1},{129,193},{193,129... | collective-permute-start | bytes 196616 | tf_op jit(solution)/shard_map/ppermute | solution.py:225
  226.9 6.1 %collective-permute-start.20 = (f32[128,128]{1,0:T(8,128)}, f32[128,128]{1,0:T(8,128)S(1)}, u32[]{:S(2)}, u32[]{:S(2)}) collective-permute-start(f32[128,128]{1,0:T(8,128)} %copy-done.21), channel_id=1, source_target_pairs={{0,128},{64,192},{128,0},{192,64},{1,129},{65,193},{129,1},{193,65... | collective-permute-start | bytes 196616 | tf_op jit(solution)/shard_map/ppermute | solution.py:225
  230.4 4.9 %collective-permute-start.21 = (f32[128,128]{1,0:T(8,128)}, f32[128,128]{1,0:T(8,128)S(1)}, u32[]{:S(2)}, u32[]{:S(2)}) collective-permute-start(f32[128,128]{1,0:T(8,128)} %copy-done.20), channel_id=1, source_target_pairs={{0,192},{64,128},{128,64},{192,0},{1,193},{65,129},{129,65},{193,1... | collective-permute-start | bytes 196616 | tf_op jit(solution)/shard_map/ppermute | solution.py:225
  236.2 5.5 %collective-permute-start.22 = (f32[128,128]{1,0:T(8,128)S(1)}, f32[128,128]{1,0:T(8,128)S(1)}, u32[]{:S(2)}, u32[]{:S(2)}) collective-permute-start(f32[128,128]{1,0:T(8,128)S(1)} %add_add_fusion.5), channel_id=1, source_target_pairs={{0,16},{16,0},{32,48},{48,32},{1,17},{17,1},{33,49},{49,33},{2,18}... | collective-permute-start | bytes 196616 | tf_op jit(solution)/shard_map/ppermute | solution.py:225
  240.0 4.0 %collective-permute-start.23 = (f32[128,128]{1,0:T(8,128)S(1)}, f32[128,128]{1,0:T(8,128)S(1)}, u32[]{:S(2)}, u32[]{:S(2)}) collective-permute-start(f32[128,128]{1,0:T(8,128)S(1)} %add_add_fusion.5), channel_id=1, source_target_pairs={{0,32},{16,48},{32,0},{48,16},{1,33},{17,49},{33,1},{49,17},{2,34}... | collective-permute-start | bytes 196616 | tf_op jit(solution)/shard_map/ppermute | solution.py:225
  240.7 5.3 %collective-permute-start.24 = (f32[128,128]{1,0:T(8,128)S(1)}, f32[128,128]{1,0:T(8,128)S(1)}, u32[]{:S(2)}, u32[]{:S(2)}) collective-permute-start(f32[128,128]{1,0:T(8,128)S(1)} %add_add_fusion.5), channel_id=1, source_target_pairs={{0,48},{16,32},{32,16},{48,0},{1,49},{17,33},{33,17},{49,1},{2,50}... | collective-permute-start | bytes 196616 | tf_op jit(solution)/shard_map/ppermute | solution.py:225
  246.7 1.0 copy-start.2
  247.7 13.9 %copy-start.6 = (f32[128,128]{1,0:T(8,128)S(1)}, f32[128,128]{1,0:T(8,128)}, u32[]{:S(2)}) copy-start(f32[128,128]{1,0:T(8,128)} %add_add_fusion.4.refs_4_) | copy-start | bytes 196612
  251.7 11.3 %copy-start.9 = (f32[256,128]{1,0:T(8,128)}, f32[256,128]{1,0:T(8,128)S(1)}, u32[]{:S(2)}) copy-start(f32[256,128]{1,0:T(8,128)S(1)} %get-tuple-element.67) | copy-start | bytes 393220
  251.7 11.3 %copy-start.18 = (f32[256,128]{1,0:T(8,128)}, f32[256,128]{1,0:T(8,128)S(1)}, u32[]{:S(2)}) copy-start(f32[256,128]{1,0:T(8,128)S(1)} %get-tuple-element.68) | copy-start | bytes 393220
  251.7 3.6 %collective-permute-start.25 = (f32[128,128]{1,0:T(8,128)S(1)}, f32[128,128]{1,0:T(8,128)S(1)}, u32[]{:S(2)}, u32[]{:S(2)}) collective-permute-start(f32[128,128]{1,0:T(8,128)S(1)} %get-tuple-element.58), channel_id=1, source_target_pairs={{0,64},{64,0},{128,192},{192,128},{1,65},{65,1},{129,193},{193,129... | collective-permute-start | bytes 196616 | tf_op jit(solution)/shard_map/ppermute | solution.py:225
  255.3 2.8 collective-permute-start.26
  256.4 3.5 %collective-permute-start.27 = (f32[128,128]{1,0:T(8,128)S(1)}, f32[128,128]{1,0:T(8,128)S(1)}, u32[]{:S(2)}, u32[]{:S(2)}) collective-permute-start(f32[128,128]{1,0:T(8,128)S(1)} %add.105.refs_0_), channel_id=1, source_target_pairs={{0,32},{16,48},{32,0},{48,16},{1,33},{17,49},{33,1},{49,17},{2,34}... | collective-permute-start | bytes 196616 | tf_op jit(solution)/shard_map/ppermute | solution.py:225
  257.0 4.6 %collective-permute-start.28 = (f32[128,128]{1,0:T(8,128)S(1)}, f32[128,128]{1,0:T(8,128)S(1)}, u32[]{:S(2)}, u32[]{:S(2)}) collective-permute-start(f32[128,128]{1,0:T(8,128)S(1)} %add.105.refs_0_), channel_id=1, source_target_pairs={{0,48},{16,32},{32,16},{48,0},{1,49},{17,33},{33,17},{49,1},{2,50}... | collective-permute-start | bytes 196616 | tf_op jit(solution)/shard_map/ppermute | solution.py:225
  289.0 5.4 %copy-start.19 = (f32[256,128]{1,0:T(8,128)S(1)}, f32[256,128]{1,0:T(8,128)}, u32[]{:S(2)}) copy-start(f32[256,128]{1,0:T(8,128)} %copy-done.18) | copy-start | bytes 393220
  289.0 5.7 %copy-start.17 = (f32[256,128]{1,0:T(8,128)S(1)}, f32[256,128]{1,0:T(8,128)}, u32[]{:S(2)}) copy-start(f32[256,128]{1,0:T(8,128)} %copy-done.16) | copy-start | bytes 393220
  289.0 7.2 %copy-start.15 = (f32[256,128]{1,0:T(8,128)S(1)}, f32[256,128]{1,0:T(8,128)}, u32[]{:S(2)}) copy-start(f32[256,128]{1,0:T(8,128)} %copy-done.14) | copy-start | bytes 393220
  289.0 7.4 %copy-start.13 = (f32[256,128]{1,0:T(8,128)S(1)}, f32[256,128]{1,0:T(8,128)}, u32[]{:S(2)}) copy-start(f32[256,128]{1,0:T(8,128)} %copy-done.12) | copy-start | bytes 393220
  289.0 9.7 %copy-start.10 = (f32[256,128]{1,0:T(8,128)S(1)}, f32[256,128]{1,0:T(8,128)}, u32[]{:S(2)}) copy-start(f32[256,128]{1,0:T(8,128)} %copy-done.9) | copy-start | bytes 393220
  289.0 14.7 %copy-start.8 = (f32[256,128]{1,0:T(8,128)S(1)}, f32[256,128]{1,0:T(8,128)}, u32[]{:S(2)}) copy-start(f32[256,128]{1,0:T(8,128)} %copy-done.7) | copy-start | bytes 393220
  289.9 21.2 %all-to-all-start.9 = ((f32[16,64,128]{2,1,0:T(8,128)}), f32[16,64,128]{2,1,0:T(8,128)S(1)}, u32[]{:S(2)}, u32[]{:S(2)}) async-start(f32[16,64,128]{2,1,0:T(8,128)} %fold.9), calls=%async_computation.9 | async-start | bytes 1048576 | tf_op jit(solution)/shard_map/all_to_all | solution.py:251
  294.4 4.3 %collective-permute-start.32 = (f32[256,128]{1,0:T(8,128)S(1)}, f32[256,128]{1,0:T(8,128)S(1)}, u32[]{:S(2)}, u32[]{:S(2)}) collective-permute-start(f32[256,128]{1,0:T(8,128)S(1)} %copy-done.19), channel_id=1, source_target_pairs={{0,64},{64,0},{128,192},{192,128},{1,65},{65,1},{129,193},{193,129... | collective-permute-start | bytes 393224 | tf_op jit(solution)/shard_map/ppermute | solution.py:225
  294.7 6.1 %collective-permute-start.33 = (f32[256,128]{1,0:T(8,128)S(1)}, f32[256,128]{1,0:T(8,128)S(1)}, u32[]{:S(2)}, u32[]{:S(2)}) collective-permute-start(f32[256,128]{1,0:T(8,128)S(1)} %copy-done.17), channel_id=1, source_target_pairs={{0,64},{64,0},{128,192},{192,128},{1,65},{65,1},{129,193},{193,129... | collective-permute-start | bytes 393224 | tf_op jit(solution)/shard_map/ppermute | solution.py:225
  296.2 7.5 %collective-permute-start.34 = (f32[256,128]{1,0:T(8,128)S(1)}, f32[256,128]{1,0:T(8,128)S(1)}, u32[]{:S(2)}, u32[]{:S(2)}) collective-permute-start(f32[256,128]{1,0:T(8,128)S(1)} %copy-done.15), channel_id=1, source_target_pairs={{0,128},{64,192},{128,0},{192,64},{1,129},{65,193},{129,1},{193,65... | collective-permute-start | bytes 393224 | tf_op jit(solution)/shard_map/ppermute | solution.py:225
  296.4 7.3 %collective-permute-start.35 = (f32[256,128]{1,0:T(8,128)S(1)}, f32[256,128]{1,0:T(8,128)S(1)}, u32[]{:S(2)}, u32[]{:S(2)}) collective-permute-start(f32[256,128]{1,0:T(8,128)S(1)} %copy-done.13), channel_id=1, source_target_pairs={{0,192},{64,128},{128,64},{192,0},{1,193},{65,129},{129,65},{193,1... | collective-permute-start | bytes 393224 | tf_op jit(solution)/shard_map/ppermute | solution.py:225
  303.8 13.0 %collective-permute-start.36 = (f32[512,128]{1,0:T(8,128)S(1)}, f32[512,128]{1,0:T(8,128)S(1)}, u32[]{:S(2)}, u32[]{:S(2)}) collective-permute-start(f32[512,128]{1,0:T(8,128)S(1)} %pad_maximum_fusion.2), channel_id=1, source_target_pairs={{0,16},{16,0},{32,48},{48,32},{1,17},{17,1},{33,49},{49,33},{2,18}... | collective-permute-start | bytes 786440 | tf_op jit(solution)/shard_map/ppermute | solution.py:225
  306.8 11.5 %collective-permute-start.37 = (f32[512,128]{1,0:T(8,128)S(1)}, f32[512,128]{1,0:T(8,128)S(1)}, u32[]{:S(2)}, u32[]{:S(2)}) collective-permute-start(f32[512,128]{1,0:T(8,128)S(1)} %pad_maximum_fusion.2), channel_id=1, source_target_pairs={{0,32},{16,48},{32,0},{48,16},{1,33},{17,49},{33,1},{49,17},{2,34}... | collective-permute-start | bytes 786440 | tf_op jit(solution)/shard_map/ppermute | solution.py:225
  307.1 14.2 %collective-permute-start.38 = (f32[512,128]{1,0:T(8,128)S(1)}, f32[512,128]{1,0:T(8,128)S(1)}, u32[]{:S(2)}, u32[]{:S(2)}) collective-permute-start(f32[512,128]{1,0:T(8,128)S(1)} %pad_maximum_fusion.2), channel_id=1, source_target_pairs={{0,48},{16,32},{32,16},{48,0},{1,49},{17,33},{33,17},{49,1},{2,50}... | collective-permute-start | bytes 786440 | tf_op jit(solution)/shard_map/ppermute | solution.py:225
  313.5 7.9 %collective-permute-start.29 = (f32[256,128]{1,0:T(8,128)S(1)}, f32[256,128]{1,0:T(8,128)S(1)}, u32[]{:S(2)}, u32[]{:S(2)}) collective-permute-start(f32[256,128]{1,0:T(8,128)S(1)} %backward_kernel0.1), channel_id=1, source_target_pairs={{0,16},{16,0},{32,48},{48,32},{1,17},{17,1},{33,49},{49,33},{2,18}... | collective-permute-start | bytes 393224 | tf_op jit(solution)/shard_map/ppermute | solution.py:225
  316.5 6.8 %collective-permute-start.30 = (f32[256,128]{1,0:T(8,128)S(1)}, f32[256,128]{1,0:T(8,128)S(1)}, u32[]{:S(2)}, u32[]{:S(2)}) collective-permute-start(f32[256,128]{1,0:T(8,128)S(1)} %backward_kernel0.1), channel_id=1, source_target_pairs={{0,32},{16,48},{32,0},{48,16},{1,33},{17,49},{33,1},{49,17},{2,34}... | collective-permute-start | bytes 393224 | tf_op jit(solution)/shard_map/ppermute | solution.py:225
  316.8 9.6 %collective-permute-start.31 = (f32[256,128]{1,0:T(8,128)S(1)}, f32[256,128]{1,0:T(8,128)S(1)}, u32[]{:S(2)}, u32[]{:S(2)}) collective-permute-start(f32[256,128]{1,0:T(8,128)S(1)} %backward_kernel0.1), channel_id=1, source_target_pairs={{0,48},{16,32},{32,16},{48,0},{1,49},{17,33},{33,17},{49,1},{2,50}... | collective-permute-start | bytes 393224 | tf_op jit(solution)/shard_map/ppermute | solution.py:225
  (7 other events, 5.5 us)

commit v6 on v4

--- a/solution.py
+++ b/solution.py
@@ -173,10 +173,10 @@
 
 def correct_kernel(slots, *refs):
     picked_refs, factor_ref, out_ref = refs[:-2], refs[-2], refs[-1]
-    pairs = []
-    for index in range(len(slots)):
-        own, core, chip, both = (ref[...] for ref in picked_refs[4 * index : 4 * index + 4])
-        pairs.append(halves((own + core) + (chip + both)))
+    own, core, chip, both = (ref[...] for ref in picked_refs)
+    total = (own + core) + (chip + both)
+    pairs = [halves(total[i * K : (i + 1) * K]) for i in range(len(slots))]
+
     @pl.loop(0, R // STEP)
     def _(step):
         cols = pl.ds(pl.multiple_of(step * STEP, STEP), STEP)
@@ -284,16 +284,14 @@
     out2 = backward(2, sub, seen, [y2], diag)
     pick12 = row_parts(sub_sum(out2[0::2]))
     part1, *later = lax.optimization_barrier([correct((2,), pick12, factor)] + list(out2[1::2]))
-    later = row_sum(sub_sum(later))
-    pick02, x2 = later[:K], later[K:]
+    later = sub_sum(later)
     out1 = backward(1, sub, seen, [y1, *col_sum(part1)], diag)
-    pick01 = row_parts(sub_sum(out1[0::2]))
-    zero = jnp.zeros_like(pick02)
-    part0, *later = lax.optimization_barrier(
-        [correct((0, 1), pick01 + [pick02, zero, zero, zero], factor)] + list(out1[1::2])
-    )
+    picked = row_parts(jnp.concatenate([sub_sum(out1[0::2]), later[:K]]))
+    part0, x2 = lax.optimization_barrier((correct((0, 1), picked, factor), later[K:]))
+    part0, x2, *later = col_sum(part0, x2, *out1[1::2])
+    x2 = row_sum(x2)
     x1 = row_sum(sub_sum(later))
-    (x0,) = backward(0, sub, rhs, [y0, *col_sum(part0)], diag)
+    (x0,) = backward(0, sub, rhs, [y0, part0], diag)
     x0 = row_sum(x0)
     return jnp.stack([x0, x1, x2])[:, None]
 

time: 320 us -> 320 us (level)
  blocking collectives: 84.6 us -> 81.3 us
    all_to_all x4, waiting for transfers between devices: 28.3 us -> 32.1 us  [col_sum(): full = lax.all_to_all(own, 'col', 0, 0).reshape(part.shape)]
    ppermute x42, starting transfers between devices: 60.4 us -> 64.2 us  [swapped(): return lax.ppermute(value, axis, pairs)]
    all_to_all x3, blocking collectives: 63.9 us -> 60.6 us  [col_sum(): lax.all_to_all(blocks, 'col', 0, 0)]
  transfers between devices with their start and end apart: 48 -> 48, of which waited for: 27 -> 24; matrix products, arithmetic and copies ran while one was open for 3% -> 2% of each run, Pallas kernels for 2% -> 2%
where the time goes in v6:
time: 320 us; the launch traced here: 318 us
  waiting for transfers between devices  101 us (32%)
  starting transfers between devices  97.5 us (30%)
  blocking collectives  81.3 us (25%)
  Pallas kernels  23.9 us (7%)
  other arithmetic  6.57 us (2%)
  local copies, waits for them, and re-layouts  5.1 us (2%)
    ppermute x42, starting transfers between devices, swapped(): return lax.ppermute(value, axis, pairs)  64.2 us
    all_to_all x3, blocking collectives, col_sum(): lax.all_to_all(blocks, 'col', 0, 0)  60.6 us
    ppermute x42, waiting for transfers between devices, swapped(): return lax.ppermute(value, axis, pairs)  43.2 us
    all_to_all x4, waiting for transfers between devices, col_sum(): full = lax.all_to_all(own, 'col', 0, 0).reshape(part.shape)  32.1 us
    all_to_all x2, waiting for transfers between devices, col_sum(): lax.all_to_all(blocks, 'col', 0, 0)  25.3 us
    all_to_all x1, blocking collectives, col_sum(): full = lax.all_to_all(own, 'col', 0, 0).reshape(part.shape)  20.7 us
    pallas_call x6, Pallas kernels, call(): pl.pallas_call(functools.partial(kernel, level), in_specs=[pl.BlockSpec(m...  18.5 us
    all_to_all x4, starting transfers between devices, col_sum(): full = lax.all_to_all(own, 'col', 0, 0).reshape(part.shape)  17.4 us
  transfers between devices with their start and end apart: 48, of which 24 were waited for; matrix products, arithmetic and copies ran while one was open for 2% of the time, Pallas kernels for 2%

profile of v6, /device:TPU:1, one launch (start us, length us, event | category | flops | bytes accessed | tf_op | source)
XLA Modules:
  0.0 318.3 jit_solution(8581089811958024681)
XLA Ops:
  1.0 2.8 forward_kernel0.1
  3.8 11.6 %all-to-all-start = ((f32[16,64,128]{2,1,0:T(8,128)}), f32[16,64,128]{2,1,0:T(8,128)S(1)}, u32[]{:S(2)}, u32[]{:S(2)}) async-start(f32[16,64,128]{2,1,0:T(8,128)} %bitcast.4), calls=%async_computation | async-start | bytes 1048576 | tf_op jit(solution)/shard_map/all_to_all | solution.py:234
  15.7 16.9 %all-to-all-done.parts_ref = f32[16,64,128]{2,1,0:T(8,128)S(1)} async-done(((f32[16,64,128]{2,1,0:T(8,128)}), f32[16,64,128]{2,1,0:T(8,128)S(1)}, u32[]{:S(2)}, u32[]{:S(2)}) %all-to-all-start) | async-done | bytes 524320 | tf_op jit(solution)/shard_map/all_to_all | solution.py:234
  33.5 4.7 %all-to-all-start.1 = ((f32[16,64,128]{2,1,0:T(8,128)}), f32[16,64,128]{2,1,0:T(8,128)S(1)}, u32[]{:S(2)}, u32[]{:S(2)}) async-start(f32[16,64,128]{2,1,0:T(8,128)} %fold.5), calls=%async_computation.1 | async-start | bytes 1048576 | tf_op jit(solution)/shard_map/all_to_all | solution.py:235
  38.2 2.8 collective-permute-start.2
  41.7 13.8 %all-to-all-done.1 = f32[16,64,128]{2,1,0:T(8,128)S(1)} async-done(((f32[16,64,128]{2,1,0:T(8,128)}), f32[16,64,128]{2,1,0:T(8,128)S(1)}, u32[]{:S(2)}, u32[]{:S(2)}) %all-to-all-start.1) | async-done | bytes 524320 | tf_op jit(solution)/shard_map/all_to_all | solution.py:235
  56.3 3.7 %collective-permute-start.5 = (f32[128,128]{1,0:T(8,128)S(1)}, f32[128,128]{1,0:T(8,128)S(1)}, u32[]{:S(2)}, u32[]{:S(2)}) collective-permute-start(f32[128,128]{1,0:T(8,128)S(1)} %convolution_bitcast_fusion.2), channel_id=1, source_target_pairs={{0,48},{16,32},{32,16},{48,0},{1,49},{17,33},{33,17},{49,1},{2,50}... | collective-permute-start | bytes 196616 | tf_op jit(solution)/shard_map/ppermute | solution.py:209
  60.9 1.3 pad_maximum_fusion.seen_ref
  62.1 1.2 collective-permute-done.5
  63.3 1.4 collective-permute-start.6
  65.7 1.3 collective-permute-done.6.refs_1_
  67.1 2.3 forward_kernel1.1
  70.2 4.2 %all-to-all-start.2 = ((f32[16,64,128]{2,1,0:T(8,128)}), f32[16,64,128]{2,1,0:T(8,128)}, u32[]{:S(2)}, u32[]{:S(2)}) async-start(f32[16,64,128]{2,1,0:T(8,128)} %bitcast.73), calls=%async_computation.2 | async-start | bytes 1048576 | tf_op jit(solution)/shard_map/all_to_all | solution.py:234
  74.5 2.5 collective-permute-start.9
  77.0 1.2 collective-permute-done.8
  78.2 3.6 %collective-permute-done.9 = f32[128,128]{1,0:T(8,128)S(1)} collective-permute-done((f32[128,128]{1,0:T(8,128)}, f32[128,128]{1,0:T(8,128)S(1)}, u32[]{:S(2)}, u32[]{:S(2)}) %collective-permute-start.9) | collective-permute-done | bytes 65568 | tf_op jit(solution)/shard_map/ppermute | solution.py:209
  81.8 1.5 add_add_fusion.3
  83.3 8.4 %all-to-all-done.2.parts_ref = f32[16,64,128]{2,1,0:T(8,128)} async-done(((f32[16,64,128]{2,1,0:T(8,128)}), f32[16,64,128]{2,1,0:T(8,128)}, u32[]{:S(2)}, u32[]{:S(2)}) %all-to-all-start.2) | async-done | bytes 524320 | tf_op jit(solution)/shard_map/all_to_all | solution.py:234
  93.5 4.7 %all-to-all-start.3 = ((f32[16,64,128]{2,1,0:T(8,128)}), f32[16,64,128]{2,1,0:T(8,128)}, u32[]{:S(2)}, u32[]{:S(2)}) async-start(f32[16,64,128]{2,1,0:T(8,128)} %copy-done.4), calls=%async_computation.3 | async-start | bytes 1048576 | tf_op jit(solution)/shard_map/all_to_all | solution.py:235
  98.3 2.8 collective-permute-start.12
  101.8 1.6 collective-permute-done.12
  103.4 2.8 collective-permute-done.11
  106.1 1.6 pad_maximum_fusion.1.refs_0_
  107.7 6.1 %all-to-all-done.3 = f32[16,64,128]{2,1,0:T(8,128)} async-done(((f32[16,64,128]{2,1,0:T(8,128)}), f32[16,64,128]{2,1,0:T(8,128)}, u32[]{:S(2)}, u32[]{:S(2)}) %all-to-all-start.3) | async-done | bytes 524320 | tf_op jit(solution)/shard_map/all_to_all | solution.py:235
  113.8 1.5 convolution_bitcast_fusion
  115.4 6.0 %collective-permute-start.15 = (f32[128,128]{1,0:T(8,128)S(1)}, f32[128,128]{1,0:T(8,128)S(1)}, u32[]{:S(2)}, u32[]{:S(2)}) collective-permute-start(f32[128,128]{1,0:T(8,128)S(1)} %convolution_bitcast_fusion), channel_id=1, source_target_pairs={{0,48},{16,32},{32,16},{48,0},{1,49},{17,33},{33,17},{49,1},{2,50}... | collective-permute-start | bytes 196616 | tf_op jit(solution)/shard_map/ppermute | solution.py:209
  121.4 2.9 collective-permute-done.15
  124.3 1.4 collective-permute-start.16
  125.7 2.6 collective-permute-start.17
  128.3 3.6 %collective-permute-done.17.refs_3_ = f32[128,128]{1,0:T(8,128)S(1)} collective-permute-done((f32[128,128]{1,0:T(8,128)S(1)}, f32[128,128]{1,0:T(8,128)S(1)}, u32[]{:S(2)}, u32[]{:S(2)}) %collective-permute-start.17) | collective-permute-done | bytes 65568 | tf_op jit(solution)/shard_map/ppermute | solution.py:209
  132.7 3.1 forward_kernel2.1
  135.8 19.3 %all_to_all.50.parts_ref = f32[16,64,128]{2,1,0:T(8,128)S(1)} all-to-all(f32[16,64,128]{2,1,0:T(8,128)S(1)} %bitcast.75), channel_id=1, replica_groups=mesh['sub'=4,'row'=4,'col'=16] {'col'}, dimensions={0} | all-to-all | bytes 1048576 | tf_op jit(solution)/shard_map/all_to_all | solution.py:234
  155.2 20.7 %all_to_all.51 = f32[16,64,128]{2,1,0:T(8,128)S(1)} all-to-all(f32[16,64,128]{2,1,0:T(8,128)S(1)} %fold.7), channel_id=1, replica_groups=mesh['sub'=4,'row'=4,'col'=16] {'col'}, dimensions={0} | all-to-all | bytes 1048576 | tf_op jit(solution)/shard_map/all_to_all | solution.py:235
  175.9 4.0 %backward_kernel2.1 = (f32[128,128]{1,0:T(8,128)S(1)}, f32[384,128]{1,0:T(8,128)S(1)}, f32[128,128]{1,0:T(8,128)S(1)}, f32[384,128]{1,0:T(8,128)S(1)}, f32[128,1...) custom-call(s32[1]{0:T(128)} %bitcast.sub_ref, ...), custom_call_target="tpu_custom_call" | custom-call | flops 805306368 | bytes 4194304 | tf_op jit(solution)/shard_map/backward_kernel2/pallas_call | solution.py:145
  180.5 3.4 %collective-permute-start.21 = (f32[128,128]{1,0:T(8,128)S(1)}, f32[128,128]{1,0:T(8,128)S(1)}, u32[]{:S(2)}, u32[]{:S(2)}) collective-permute-start(f32[128,128]{1,0:T(8,128)S(1)} %get-tuple-element.47), channel_id=1, source_target_pairs={{0,192},{64,128},{128,64},{192,0},{1,193},{65,129},{129,65},{193,1... | collective-permute-start | bytes 196616 | tf_op jit(solution)/shard_map/ppermute | solution.py:209
  183.9 1.3 collective-permute-start.20
  185.5 1.5 collective-permute-done.19
  187.0 1.5 collective-permute-done.20
  188.5 3.8 %collective-permute-start.22 = (f32[128,128]{1,0:T(8,128)S(1)}, f32[128,128]{1,0:T(8,128)S(1)}, u32[]{:S(2)}, u32[]{:S(2)}) collective-permute-start(f32[128,128]{1,0:T(8,128)S(1)} %add_add_fusion.1.refs_0_), channel_id=1, source_target_pairs={{0,16},{16,0},{32,48},{48,32},{1,17},{17,1},{33,49},{49,33},{2,18}... | collective-permute-start | bytes 196616 | tf_op jit(solution)/shard_map/ppermute | solution.py:209
  192.4 1.7 collective-permute-start.24
  194.1 1.8 collective-permute-done.23.refs_2_
  195.9 1.7 collective-permute-done.24.refs_3_
  198.7 20.3 %all_to_all.52.parts_ref = f32[16,64,128]{2,1,0:T(8,128)S(1)} all-to-all(f32[16,64,128]{2,1,0:T(8,128)S(1)} %bitcast.77), channel_id=1, replica_groups=mesh['sub'=4,'row'=4,'col'=16] {'col'}, dimensions={0} | all-to-all | bytes 1048576 | tf_op jit(solution)/shard_map/all_to_all | solution.py:234
  219.8 4.3 %all-to-all-start.7 = ((f32[16,64,128]{2,1,0:T(8,128)}), f32[16,64,128]{2,1,0:T(8,128)}, u32[]{:S(2)}, u32[]{:S(2)}) async-start(f32[16,64,128]{2,1,0:T(8,128)} %copy-done.5), calls=%async_computation.7 | async-start | bytes 1048576 | tf_op jit(solution)/shard_map/all_to_all | solution.py:235
  224.2 1.7 collective-permute-start.28
  226.2 1.9 collective-permute-start.27
  228.1 12.1 %all-to-all-done.7 = f32[16,64,128]{2,1,0:T(8,128)} async-done(((f32[16,64,128]{2,1,0:T(8,128)}), f32[16,64,128]{2,1,0:T(8,128)}, u32[]{:S(2)}, u32[]{:S(2)}) %all-to-all-start.7) | async-done | bytes 524320 | tf_op jit(solution)/shard_map/all_to_all | solution.py:235
  240.3 4.1 %backward_kernel1.1 = (f32[128,128]{1,0:T(8,128)S(1)}, f32[256,128]{1,0:T(8,128)S(1)}, f32[128,128]{1,0:T(8,128)S(1)}, f32[256,128]{1,0:T(8,128)S(1)}) custom-call(s32[1]{0:T(128)} %bitcast.sub_ref, f32[4,520,128]{2,1,0:T(8,128)S(1)} %pad_maximum_fusion.seen_ref, f32[1024,128]{1,0:T(8,128)} %bitcast.17.base_ref, f32[1024,128]{1,0:T(8,128)} %bitcast.24.refs_0_, ...), custom_call_target="tpu_custom_call" | custom-call | flops 402653184 | bytes 2097152 | tf_op jit(solution)/shard_map/backward_kernel1/pallas_call | solution.py:145
  244.4 1.8 collective-permute-start.25
  247.9 5.0 %collective-permute-start.29 = (f32[256,128]{1,0:T(8,128)S(1)}, f32[256,128]{1,0:T(8,128)S(1)}, u32[]{:S(2)}, u32[]{:S(2)}) collective-permute-start(f32[256,128]{1,0:T(8,128)S(1)} %pad_maximum_fusion.2.refs_0_), channel_id=1, source_target_pairs={{0,16},{16,0},{32,48},{48,32},{1,17},{17,1},{33,49},{49,33},{2,18}... | collective-permute-start | bytes 393224 | tf_op jit(solution)/shard_map/ppermute | solution.py:209
  253.3 1.6 collective-permute-start.31
  254.9 2.8 collective-permute-done.30.refs_2_
  257.6 3.3 %collective-permute-done.31.refs_3_ = f32[256,128]{1,0:T(8,128)S(1)} collective-permute-done((f32[256,128]{1,0:T(8,128)S(1)}, f32[256,128]{1,0:T(8,128)S(1)}, u32[]{:S(2)}, u32[]{:S(2)}) %collective-permute-start.31) | collective-permute-done | bytes 131104 | tf_op jit(solution)/shard_map/ppermute | solution.py:209
  260.9 1.3 correct2.1
  262.3 21.0 %all_to_all.53.parts_ref = f32[16,64,128]{2,1,0:T(8,128)S(1)} all-to-all(f32[16,64,128]{2,1,0:T(8,128)S(1)} %bitcast.76), channel_id=1, replica_groups=mesh['sub'=4,'row'=4,'col'=16] {'col'}, dimensions={0} | all-to-all | bytes 1048576 | tf_op jit(solution)/shard_map/all_to_all | solution.py:234
  284.2 3.7 %all-to-all-start.9 = ((f32[16,64,128]{2,1,0:T(8,128)}), f32[16,64,128]{2,1,0:T(8,128)S(1)}, u32[]{:S(2)}, u32[]{:S(2)}) async-start(f32[16,64,128]{2,1,0:T(8,128)} %fold.9), calls=%async_computation.9 | async-start | bytes 1048576 | tf_op jit(solution)/shard_map/all_to_all | solution.py:235
  287.9 1.8 collective-permute-start.35
  290.1 3.5 %collective-permute-start.41 = (f32[256,128]{1,0:T(8,128)S(1)}, f32[256,128]{1,0:T(8,128)S(1)}, u32[]{:S(2)}, u32[]{:S(2)}) collective-permute-start(f32[256,128]{1,0:T(8,128)S(1)} %slice.29), channel_id=1, source_target_pairs={{0,48},{16,32},{32,16},{48,0},{1,49},{17,33},{33,17},{49,1},{2,50}... | collective-permute-start | bytes 393224 | tf_op jit(solution)/shard_map/ppermute | solution.py:209
  294.1 2.6 collective-permute-start.38
  296.7 2.7 collective-permute-start.36
  299.4 5.5 %collective-permute-done.41 = f32[256,128]{1,0:T(8,128)S(1)} collective-permute-done((f32[256,128]{1,0:T(8,128)S(1)}, f32[256,128]{1,0:T(8,128)S(1)}, u32[]{:S(2)}, u32[]{:S(2)}) %collective-permute-start.41) | collective-permute-done | bytes 131104 | tf_op jit(solution)/shard_map/ppermute | solution.py:209
  304.9 2.3 backward_kernel0.1
  307.4 4.7 %collective-permute-start.34 = (f32[256,128]{1,0:T(8,128)S(1)}, f32[256,128]{1,0:T(8,128)S(1)}, u32[]{:S(2)}, u32[]{:S(2)}) collective-permute-start(f32[256,128]{1,0:T(8,128)S(1)} %backward_kernel0.1), channel_id=1, source_target_pairs={{0,48},{16,32},{32,16},{48,0},{1,49},{17,33},{33,17},{49,1},{2,50}... | collective-permute-start | bytes 393224 | tf_op jit(solution)/shard_map/ppermute | solution.py:209
  312.1 5.4 %collective-permute-done.34 = f32[256,128]{1,0:T(8,128)S(1)} collective-permute-done((f32[256,128]{1,0:T(8,128)S(1)}, f32[256,128]{1,0:T(8,128)S(1)}, u32[]{:S(2)}, u32[]{:S(2)}) %collective-permute-start.34) | collective-permute-done | bytes 131104 | tf_op jit(solution)/shard_map/ppermute | solution.py:209
  (115 shorter events, 18.2 us)
Async XLA Ops:
  0.0 1.0 copy-start.1
  1.0 14.4 %copy-start.2 = (f32[3,1,256,128]{3,2,1,0:T(8,128)S(1)}, f32[3,1,256,128]{3,2,1,0:T(8,128)}, u32[]{:S(2)}) copy-start(f32[3,1,256,128]{3,2,1,0:T(8,128)} %param.4) | copy-start | bytes 1179652
  3.8 11.7 %copy-start.20 = (s32[3,1,128]{2,1,0:T(1,128)S(1)}, s32[3,1,128]{2,1,0:T(1,128)}, u32[]{:S(2)}) copy-start(s32[3,1,128]{2,1,0:T(1,128)} %param.7) | copy-start | bytes 4612
  3.8 28.8 %all-to-all-start = ((f32[16,64,128]{2,1,0:T(8,128)}), f32[16,64,128]{2,1,0:T(8,128)S(1)}, u32[]{:S(2)}, u32[]{:S(2)}) async-start(f32[16,64,128]{2,1,0:T(8,128)} %bitcast.4), calls=%async_computation | async-start | bytes 1048576 | tf_op jit(solution)/shard_map/all_to_all | solution.py:234
  15.4 40.1 %copy-start = (f32[3,1,128,1024]{3,2,1,0:T(8,128)S(1)}, f32[3,1,128,1024]{3,2,1,0:T(8,128)}, u32[]{:S(2)}) copy-start(f32[3,1,128,1024]{3,2,1,0:T(8,128)} %param.6) | copy-start | bytes 4718596
  15.7 40.2 %copy-start.16 = (f32[520,128]{1,0:T(8,128)}, f32[520,128]{1,0:T(8,128)S(1)}, u32[]{:S(2)}) copy-start(f32[520,128]{1,0:T(8,128)S(1)} %maximum_maximum_fusion) | copy-start | bytes 798724
  33.5 22.0 %all-to-all-start.1 = ((f32[16,64,128]{2,1,0:T(8,128)}), f32[16,64,128]{2,1,0:T(8,128)S(1)}, u32[]{:S(2)}, u32[]{:S(2)}) async-start(f32[16,64,128]{2,1,0:T(8,128)} %fold.5), calls=%async_computation.1 | async-start | bytes 1048576 | tf_op jit(solution)/shard_map/all_to_all | solution.py:235
  38.2 21.8 %collective-permute-start.2 = (f32[520,128]{1,0:T(8,128)S(1)}, f32[520,128]{1,0:T(8,128)S(1)}, u32[]{:S(2)}, u32[]{:S(2)}) collective-permute-start(f32[520,128]{1,0:T(8,128)S(1)} %maximum_maximum_fusion), channel_id=1, source_target_pairs={{0,192},{64,128},{128,64},{192,0},{1,193},{65,129},{129,65},{193,1... | collective-permute-start | bytes 798728 | tf_op jit(solution)/shard_map/ppermute | solution.py:209
  41.0 19.0 %collective-permute-start.1 = (f32[520,128]{1,0:T(8,128)S(1)}, f32[520,128]{1,0:T(8,128)S(1)}, u32[]{:S(2)}, u32[]{:S(2)}) collective-permute-start(f32[520,128]{1,0:T(8,128)S(1)} %maximum_maximum_fusion), channel_id=1, source_target_pairs={{0,128},{64,192},{128,0},{192,64},{1,129},{65,193},{129,1},{193,65... | collective-permute-start | bytes 798728 | tf_op jit(solution)/shard_map/ppermute | solution.py:209
  41.4 18.6 %collective-permute-start = (f32[520,128]{1,0:T(8,128)S(1)}, f32[520,128]{1,0:T(8,128)S(1)}, u32[]{:S(2)}, u32[]{:S(2)}) collective-permute-start(f32[520,128]{1,0:T(8,128)S(1)} %maximum_maximum_fusion), channel_id=1, source_target_pairs={{0,64},{64,0},{128,192},{192,128},{1,65},{65,1},{129,193},{193,129... | collective-permute-start | bytes 798728 | tf_op jit(solution)/shard_map/ppermute | solution.py:209
  55.9 6.2 %collective-permute-start.4 = (f32[128,128]{1,0:T(8,128)S(1)}, f32[128,128]{1,0:T(8,128)S(1)}, u32[]{:S(2)}, u32[]{:S(2)}) collective-permute-start(f32[128,128]{1,0:T(8,128)S(1)} %convolution_bitcast_fusion.2), channel_id=1, source_target_pairs={{0,32},{16,48},{32,0},{48,16},{1,33},{17,49},{33,1},{49,17},{2,34}... | collective-permute-start | bytes 196616 | tf_op jit(solution)/shard_map/ppermute | solution.py:209
  56.3 7.0 %collective-permute-start.5 = (f32[128,128]{1,0:T(8,128)S(1)}, f32[128,128]{1,0:T(8,128)S(1)}, u32[]{:S(2)}, u32[]{:S(2)}) collective-permute-start(f32[128,128]{1,0:T(8,128)S(1)} %convolution_bitcast_fusion.2), channel_id=1, source_target_pairs={{0,48},{16,32},{32,16},{48,0},{1,49},{17,33},{33,17},{49,1},{2,50}... | collective-permute-start | bytes 196616 | tf_op jit(solution)/shard_map/ppermute | solution.py:209
  60.0 3.3 %collective-permute-start.3 = (f32[128,128]{1,0:T(8,128)S(1)}, f32[128,128]{1,0:T(8,128)S(1)}, u32[]{:S(2)}, u32[]{:S(2)}) collective-permute-start(f32[128,128]{1,0:T(8,128)S(1)} %convolution_bitcast_fusion.2), channel_id=1, source_target_pairs={{0,16},{16,0},{32,48},{48,32},{1,17},{17,1},{33,49},{49,33},{2,18}... | collective-permute-start | bytes 196616 | tf_op jit(solution)/shard_map/ppermute | solution.py:209
  60.0 0.9 copy-start.19
  63.3 3.7 %collective-permute-start.6 = (f32[128,128]{1,0:T(8,128)S(1)}, f32[128,128]{1,0:T(8,128)S(1)}, u32[]{:S(2)}, u32[]{:S(2)}) collective-permute-start(f32[128,128]{1,0:T(8,128)S(1)} %add_add_fusion.4.refs_0_), channel_id=1, source_target_pairs={{0,64},{64,0},{128,192},{192,128},{1,65},{65,1},{129,193},{193,129... | collective-permute-start | bytes 196616 | tf_op jit(solution)/shard_map/ppermute | solution.py:209
  70.2 21.5 %all-to-all-start.2 = ((f32[16,64,128]{2,1,0:T(8,128)}), f32[16,64,128]{2,1,0:T(8,128)}, u32[]{:S(2)}, u32[]{:S(2)}) async-start(f32[16,64,128]{2,1,0:T(8,128)} %bitcast.73), calls=%async_computation.2 | async-start | bytes 1048576 | tf_op jit(solution)/shard_map/all_to_all | solution.py:234
  74.4 3.8 %collective-permute-start.8 = (f32[128,128]{1,0:T(8,128)}, f32[128,128]{1,0:T(8,128)S(1)}, u32[]{:S(2)}, u32[]{:S(2)}) collective-permute-start(f32[128,128]{1,0:T(8,128)} %convolution_bitcast_fusion.1), channel_id=1, source_target_pairs={{0,32},{16,48},{32,0},{48,16},{1,33},{17,49},{33,1},{49,17},{2,34}... | collective-permute-start | bytes 196616 | tf_op jit(solution)/shard_map/ppermute | solution.py:209
  74.5 7.3 %collective-permute-start.9 = (f32[128,128]{1,0:T(8,128)}, f32[128,128]{1,0:T(8,128)S(1)}, u32[]{:S(2)}, u32[]{:S(2)}) collective-permute-start(f32[128,128]{1,0:T(8,128)} %convolution_bitcast_fusion.1), channel_id=1, source_target_pairs={{0,48},{16,32},{32,16},{48,0},{1,49},{17,33},{33,17},{49,1},{2,50}... | collective-permute-start | bytes 196616 | tf_op jit(solution)/shard_map/ppermute | solution.py:209
  77.0 4.8 %collective-permute-start.7 = (f32[128,128]{1,0:T(8,128)}, f32[128,128]{1,0:T(8,128)S(1)}, u32[]{:S(2)}, u32[]{:S(2)}) collective-permute-start(f32[128,128]{1,0:T(8,128)} %convolution_bitcast_fusion.1), channel_id=1, source_target_pairs={{0,16},{16,0},{32,48},{48,32},{1,17},{17,1},{33,49},{49,33},{2,18}... | collective-permute-start | bytes 196616 | tf_op jit(solution)/shard_map/ppermute | solution.py:209
  93.5 20.3 %all-to-all-start.3 = ((f32[16,64,128]{2,1,0:T(8,128)}), f32[16,64,128]{2,1,0:T(8,128)}, u32[]{:S(2)}, u32[]{:S(2)}) async-start(f32[16,64,128]{2,1,0:T(8,128)} %copy-done.4), calls=%async_computation.3 | async-start | bytes 1048576 | tf_op jit(solution)/shard_map/all_to_all | solution.py:235
  98.3 5.1 %collective-permute-start.12 = (f32[128,128]{1,0:T(8,128)}, f32[128,128]{1,0:T(8,128)S(1)}, u32[]{:S(2)}, u32[]{:S(2)}) collective-permute-start(f32[128,128]{1,0:T(8,128)} %add_add_fusion.3), channel_id=1, source_target_pairs={{0,192},{64,128},{128,64},{192,0},{1,193},{65,129},{129,65},{193,1... | collective-permute-start | bytes 196616 | tf_op jit(solution)/shard_map/ppermute | solution.py:209
  101.1 5.0 %collective-permute-start.11 = (f32[128,128]{1,0:T(8,128)}, f32[128,128]{1,0:T(8,128)S(1)}, u32[]{:S(2)}, u32[]{:S(2)}) collective-permute-start(f32[128,128]{1,0:T(8,128)} %add_add_fusion.3), channel_id=1, source_target_pairs={{0,128},{64,192},{128,0},{192,64},{1,129},{65,193},{129,1},{193,65... | collective-permute-start | bytes 196616 | tf_op jit(solution)/shard_map/ppermute | solution.py:209
  101.5 4.6 %collective-permute-start.10 = (f32[128,128]{1,0:T(8,128)}, f32[128,128]{1,0:T(8,128)S(1)}, u32[]{:S(2)}, u32[]{:S(2)}) collective-permute-start(f32[128,128]{1,0:T(8,128)} %add_add_fusion.3), channel_id=1, source_target_pairs={{0,64},{64,0},{128,192},{192,128},{1,65},{65,1},{129,193},{193,129... | collective-permute-start | bytes 196616 | tf_op jit(solution)/shard_map/ppermute | solution.py:209
  113.8 18.9 %copy-start.6 = (f32[512,128]{1,0:T(8,128)S(1)}, f32[512,128]{1,0:T(8,128)}, u32[]{:S(2)}) copy-start(f32[512,128]{1,0:T(8,128)} %pad_maximum_fusion.1.refs_0_) | copy-start | bytes 786436
  115.3 6.1 %collective-permute-start.14 = (f32[128,128]{1,0:T(8,128)S(1)}, f32[128,128]{1,0:T(8,128)S(1)}, u32[]{:S(2)}, u32[]{:S(2)}) collective-permute-start(f32[128,128]{1,0:T(8,128)S(1)} %convolution_bitcast_fusion), channel_id=1, source_target_pairs={{0,32},{16,48},{32,0},{48,16},{1,33},{17,49},{33,1},{49,17},{2,34}... | collective-permute-start | bytes 196616 | tf_op jit(solution)/shard_map/ppermute | solution.py:209
  115.4 8.8 %collective-permute-start.15 = (f32[128,128]{1,0:T(8,128)S(1)}, f32[128,128]{1,0:T(8,128)S(1)}, u32[]{:S(2)}, u32[]{:S(2)}) collective-permute-start(f32[128,128]{1,0:T(8,128)S(1)} %convolution_bitcast_fusion), channel_id=1, source_target_pairs={{0,48},{16,32},{32,16},{48,0},{1,49},{17,33},{33,17},{49,1},{2,50}... | collective-permute-start | bytes 196616 | tf_op jit(solution)/shard_map/ppermute | solution.py:209
  121.4 2.9 collective-permute-start.13
  124.3 4.0 %collective-permute-start.16 = (f32[128,128]{1,0:T(8,128)S(1)}, f32[128,128]{1,0:T(8,128)S(1)}, u32[]{:S(2)}, u32[]{:S(2)}) collective-permute-start(f32[128,128]{1,0:T(8,128)S(1)} %add_add_fusion.2.refs_1_), channel_id=1, source_target_pairs={{0,64},{64,0},{128,192},{192,128},{1,65},{65,1},{129,193},{193,129... | collective-permute-start | bytes 196616 | tf_op jit(solution)/shard_map/ppermute | solution.py:209
  125.7 6.2 %collective-permute-start.17 = (f32[128,128]{1,0:T(8,128)S(1)}, f32[128,128]{1,0:T(8,128)S(1)}, u32[]{:S(2)}, u32[]{:S(2)}) collective-permute-start(f32[128,128]{1,0:T(8,128)S(1)} %add_add_fusion.2.refs_1_), channel_id=1, source_target_pairs={{0,128},{64,192},{128,0},{192,64},{1,129},{65,193},{129,1},{193,65... | collective-permute-start | bytes 196616 | tf_op jit(solution)/shard_map/ppermute | solution.py:209
  128.3 4.5 %collective-permute-start.18 = (f32[128,128]{1,0:T(8,128)S(1)}, f32[128,128]{1,0:T(8,128)S(1)}, u32[]{:S(2)}, u32[]{:S(2)}) collective-permute-start(f32[128,128]{1,0:T(8,128)S(1)} %add_add_fusion.2.refs_1_), channel_id=1, source_target_pairs={{0,192},{64,128},{128,64},{192,0},{1,193},{65,129},{129,65},{193,1... | collective-permute-start | bytes 196616 | tf_op jit(solution)/shard_map/ppermute | solution.py:209
  180.5 18.2 %copy-start.11 = (f32[384,128]{1,0:T(8,128)}, f32[384,128]{1,0:T(8,128)S(1)}, u32[]{:S(2)}) copy-start(f32[384,128]{1,0:T(8,128)S(1)} %get-tuple-element.57) | copy-start | bytes 589828
  180.5 18.2 %copy-start.13 = (f32[384,128]{1,0:T(8,128)}, f32[384,128]{1,0:T(8,128)S(1)}, u32[]{:S(2)}) copy-start(f32[384,128]{1,0:T(8,128)S(1)} %get-tuple-element.58) | copy-start | bytes 589828
  180.5 38.4 %copy-start.7 = (f32[384,128]{1,0:T(8,128)}, f32[384,128]{1,0:T(8,128)S(1)}, u32[]{:S(2)}) copy-start(f32[384,128]{1,0:T(8,128)S(1)} %get-tuple-element.55) | copy-start | bytes 589828
  180.5 5.0 %collective-permute-start.21 = (f32[128,128]{1,0:T(8,128)S(1)}, f32[128,128]{1,0:T(8,128)S(1)}, u32[]{:S(2)}, u32[]{:S(2)}) collective-permute-start(f32[128,128]{1,0:T(8,128)S(1)} %get-tuple-element.47), channel_id=1, source_target_pairs={{0,192},{64,128},{128,64},{192,0},{1,193},{65,129},{129,65},{193,1... | collective-permute-start | bytes 196616 | tf_op jit(solution)/shard_map/ppermute | solution.py:209
  183.9 3.1 collective-permute-start.19
  183.9 4.6 %collective-permute-start.20 = (f32[128,128]{1,0:T(8,128)S(1)}, f32[128,128]{1,0:T(8,128)S(1)}, u32[]{:S(2)}, u32[]{:S(2)}) collective-permute-start(f32[128,128]{1,0:T(8,128)S(1)} %get-tuple-element.46), channel_id=1, source_target_pairs={{0,128},{64,192},{128,0},{192,64},{1,129},{65,193},{129,1},{193,65... | collective-permute-start | bytes 196616 | tf_op jit(solution)/shard_map/ppermute | solution.py:209
  188.5 5.6 %collective-permute-start.22 = (f32[128,128]{1,0:T(8,128)S(1)}, f32[128,128]{1,0:T(8,128)S(1)}, u32[]{:S(2)}, u32[]{:S(2)}) collective-permute-start(f32[128,128]{1,0:T(8,128)S(1)} %add_add_fusion.1.refs_0_), channel_id=1, source_target_pairs={{0,16},{16,0},{32,48},{48,32},{1,17},{17,1},{33,49},{49,33},{2,18}... | collective-permute-start | bytes 196616 | tf_op jit(solution)/shard_map/ppermute | solution.py:209
  192.4 3.5 %collective-permute-start.23 = (f32[128,128]{1,0:T(8,128)S(1)}, f32[128,128]{1,0:T(8,128)S(1)}, u32[]{:S(2)}, u32[]{:S(2)}) collective-permute-start(f32[128,128]{1,0:T(8,128)S(1)} %add_add_fusion.1.refs_0_), channel_id=1, source_target_pairs={{0,32},{16,48},{32,0},{48,16},{1,33},{17,49},{33,1},{49,17},{2,34}... | collective-permute-start | bytes 196616 | tf_op jit(solution)/shard_map/ppermute | solution.py:209
  192.4 5.2 %collective-permute-start.24 = (f32[128,128]{1,0:T(8,128)S(1)}, f32[128,128]{1,0:T(8,128)S(1)}, u32[]{:S(2)}, u32[]{:S(2)}) collective-permute-start(f32[128,128]{1,0:T(8,128)S(1)} %add_add_fusion.1.refs_0_), channel_id=1, source_target_pairs={{0,48},{16,32},{32,16},{48,0},{1,49},{17,33},{33,17},{49,1},{2,50}... | collective-permute-start | bytes 196616 | tf_op jit(solution)/shard_map/ppermute | solution.py:209
  219.0 0.8 copy-start.5
  219.8 20.4 %all-to-all-start.7 = ((f32[16,64,128]{2,1,0:T(8,128)}), f32[16,64,128]{2,1,0:T(8,128)}, u32[]{:S(2)}, u32[]{:S(2)}) async-start(f32[16,64,128]{2,1,0:T(8,128)} %copy-done.5), calls=%async_computation.7 | async-start | bytes 1048576 | tf_op jit(solution)/shard_map/all_to_all | solution.py:235
  224.2 22.1 %collective-permute-start.28 = (f32[384,128]{1,0:T(8,128)}, f32[384,128]{1,0:T(8,128)}, u32[]{:S(2)}, u32[]{:S(2)}) collective-permute-start(f32[384,128]{1,0:T(8,128)} %copy-done.13), channel_id=1, source_target_pairs={{0,192},{64,128},{128,64},{192,0},{1,193},{65,129},{129,65},{193,1... | collective-permute-start | bytes 589832 | tf_op jit(solution)/shard_map/ppermute | solution.py:209
  225.8 20.4 %collective-permute-start.26 = (f32[384,128]{1,0:T(8,128)}, f32[384,128]{1,0:T(8,128)}, u32[]{:S(2)}, u32[]{:S(2)}) collective-permute-start(f32[384,128]{1,0:T(8,128)} %copy-done.12), channel_id=1, source_target_pairs={{0,64},{64,0},{128,192},{192,128},{1,65},{65,1},{129,193},{193,129... | collective-permute-start | bytes 589832 | tf_op jit(solution)/shard_map/ppermute | solution.py:209
  226.2 20.1 %collective-permute-start.27 = (f32[384,128]{1,0:T(8,128)}, f32[384,128]{1,0:T(8,128)}, u32[]{:S(2)}, u32[]{:S(2)}) collective-permute-start(f32[384,128]{1,0:T(8,128)} %copy-done.11), channel_id=1, source_target_pairs={{0,128},{64,192},{128,0},{192,64},{1,129},{65,193},{129,1},{193,65... | collective-permute-start | bytes 589832 | tf_op jit(solution)/shard_map/ppermute | solution.py:209
  240.3 6.0 %copy-start.8 = (f32[384,128]{1,0:T(8,128)S(1)}, f32[384,128]{1,0:T(8,128)}, u32[]{:S(2)}) copy-start(f32[384,128]{1,0:T(8,128)} %copy-done.7) | copy-start | bytes 589828
  244.4 17.9 %copy-start.9 = (f32[256,128]{1,0:T(8,128)}, f32[256,128]{1,0:T(8,128)S(1)}, u32[]{:S(2)}) copy-start(f32[256,128]{1,0:T(8,128)S(1)} %get-tuple-element.64) | copy-start | bytes 393220
  244.4 17.9 %copy-start.14 = (f32[256,128]{1,0:T(8,128)}, f32[256,128]{1,0:T(8,128)S(1)}, u32[]{:S(2)}) copy-start(f32[256,128]{1,0:T(8,128)S(1)} %get-tuple-element.65) | copy-start | bytes 393220
  244.4 3.5 %collective-permute-start.25 = (f32[128,128]{1,0:T(8,128)S(1)}, f32[128,128]{1,0:T(8,128)S(1)}, u32[]{:S(2)}, u32[]{:S(2)}) collective-permute-start(f32[128,128]{1,0:T(8,128)S(1)} %get-tuple-element.54), channel_id=1, source_target_pairs={{0,64},{64,0},{128,192},{192,128},{1,65},{65,1},{129,193},{193,129... | collective-permute-start | bytes 196616 | tf_op jit(solution)/shard_map/ppermute | solution.py:209
  247.9 6.9 %collective-permute-start.29 = (f32[256,128]{1,0:T(8,128)S(1)}, f32[256,128]{1,0:T(8,128)S(1)}, u32[]{:S(2)}, u32[]{:S(2)}) collective-permute-start(f32[256,128]{1,0:T(8,128)S(1)} %pad_maximum_fusion.2.refs_0_), channel_id=1, source_target_pairs={{0,16},{16,0},{32,48},{48,32},{1,17},{17,1},{33,49},{49,33},{2,18}... | collective-permute-start | bytes 393224 | tf_op jit(solution)/shard_map/ppermute | solution.py:209
  252.9 4.7 %collective-permute-start.30 = (f32[256,128]{1,0:T(8,128)S(1)}, f32[256,128]{1,0:T(8,128)S(1)}, u32[]{:S(2)}, u32[]{:S(2)}) collective-permute-start(f32[256,128]{1,0:T(8,128)S(1)} %pad_maximum_fusion.2.refs_0_), channel_id=1, source_target_pairs={{0,32},{16,48},{32,0},{48,16},{1,33},{17,49},{33,1},{49,17},{2,34}... | collective-permute-start | bytes 393224 | tf_op jit(solution)/shard_map/ppermute | solution.py:209
  253.3 7.7 %collective-permute-start.31 = (f32[256,128]{1,0:T(8,128)S(1)}, f32[256,128]{1,0:T(8,128)S(1)}, u32[]{:S(2)}, u32[]{:S(2)}) collective-permute-start(f32[256,128]{1,0:T(8,128)S(1)} %pad_maximum_fusion.2.refs_0_), channel_id=1, source_target_pairs={{0,48},{16,32},{32,16},{48,0},{1,49},{17,33},{33,17},{49,1},{2,50}... | collective-permute-start | bytes 393224 | tf_op jit(solution)/shard_map/ppermute | solution.py:209
  262.3 25.6 %copy-start.15 = (f32[256,128]{1,0:T(8,128)S(1)}, f32[256,128]{1,0:T(8,128)}, u32[]{:S(2)}) copy-start(f32[256,128]{1,0:T(8,128)} %copy-done.14) | copy-start | bytes 393220
  262.3 31.3 %copy-start.10 = (f32[256,128]{1,0:T(8,128)S(1)}, f32[256,128]{1,0:T(8,128)}, u32[]{:S(2)}) copy-start(f32[256,128]{1,0:T(8,128)} %copy-done.9) | copy-start | bytes 393220
  284.2 20.7 %all-to-all-start.9 = ((f32[16,64,128]{2,1,0:T(8,128)}), f32[16,64,128]{2,1,0:T(8,128)S(1)}, u32[]{:S(2)}, u32[]{:S(2)}) async-start(f32[16,64,128]{2,1,0:T(8,128)} %fold.9), calls=%async_computation.9 | async-start | bytes 1048576 | tf_op jit(solution)/shard_map/all_to_all | solution.py:235
  287.9 5.7 %collective-permute-start.35 = (f32[256,128]{1,0:T(8,128)S(1)}, f32[256,128]{1,0:T(8,128)S(1)}, u32[]{:S(2)}, u32[]{:S(2)}) collective-permute-start(f32[256,128]{1,0:T(8,128)S(1)} %copy-done.15), channel_id=1, source_target_pairs={{0,64},{64,0},{128,192},{192,128},{1,65},{65,1},{129,193},{193,129... | collective-permute-start | bytes 393224 | tf_op jit(solution)/shard_map/ppermute | solution.py:209
  289.7 7.0 %collective-permute-start.40 = (f32[256,128]{1,0:T(8,128)S(1)}, f32[256,128]{1,0:T(8,128)S(1)}, u32[]{:S(2)}, u32[]{:S(2)}) collective-permute-start(f32[256,128]{1,0:T(8,128)S(1)} %slice.29), channel_id=1, source_target_pairs={{0,32},{16,48},{32,0},{48,16},{1,33},{17,49},{33,1},{49,17},{2,34}... | collective-permute-start | bytes 393224 | tf_op jit(solution)/shard_map/ppermute | solution.py:209
  290.1 14.8 %collective-permute-start.41 = (f32[256,128]{1,0:T(8,128)S(1)}, f32[256,128]{1,0:T(8,128)S(1)}, u32[]{:S(2)}, u32[]{:S(2)}) collective-permute-start(f32[256,128]{1,0:T(8,128)S(1)} %slice.29), channel_id=1, source_target_pairs={{0,48},{16,32},{32,16},{48,0},{1,49},{17,33},{33,17},{49,1},{2,50}... | collective-permute-start | bytes 393224 | tf_op jit(solution)/shard_map/ppermute | solution.py:209
  293.6 11.3 %collective-permute-start.39 = (f32[256,128]{1,0:T(8,128)S(1)}, f32[256,128]{1,0:T(8,128)S(1)}, u32[]{:S(2)}, u32[]{:S(2)}) collective-permute-start(f32[256,128]{1,0:T(8,128)S(1)} %slice.29), channel_id=1, source_target_pairs={{0,16},{16,0},{32,48},{48,32},{1,17},{17,1},{33,49},{49,33},{2,18}... | collective-permute-start | bytes 393224 | tf_op jit(solution)/shard_map/ppermute | solution.py:209
  293.6 18.4 %collective-permute-start.37 = (f32[256,128]{1,0:T(8,128)S(1)}, f32[256,128]{1,0:T(8,128)S(1)}, u32[]{:S(2)}, u32[]{:S(2)}) collective-permute-start(f32[256,128]{1,0:T(8,128)S(1)} %add.109), channel_id=1, source_target_pairs={{0,32},{16,48},{32,0},{48,16},{1,33},{17,49},{33,1},{49,17},{2,34}... | collective-permute-start | bytes 393224 | tf_op jit(solution)/shard_map/ppermute | solution.py:209
  294.1 17.9 %collective-permute-start.38 = (f32[256,128]{1,0:T(8,128)S(1)}, f32[256,128]{1,0:T(8,128)S(1)}, u32[]{:S(2)}, u32[]{:S(2)}) collective-permute-start(f32[256,128]{1,0:T(8,128)S(1)} %add.109), channel_id=1, source_target_pairs={{0,48},{16,32},{32,16},{48,0},{1,49},{17,33},{33,17},{49,1},{2,50}... | collective-permute-start | bytes 393224 | tf_op jit(solution)/shard_map/ppermute | solution.py:209
  296.7 15.4 %collective-permute-start.36 = (f32[256,128]{1,0:T(8,128)S(1)}, f32[256,128]{1,0:T(8,128)S(1)}, u32[]{:S(2)}, u32[]{:S(2)}) collective-permute-start(f32[256,128]{1,0:T(8,128)S(1)} %add.109), channel_id=1, source_target_pairs={{0,16},{16,0},{32,48},{48,32},{1,17},{17,1},{33,49},{49,33},{2,18}... | collective-permute-start | bytes 393224 | tf_op jit(solution)/shard_map/ppermute | solution.py:209
  307.2 4.8 %collective-permute-start.33 = (f32[256,128]{1,0:T(8,128)S(1)}, f32[256,128]{1,0:T(8,128)S(1)}, u32[]{:S(2)}, u32[]{:S(2)}) collective-permute-start(f32[256,128]{1,0:T(8,128)S(1)} %backward_kernel0.1), channel_id=1, source_target_pairs={{0,32},{16,48},{32,0},{48,16},{1,33},{17,49},{33,1},{49,17},{2,34}... | collective-permute-start | bytes 393224 | tf_op jit(solution)/shard_map/ppermute | solution.py:209
  307.4 10.1 %collective-permute-start.34 = (f32[256,128]{1,0:T(8,128)S(1)}, f32[256,128]{1,0:T(8,128)S(1)}, u32[]{:S(2)}, u32[]{:S(2)}) collective-permute-start(f32[256,128]{1,0:T(8,128)S(1)} %backward_kernel0.1), channel_id=1, source_target_pairs={{0,48},{16,32},{32,16},{48,0},{1,49},{17,33},{33,17},{49,1},{2,50}... | collective-permute-start | bytes 393224 | tf_op jit(solution)/shard_map/ppermute | solution.py:209
  312.0 5.5 %collective-permute-start.32 = (f32[256,128]{1,0:T(8,128)S(1)}, f32[256,128]{1,0:T(8,128)S(1)}, u32[]{:S(2)}, u32[]{:S(2)}) collective-permute-start(f32[256,128]{1,0:T(8,128)S(1)} %backward_kernel0.1), channel_id=1, source_target_pairs={{0,16},{16,0},{32,48},{48,32},{1,17},{17,1},{33,49},{49,33},{2,18}... | collective-permute-start | bytes 393224 | tf_op jit(solution)/shard_map/ppermute | solution.py:209
  (5 other events, 3.8 us)

commit v7 on v6

--- a/solution.py
+++ b/solution.py
@@ -15,7 +15,7 @@
 STEP = 256
 LEVELS = 3
 VMEM_LIMIT = 46 * 2**20
-FIRST_LIMIT = 48 * 2**20
+FIRST_LIMIT = 58 * 2**20
 LIST_AT = 2 * C
 PACKED = 2 * C + 8
 mode = lax.Precision.HIGH
@@ -56,10 +56,16 @@
 
 def forward_kernel(level, sub_ref, seen_ref, *refs):
     spans = 2**level
-    update_refs, (diag_ref, out_ref, right_ref, buffer_ref, sems) = refs[:-5], refs[-5:]
+    if level:
+        update_refs, (diag_ref, out_ref, right_ref, buffer_ref, sems) = refs[:-5], refs[-5:]
+    else:
+        diag_ref, out_ref, right_ref, buffer_ref, sems, plain_ref = refs
+        first = pltpu.make_async_copy(seen_ref.at[0], plain_ref, sems.at[R // STEP])
+        first.start()
     fetch(spans, diag_ref, buffer_ref, sems)
     if level == 0:
-        high, low = halves(seen_ref[0])
+        first.wait()
+        high, low = halves(plain_ref[...])
         right_ref[0] = jnp.concatenate([high, low], axis=1)
     else:
         sub = sub_ref[0] % spans
@@ -96,18 +102,28 @@
 def backward_kernel(level, sub_ref, seen_ref, base_ref, *refs):
     spans = 2**level
     minus = level < LEVELS - 1
-    if minus:
-        minus_ref, refs = refs[0], refs[1:]
-    diag_ref, out_refs, (total_ref, buffer_ref, sems) = refs[0], refs[1:-3], refs[-3:]
+    count = 2 if minus else 1
+    plain, refs = refs[-count:], refs[:-count]
+    total_ref, buffer_ref, sems = refs[-3:]
+    diag_ref, out_refs = refs[count - 1], refs[count:-3]
+    pairs = list(zip([base_ref, refs[0]], plain))
+    copies = [
+        pltpu.make_async_copy(source, target, sems.at[R // STEP + i])
+        for i, (source, target) in enumerate(pairs)
+    ]
+    for copy in copies:
+        copy.start()
     fetch(spans, diag_ref, buffer_ref, sems)
     total_ref[...] = jnp.zeros_like(total_ref)
+    for copy in copies:
+        copy.wait()
 
     @pl.loop(0, R // STEP)
     def _(step):
         rows = pl.ds(pl.multiple_of(step * STEP, STEP), STEP)
-        residue = base_ref[rows, :]
+        residue = plain[0][rows, :]
         if minus:
-            residue = residue - minus_ref[rows, :]
+            residue = residue - plain[1][rows, :]
         high, low = halves(residue.T)
         both = jnp.concatenate([high, low], axis=0)
         piece(spans, step, diag_ref, buffer_ref, sems).wait()
@@ -137,11 +153,13 @@
             later_ref[...] = own
 
 
-def call(kernel, level, heights, scratch, sub, *arrays):
+def call(kernel, level, heights, scratch, plain, sub, *arrays):
     spans = 2**level
     vmem = pl.BlockSpec(memory_space=pltpu.VMEM)
     limit = FIRST_LIMIT if len(arrays) == 2 else VMEM_LIMIT
-    specs = [vmem] * (len(arrays) - 1) + [pl.BlockSpec(memory_space=pltpu.HBM)]
+    specs = [vmem] * len(arrays)
+    for place in [*plain, len(arrays) - 1]:
+        specs[place] = pl.BlockSpec(memory_space=pltpu.HBM)
     return pl.pallas_call(
         functools.partial(kernel, level),
         in_specs=[pl.BlockSpec(memory_space=pltpu.SMEM)] + specs,
@@ -149,8 +167,9 @@
         scratch_shapes=[
             scratch,
             pltpu.VMEM((spans, R, C), jnp.float32),
-            pltpu.SemaphoreType.DMA((R // STEP,)),
-        ],
+            pltpu.SemaphoreType.DMA((R // STEP + len(plain),)),
+        ]
+        + [pltpu.VMEM((rows, N), jnp.float32) for rows in plain.values()],
         out_shape=[jax.ShapeDtypeStruct((h, N), jnp.float32) for h in heights],
         compiler_params=pltpu.CompilerParams(vmem_limit_bytes=limit),
         cost_estimate=pl.CostEstimate(
@@ -162,13 +181,15 @@
 
 def forward(level, sub, seen, updates, diag):
     scratch = pltpu.VMEM((2**level, C, 2 * N), jnp.bfloat16)
-    return call(forward_kernel, level, [R], scratch, sub, seen, *updates, diag)[0]
+    plain = {} if level else {0: C}
+    return call(forward_kernel, level, [R], scratch, plain, sub, seen, *updates, diag)[0]
 
 
 def backward(level, sub, seen, residue, diag):
     heights = {0: [C], 1: [K, C] * 2, 2: [K, K + C] * 4}[level]
     scratch = pltpu.VMEM((2**level, N, C), jnp.float32)
-    return call(backward_kernel, level, heights, scratch, sub, seen, *residue, diag)
+    plain = {1 + place: R for place in range(len(residue))}
+    return call(backward_kernel, level, heights, scratch, plain, sub, seen, *residue, diag)
 
 
 def correct_kernel(slots, *refs):

time: 320 us -> 318 us (level)
  no operation moved by 1% of the time
where the time goes in v7:
time: 318 us; the launch traced here: 317 us
  waiting for transfers between devices  101 us (32%)
  starting transfers between devices  97.4 us (31%)
  blocking collectives  81.3 us (26%)
  Pallas kernels  23.2 us (7%)
  other arithmetic  6.57 us (2%)
  local copies, waits for them, and re-layouts  4.06 us (1%)
    ppermute x42, starting transfers between devices, swapped(): return lax.ppermute(value, axis, pairs)  64.2 us
    all_to_all x3, blocking collectives, col_sum(): lax.all_to_all(blocks, 'col', 0, 0)  60.6 us
    ppermute x42, waiting for transfers between devices, swapped(): return lax.ppermute(value, axis, pairs)  43.2 us
    all_to_all x4, waiting for transfers between devices, col_sum(): full = lax.all_to_all(own, 'col', 0, 0).reshape(part.shape)  32.2 us
    all_to_all x2, waiting for transfers between devices, col_sum(): lax.all_to_all(blocks, 'col', 0, 0)  25.3 us
    all_to_all x1, blocking collectives, col_sum(): full = lax.all_to_all(own, 'col', 0, 0).reshape(part.shape)  20.7 us
    pallas_call x6, Pallas kernels, call(): pl.pallas_call(functools.partial(kernel, level), in_specs=[pl.BlockSpec(m...  17.8 us
    all_to_all x4, starting transfers between devices, col_sum(): full = lax.all_to_all(own, 'col', 0, 0).reshape(part.shape)  17.4 us
  transfers between devices with their start and end apart: 48, of which 24 were waited for; matrix products, arithmetic and copies ran while one was open for 2% of the time, Pallas kernels for 2%

profile of v7, /device:TPU:1, one launch (start us, length us, event | category | flops | bytes accessed | tf_op | source)
XLA Modules:
  0.0 316.6 jit_solution(6038796940268691582)
XLA Ops:
  0.0 2.8 forward_kernel0.1
  2.9 11.6 %all-to-all-start = ((f32[16,64,128]{2,1,0:T(8,128)}), f32[16,64,128]{2,1,0:T(8,128)S(1)}, u32[]{:S(2)}, u32[]{:S(2)}) async-start(f32[16,64,128]{2,1,0:T(8,128)} %bitcast.84), calls=%async_computation | async-start | bytes 1048576 | tf_op jit(solution)/shard_map/all_to_all | solution.py:255
  14.8 16.9 %all-to-all-done.parts_ref = f32[16,64,128]{2,1,0:T(8,128)S(1)} async-done(((f32[16,64,128]{2,1,0:T(8,128)}), f32[16,64,128]{2,1,0:T(8,128)S(1)}, u32[]{:S(2)}, u32[]{:S(2)}) %all-to-all-start) | async-done | bytes 524320 | tf_op jit(solution)/shard_map/all_to_all | solution.py:255
  32.5 4.7 %all-to-all-start.1 = ((f32[16,64,128]{2,1,0:T(8,128)}), f32[16,64,128]{2,1,0:T(8,128)S(1)}, u32[]{:S(2)}, u32[]{:S(2)}) async-start(f32[16,64,128]{2,1,0:T(8,128)} %fold.5), calls=%async_computation.1 | async-start | bytes 1048576 | tf_op jit(solution)/shard_map/all_to_all | solution.py:256
  37.3 2.8 collective-permute-start.2
  40.8 13.8 %all-to-all-done.1 = f32[16,64,128]{2,1,0:T(8,128)S(1)} async-done(((f32[16,64,128]{2,1,0:T(8,128)}), f32[16,64,128]{2,1,0:T(8,128)S(1)}, u32[]{:S(2)}, u32[]{:S(2)}) %all-to-all-start.1) | async-done | bytes 524320 | tf_op jit(solution)/shard_map/all_to_all | solution.py:256
  55.4 3.7 %collective-permute-start.5 = (f32[128,128]{1,0:T(8,128)S(1)}, f32[128,128]{1,0:T(8,128)S(1)}, u32[]{:S(2)}, u32[]{:S(2)}) collective-permute-start(f32[128,128]{1,0:T(8,128)S(1)} %convolution_bitcast_fusion.2), channel_id=1, source_target_pairs={{0,48},{16,32},{32,16},{48,0},{1,49},{17,33},{33,17},{49,1},{2,50}... | collective-permute-start | bytes 196616 | tf_op jit(solution)/shard_map/ppermute | solution.py:230
  60.0 1.3 pad_maximum_fusion.seen_ref
  61.2 1.2 collective-permute-done.5
  62.4 1.4 collective-permute-start.6
  64.8 1.3 collective-permute-done.6.refs_1_
  66.2 2.3 forward_kernel1.1
  69.2 4.2 %all-to-all-start.2 = ((f32[16,64,128]{2,1,0:T(8,128)}), f32[16,64,128]{2,1,0:T(8,128)}, u32[]{:S(2)}, u32[]{:S(2)}) async-start(f32[16,64,128]{2,1,0:T(8,128)} %bitcast.73), calls=%async_computation.2 | async-start | bytes 1048576 | tf_op jit(solution)/shard_map/all_to_all | solution.py:255
  73.6 2.5 collective-permute-start.9
  76.1 1.2 collective-permute-done.8
  77.2 3.6 %collective-permute-done.9 = f32[128,128]{1,0:T(8,128)S(1)} collective-permute-done((f32[128,128]{1,0:T(8,128)}, f32[128,128]{1,0:T(8,128)S(1)}, u32[]{:S(2)}, u32[]{:S(2)}) %collective-permute-start.9) | collective-permute-done | bytes 65568 | tf_op jit(solution)/shard_map/ppermute | solution.py:230
  80.8 1.5 add_add_fusion.3
  82.3 8.4 %all-to-all-done.2.parts_ref = f32[16,64,128]{2,1,0:T(8,128)} async-done(((f32[16,64,128]{2,1,0:T(8,128)}), f32[16,64,128]{2,1,0:T(8,128)}, u32[]{:S(2)}, u32[]{:S(2)}) %all-to-all-start.2) | async-done | bytes 524320 | tf_op jit(solution)/shard_map/all_to_all | solution.py:255
  92.6 4.7 %all-to-all-start.3 = ((f32[16,64,128]{2,1,0:T(8,128)}), f32[16,64,128]{2,1,0:T(8,128)}, u32[]{:S(2)}, u32[]{:S(2)}) async-start(f32[16,64,128]{2,1,0:T(8,128)} %copy-done.3), calls=%async_computation.3 | async-start | bytes 1048576 | tf_op jit(solution)/shard_map/all_to_all | solution.py:256
  97.3 2.8 collective-permute-start.12
  100.8 1.6 collective-permute-done.12
  102.4 2.8 collective-permute-done.11
  105.2 1.6 pad_maximum_fusion.1.refs_0_
  106.7 6.3 %all-to-all-done.3 = f32[16,64,128]{2,1,0:T(8,128)} async-done(((f32[16,64,128]{2,1,0:T(8,128)}), f32[16,64,128]{2,1,0:T(8,128)}, u32[]{:S(2)}, u32[]{:S(2)}) %all-to-all-start.3) | async-done | bytes 524320 | tf_op jit(solution)/shard_map/all_to_all | solution.py:256
  113.0 1.5 convolution_bitcast_fusion
  114.6 5.9 %collective-permute-start.15 = (f32[128,128]{1,0:T(8,128)S(1)}, f32[128,128]{1,0:T(8,128)S(1)}, u32[]{:S(2)}, u32[]{:S(2)}) collective-permute-start(f32[128,128]{1,0:T(8,128)S(1)} %convolution_bitcast_fusion), channel_id=1, source_target_pairs={{0,48},{16,32},{32,16},{48,0},{1,49},{17,33},{33,17},{49,1},{2,50}... | collective-permute-start | bytes 196616 | tf_op jit(solution)/shard_map/ppermute | solution.py:230
  120.5 2.9 collective-permute-done.15
  123.4 1.4 collective-permute-start.16
  124.8 2.6 collective-permute-start.17
  127.4 3.6 %collective-permute-done.17.refs_3_ = f32[128,128]{1,0:T(8,128)S(1)} collective-permute-done((f32[128,128]{1,0:T(8,128)S(1)}, f32[128,128]{1,0:T(8,128)S(1)}, u32[]{:S(2)}, u32[]{:S(2)}) %collective-permute-start.17) | collective-permute-done | bytes 65568 | tf_op jit(solution)/shard_map/ppermute | solution.py:230
  131.9 3.1 forward_kernel2.1
  134.9 19.3 %all_to_all.50.parts_ref = f32[16,64,128]{2,1,0:T(8,128)S(1)} all-to-all(f32[16,64,128]{2,1,0:T(8,128)S(1)} %bitcast.75), channel_id=1, replica_groups=mesh['sub'=4,'row'=4,'col'=16] {'col'}, dimensions={0} | all-to-all | bytes 1048576 | tf_op jit(solution)/shard_map/all_to_all | solution.py:255
  154.3 20.7 %all_to_all.51 = f32[16,64,128]{2,1,0:T(8,128)S(1)} all-to-all(f32[16,64,128]{2,1,0:T(8,128)S(1)} %fold.7), channel_id=1, replica_groups=mesh['sub'=4,'row'=4,'col'=16] {'col'}, dimensions={0} | all-to-all | bytes 1048576 | tf_op jit(solution)/shard_map/all_to_all | solution.py:256
  175.0 4.0 %backward_kernel2.1 = (f32[128,128]{1,0:T(8,128)S(1)}, f32[384,128]{1,0:T(8,128)S(1)}, f32[128,128]{1,0:T(8,128)S(1)}, f32[384,128]{1,0:T(8,128)S(1)}, f32[128,1...) custom-call(s32[1]{0:T(128)} %bitcast.sub_ref, ...), custom_call_target="tpu_custom_call" | custom-call | flops 805306368 | bytes 4194304 | tf_op jit(solution)/shard_map/backward_kernel2/pallas_call | solution.py:163
  179.7 3.4 %collective-permute-start.21 = (f32[128,128]{1,0:T(8,128)S(1)}, f32[128,128]{1,0:T(8,128)S(1)}, u32[]{:S(2)}, u32[]{:S(2)}) collective-permute-start(f32[128,128]{1,0:T(8,128)S(1)} %get-tuple-element.47), channel_id=1, source_target_pairs={{0,192},{64,128},{128,64},{192,0},{1,193},{65,129},{129,65},{193,1... | collective-permute-start | bytes 196616 | tf_op jit(solution)/shard_map/ppermute | solution.py:230
  183.1 1.3 collective-permute-start.20
  184.7 1.5 collective-permute-done.19
  186.2 1.5 collective-permute-done.20
  187.7 3.8 %collective-permute-start.22 = (f32[128,128]{1,0:T(8,128)S(1)}, f32[128,128]{1,0:T(8,128)S(1)}, u32[]{:S(2)}, u32[]{:S(2)}) collective-permute-start(f32[128,128]{1,0:T(8,128)S(1)} %add_add_fusion.1.refs_0_), channel_id=1, source_target_pairs={{0,16},{16,0},{32,48},{48,32},{1,17},{17,1},{33,49},{49,33},{2,18}... | collective-permute-start | bytes 196616 | tf_op jit(solution)/shard_map/ppermute | solution.py:230
  191.5 1.7 collective-permute-start.24
  193.3 1.8 collective-permute-done.23.refs_2_
  195.1 1.7 collective-permute-done.24.refs_3_
  197.9 20.3 %all_to_all.52.parts_ref = f32[16,64,128]{2,1,0:T(8,128)S(1)} all-to-all(f32[16,64,128]{2,1,0:T(8,128)S(1)} %bitcast.77), channel_id=1, replica_groups=mesh['sub'=4,'row'=4,'col'=16] {'col'}, dimensions={0} | all-to-all | bytes 1048576 | tf_op jit(solution)/shard_map/all_to_all | solution.py:255
  219.0 4.3 %all-to-all-start.7 = ((f32[16,64,128]{2,1,0:T(8,128)}), f32[16,64,128]{2,1,0:T(8,128)}, u32[]{:S(2)}, u32[]{:S(2)}) async-start(f32[16,64,128]{2,1,0:T(8,128)} %copy-done.4), calls=%async_computation.7 | async-start | bytes 1048576 | tf_op jit(solution)/shard_map/all_to_all | solution.py:256
  223.3 1.7 collective-permute-start.28
  225.3 1.9 collective-permute-start.27
  227.3 12.1 %all-to-all-done.7 = f32[16,64,128]{2,1,0:T(8,128)} async-done(((f32[16,64,128]{2,1,0:T(8,128)}), f32[16,64,128]{2,1,0:T(8,128)}, u32[]{:S(2)}, u32[]{:S(2)}) %all-to-all-start.7) | async-done | bytes 524320 | tf_op jit(solution)/shard_map/all_to_all | solution.py:256
  239.4 3.3 %backward_kernel1.1 = (f32[128,128]{1,0:T(8,128)S(1)}, f32[256,128]{1,0:T(8,128)S(1)}, f32[128,128]{1,0:T(8,128)S(1)}, f32[256,128]{1,0:T(8,128)S(1)}) custom-call(s32[1]{0:T(128)} %bitcast.sub_ref, f32[4,520,128]{2,1,0:T(8,128)S(1)} %pad_maximum_fusion.seen_ref, f32[1024,128]{1,0:T(8,128)} %bitcast.17.base_ref, f32[1024,128]{1,0:T(8,128)} %bitcast.24.refs_0_, ...), custom_call_target="tpu_custom_call" | custom-call | flops 402653184 | bytes 2097152 | tf_op jit(solution)/shard_map/backward_kernel1/pallas_call | solution.py:163
  242.7 1.8 collective-permute-start.25
  246.2 5.0 %collective-permute-start.29 = (f32[256,128]{1,0:T(8,128)S(1)}, f32[256,128]{1,0:T(8,128)S(1)}, u32[]{:S(2)}, u32[]{:S(2)}) collective-permute-start(f32[256,128]{1,0:T(8,128)S(1)} %pad_maximum_fusion.2.refs_0_), channel_id=1, source_target_pairs={{0,16},{16,0},{32,48},{48,32},{1,17},{17,1},{33,49},{49,33},{2,18}... | collective-permute-start | bytes 393224 | tf_op jit(solution)/shard_map/ppermute | solution.py:230
  251.5 1.6 collective-permute-start.31
  253.1 2.8 collective-permute-done.30.refs_2_
  255.9 3.3 %collective-permute-done.31.refs_3_ = f32[256,128]{1,0:T(8,128)S(1)} collective-permute-done((f32[256,128]{1,0:T(8,128)S(1)}, f32[256,128]{1,0:T(8,128)S(1)}, u32[]{:S(2)}, u32[]{:S(2)}) %collective-permute-start.31) | collective-permute-done | bytes 131104 | tf_op jit(solution)/shard_map/ppermute | solution.py:230
  259.2 1.3 correct2.1
  260.6 21.0 %all_to_all.53.parts_ref = f32[16,64,128]{2,1,0:T(8,128)S(1)} all-to-all(f32[16,64,128]{2,1,0:T(8,128)S(1)} %bitcast.76), channel_id=1, replica_groups=mesh['sub'=4,'row'=4,'col'=16] {'col'}, dimensions={0} | all-to-all | bytes 1048576 | tf_op jit(solution)/shard_map/all_to_all | solution.py:255
  282.5 3.7 %all-to-all-start.9 = ((f32[16,64,128]{2,1,0:T(8,128)}), f32[16,64,128]{2,1,0:T(8,128)S(1)}, u32[]{:S(2)}, u32[]{:S(2)}) async-start(f32[16,64,128]{2,1,0:T(8,128)} %fold.9), calls=%async_computation.9 | async-start | bytes 1048576 | tf_op jit(solution)/shard_map/all_to_all | solution.py:256
  286.1 1.8 collective-permute-start.35
  288.3 3.5 %collective-permute-start.41 = (f32[256,128]{1,0:T(8,128)S(1)}, f32[256,128]{1,0:T(8,128)S(1)}, u32[]{:S(2)}, u32[]{:S(2)}) collective-permute-start(f32[256,128]{1,0:T(8,128)S(1)} %slice.29), channel_id=1, source_target_pairs={{0,48},{16,32},{32,16},{48,0},{1,49},{17,33},{33,17},{49,1},{2,50}... | collective-permute-start | bytes 393224 | tf_op jit(solution)/shard_map/ppermute | solution.py:230
  292.4 2.6 collective-permute-start.38
  294.9 2.7 collective-permute-start.36
  297.7 5.5 %collective-permute-done.41 = f32[256,128]{1,0:T(8,128)S(1)} collective-permute-done((f32[256,128]{1,0:T(8,128)S(1)}, f32[256,128]{1,0:T(8,128)S(1)}, u32[]{:S(2)}, u32[]{:S(2)}) %collective-permute-start.41) | collective-permute-done | bytes 131104 | tf_op jit(solution)/shard_map/ppermute | solution.py:230
  303.2 2.4 backward_kernel0.1
  305.7 4.6 %collective-permute-start.34 = (f32[256,128]{1,0:T(8,128)S(1)}, f32[256,128]{1,0:T(8,128)S(1)}, u32[]{:S(2)}, u32[]{:S(2)}) collective-permute-start(f32[256,128]{1,0:T(8,128)S(1)} %backward_kernel0.1), channel_id=1, source_target_pairs={{0,48},{16,32},{32,16},{48,0},{1,49},{17,33},{33,17},{49,1},{2,50}... | collective-permute-start | bytes 393224 | tf_op jit(solution)/shard_map/ppermute | solution.py:230
  310.4 5.4 %collective-permute-done.34 = f32[256,128]{1,0:T(8,128)S(1)} collective-permute-done((f32[256,128]{1,0:T(8,128)S(1)}, f32[256,128]{1,0:T(8,128)S(1)}, u32[]{:S(2)}, u32[]{:S(2)}) %collective-permute-start.34) | collective-permute-done | bytes 131104 | tf_op jit(solution)/shard_map/ppermute | solution.py:230
  (113 shorter events, 17.1 us)
Async XLA Ops:
  0.0 14.4 %copy-start.1 = (f32[3,1,256,128]{3,2,1,0:T(8,128)S(1)}, f32[3,1,256,128]{3,2,1,0:T(8,128)}, u32[]{:S(2)}) copy-start(f32[3,1,256,128]{3,2,1,0:T(8,128)} %param.4) | copy-start | bytes 1179652
  2.8 11.7 %copy-start.19 = (s32[3,1,128]{2,1,0:T(1,128)S(1)}, s32[3,1,128]{2,1,0:T(1,128)}, u32[]{:S(2)}) copy-start(s32[3,1,128]{2,1,0:T(1,128)} %param.7) | copy-start | bytes 4612
  2.9 28.8 %all-to-all-start = ((f32[16,64,128]{2,1,0:T(8,128)}), f32[16,64,128]{2,1,0:T(8,128)S(1)}, u32[]{:S(2)}, u32[]{:S(2)}) async-start(f32[16,64,128]{2,1,0:T(8,128)} %bitcast.84), calls=%async_computation | async-start | bytes 1048576 | tf_op jit(solution)/shard_map/all_to_all | solution.py:255
  14.5 40.1 %copy-start = (f32[3,1,128,1024]{3,2,1,0:T(8,128)S(1)}, f32[3,1,128,1024]{3,2,1,0:T(8,128)}, u32[]{:S(2)}) copy-start(f32[3,1,128,1024]{3,2,1,0:T(8,128)} %param.6) | copy-start | bytes 4718596
  14.7 40.2 %copy-start.15 = (f32[520,128]{1,0:T(8,128)}, f32[520,128]{1,0:T(8,128)S(1)}, u32[]{:S(2)}) copy-start(f32[520,128]{1,0:T(8,128)S(1)} %maximum_maximum_fusion) | copy-start | bytes 798724
  32.5 22.0 %all-to-all-start.1 = ((f32[16,64,128]{2,1,0:T(8,128)}), f32[16,64,128]{2,1,0:T(8,128)S(1)}, u32[]{:S(2)}, u32[]{:S(2)}) async-start(f32[16,64,128]{2,1,0:T(8,128)} %fold.5), calls=%async_computation.1 | async-start | bytes 1048576 | tf_op jit(solution)/shard_map/all_to_all | solution.py:256
  37.3 21.8 %collective-permute-start.2 = (f32[520,128]{1,0:T(8,128)S(1)}, f32[520,128]{1,0:T(8,128)S(1)}, u32[]{:S(2)}, u32[]{:S(2)}) collective-permute-start(f32[520,128]{1,0:T(8,128)S(1)} %maximum_maximum_fusion), channel_id=1, source_target_pairs={{0,192},{64,128},{128,64},{192,0},{1,193},{65,129},{129,65},{193,1... | collective-permute-start | bytes 798728 | tf_op jit(solution)/shard_map/ppermute | solution.py:230
  40.1 19.0 %collective-permute-start.1 = (f32[520,128]{1,0:T(8,128)S(1)}, f32[520,128]{1,0:T(8,128)S(1)}, u32[]{:S(2)}, u32[]{:S(2)}) collective-permute-start(f32[520,128]{1,0:T(8,128)S(1)} %maximum_maximum_fusion), channel_id=1, source_target_pairs={{0,128},{64,192},{128,0},{192,64},{1,129},{65,193},{129,1},{193,65... | collective-permute-start | bytes 798728 | tf_op jit(solution)/shard_map/ppermute | solution.py:230
  40.4 18.7 %collective-permute-start = (f32[520,128]{1,0:T(8,128)S(1)}, f32[520,128]{1,0:T(8,128)S(1)}, u32[]{:S(2)}, u32[]{:S(2)}) collective-permute-start(f32[520,128]{1,0:T(8,128)S(1)} %maximum_maximum_fusion), channel_id=1, source_target_pairs={{0,64},{64,0},{128,192},{192,128},{1,65},{65,1},{129,193},{193,129... | collective-permute-start | bytes 798728 | tf_op jit(solution)/shard_map/ppermute | solution.py:230
  55.0 6.3 %collective-permute-start.4 = (f32[128,128]{1,0:T(8,128)S(1)}, f32[128,128]{1,0:T(8,128)S(1)}, u32[]{:S(2)}, u32[]{:S(2)}) collective-permute-start(f32[128,128]{1,0:T(8,128)S(1)} %convolution_bitcast_fusion.2), channel_id=1, source_target_pairs={{0,32},{16,48},{32,0},{48,16},{1,33},{17,49},{33,1},{49,17},{2,34}... | collective-permute-start | bytes 196616 | tf_op jit(solution)/shard_map/ppermute | solution.py:230
  55.4 7.0 %collective-permute-start.5 = (f32[128,128]{1,0:T(8,128)S(1)}, f32[128,128]{1,0:T(8,128)S(1)}, u32[]{:S(2)}, u32[]{:S(2)}) collective-permute-start(f32[128,128]{1,0:T(8,128)S(1)} %convolution_bitcast_fusion.2), channel_id=1, source_target_pairs={{0,48},{16,32},{32,16},{48,0},{1,49},{17,33},{33,17},{49,1},{2,50}... | collective-permute-start | bytes 196616 | tf_op jit(solution)/shard_map/ppermute | solution.py:230
  59.1 3.3 %collective-permute-start.3 = (f32[128,128]{1,0:T(8,128)S(1)}, f32[128,128]{1,0:T(8,128)S(1)}, u32[]{:S(2)}, u32[]{:S(2)}) collective-permute-start(f32[128,128]{1,0:T(8,128)S(1)} %convolution_bitcast_fusion.2), channel_id=1, source_target_pairs={{0,16},{16,0},{32,48},{48,32},{1,17},{17,1},{33,49},{49,33},{2,18}... | collective-permute-start | bytes 196616 | tf_op jit(solution)/shard_map/ppermute | solution.py:230
  59.1 0.9 copy-start.18
  62.4 3.7 %collective-permute-start.6 = (f32[128,128]{1,0:T(8,128)S(1)}, f32[128,128]{1,0:T(8,128)S(1)}, u32[]{:S(2)}, u32[]{:S(2)}) collective-permute-start(f32[128,128]{1,0:T(8,128)S(1)} %add_add_fusion.4.refs_0_), channel_id=1, source_target_pairs={{0,64},{64,0},{128,192},{192,128},{1,65},{65,1},{129,193},{193,129... | collective-permute-start | bytes 196616 | tf_op jit(solution)/shard_map/ppermute | solution.py:230
  68.4 0.8 copy-start.2
  69.2 21.5 %all-to-all-start.2 = ((f32[16,64,128]{2,1,0:T(8,128)}), f32[16,64,128]{2,1,0:T(8,128)}, u32[]{:S(2)}, u32[]{:S(2)}) async-start(f32[16,64,128]{2,1,0:T(8,128)} %bitcast.73), calls=%async_computation.2 | async-start | bytes 1048576 | tf_op jit(solution)/shard_map/all_to_all | solution.py:255
  73.5 3.8 %collective-permute-start.8 = (f32[128,128]{1,0:T(8,128)}, f32[128,128]{1,0:T(8,128)S(1)}, u32[]{:S(2)}, u32[]{:S(2)}) collective-permute-start(f32[128,128]{1,0:T(8,128)} %convolution_bitcast_fusion.1), channel_id=1, source_target_pairs={{0,32},{16,48},{32,0},{48,16},{1,33},{17,49},{33,1},{49,17},{2,34}... | collective-permute-start | bytes 196616 | tf_op jit(solution)/shard_map/ppermute | solution.py:230
  73.6 7.2 %collective-permute-start.9 = (f32[128,128]{1,0:T(8,128)}, f32[128,128]{1,0:T(8,128)S(1)}, u32[]{:S(2)}, u32[]{:S(2)}) collective-permute-start(f32[128,128]{1,0:T(8,128)} %convolution_bitcast_fusion.1), channel_id=1, source_target_pairs={{0,48},{16,32},{32,16},{48,0},{1,49},{17,33},{33,17},{49,1},{2,50}... | collective-permute-start | bytes 196616 | tf_op jit(solution)/shard_map/ppermute | solution.py:230
  76.1 4.8 %collective-permute-start.7 = (f32[128,128]{1,0:T(8,128)}, f32[128,128]{1,0:T(8,128)S(1)}, u32[]{:S(2)}, u32[]{:S(2)}) collective-permute-start(f32[128,128]{1,0:T(8,128)} %convolution_bitcast_fusion.1), channel_id=1, source_target_pairs={{0,16},{16,0},{32,48},{48,32},{1,17},{17,1},{33,49},{49,33},{2,18}... | collective-permute-start | bytes 196616 | tf_op jit(solution)/shard_map/ppermute | solution.py:230
  91.8 0.8 copy-start.3
  92.6 20.4 %all-to-all-start.3 = ((f32[16,64,128]{2,1,0:T(8,128)}), f32[16,64,128]{2,1,0:T(8,128)}, u32[]{:S(2)}, u32[]{:S(2)}) async-start(f32[16,64,128]{2,1,0:T(8,128)} %copy-done.3), calls=%async_computation.3 | async-start | bytes 1048576 | tf_op jit(solution)/shard_map/all_to_all | solution.py:256
  97.3 5.1 %collective-permute-start.12 = (f32[128,128]{1,0:T(8,128)}, f32[128,128]{1,0:T(8,128)S(1)}, u32[]{:S(2)}, u32[]{:S(2)}) collective-permute-start(f32[128,128]{1,0:T(8,128)} %add_add_fusion.3), channel_id=1, source_target_pairs={{0,192},{64,128},{128,64},{192,0},{1,193},{65,129},{129,65},{193,1... | collective-permute-start | bytes 196616 | tf_op jit(solution)/shard_map/ppermute | solution.py:230
  100.2 5.0 %collective-permute-start.11 = (f32[128,128]{1,0:T(8,128)}, f32[128,128]{1,0:T(8,128)S(1)}, u32[]{:S(2)}, u32[]{:S(2)}) collective-permute-start(f32[128,128]{1,0:T(8,128)} %add_add_fusion.3), channel_id=1, source_target_pairs={{0,128},{64,192},{128,0},{192,64},{1,129},{65,193},{129,1},{193,65... | collective-permute-start | bytes 196616 | tf_op jit(solution)/shard_map/ppermute | solution.py:230
  100.5 4.6 %collective-permute-start.10 = (f32[128,128]{1,0:T(8,128)}, f32[128,128]{1,0:T(8,128)S(1)}, u32[]{:S(2)}, u32[]{:S(2)}) collective-permute-start(f32[128,128]{1,0:T(8,128)} %add_add_fusion.3), channel_id=1, source_target_pairs={{0,64},{64,0},{128,192},{192,128},{1,65},{65,1},{129,193},{193,129... | collective-permute-start | bytes 196616 | tf_op jit(solution)/shard_map/ppermute | solution.py:230
  113.0 18.9 %copy-start.5 = (f32[512,128]{1,0:T(8,128)S(1)}, f32[512,128]{1,0:T(8,128)}, u32[]{:S(2)}) copy-start(f32[512,128]{1,0:T(8,128)} %pad_maximum_fusion.1.refs_0_) | copy-start | bytes 786436
  114.5 6.0 %collective-permute-start.14 = (f32[128,128]{1,0:T(8,128)S(1)}, f32[128,128]{1,0:T(8,128)S(1)}, u32[]{:S(2)}, u32[]{:S(2)}) collective-permute-start(f32[128,128]{1,0:T(8,128)S(1)} %convolution_bitcast_fusion), channel_id=1, source_target_pairs={{0,32},{16,48},{32,0},{48,16},{1,33},{17,49},{33,1},{49,17},{2,34}... | collective-permute-start | bytes 196616 | tf_op jit(solution)/shard_map/ppermute | solution.py:230
  114.6 8.8 %collective-permute-start.15 = (f32[128,128]{1,0:T(8,128)S(1)}, f32[128,128]{1,0:T(8,128)S(1)}, u32[]{:S(2)}, u32[]{:S(2)}) collective-permute-start(f32[128,128]{1,0:T(8,128)S(1)} %convolution_bitcast_fusion), channel_id=1, source_target_pairs={{0,48},{16,32},{32,16},{48,0},{1,49},{17,33},{33,17},{49,1},{2,50}... | collective-permute-start | bytes 196616 | tf_op jit(solution)/shard_map/ppermute | solution.py:230
  120.5 2.9 collective-permute-start.13
  123.4 4.0 %collective-permute-start.16 = (f32[128,128]{1,0:T(8,128)S(1)}, f32[128,128]{1,0:T(8,128)S(1)}, u32[]{:S(2)}, u32[]{:S(2)}) collective-permute-start(f32[128,128]{1,0:T(8,128)S(1)} %add_add_fusion.2.refs_1_), channel_id=1, source_target_pairs={{0,64},{64,0},{128,192},{192,128},{1,65},{65,1},{129,193},{193,129... | collective-permute-start | bytes 196616 | tf_op jit(solution)/shard_map/ppermute | solution.py:230
  124.8 6.2 %collective-permute-start.17 = (f32[128,128]{1,0:T(8,128)S(1)}, f32[128,128]{1,0:T(8,128)S(1)}, u32[]{:S(2)}, u32[]{:S(2)}) collective-permute-start(f32[128,128]{1,0:T(8,128)S(1)} %add_add_fusion.2.refs_1_), channel_id=1, source_target_pairs={{0,128},{64,192},{128,0},{192,64},{1,129},{65,193},{129,1},{193,65... | collective-permute-start | bytes 196616 | tf_op jit(solution)/shard_map/ppermute | solution.py:230
  127.4 4.5 %collective-permute-start.18 = (f32[128,128]{1,0:T(8,128)S(1)}, f32[128,128]{1,0:T(8,128)S(1)}, u32[]{:S(2)}, u32[]{:S(2)}) collective-permute-start(f32[128,128]{1,0:T(8,128)S(1)} %add_add_fusion.2.refs_1_), channel_id=1, source_target_pairs={{0,192},{64,128},{128,64},{192,0},{1,193},{65,129},{129,65},{193,1... | collective-permute-start | bytes 196616 | tf_op jit(solution)/shard_map/ppermute | solution.py:230
  179.7 18.2 %copy-start.10 = (f32[384,128]{1,0:T(8,128)}, f32[384,128]{1,0:T(8,128)S(1)}, u32[]{:S(2)}) copy-start(f32[384,128]{1,0:T(8,128)S(1)} %get-tuple-element.57) | copy-start | bytes 589828
  179.7 18.2 %copy-start.12 = (f32[384,128]{1,0:T(8,128)}, f32[384,128]{1,0:T(8,128)S(1)}, u32[]{:S(2)}) copy-start(f32[384,128]{1,0:T(8,128)S(1)} %get-tuple-element.58) | copy-start | bytes 589828
  179.7 38.4 %copy-start.6 = (f32[384,128]{1,0:T(8,128)}, f32[384,128]{1,0:T(8,128)S(1)}, u32[]{:S(2)}) copy-start(f32[384,128]{1,0:T(8,128)S(1)} %get-tuple-element.55) | copy-start | bytes 589828
  179.7 5.0 %collective-permute-start.21 = (f32[128,128]{1,0:T(8,128)S(1)}, f32[128,128]{1,0:T(8,128)S(1)}, u32[]{:S(2)}, u32[]{:S(2)}) collective-permute-start(f32[128,128]{1,0:T(8,128)S(1)} %get-tuple-element.47), channel_id=1, source_target_pairs={{0,192},{64,128},{128,64},{192,0},{1,193},{65,129},{129,65},{193,1... | collective-permute-start | bytes 196616 | tf_op jit(solution)/shard_map/ppermute | solution.py:230
  183.1 3.1 collective-permute-start.19
  183.1 4.6 %collective-permute-start.20 = (f32[128,128]{1,0:T(8,128)S(1)}, f32[128,128]{1,0:T(8,128)S(1)}, u32[]{:S(2)}, u32[]{:S(2)}) collective-permute-start(f32[128,128]{1,0:T(8,128)S(1)} %get-tuple-element.46), channel_id=1, source_target_pairs={{0,128},{64,192},{128,0},{192,64},{1,129},{65,193},{129,1},{193,65... | collective-permute-start | bytes 196616 | tf_op jit(solution)/shard_map/ppermute | solution.py:230
  187.7 5.6 %collective-permute-start.22 = (f32[128,128]{1,0:T(8,128)S(1)}, f32[128,128]{1,0:T(8,128)S(1)}, u32[]{:S(2)}, u32[]{:S(2)}) collective-permute-start(f32[128,128]{1,0:T(8,128)S(1)} %add_add_fusion.1.refs_0_), channel_id=1, source_target_pairs={{0,16},{16,0},{32,48},{48,32},{1,17},{17,1},{33,49},{49,33},{2,18}... | collective-permute-start | bytes 196616 | tf_op jit(solution)/shard_map/ppermute | solution.py:230
  191.5 3.5 %collective-permute-start.23 = (f32[128,128]{1,0:T(8,128)S(1)}, f32[128,128]{1,0:T(8,128)S(1)}, u32[]{:S(2)}, u32[]{:S(2)}) collective-permute-start(f32[128,128]{1,0:T(8,128)S(1)} %add_add_fusion.1.refs_0_), channel_id=1, source_target_pairs={{0,32},{16,48},{32,0},{48,16},{1,33},{17,49},{33,1},{49,17},{2,34}... | collective-permute-start | bytes 196616 | tf_op jit(solution)/shard_map/ppermute | solution.py:230
  191.5 5.2 %collective-permute-start.24 = (f32[128,128]{1,0:T(8,128)S(1)}, f32[128,128]{1,0:T(8,128)S(1)}, u32[]{:S(2)}, u32[]{:S(2)}) collective-permute-start(f32[128,128]{1,0:T(8,128)S(1)} %add_add_fusion.1.refs_0_), channel_id=1, source_target_pairs={{0,48},{16,32},{32,16},{48,0},{1,49},{17,33},{33,17},{49,1},{2,50}... | collective-permute-start | bytes 196616 | tf_op jit(solution)/shard_map/ppermute | solution.py:230
  219.0 20.4 %all-to-all-start.7 = ((f32[16,64,128]{2,1,0:T(8,128)}), f32[16,64,128]{2,1,0:T(8,128)}, u32[]{:S(2)}, u32[]{:S(2)}) async-start(f32[16,64,128]{2,1,0:T(8,128)} %copy-done.4), calls=%async_computation.7 | async-start | bytes 1048576 | tf_op jit(solution)/shard_map/all_to_all | solution.py:256
  223.3 21.2 %collective-permute-start.28 = (f32[384,128]{1,0:T(8,128)}, f32[384,128]{1,0:T(8,128)}, u32[]{:S(2)}, u32[]{:S(2)}) collective-permute-start(f32[384,128]{1,0:T(8,128)} %copy-done.12), channel_id=1, source_target_pairs={{0,192},{64,128},{128,64},{192,0},{1,193},{65,129},{129,65},{193,1... | collective-permute-start | bytes 589832 | tf_op jit(solution)/shard_map/ppermute | solution.py:230
  225.0 19.5 %collective-permute-start.26 = (f32[384,128]{1,0:T(8,128)}, f32[384,128]{1,0:T(8,128)}, u32[]{:S(2)}, u32[]{:S(2)}) collective-permute-start(f32[384,128]{1,0:T(8,128)} %copy-done.11), channel_id=1, source_target_pairs={{0,64},{64,0},{128,192},{192,128},{1,65},{65,1},{129,193},{193,129... | collective-permute-start | bytes 589832 | tf_op jit(solution)/shard_map/ppermute | solution.py:230
  225.3 19.2 %collective-permute-start.27 = (f32[384,128]{1,0:T(8,128)}, f32[384,128]{1,0:T(8,128)}, u32[]{:S(2)}, u32[]{:S(2)}) collective-permute-start(f32[384,128]{1,0:T(8,128)} %copy-done.10), channel_id=1, source_target_pairs={{0,128},{64,192},{128,0},{192,64},{1,129},{65,193},{129,1},{193,65... | collective-permute-start | bytes 589832 | tf_op jit(solution)/shard_map/ppermute | solution.py:230
  239.4 5.1 %copy-start.7 = (f32[384,128]{1,0:T(8,128)S(1)}, f32[384,128]{1,0:T(8,128)}, u32[]{:S(2)}) copy-start(f32[384,128]{1,0:T(8,128)} %copy-done.6) | copy-start | bytes 589828
  242.7 17.9 %copy-start.8 = (f32[256,128]{1,0:T(8,128)}, f32[256,128]{1,0:T(8,128)S(1)}, u32[]{:S(2)}) copy-start(f32[256,128]{1,0:T(8,128)S(1)} %get-tuple-element.64) | copy-start | bytes 393220
  242.7 17.9 %copy-start.13 = (f32[256,128]{1,0:T(8,128)}, f32[256,128]{1,0:T(8,128)S(1)}, u32[]{:S(2)}) copy-start(f32[256,128]{1,0:T(8,128)S(1)} %get-tuple-element.65) | copy-start | bytes 393220
  242.7 3.5 %collective-permute-start.25 = (f32[128,128]{1,0:T(8,128)S(1)}, f32[128,128]{1,0:T(8,128)S(1)}, u32[]{:S(2)}, u32[]{:S(2)}) collective-permute-start(f32[128,128]{1,0:T(8,128)S(1)} %get-tuple-element.54), channel_id=1, source_target_pairs={{0,64},{64,0},{128,192},{192,128},{1,65},{65,1},{129,193},{193,129... | collective-permute-start | bytes 196616 | tf_op jit(solution)/shard_map/ppermute | solution.py:230
  246.2 6.9 %collective-permute-start.29 = (f32[256,128]{1,0:T(8,128)S(1)}, f32[256,128]{1,0:T(8,128)S(1)}, u32[]{:S(2)}, u32[]{:S(2)}) collective-permute-start(f32[256,128]{1,0:T(8,128)S(1)} %pad_maximum_fusion.2.refs_0_), channel_id=1, source_target_pairs={{0,16},{16,0},{32,48},{48,32},{1,17},{17,1},{33,49},{49,33},{2,18}... | collective-permute-start | bytes 393224 | tf_op jit(solution)/shard_map/ppermute | solution.py:230
  251.2 4.7 %collective-permute-start.30 = (f32[256,128]{1,0:T(8,128)S(1)}, f32[256,128]{1,0:T(8,128)S(1)}, u32[]{:S(2)}, u32[]{:S(2)}) collective-permute-start(f32[256,128]{1,0:T(8,128)S(1)} %pad_maximum_fusion.2.refs_0_), channel_id=1, source_target_pairs={{0,32},{16,48},{32,0},{48,16},{1,33},{17,49},{33,1},{49,17},{2,34}... | collective-permute-start | bytes 393224 | tf_op jit(solution)/shard_map/ppermute | solution.py:230
  251.5 7.7 %collective-permute-start.31 = (f32[256,128]{1,0:T(8,128)S(1)}, f32[256,128]{1,0:T(8,128)S(1)}, u32[]{:S(2)}, u32[]{:S(2)}) collective-permute-start(f32[256,128]{1,0:T(8,128)S(1)} %pad_maximum_fusion.2.refs_0_), channel_id=1, source_target_pairs={{0,48},{16,32},{32,16},{48,0},{1,49},{17,33},{33,17},{49,1},{2,50}... | collective-permute-start | bytes 393224 | tf_op jit(solution)/shard_map/ppermute | solution.py:230
  260.5 25.6 %copy-start.14 = (f32[256,128]{1,0:T(8,128)S(1)}, f32[256,128]{1,0:T(8,128)}, u32[]{:S(2)}) copy-start(f32[256,128]{1,0:T(8,128)} %copy-done.13) | copy-start | bytes 393220
  260.5 31.3 %copy-start.9 = (f32[256,128]{1,0:T(8,128)S(1)}, f32[256,128]{1,0:T(8,128)}, u32[]{:S(2)}) copy-start(f32[256,128]{1,0:T(8,128)} %copy-done.8) | copy-start | bytes 393220
  282.5 20.7 %all-to-all-start.9 = ((f32[16,64,128]{2,1,0:T(8,128)}), f32[16,64,128]{2,1,0:T(8,128)S(1)}, u32[]{:S(2)}, u32[]{:S(2)}) async-start(f32[16,64,128]{2,1,0:T(8,128)} %fold.9), calls=%async_computation.9 | async-start | bytes 1048576 | tf_op jit(solution)/shard_map/all_to_all | solution.py:256
  286.1 5.7 %collective-permute-start.35 = (f32[256,128]{1,0:T(8,128)S(1)}, f32[256,128]{1,0:T(8,128)S(1)}, u32[]{:S(2)}, u32[]{:S(2)}) collective-permute-start(f32[256,128]{1,0:T(8,128)S(1)} %copy-done.14), channel_id=1, source_target_pairs={{0,64},{64,0},{128,192},{192,128},{1,65},{65,1},{129,193},{193,129... | collective-permute-start | bytes 393224 | tf_op jit(solution)/shard_map/ppermute | solution.py:230
  288.0 7.0 %collective-permute-start.40 = (f32[256,128]{1,0:T(8,128)S(1)}, f32[256,128]{1,0:T(8,128)S(1)}, u32[]{:S(2)}, u32[]{:S(2)}) collective-permute-start(f32[256,128]{1,0:T(8,128)S(1)} %slice.29), channel_id=1, source_target_pairs={{0,32},{16,48},{32,0},{48,16},{1,33},{17,49},{33,1},{49,17},{2,34}... | collective-permute-start | bytes 393224 | tf_op jit(solution)/shard_map/ppermute | solution.py:230
  288.3 14.8 %collective-permute-start.41 = (f32[256,128]{1,0:T(8,128)S(1)}, f32[256,128]{1,0:T(8,128)S(1)}, u32[]{:S(2)}, u32[]{:S(2)}) collective-permute-start(f32[256,128]{1,0:T(8,128)S(1)} %slice.29), channel_id=1, source_target_pairs={{0,48},{16,32},{32,16},{48,0},{1,49},{17,33},{33,17},{49,1},{2,50}... | collective-permute-start | bytes 393224 | tf_op jit(solution)/shard_map/ppermute | solution.py:230
  291.9 11.3 %collective-permute-start.39 = (f32[256,128]{1,0:T(8,128)S(1)}, f32[256,128]{1,0:T(8,128)S(1)}, u32[]{:S(2)}, u32[]{:S(2)}) collective-permute-start(f32[256,128]{1,0:T(8,128)S(1)} %slice.29), channel_id=1, source_target_pairs={{0,16},{16,0},{32,48},{48,32},{1,17},{17,1},{33,49},{49,33},{2,18}... | collective-permute-start | bytes 393224 | tf_op jit(solution)/shard_map/ppermute | solution.py:230
  291.9 18.5 %collective-permute-start.37 = (f32[256,128]{1,0:T(8,128)S(1)}, f32[256,128]{1,0:T(8,128)S(1)}, u32[]{:S(2)}, u32[]{:S(2)}) collective-permute-start(f32[256,128]{1,0:T(8,128)S(1)} %add.109), channel_id=1, source_target_pairs={{0,32},{16,48},{32,0},{48,16},{1,33},{17,49},{33,1},{49,17},{2,34}... | collective-permute-start | bytes 393224 | tf_op jit(solution)/shard_map/ppermute | solution.py:230
  292.4 18.0 %collective-permute-start.38 = (f32[256,128]{1,0:T(8,128)S(1)}, f32[256,128]{1,0:T(8,128)S(1)}, u32[]{:S(2)}, u32[]{:S(2)}) collective-permute-start(f32[256,128]{1,0:T(8,128)S(1)} %add.109), channel_id=1, source_target_pairs={{0,48},{16,32},{32,16},{48,0},{1,49},{17,33},{33,17},{49,1},{2,50}... | collective-permute-start | bytes 393224 | tf_op jit(solution)/shard_map/ppermute | solution.py:230
  294.9 15.5 %collective-permute-start.36 = (f32[256,128]{1,0:T(8,128)S(1)}, f32[256,128]{1,0:T(8,128)S(1)}, u32[]{:S(2)}, u32[]{:S(2)}) collective-permute-start(f32[256,128]{1,0:T(8,128)S(1)} %add.109), channel_id=1, source_target_pairs={{0,16},{16,0},{32,48},{48,32},{1,17},{17,1},{33,49},{49,33},{2,18}... | collective-permute-start | bytes 393224 | tf_op jit(solution)/shard_map/ppermute | solution.py:230
  305.6 4.8 %collective-permute-start.33 = (f32[256,128]{1,0:T(8,128)S(1)}, f32[256,128]{1,0:T(8,128)S(1)}, u32[]{:S(2)}, u32[]{:S(2)}) collective-permute-start(f32[256,128]{1,0:T(8,128)S(1)} %backward_kernel0.1), channel_id=1, source_target_pairs={{0,32},{16,48},{32,0},{48,16},{1,33},{17,49},{33,1},{49,17},{2,34}... | collective-permute-start | bytes 393224 | tf_op jit(solution)/shard_map/ppermute | solution.py:230
  305.7 10.1 %collective-permute-start.34 = (f32[256,128]{1,0:T(8,128)S(1)}, f32[256,128]{1,0:T(8,128)S(1)}, u32[]{:S(2)}, u32[]{:S(2)}) collective-permute-start(f32[256,128]{1,0:T(8,128)S(1)} %backward_kernel0.1), channel_id=1, source_target_pairs={{0,48},{16,32},{32,16},{48,0},{1,49},{17,33},{33,17},{49,1},{2,50}... | collective-permute-start | bytes 393224 | tf_op jit(solution)/shard_map/ppermute | solution.py:230
  310.4 5.5 %collective-permute-start.32 = (f32[256,128]{1,0:T(8,128)S(1)}, f32[256,128]{1,0:T(8,128)S(1)}, u32[]{:S(2)}, u32[]{:S(2)}) collective-permute-start(f32[256,128]{1,0:T(8,128)S(1)} %backward_kernel0.1), channel_id=1, source_target_pairs={{0,16},{16,0},{32,48},{48,32},{1,17},{17,1},{33,49},{49,33},{2,18}... | collective-permute-start | bytes 393224 | tf_op jit(solution)/shard_map/ppermute | solution.py:230
  (4 other events, 2.9 us)

commit v8 on v7

--- a/solution.py
+++ b/solution.py
@@ -136,20 +136,27 @@
         out_refs[0][...] = total_ref[0].T
         return
     sub = sub_ref[0] % spans
-    pieces = jnp.concatenate([total_ref[a] for a in range(spans)], axis=1)
-    high, low = halves(pieces)
-    both = jnp.concatenate([high, low], axis=0)
+    pieces_ref = plain[0]
+    for a in range(spans):
+        pieces_ref[a * C : (a + 1) * C, :] = total_ref[a].T
+    high, low = halves(pieces_ref[: spans * C, :])
+    both = jnp.concatenate([high, low], axis=1)
+    columns = lax.broadcasted_iota(jnp.int32, (K, spans * C), 1)
     for m in range(spans):
-        picked = mm(both, hits(seen_ref, m, SLOTS_OF[level], spans))
-        picked = (picked[:N] + picked[N:]).T
-        own = total_ref[m ^ sub].T
+        lists = seen_ref[m, LIST_AT : LIST_AT + 8, :].T.astype(jnp.int32)
+        picked = []
+        for t in SLOTS_OF[level]:
+            chosen = jnp.where(columns == lists[:, t : t + 1], 1.0, 0.0).astype(jnp.bfloat16)
+            wide = mm(chosen, both)
+            picked.append(wide[:, :N] + wide[:, N:])
+        own = pieces_ref[pl.ds(pl.multiple_of((m ^ sub) * C, C), C), :]
         soon_ref, later_ref = out_refs[2 * m], out_refs[2 * m + 1]
         if level == 2:
-            soon_ref[...] = picked[K:]
-            later_ref[:K, :] = picked[:K]
+            soon_ref[...] = picked[1]
+            later_ref[:K, :] = picked[0]
             later_ref[K:, :] = own
         else:
-            soon_ref[...] = picked
+            soon_ref[...] = picked[0]
             later_ref[...] = own
 
 

time: 318 us -> 318 us (level)
  no operation moved by 1% of the time
where the time goes in v8:
time: 318 us; the launch traced here: 317 us
  waiting for transfers between devices  101 us (32%)
  starting transfers between devices  97.5 us (31%)
  blocking collectives  81.3 us (26%)
  Pallas kernels  23.7 us (7%)
  other arithmetic  6.57 us (2%)
  local copies, waits for them, and re-layouts  4.06 us (1%)
    ppermute x42, starting transfers between devices, swapped(): return lax.ppermute(value, axis, pairs)  64.3 us
    all_to_all x3, blocking collectives, col_sum(): lax.all_to_all(blocks, 'col', 0, 0)  60.6 us
    ppermute x42, waiting for transfers between devices, swapped(): return lax.ppermute(value, axis, pairs)  43.2 us
    all_to_all x4, waiting for transfers between devices, col_sum(): full = lax.all_to_all(own, 'col', 0, 0).reshape(part.shape)  32.2 us
    all_to_all x2, waiting for transfers between devices, col_sum(): lax.all_to_all(blocks, 'col', 0, 0)  25.3 us
    all_to_all x1, blocking collectives, col_sum(): full = lax.all_to_all(own, 'col', 0, 0).reshape(part.shape)  20.7 us
    pallas_call x6, Pallas kernels, call(): pl.pallas_call(functools.partial(kernel, level), in_specs=[pl.BlockSpec(m...  18.3 us
    all_to_all x4, starting transfers between devices, col_sum(): full = lax.all_to_all(own, 'col', 0, 0).reshape(part.shape)  17.4 us
  transfers between devices with their start and end apart: 48, of which 24 were waited for; matrix products, arithmetic and copies ran while one was open for 2% of the time, Pallas kernels for 2%

profile of v8, /device:TPU:1, one launch (start us, length us, event | category | flops | bytes accessed | tf_op | source)
XLA Modules:
  0.0 317.1 jit_solution(13605351310403899533)
XLA Ops:
  0.0 2.8 forward_kernel0.1
  2.9 11.6 %all-to-all-start = ((f32[16,64,128]{2,1,0:T(8,128)}), f32[16,64,128]{2,1,0:T(8,128)S(1)}, u32[]{:S(2)}, u32[]{:S(2)}) async-start(f32[16,64,128]{2,1,0:T(8,128)} %bitcast.84), calls=%async_computation | async-start | bytes 1048576 | tf_op jit(solution)/shard_map/all_to_all | solution.py:262
  14.8 16.9 %all-to-all-done.parts_ref = f32[16,64,128]{2,1,0:T(8,128)S(1)} async-done(((f32[16,64,128]{2,1,0:T(8,128)}), f32[16,64,128]{2,1,0:T(8,128)S(1)}, u32[]{:S(2)}, u32[]{:S(2)}) %all-to-all-start) | async-done | bytes 524320 | tf_op jit(solution)/shard_map/all_to_all | solution.py:262
  32.5 4.7 %all-to-all-start.1 = ((f32[16,64,128]{2,1,0:T(8,128)}), f32[16,64,128]{2,1,0:T(8,128)S(1)}, u32[]{:S(2)}, u32[]{:S(2)}) async-start(f32[16,64,128]{2,1,0:T(8,128)} %fold.5), calls=%async_computation.1 | async-start | bytes 1048576 | tf_op jit(solution)/shard_map/all_to_all | solution.py:263
  37.3 2.8 collective-permute-start.2
  40.8 13.8 %all-to-all-done.1 = f32[16,64,128]{2,1,0:T(8,128)S(1)} async-done(((f32[16,64,128]{2,1,0:T(8,128)}), f32[16,64,128]{2,1,0:T(8,128)S(1)}, u32[]{:S(2)}, u32[]{:S(2)}) %all-to-all-start.1) | async-done | bytes 524320 | tf_op jit(solution)/shard_map/all_to_all | solution.py:263
  55.4 3.7 %collective-permute-start.5 = (f32[128,128]{1,0:T(8,128)S(1)}, f32[128,128]{1,0:T(8,128)S(1)}, u32[]{:S(2)}, u32[]{:S(2)}) collective-permute-start(f32[128,128]{1,0:T(8,128)S(1)} %convolution_bitcast_fusion.2), channel_id=1, source_target_pairs={{0,48},{16,32},{32,16},{48,0},{1,49},{17,33},{33,17},{49,1},{2,50}... | collective-permute-start | bytes 196616 | tf_op jit(solution)/shard_map/ppermute | solution.py:237
  60.0 1.3 pad_maximum_fusion.seen_ref
  61.2 1.2 collective-permute-done.5
  62.4 1.4 collective-permute-start.6
  64.8 1.3 collective-permute-done.6.refs_1_
  66.2 2.3 forward_kernel1.1
  69.2 4.2 %all-to-all-start.2 = ((f32[16,64,128]{2,1,0:T(8,128)}), f32[16,64,128]{2,1,0:T(8,128)}, u32[]{:S(2)}, u32[]{:S(2)}) async-start(f32[16,64,128]{2,1,0:T(8,128)} %bitcast.73), calls=%async_computation.2 | async-start | bytes 1048576 | tf_op jit(solution)/shard_map/all_to_all | solution.py:262
  73.6 2.5 collective-permute-start.9
  76.1 1.2 collective-permute-done.8
  77.2 3.6 %collective-permute-done.9 = f32[128,128]{1,0:T(8,128)S(1)} collective-permute-done((f32[128,128]{1,0:T(8,128)}, f32[128,128]{1,0:T(8,128)S(1)}, u32[]{:S(2)}, u32[]{:S(2)}) %collective-permute-start.9) | collective-permute-done | bytes 65568 | tf_op jit(solution)/shard_map/ppermute | solution.py:237
  80.8 1.5 add_add_fusion.3
  82.3 8.4 %all-to-all-done.2.parts_ref = f32[16,64,128]{2,1,0:T(8,128)} async-done(((f32[16,64,128]{2,1,0:T(8,128)}), f32[16,64,128]{2,1,0:T(8,128)}, u32[]{:S(2)}, u32[]{:S(2)}) %all-to-all-start.2) | async-done | bytes 524320 | tf_op jit(solution)/shard_map/all_to_all | solution.py:262
  92.6 4.7 %all-to-all-start.3 = ((f32[16,64,128]{2,1,0:T(8,128)}), f32[16,64,128]{2,1,0:T(8,128)}, u32[]{:S(2)}, u32[]{:S(2)}) async-start(f32[16,64,128]{2,1,0:T(8,128)} %copy-done.3), calls=%async_computation.3 | async-start | bytes 1048576 | tf_op jit(solution)/shard_map/all_to_all | solution.py:263
  97.3 2.8 collective-permute-start.12
  100.8 1.6 collective-permute-done.12
  102.4 2.8 collective-permute-done.11
  105.2 1.6 pad_maximum_fusion.1.refs_0_
  106.7 6.3 %all-to-all-done.3 = f32[16,64,128]{2,1,0:T(8,128)} async-done(((f32[16,64,128]{2,1,0:T(8,128)}), f32[16,64,128]{2,1,0:T(8,128)}, u32[]{:S(2)}, u32[]{:S(2)}) %all-to-all-start.3) | async-done | bytes 524320 | tf_op jit(solution)/shard_map/all_to_all | solution.py:263
  113.0 1.5 convolution_bitcast_fusion
  114.6 5.9 %collective-permute-start.15 = (f32[128,128]{1,0:T(8,128)S(1)}, f32[128,128]{1,0:T(8,128)S(1)}, u32[]{:S(2)}, u32[]{:S(2)}) collective-permute-start(f32[128,128]{1,0:T(8,128)S(1)} %convolution_bitcast_fusion), channel_id=1, source_target_pairs={{0,48},{16,32},{32,16},{48,0},{1,49},{17,33},{33,17},{49,1},{2,50}... | collective-permute-start | bytes 196616 | tf_op jit(solution)/shard_map/ppermute | solution.py:237
  120.5 2.9 collective-permute-done.15
  123.4 1.4 collective-permute-start.16
  124.8 2.6 collective-permute-start.17
  127.4 3.6 %collective-permute-done.17.refs_3_ = f32[128,128]{1,0:T(8,128)S(1)} collective-permute-done((f32[128,128]{1,0:T(8,128)S(1)}, f32[128,128]{1,0:T(8,128)S(1)}, u32[]{:S(2)}, u32[]{:S(2)}) %collective-permute-start.17) | collective-permute-done | bytes 65568 | tf_op jit(solution)/shard_map/ppermute | solution.py:237
  131.9 3.1 forward_kernel2.1
  134.9 19.3 %all_to_all.50.parts_ref = f32[16,64,128]{2,1,0:T(8,128)S(1)} all-to-all(f32[16,64,128]{2,1,0:T(8,128)S(1)} %bitcast.75), channel_id=1, replica_groups=mesh['sub'=4,'row'=4,'col'=16] {'col'}, dimensions={0} | all-to-all | bytes 1048576 | tf_op jit(solution)/shard_map/all_to_all | solution.py:262
  154.3 20.7 %all_to_all.51 = f32[16,64,128]{2,1,0:T(8,128)S(1)} all-to-all(f32[16,64,128]{2,1,0:T(8,128)S(1)} %fold.7), channel_id=1, replica_groups=mesh['sub'=4,'row'=4,'col'=16] {'col'}, dimensions={0} | all-to-all | bytes 1048576 | tf_op jit(solution)/shard_map/all_to_all | solution.py:263
  175.0 4.3 %backward_kernel2.1 = (f32[128,128]{1,0:T(8,128)S(1)}, f32[384,128]{1,0:T(8,128)S(1)}, f32[128,128]{1,0:T(8,128)S(1)}, f32[384,128]{1,0:T(8,128)S(1)}, f32[128,1...) custom-call(s32[1]{0:T(128)} %bitcast.sub_ref, ...), custom_call_target="tpu_custom_call" | custom-call | flops 805306368 | bytes 4194304 | tf_op jit(solution)/shard_map/backward_kernel2/pallas_call | solution.py:170
  180.0 3.4 %collective-permute-start.21 = (f32[128,128]{1,0:T(8,128)S(1)}, f32[128,128]{1,0:T(8,128)S(1)}, u32[]{:S(2)}, u32[]{:S(2)}) collective-permute-start(f32[128,128]{1,0:T(8,128)S(1)} %get-tuple-element.47), channel_id=1, source_target_pairs={{0,192},{64,128},{128,64},{192,0},{1,193},{65,129},{129,65},{193,1... | collective-permute-start | bytes 196616 | tf_op jit(solution)/shard_map/ppermute | solution.py:237
  183.4 1.3 collective-permute-start.20
  185.0 1.5 collective-permute-done.19
  186.5 1.5 collective-permute-done.20
  188.0 3.8 %collective-permute-start.22 = (f32[128,128]{1,0:T(8,128)S(1)}, f32[128,128]{1,0:T(8,128)S(1)}, u32[]{:S(2)}, u32[]{:S(2)}) collective-permute-start(f32[128,128]{1,0:T(8,128)S(1)} %add_add_fusion.1.refs_0_), channel_id=1, source_target_pairs={{0,16},{16,0},{32,48},{48,32},{1,17},{17,1},{33,49},{49,33},{2,18}... | collective-permute-start | bytes 196616 | tf_op jit(solution)/shard_map/ppermute | solution.py:237
  191.8 1.7 collective-permute-start.24
  193.6 1.8 collective-permute-done.23.refs_2_
  195.4 1.7 collective-permute-done.24.refs_3_
  198.2 20.3 %all_to_all.52.parts_ref = f32[16,64,128]{2,1,0:T(8,128)S(1)} all-to-all(f32[16,64,128]{2,1,0:T(8,128)S(1)} %bitcast.77), channel_id=1, replica_groups=mesh['sub'=4,'row'=4,'col'=16] {'col'}, dimensions={0} | all-to-all | bytes 1048576 | tf_op jit(solution)/shard_map/all_to_all | solution.py:262
  219.3 4.3 %all-to-all-start.7 = ((f32[16,64,128]{2,1,0:T(8,128)}), f32[16,64,128]{2,1,0:T(8,128)}, u32[]{:S(2)}, u32[]{:S(2)}) async-start(f32[16,64,128]{2,1,0:T(8,128)} %copy-done.4), calls=%async_computation.7 | async-start | bytes 1048576 | tf_op jit(solution)/shard_map/all_to_all | solution.py:263
  223.6 1.7 collective-permute-start.28
  225.6 1.9 collective-permute-start.27
  227.6 12.1 %all-to-all-done.7 = f32[16,64,128]{2,1,0:T(8,128)} async-done(((f32[16,64,128]{2,1,0:T(8,128)}), f32[16,64,128]{2,1,0:T(8,128)}, u32[]{:S(2)}, u32[]{:S(2)}) %all-to-all-start.7) | async-done | bytes 524320 | tf_op jit(solution)/shard_map/all_to_all | solution.py:263
  239.7 3.4 %backward_kernel1.1 = (f32[128,128]{1,0:T(8,128)S(1)}, f32[256,128]{1,0:T(8,128)S(1)}, f32[128,128]{1,0:T(8,128)S(1)}, f32[256,128]{1,0:T(8,128)S(1)}) custom-call(s32[1]{0:T(128)} %bitcast.sub_ref, f32[4,520,128]{2,1,0:T(8,128)S(1)} %pad_maximum_fusion.seen_ref, f32[1024,128]{1,0:T(8,128)} %bitcast.17.base_ref, f32[1024,128]{1,0:T(8,128)} %bitcast.24.refs_0_, ...), custom_call_target="tpu_custom_call" | custom-call | flops 402653184 | bytes 2097152 | tf_op jit(solution)/shard_map/backward_kernel1/pallas_call | solution.py:170
  243.1 1.8 collective-permute-start.25
  246.7 5.0 %collective-permute-start.29 = (f32[256,128]{1,0:T(8,128)S(1)}, f32[256,128]{1,0:T(8,128)S(1)}, u32[]{:S(2)}, u32[]{:S(2)}) collective-permute-start(f32[256,128]{1,0:T(8,128)S(1)} %pad_maximum_fusion.2.refs_0_), channel_id=1, source_target_pairs={{0,16},{16,0},{32,48},{48,32},{1,17},{17,1},{33,49},{49,33},{2,18}... | collective-permute-start | bytes 393224 | tf_op jit(solution)/shard_map/ppermute | solution.py:237
  252.0 1.6 collective-permute-start.31
  253.6 2.8 collective-permute-done.30.refs_2_
  256.4 3.3 %collective-permute-done.31.refs_3_ = f32[256,128]{1,0:T(8,128)S(1)} collective-permute-done((f32[256,128]{1,0:T(8,128)S(1)}, f32[256,128]{1,0:T(8,128)S(1)}, u32[]{:S(2)}, u32[]{:S(2)}) %collective-permute-start.31) | collective-permute-done | bytes 131104 | tf_op jit(solution)/shard_map/ppermute | solution.py:237
  259.7 1.3 correct2.1
  261.0 21.0 %all_to_all.53.parts_ref = f32[16,64,128]{2,1,0:T(8,128)S(1)} all-to-all(f32[16,64,128]{2,1,0:T(8,128)S(1)} %bitcast.76), channel_id=1, replica_groups=mesh['sub'=4,'row'=4,'col'=16] {'col'}, dimensions={0} | all-to-all | bytes 1048576 | tf_op jit(solution)/shard_map/all_to_all | solution.py:262
  283.0 3.7 %all-to-all-start.9 = ((f32[16,64,128]{2,1,0:T(8,128)}), f32[16,64,128]{2,1,0:T(8,128)S(1)}, u32[]{:S(2)}, u32[]{:S(2)}) async-start(f32[16,64,128]{2,1,0:T(8,128)} %fold.9), calls=%async_computation.9 | async-start | bytes 1048576 | tf_op jit(solution)/shard_map/all_to_all | solution.py:263
  286.6 1.8 collective-permute-start.35
  288.8 3.5 %collective-permute-start.41 = (f32[256,128]{1,0:T(8,128)S(1)}, f32[256,128]{1,0:T(8,128)S(1)}, u32[]{:S(2)}, u32[]{:S(2)}) collective-permute-start(f32[256,128]{1,0:T(8,128)S(1)} %slice.29), channel_id=1, source_target_pairs={{0,48},{16,32},{32,16},{48,0},{1,49},{17,33},{33,17},{49,1},{2,50}... | collective-permute-start | bytes 393224 | tf_op jit(solution)/shard_map/ppermute | solution.py:237
  292.8 2.6 collective-permute-start.38
  295.4 2.8 collective-permute-start.36
  298.2 5.4 %collective-permute-done.41 = f32[256,128]{1,0:T(8,128)S(1)} collective-permute-done((f32[256,128]{1,0:T(8,128)S(1)}, f32[256,128]{1,0:T(8,128)S(1)}, u32[]{:S(2)}, u32[]{:S(2)}) %collective-permute-start.41) | collective-permute-done | bytes 131104 | tf_op jit(solution)/shard_map/ppermute | solution.py:237
  303.7 2.4 backward_kernel0.1
  306.2 4.6 %collective-permute-start.34 = (f32[256,128]{1,0:T(8,128)S(1)}, f32[256,128]{1,0:T(8,128)S(1)}, u32[]{:S(2)}, u32[]{:S(2)}) collective-permute-start(f32[256,128]{1,0:T(8,128)S(1)} %backward_kernel0.1), channel_id=1, source_target_pairs={{0,48},{16,32},{32,16},{48,0},{1,49},{17,33},{33,17},{49,1},{2,50}... | collective-permute-start | bytes 393224 | tf_op jit(solution)/shard_map/ppermute | solution.py:237
  310.9 5.4 %collective-permute-done.34 = f32[256,128]{1,0:T(8,128)S(1)} collective-permute-done((f32[256,128]{1,0:T(8,128)S(1)}, f32[256,128]{1,0:T(8,128)S(1)}, u32[]{:S(2)}, u32[]{:S(2)}) %collective-permute-start.34) | collective-permute-done | bytes 131104 | tf_op jit(solution)/shard_map/ppermute | solution.py:237
  (113 shorter events, 17.1 us)
Async XLA Ops:
  0.0 14.4 %copy-start.1 = (f32[3,1,256,128]{3,2,1,0:T(8,128)S(1)}, f32[3,1,256,128]{3,2,1,0:T(8,128)}, u32[]{:S(2)}) copy-start(f32[3,1,256,128]{3,2,1,0:T(8,128)} %param.4) | copy-start | bytes 1179652
  2.8 11.7 %copy-start.19 = (s32[3,1,128]{2,1,0:T(1,128)S(1)}, s32[3,1,128]{2,1,0:T(1,128)}, u32[]{:S(2)}) copy-start(s32[3,1,128]{2,1,0:T(1,128)} %param.7) | copy-start | bytes 4612
  2.9 28.8 %all-to-all-start = ((f32[16,64,128]{2,1,0:T(8,128)}), f32[16,64,128]{2,1,0:T(8,128)S(1)}, u32[]{:S(2)}, u32[]{:S(2)}) async-start(f32[16,64,128]{2,1,0:T(8,128)} %bitcast.84), calls=%async_computation | async-start | bytes 1048576 | tf_op jit(solution)/shard_map/all_to_all | solution.py:262
  14.5 40.1 %copy-start = (f32[3,1,128,1024]{3,2,1,0:T(8,128)S(1)}, f32[3,1,128,1024]{3,2,1,0:T(8,128)}, u32[]{:S(2)}) copy-start(f32[3,1,128,1024]{3,2,1,0:T(8,128)} %param.6) | copy-start | bytes 4718596
  14.7 40.2 %copy-start.15 = (f32[520,128]{1,0:T(8,128)}, f32[520,128]{1,0:T(8,128)S(1)}, u32[]{:S(2)}) copy-start(f32[520,128]{1,0:T(8,128)S(1)} %maximum_maximum_fusion) | copy-start | bytes 798724
  32.5 22.0 %all-to-all-start.1 = ((f32[16,64,128]{2,1,0:T(8,128)}), f32[16,64,128]{2,1,0:T(8,128)S(1)}, u32[]{:S(2)}, u32[]{:S(2)}) async-start(f32[16,64,128]{2,1,0:T(8,128)} %fold.5), calls=%async_computation.1 | async-start | bytes 1048576 | tf_op jit(solution)/shard_map/all_to_all | solution.py:263
  37.3 21.8 %collective-permute-start.2 = (f32[520,128]{1,0:T(8,128)S(1)}, f32[520,128]{1,0:T(8,128)S(1)}, u32[]{:S(2)}, u32[]{:S(2)}) collective-permute-start(f32[520,128]{1,0:T(8,128)S(1)} %maximum_maximum_fusion), channel_id=1, source_target_pairs={{0,192},{64,128},{128,64},{192,0},{1,193},{65,129},{129,65},{193,1... | collective-permute-start | bytes 798728 | tf_op jit(solution)/shard_map/ppermute | solution.py:237
  40.1 19.0 %collective-permute-start.1 = (f32[520,128]{1,0:T(8,128)S(1)}, f32[520,128]{1,0:T(8,128)S(1)}, u32[]{:S(2)}, u32[]{:S(2)}) collective-permute-start(f32[520,128]{1,0:T(8,128)S(1)} %maximum_maximum_fusion), channel_id=1, source_target_pairs={{0,128},{64,192},{128,0},{192,64},{1,129},{65,193},{129,1},{193,65... | collective-permute-start | bytes 798728 | tf_op jit(solution)/shard_map/ppermute | solution.py:237
  40.4 18.7 %collective-permute-start = (f32[520,128]{1,0:T(8,128)S(1)}, f32[520,128]{1,0:T(8,128)S(1)}, u32[]{:S(2)}, u32[]{:S(2)}) collective-permute-start(f32[520,128]{1,0:T(8,128)S(1)} %maximum_maximum_fusion), channel_id=1, source_target_pairs={{0,64},{64,0},{128,192},{192,128},{1,65},{65,1},{129,193},{193,129... | collective-permute-start | bytes 798728 | tf_op jit(solution)/shard_map/ppermute | solution.py:237
  55.0 6.3 %collective-permute-start.4 = (f32[128,128]{1,0:T(8,128)S(1)}, f32[128,128]{1,0:T(8,128)S(1)}, u32[]{:S(2)}, u32[]{:S(2)}) collective-permute-start(f32[128,128]{1,0:T(8,128)S(1)} %convolution_bitcast_fusion.2), channel_id=1, source_target_pairs={{0,32},{16,48},{32,0},{48,16},{1,33},{17,49},{33,1},{49,17},{2,34}... | collective-permute-start | bytes 196616 | tf_op jit(solution)/shard_map/ppermute | solution.py:237
  55.4 7.0 %collective-permute-start.5 = (f32[128,128]{1,0:T(8,128)S(1)}, f32[128,128]{1,0:T(8,128)S(1)}, u32[]{:S(2)}, u32[]{:S(2)}) collective-permute-start(f32[128,128]{1,0:T(8,128)S(1)} %convolution_bitcast_fusion.2), channel_id=1, source_target_pairs={{0,48},{16,32},{32,16},{48,0},{1,49},{17,33},{33,17},{49,1},{2,50}... | collective-permute-start | bytes 196616 | tf_op jit(solution)/shard_map/ppermute | solution.py:237
  59.1 3.3 %collective-permute-start.3 = (f32[128,128]{1,0:T(8,128)S(1)}, f32[128,128]{1,0:T(8,128)S(1)}, u32[]{:S(2)}, u32[]{:S(2)}) collective-permute-start(f32[128,128]{1,0:T(8,128)S(1)} %convolution_bitcast_fusion.2), channel_id=1, source_target_pairs={{0,16},{16,0},{32,48},{48,32},{1,17},{17,1},{33,49},{49,33},{2,18}... | collective-permute-start | bytes 196616 | tf_op jit(solution)/shard_map/ppermute | solution.py:237
  59.1 0.9 copy-start.18
  62.4 3.7 %collective-permute-start.6 = (f32[128,128]{1,0:T(8,128)S(1)}, f32[128,128]{1,0:T(8,128)S(1)}, u32[]{:S(2)}, u32[]{:S(2)}) collective-permute-start(f32[128,128]{1,0:T(8,128)S(1)} %add_add_fusion.4.refs_0_), channel_id=1, source_target_pairs={{0,64},{64,0},{128,192},{192,128},{1,65},{65,1},{129,193},{193,129... | collective-permute-start | bytes 196616 | tf_op jit(solution)/shard_map/ppermute | solution.py:237
  68.4 0.8 copy-start.2
  69.2 21.5 %all-to-all-start.2 = ((f32[16,64,128]{2,1,0:T(8,128)}), f32[16,64,128]{2,1,0:T(8,128)}, u32[]{:S(2)}, u32[]{:S(2)}) async-start(f32[16,64,128]{2,1,0:T(8,128)} %bitcast.73), calls=%async_computation.2 | async-start | bytes 1048576 | tf_op jit(solution)/shard_map/all_to_all | solution.py:262
  73.5 3.8 %collective-permute-start.8 = (f32[128,128]{1,0:T(8,128)}, f32[128,128]{1,0:T(8,128)S(1)}, u32[]{:S(2)}, u32[]{:S(2)}) collective-permute-start(f32[128,128]{1,0:T(8,128)} %convolution_bitcast_fusion.1), channel_id=1, source_target_pairs={{0,32},{16,48},{32,0},{48,16},{1,33},{17,49},{33,1},{49,17},{2,34}... | collective-permute-start | bytes 196616 | tf_op jit(solution)/shard_map/ppermute | solution.py:237
  73.6 7.2 %collective-permute-start.9 = (f32[128,128]{1,0:T(8,128)}, f32[128,128]{1,0:T(8,128)S(1)}, u32[]{:S(2)}, u32[]{:S(2)}) collective-permute-start(f32[128,128]{1,0:T(8,128)} %convolution_bitcast_fusion.1), channel_id=1, source_target_pairs={{0,48},{16,32},{32,16},{48,0},{1,49},{17,33},{33,17},{49,1},{2,50}... | collective-permute-start | bytes 196616 | tf_op jit(solution)/shard_map/ppermute | solution.py:237
  76.1 4.8 %collective-permute-start.7 = (f32[128,128]{1,0:T(8,128)}, f32[128,128]{1,0:T(8,128)S(1)}, u32[]{:S(2)}, u32[]{:S(2)}) collective-permute-start(f32[128,128]{1,0:T(8,128)} %convolution_bitcast_fusion.1), channel_id=1, source_target_pairs={{0,16},{16,0},{32,48},{48,32},{1,17},{17,1},{33,49},{49,33},{2,18}... | collective-permute-start | bytes 196616 | tf_op jit(solution)/shard_map/ppermute | solution.py:237
  91.8 0.8 copy-start.3
  92.6 20.4 %all-to-all-start.3 = ((f32[16,64,128]{2,1,0:T(8,128)}), f32[16,64,128]{2,1,0:T(8,128)}, u32[]{:S(2)}, u32[]{:S(2)}) async-start(f32[16,64,128]{2,1,0:T(8,128)} %copy-done.3), calls=%async_computation.3 | async-start | bytes 1048576 | tf_op jit(solution)/shard_map/all_to_all | solution.py:263
  97.3 5.1 %collective-permute-start.12 = (f32[128,128]{1,0:T(8,128)}, f32[128,128]{1,0:T(8,128)S(1)}, u32[]{:S(2)}, u32[]{:S(2)}) collective-permute-start(f32[128,128]{1,0:T(8,128)} %add_add_fusion.3), channel_id=1, source_target_pairs={{0,192},{64,128},{128,64},{192,0},{1,193},{65,129},{129,65},{193,1... | collective-permute-start | bytes 196616 | tf_op jit(solution)/shard_map/ppermute | solution.py:237
  100.2 5.0 %collective-permute-start.11 = (f32[128,128]{1,0:T(8,128)}, f32[128,128]{1,0:T(8,128)S(1)}, u32[]{:S(2)}, u32[]{:S(2)}) collective-permute-start(f32[128,128]{1,0:T(8,128)} %add_add_fusion.3), channel_id=1, source_target_pairs={{0,128},{64,192},{128,0},{192,64},{1,129},{65,193},{129,1},{193,65... | collective-permute-start | bytes 196616 | tf_op jit(solution)/shard_map/ppermute | solution.py:237
  100.5 4.6 %collective-permute-start.10 = (f32[128,128]{1,0:T(8,128)}, f32[128,128]{1,0:T(8,128)S(1)}, u32[]{:S(2)}, u32[]{:S(2)}) collective-permute-start(f32[128,128]{1,0:T(8,128)} %add_add_fusion.3), channel_id=1, source_target_pairs={{0,64},{64,0},{128,192},{192,128},{1,65},{65,1},{129,193},{193,129... | collective-permute-start | bytes 196616 | tf_op jit(solution)/shard_map/ppermute | solution.py:237
  113.0 18.9 %copy-start.5 = (f32[512,128]{1,0:T(8,128)S(1)}, f32[512,128]{1,0:T(8,128)}, u32[]{:S(2)}) copy-start(f32[512,128]{1,0:T(8,128)} %pad_maximum_fusion.1.refs_0_) | copy-start | bytes 786436
  114.5 6.0 %collective-permute-start.14 = (f32[128,128]{1,0:T(8,128)S(1)}, f32[128,128]{1,0:T(8,128)S(1)}, u32[]{:S(2)}, u32[]{:S(2)}) collective-permute-start(f32[128,128]{1,0:T(8,128)S(1)} %convolution_bitcast_fusion), channel_id=1, source_target_pairs={{0,32},{16,48},{32,0},{48,16},{1,33},{17,49},{33,1},{49,17},{2,34}... | collective-permute-start | bytes 196616 | tf_op jit(solution)/shard_map/ppermute | solution.py:237
  114.6 8.8 %collective-permute-start.15 = (f32[128,128]{1,0:T(8,128)S(1)}, f32[128,128]{1,0:T(8,128)S(1)}, u32[]{:S(2)}, u32[]{:S(2)}) collective-permute-start(f32[128,128]{1,0:T(8,128)S(1)} %convolution_bitcast_fusion), channel_id=1, source_target_pairs={{0,48},{16,32},{32,16},{48,0},{1,49},{17,33},{33,17},{49,1},{2,50}... | collective-permute-start | bytes 196616 | tf_op jit(solution)/shard_map/ppermute | solution.py:237
  120.5 2.9 collective-permute-start.13
  123.4 4.0 %collective-permute-start.16 = (f32[128,128]{1,0:T(8,128)S(1)}, f32[128,128]{1,0:T(8,128)S(1)}, u32[]{:S(2)}, u32[]{:S(2)}) collective-permute-start(f32[128,128]{1,0:T(8,128)S(1)} %add_add_fusion.2.refs_1_), channel_id=1, source_target_pairs={{0,64},{64,0},{128,192},{192,128},{1,65},{65,1},{129,193},{193,129... | collective-permute-start | bytes 196616 | tf_op jit(solution)/shard_map/ppermute | solution.py:237
  124.8 6.2 %collective-permute-start.17 = (f32[128,128]{1,0:T(8,128)S(1)}, f32[128,128]{1,0:T(8,128)S(1)}, u32[]{:S(2)}, u32[]{:S(2)}) collective-permute-start(f32[128,128]{1,0:T(8,128)S(1)} %add_add_fusion.2.refs_1_), channel_id=1, source_target_pairs={{0,128},{64,192},{128,0},{192,64},{1,129},{65,193},{129,1},{193,65... | collective-permute-start | bytes 196616 | tf_op jit(solution)/shard_map/ppermute | solution.py:237
  127.4 4.5 %collective-permute-start.18 = (f32[128,128]{1,0:T(8,128)S(1)}, f32[128,128]{1,0:T(8,128)S(1)}, u32[]{:S(2)}, u32[]{:S(2)}) collective-permute-start(f32[128,128]{1,0:T(8,128)S(1)} %add_add_fusion.2.refs_1_), channel_id=1, source_target_pairs={{0,192},{64,128},{128,64},{192,0},{1,193},{65,129},{129,65},{193,1... | collective-permute-start | bytes 196616 | tf_op jit(solution)/shard_map/ppermute | solution.py:237
  180.0 18.1 %copy-start.10 = (f32[384,128]{1,0:T(8,128)}, f32[384,128]{1,0:T(8,128)S(1)}, u32[]{:S(2)}) copy-start(f32[384,128]{1,0:T(8,128)S(1)} %get-tuple-element.57) | copy-start | bytes 589828
  180.0 18.2 %copy-start.12 = (f32[384,128]{1,0:T(8,128)}, f32[384,128]{1,0:T(8,128)S(1)}, u32[]{:S(2)}) copy-start(f32[384,128]{1,0:T(8,128)S(1)} %get-tuple-element.58) | copy-start | bytes 589828
  180.0 38.4 %copy-start.6 = (f32[384,128]{1,0:T(8,128)}, f32[384,128]{1,0:T(8,128)S(1)}, u32[]{:S(2)}) copy-start(f32[384,128]{1,0:T(8,128)S(1)} %get-tuple-element.55) | copy-start | bytes 589828
  180.0 5.0 %collective-permute-start.21 = (f32[128,128]{1,0:T(8,128)S(1)}, f32[128,128]{1,0:T(8,128)S(1)}, u32[]{:S(2)}, u32[]{:S(2)}) collective-permute-start(f32[128,128]{1,0:T(8,128)S(1)} %get-tuple-element.47), channel_id=1, source_target_pairs={{0,192},{64,128},{128,64},{192,0},{1,193},{65,129},{129,65},{193,1... | collective-permute-start | bytes 196616 | tf_op jit(solution)/shard_map/ppermute | solution.py:237
  183.4 3.1 collective-permute-start.19
  183.4 4.6 %collective-permute-start.20 = (f32[128,128]{1,0:T(8,128)S(1)}, f32[128,128]{1,0:T(8,128)S(1)}, u32[]{:S(2)}, u32[]{:S(2)}) collective-permute-start(f32[128,128]{1,0:T(8,128)S(1)} %get-tuple-element.46), channel_id=1, source_target_pairs={{0,128},{64,192},{128,0},{192,64},{1,129},{65,193},{129,1},{193,65... | collective-permute-start | bytes 196616 | tf_op jit(solution)/shard_map/ppermute | solution.py:237
  188.0 5.5 %collective-permute-start.22 = (f32[128,128]{1,0:T(8,128)S(1)}, f32[128,128]{1,0:T(8,128)S(1)}, u32[]{:S(2)}, u32[]{:S(2)}) collective-permute-start(f32[128,128]{1,0:T(8,128)S(1)} %add_add_fusion.1.refs_0_), channel_id=1, source_target_pairs={{0,16},{16,0},{32,48},{48,32},{1,17},{17,1},{33,49},{49,33},{2,18}... | collective-permute-start | bytes 196616 | tf_op jit(solution)/shard_map/ppermute | solution.py:237
  191.8 3.5 %collective-permute-start.23 = (f32[128,128]{1,0:T(8,128)S(1)}, f32[128,128]{1,0:T(8,128)S(1)}, u32[]{:S(2)}, u32[]{:S(2)}) collective-permute-start(f32[128,128]{1,0:T(8,128)S(1)} %add_add_fusion.1.refs_0_), channel_id=1, source_target_pairs={{0,32},{16,48},{32,0},{48,16},{1,33},{17,49},{33,1},{49,17},{2,34}... | collective-permute-start | bytes 196616 | tf_op jit(solution)/shard_map/ppermute | solution.py:237
  191.8 5.2 %collective-permute-start.24 = (f32[128,128]{1,0:T(8,128)S(1)}, f32[128,128]{1,0:T(8,128)S(1)}, u32[]{:S(2)}, u32[]{:S(2)}) collective-permute-start(f32[128,128]{1,0:T(8,128)S(1)} %add_add_fusion.1.refs_0_), channel_id=1, source_target_pairs={{0,48},{16,32},{32,16},{48,0},{1,49},{17,33},{33,17},{49,1},{2,50}... | collective-permute-start | bytes 196616 | tf_op jit(solution)/shard_map/ppermute | solution.py:237
  219.3 20.4 %all-to-all-start.7 = ((f32[16,64,128]{2,1,0:T(8,128)}), f32[16,64,128]{2,1,0:T(8,128)}, u32[]{:S(2)}, u32[]{:S(2)}) async-start(f32[16,64,128]{2,1,0:T(8,128)} %copy-done.4), calls=%async_computation.7 | async-start | bytes 1048576 | tf_op jit(solution)/shard_map/all_to_all | solution.py:263
  223.6 21.4 %collective-permute-start.28 = (f32[384,128]{1,0:T(8,128)}, f32[384,128]{1,0:T(8,128)}, u32[]{:S(2)}, u32[]{:S(2)}) collective-permute-start(f32[384,128]{1,0:T(8,128)} %copy-done.12), channel_id=1, source_target_pairs={{0,192},{64,128},{128,64},{192,0},{1,193},{65,129},{129,65},{193,1... | collective-permute-start | bytes 589832 | tf_op jit(solution)/shard_map/ppermute | solution.py:237
  225.3 19.7 %collective-permute-start.26 = (f32[384,128]{1,0:T(8,128)}, f32[384,128]{1,0:T(8,128)}, u32[]{:S(2)}, u32[]{:S(2)}) collective-permute-start(f32[384,128]{1,0:T(8,128)} %copy-done.11), channel_id=1, source_target_pairs={{0,64},{64,0},{128,192},{192,128},{1,65},{65,1},{129,193},{193,129... | collective-permute-start | bytes 589832 | tf_op jit(solution)/shard_map/ppermute | solution.py:237
  225.6 19.3 %collective-permute-start.27 = (f32[384,128]{1,0:T(8,128)}, f32[384,128]{1,0:T(8,128)}, u32[]{:S(2)}, u32[]{:S(2)}) collective-permute-start(f32[384,128]{1,0:T(8,128)} %copy-done.10), channel_id=1, source_target_pairs={{0,128},{64,192},{128,0},{192,64},{1,129},{65,193},{129,1},{193,65... | collective-permute-start | bytes 589832 | tf_op jit(solution)/shard_map/ppermute | solution.py:237
  239.7 5.3 %copy-start.7 = (f32[384,128]{1,0:T(8,128)S(1)}, f32[384,128]{1,0:T(8,128)}, u32[]{:S(2)}) copy-start(f32[384,128]{1,0:T(8,128)} %copy-done.6) | copy-start | bytes 589828
  243.1 17.9 %copy-start.8 = (f32[256,128]{1,0:T(8,128)}, f32[256,128]{1,0:T(8,128)S(1)}, u32[]{:S(2)}) copy-start(f32[256,128]{1,0:T(8,128)S(1)} %get-tuple-element.64) | copy-start | bytes 393220
  243.1 17.9 %copy-start.13 = (f32[256,128]{1,0:T(8,128)}, f32[256,128]{1,0:T(8,128)S(1)}, u32[]{:S(2)}) copy-start(f32[256,128]{1,0:T(8,128)S(1)} %get-tuple-element.65) | copy-start | bytes 393220
  243.1 3.5 %collective-permute-start.25 = (f32[128,128]{1,0:T(8,128)S(1)}, f32[128,128]{1,0:T(8,128)S(1)}, u32[]{:S(2)}, u32[]{:S(2)}) collective-permute-start(f32[128,128]{1,0:T(8,128)S(1)} %get-tuple-element.54), channel_id=1, source_target_pairs={{0,64},{64,0},{128,192},{192,128},{1,65},{65,1},{129,193},{193,129... | collective-permute-start | bytes 196616 | tf_op jit(solution)/shard_map/ppermute | solution.py:237
  246.7 7.0 %collective-permute-start.29 = (f32[256,128]{1,0:T(8,128)S(1)}, f32[256,128]{1,0:T(8,128)S(1)}, u32[]{:S(2)}, u32[]{:S(2)}) collective-permute-start(f32[256,128]{1,0:T(8,128)S(1)} %pad_maximum_fusion.2.refs_0_), channel_id=1, source_target_pairs={{0,16},{16,0},{32,48},{48,32},{1,17},{17,1},{33,49},{49,33},{2,18}... | collective-permute-start | bytes 393224 | tf_op jit(solution)/shard_map/ppermute | solution.py:237
  251.7 4.7 %collective-permute-start.30 = (f32[256,128]{1,0:T(8,128)S(1)}, f32[256,128]{1,0:T(8,128)S(1)}, u32[]{:S(2)}, u32[]{:S(2)}) collective-permute-start(f32[256,128]{1,0:T(8,128)S(1)} %pad_maximum_fusion.2.refs_0_), channel_id=1, source_target_pairs={{0,32},{16,48},{32,0},{48,16},{1,33},{17,49},{33,1},{49,17},{2,34}... | collective-permute-start | bytes 393224 | tf_op jit(solution)/shard_map/ppermute | solution.py:237
  252.0 7.7 %collective-permute-start.31 = (f32[256,128]{1,0:T(8,128)S(1)}, f32[256,128]{1,0:T(8,128)S(1)}, u32[]{:S(2)}, u32[]{:S(2)}) collective-permute-start(f32[256,128]{1,0:T(8,128)S(1)} %pad_maximum_fusion.2.refs_0_), channel_id=1, source_target_pairs={{0,48},{16,32},{32,16},{48,0},{1,49},{17,33},{33,17},{49,1},{2,50}... | collective-permute-start | bytes 393224 | tf_op jit(solution)/shard_map/ppermute | solution.py:237
  261.0 25.6 %copy-start.14 = (f32[256,128]{1,0:T(8,128)S(1)}, f32[256,128]{1,0:T(8,128)}, u32[]{:S(2)}) copy-start(f32[256,128]{1,0:T(8,128)} %copy-done.13) | copy-start | bytes 393220
  261.0 31.3 %copy-start.9 = (f32[256,128]{1,0:T(8,128)S(1)}, f32[256,128]{1,0:T(8,128)}, u32[]{:S(2)}) copy-start(f32[256,128]{1,0:T(8,128)} %copy-done.8) | copy-start | bytes 393220
  283.0 20.7 %all-to-all-start.9 = ((f32[16,64,128]{2,1,0:T(8,128)}), f32[16,64,128]{2,1,0:T(8,128)S(1)}, u32[]{:S(2)}, u32[]{:S(2)}) async-start(f32[16,64,128]{2,1,0:T(8,128)} %fold.9), calls=%async_computation.9 | async-start | bytes 1048576 | tf_op jit(solution)/shard_map/all_to_all | solution.py:263
  286.6 5.7 %collective-permute-start.35 = (f32[256,128]{1,0:T(8,128)S(1)}, f32[256,128]{1,0:T(8,128)S(1)}, u32[]{:S(2)}, u32[]{:S(2)}) collective-permute-start(f32[256,128]{1,0:T(8,128)S(1)} %copy-done.14), channel_id=1, source_target_pairs={{0,64},{64,0},{128,192},{192,128},{1,65},{65,1},{129,193},{193,129... | collective-permute-start | bytes 393224 | tf_op jit(solution)/shard_map/ppermute | solution.py:237
  288.5 7.0 %collective-permute-start.40 = (f32[256,128]{1,0:T(8,128)S(1)}, f32[256,128]{1,0:T(8,128)S(1)}, u32[]{:S(2)}, u32[]{:S(2)}) collective-permute-start(f32[256,128]{1,0:T(8,128)S(1)} %slice.29), channel_id=1, source_target_pairs={{0,32},{16,48},{32,0},{48,16},{1,33},{17,49},{33,1},{49,17},{2,34}... | collective-permute-start | bytes 393224 | tf_op jit(solution)/shard_map/ppermute | solution.py:237
  288.8 14.8 %collective-permute-start.41 = (f32[256,128]{1,0:T(8,128)S(1)}, f32[256,128]{1,0:T(8,128)S(1)}, u32[]{:S(2)}, u32[]{:S(2)}) collective-permute-start(f32[256,128]{1,0:T(8,128)S(1)} %slice.29), channel_id=1, source_target_pairs={{0,48},{16,32},{32,16},{48,0},{1,49},{17,33},{33,17},{49,1},{2,50}... | collective-permute-start | bytes 393224 | tf_op jit(solution)/shard_map/ppermute | solution.py:237
  292.4 11.3 %collective-permute-start.39 = (f32[256,128]{1,0:T(8,128)S(1)}, f32[256,128]{1,0:T(8,128)S(1)}, u32[]{:S(2)}, u32[]{:S(2)}) collective-permute-start(f32[256,128]{1,0:T(8,128)S(1)} %slice.29), channel_id=1, source_target_pairs={{0,16},{16,0},{32,48},{48,32},{1,17},{17,1},{33,49},{49,33},{2,18}... | collective-permute-start | bytes 393224 | tf_op jit(solution)/shard_map/ppermute | solution.py:237
  292.4 18.5 %collective-permute-start.37 = (f32[256,128]{1,0:T(8,128)S(1)}, f32[256,128]{1,0:T(8,128)S(1)}, u32[]{:S(2)}, u32[]{:S(2)}) collective-permute-start(f32[256,128]{1,0:T(8,128)S(1)} %add.109), channel_id=1, source_target_pairs={{0,32},{16,48},{32,0},{48,16},{1,33},{17,49},{33,1},{49,17},{2,34}... | collective-permute-start | bytes 393224 | tf_op jit(solution)/shard_map/ppermute | solution.py:237
  292.8 18.0 %collective-permute-start.38 = (f32[256,128]{1,0:T(8,128)S(1)}, f32[256,128]{1,0:T(8,128)S(1)}, u32[]{:S(2)}, u32[]{:S(2)}) collective-permute-start(f32[256,128]{1,0:T(8,128)S(1)} %add.109), channel_id=1, source_target_pairs={{0,48},{16,32},{32,16},{48,0},{1,49},{17,33},{33,17},{49,1},{2,50}... | collective-permute-start | bytes 393224 | tf_op jit(solution)/shard_map/ppermute | solution.py:237
  295.4 15.5 %collective-permute-start.36 = (f32[256,128]{1,0:T(8,128)S(1)}, f32[256,128]{1,0:T(8,128)S(1)}, u32[]{:S(2)}, u32[]{:S(2)}) collective-permute-start(f32[256,128]{1,0:T(8,128)S(1)} %add.109), channel_id=1, source_target_pairs={{0,16},{16,0},{32,48},{48,32},{1,17},{17,1},{33,49},{49,33},{2,18}... | collective-permute-start | bytes 393224 | tf_op jit(solution)/shard_map/ppermute | solution.py:237
  306.1 4.8 %collective-permute-start.33 = (f32[256,128]{1,0:T(8,128)S(1)}, f32[256,128]{1,0:T(8,128)S(1)}, u32[]{:S(2)}, u32[]{:S(2)}) collective-permute-start(f32[256,128]{1,0:T(8,128)S(1)} %backward_kernel0.1), channel_id=1, source_target_pairs={{0,32},{16,48},{32,0},{48,16},{1,33},{17,49},{33,1},{49,17},{2,34}... | collective-permute-start | bytes 393224 | tf_op jit(solution)/shard_map/ppermute | solution.py:237
  306.2 10.1 %collective-permute-start.34 = (f32[256,128]{1,0:T(8,128)S(1)}, f32[256,128]{1,0:T(8,128)S(1)}, u32[]{:S(2)}, u32[]{:S(2)}) collective-permute-start(f32[256,128]{1,0:T(8,128)S(1)} %backward_kernel0.1), channel_id=1, source_target_pairs={{0,48},{16,32},{32,16},{48,0},{1,49},{17,33},{33,17},{49,1},{2,50}... | collective-permute-start | bytes 393224 | tf_op jit(solution)/shard_map/ppermute | solution.py:237
  310.9 5.5 %collective-permute-start.32 = (f32[256,128]{1,0:T(8,128)S(1)}, f32[256,128]{1,0:T(8,128)S(1)}, u32[]{:S(2)}, u32[]{:S(2)}) collective-permute-start(f32[256,128]{1,0:T(8,128)S(1)} %backward_kernel0.1), channel_id=1, source_target_pairs={{0,16},{16,0},{32,48},{48,32},{1,17},{17,1},{33,49},{49,33},{2,18}... | collective-permute-start | bytes 393224 | tf_op jit(solution)/shard_map/ppermute | solution.py:237
  (4 other events, 2.9 us)

commit v9 on v7

--- a/solution.py
+++ b/solution.py
@@ -31,11 +31,11 @@
     return jnp.dot(a, b, preferred_element_type=jnp.float32)
 
 
-def hits(seen_ref, place, slots, panels):
+def hits(seen_ref, lists, panels):
     targets = jnp.concatenate(
-        [seen_ref[place, LIST_AT + t : LIST_AT + t + 1, :] for t in slots], axis=1
+        [seen_ref[m, LIST_AT + t : LIST_AT + t + 1, :] for m, t in lists], axis=1
     ).astype(jnp.int32)
-    shape = (panels * C, K * len(slots))
+    shape = (panels * C, K * len(lists))
     rows = lax.broadcasted_iota(jnp.int32, shape, 0)
     return jnp.where(rows == targets, 1.0, 0.0).astype(jnp.bfloat16)
 
@@ -78,7 +78,7 @@
                 own = jnp.concatenate([early, update_refs[m + 1][...]], axis=0)
             high, low = halves(own)
             pair = jnp.concatenate([high, low], axis=1)
-            term = mm(hits(seen_ref, m, SLOTS_OF[level], spans), pair)
+            term = mm(hits(seen_ref, [(m, t) for t in SLOTS_OF[level]], spans), pair)
             total = term if total is None else total + term
         total = total[:, :N] + total[:, N:]
         for a in range(spans):
@@ -135,27 +135,52 @@
     if level == 0:
         out_refs[0][...] = total_ref[0].T
         return
+    picks(seen_ref, total_ref, spans, 0 if level == 1 else 2, out_refs)
+    if level == 2:
+        out_refs[spans][...] = total_ref[...]
+        return
     sub = sub_ref[0] % spans
+    for m in range(spans):
+        out_refs[spans + m][...] = total_ref[m ^ sub].T
+
+
+def picks(seen_ref, total_ref, spans, slot, out_refs):
     pieces = jnp.concatenate([total_ref[a] for a in range(spans)], axis=1)
     high, low = halves(pieces)
     both = jnp.concatenate([high, low], axis=0)
+    for m in range(0, spans, 2):
+        picked = mm(both, hits(seen_ref, [(m, slot), (m + 1, slot)], spans))
+        picked = (picked[:N] + picked[N:]).T
+        out_refs[m][:K, :] = picked[:K]
+        out_refs[m + 1][:K, :] = picked[K:]
+
+
+def rest_kernel(sub_ref, seen_ref, total_ref, *out_refs):
+    spans = 2 ** (LEVELS - 1)
+    picks(seen_ref, total_ref, spans, 1, out_refs)
     for m in range(spans):
-        picked = mm(both, hits(seen_ref, m, SLOTS_OF[level], spans))
-        picked = (picked[:N] + picked[N:]).T
-        own = total_ref[m ^ sub].T
-        soon_ref, later_ref = out_refs[2 * m], out_refs[2 * m + 1]
-        if level == 2:
-            soon_ref[...] = picked[K:]
-            later_ref[:K, :] = picked[:K]
-            later_ref[K:, :] = own
-        else:
-            soon_ref[...] = picked
-            later_ref[...] = own
+        out_refs[m][K:, :] = total_ref[m ^ sub_ref[0]].T
+
+
+def rest(sub, seen, total):
+    vmem = pl.BlockSpec(memory_space=pltpu.VMEM)
+    shape = jax.ShapeDtypeStruct((K + C, N), jnp.float32)
+    return pl.pallas_call(
+        rest_kernel,
+        in_specs=[pl.BlockSpec(memory_space=pltpu.SMEM), vmem, vmem],
+        out_specs=[vmem] * 4,
+        out_shape=[shape] * 4,
+        compiler_params=pltpu.CompilerParams(vmem_limit_bytes=16 * 2**20),
+        name="rest",
+    )(sub, seen, total)
 
 
 def call(kernel, level, heights, scratch, plain, sub, *arrays):
     spans = 2**level
     vmem = pl.BlockSpec(memory_space=pltpu.VMEM)
+    shapes = [(h, N) for h in heights]
+    if len(heights) == 4 and level == 2:
+        shapes.append((spans, N, C))
     limit = FIRST_LIMIT if len(arrays) == 2 else VMEM_LIMIT
     specs = [vmem] * len(arrays)
     for place in [*plain, len(arrays) - 1]:
@@ -163,14 +188,14 @@
     return pl.pallas_call(
         functools.partial(kernel, level),
         in_specs=[pl.BlockSpec(memory_space=pltpu.SMEM)] + specs,
-        out_specs=[vmem] * len(heights),
+        out_specs=[vmem] * len(shapes),
         scratch_shapes=[
             scratch,
             pltpu.VMEM((spans, R, C), jnp.float32),
             pltpu.SemaphoreType.DMA((R // STEP + len(plain),)),
         ]
         + [pltpu.VMEM((rows, N), jnp.float32) for rows in plain.values()],
-        out_shape=[jax.ShapeDtypeStruct((h, N), jnp.float32) for h in heights],
+        out_shape=[jax.ShapeDtypeStruct(shape, jnp.float32) for shape in shapes],
         compiler_params=pltpu.CompilerParams(vmem_limit_bytes=limit),
         cost_estimate=pl.CostEstimate(
             flops=6 * R * spans * C * N, bytes_accessed=4 * R * spans * C, transcendentals=0
@@ -186,7 +211,7 @@
 
 
 def backward(level, sub, seen, residue, diag):
-    heights = {0: [C], 1: [K, C] * 2, 2: [K, K + C] * 4}[level]
+    heights = {0: [C], 1: [K, K, C, C], 2: [K] * 4}[level]
     scratch = pltpu.VMEM((2**level, N, C), jnp.float32)
     plain = {1 + place: R for place in range(len(residue))}
     return call(backward_kernel, level, heights, scratch, plain, sub, seen, *residue, diag)
@@ -302,14 +327,13 @@
     u12 = sub_parts(row_sum(update(2, y1)))
     (y2,) = col_sum(forward(2, sub, seen, [u02] + u12, diag))
 
-    out2 = backward(2, sub, seen, [y2], diag)
-    pick12 = row_parts(sub_sum(out2[0::2]))
-    part1, *later = lax.optimization_barrier([correct((2,), pick12, factor)] + list(out2[1::2]))
-    later = sub_sum(later)
-    out1 = backward(1, sub, seen, [y1, *col_sum(part1)], diag)
-    picked = row_parts(jnp.concatenate([sub_sum(out1[0::2]), later[:K]]))
+    *soon, total = backward(2, sub, seen, [y2], diag)
+    part1, total = col_sum(correct((2,), row_parts(sub_sum(soon)), factor), total)
+    later = sub_sum(rest(sub, seen, total))
+    out1 = backward(1, sub, seen, [y1, part1], diag)
+    picked = row_parts(jnp.concatenate([sub_sum(out1[:2]), later[:K]]))
     part0, x2 = lax.optimization_barrier((correct((0, 1), picked, factor), later[K:]))
-    part0, x2, *later = col_sum(part0, x2, *out1[1::2])
+    part0, x2, *later = col_sum(part0, x2, *out1[2:])
     x2 = row_sum(x2)
     x1 = row_sum(sub_sum(later))
     (x0,) = backward(0, sub, rhs, [y0, part0], diag)

time: 318 us -> 315 us (level)
  starting transfers between devices: 97.4 us -> 94 us
    ppermute x42, starting transfers between devices: 64.2 us -> 60 us  [swapped(): return lax.ppermute(value, axis, pairs)]
  transfers between devices with their start and end apart: 48 -> 48, of which waited for: 24 -> 28; matrix products, arithmetic and copies ran while one was open for 2% -> 2% of each run, Pallas kernels for 2% -> 2%
where the time goes in v9:
time: 315 us; the launch traced here: 314 us
  waiting for transfers between devices  102 us (32%)
  starting transfers between devices  94 us (30%)
  blocking collectives  78.7 us (25%)
  Pallas kernels  24.2 us (8%)
  other arithmetic  6.57 us (2%)
  local copies, waits for them, and re-layouts  5.1 us (2%)
    ppermute x42, starting transfers between devices, swapped(): return lax.ppermute(value, axis, pairs)  60 us
    all_to_all x3, blocking collectives, col_sum(): lax.all_to_all(blocks, 'col', 0, 0)  59.4 us
    ppermute x42, waiting for transfers between devices, swapped(): return lax.ppermute(value, axis, pairs)  45.3 us
    all_to_all x4, waiting for transfers between devices, col_sum(): full = lax.all_to_all(own, 'col', 0, 0).reshape(part.shape)  32.5 us
    all_to_all x2, waiting for transfers between devices, col_sum(): lax.all_to_all(blocks, 'col', 0, 0)  24.1 us
    all_to_all x1, blocking collectives, col_sum(): full = lax.all_to_all(own, 'col', 0, 0).reshape(part.shape)  19.3 us
    all_to_all x4, starting transfers between devices, col_sum(): full = lax.all_to_all(own, 'col', 0, 0).reshape(part.shape)  18.2 us
    pallas_call x6, Pallas kernels, call(): pl.pallas_call(functools.partial(kernel, level), in_specs=[pl.BlockSpec(m...  17.5 us
  transfers between devices with their start and end apart: 48, of which 28 were waited for; matrix products, arithmetic and copies ran while one was open for 2% of the time, Pallas kernels for 2%

profile of v9, /device:TPU:1, one launch (start us, length us, event | category | flops | bytes accessed | tf_op | source)
XLA Modules:
  0.0 313.8 jit_solution(1013608352828394575)
XLA Ops:
  0.0 2.8 forward_kernel0.1
  2.9 11.6 %all-to-all-start = ((f32[16,64,128]{2,1,0:T(8,128)}), f32[16,64,128]{2,1,0:T(8,128)S(1)}, u32[]{:S(2)}, u32[]{:S(2)}) async-start(f32[16,64,128]{2,1,0:T(8,128)} %bitcast.84), calls=%async_computation | async-start | bytes 1048576 | tf_op jit(solution)/shard_map/all_to_all | solution.py:280
  14.8 16.9 %all-to-all-done.parts_ref = f32[16,64,128]{2,1,0:T(8,128)S(1)} async-done(((f32[16,64,128]{2,1,0:T(8,128)}), f32[16,64,128]{2,1,0:T(8,128)S(1)}, u32[]{:S(2)}, u32[]{:S(2)}) %all-to-all-start) | async-done | bytes 524320 | tf_op jit(solution)/shard_map/all_to_all | solution.py:280
  32.5 4.7 %all-to-all-start.1 = ((f32[16,64,128]{2,1,0:T(8,128)}), f32[16,64,128]{2,1,0:T(8,128)S(1)}, u32[]{:S(2)}, u32[]{:S(2)}) async-start(f32[16,64,128]{2,1,0:T(8,128)} %fold.5), calls=%async_computation.1 | async-start | bytes 1048576 | tf_op jit(solution)/shard_map/all_to_all | solution.py:281
  37.3 2.8 collective-permute-start.2
  40.8 13.8 %all-to-all-done.1 = f32[16,64,128]{2,1,0:T(8,128)S(1)} async-done(((f32[16,64,128]{2,1,0:T(8,128)}), f32[16,64,128]{2,1,0:T(8,128)S(1)}, u32[]{:S(2)}, u32[]{:S(2)}) %all-to-all-start.1) | async-done | bytes 524320 | tf_op jit(solution)/shard_map/all_to_all | solution.py:281
  55.0 2.6 collective-permute-start.5
  57.6 1.2 collective-permute-start.4
  59.7 1.3 pad_maximum_fusion.seen_ref
  61.0 1.1 collective-permute-done.4
  62.1 1.4 collective-permute-start.6
  65.3 2.3 forward_kernel1.1
  68.4 4.2 %all-to-all-start.2 = ((f32[16,64,128]{2,1,0:T(8,128)}), f32[16,64,128]{2,1,0:T(8,128)}, u32[]{:S(2)}, u32[]{:S(2)}) async-start(f32[16,64,128]{2,1,0:T(8,128)} %bitcast.73), calls=%async_computation.2 | async-start | bytes 1048576 | tf_op jit(solution)/shard_map/all_to_all | solution.py:280
  72.6 2.5 collective-permute-start.9
  75.7 3.2 %collective-permute-done.9 = f32[128,128]{1,0:T(8,128)S(1)} collective-permute-done((f32[128,128]{1,0:T(8,128)}, f32[128,128]{1,0:T(8,128)S(1)}, u32[]{:S(2)}, u32[]{:S(2)}) %collective-permute-start.9) | collective-permute-done | bytes 65568 | tf_op jit(solution)/shard_map/ppermute | solution.py:255
  78.9 1.8 collective-permute-done.8
  80.7 1.5 add_add_fusion.3
  82.2 7.2 %all-to-all-done.2.parts_ref = f32[16,64,128]{2,1,0:T(8,128)} async-done(((f32[16,64,128]{2,1,0:T(8,128)}), f32[16,64,128]{2,1,0:T(8,128)}, u32[]{:S(2)}, u32[]{:S(2)}) %all-to-all-start.2) | async-done | bytes 524320 | tf_op jit(solution)/shard_map/all_to_all | solution.py:280
  91.3 4.5 %all-to-all-start.3 = ((f32[16,64,128]{2,1,0:T(8,128)}), f32[16,64,128]{2,1,0:T(8,128)}, u32[]{:S(2)}, u32[]{:S(2)}) async-start(f32[16,64,128]{2,1,0:T(8,128)} %copy-done.3), calls=%async_computation.3 | async-start | bytes 1048576 | tf_op jit(solution)/shard_map/all_to_all | solution.py:281
  95.8 2.8 collective-permute-start.12
  99.3 1.6 collective-permute-done.12
  100.9 2.6 collective-permute-done.11
  103.4 1.6 pad_maximum_fusion.1.refs_0_
  105.0 5.7 %all-to-all-done.3 = f32[16,64,128]{2,1,0:T(8,128)} async-done(((f32[16,64,128]{2,1,0:T(8,128)}), f32[16,64,128]{2,1,0:T(8,128)}, u32[]{:S(2)}, u32[]{:S(2)}) %all-to-all-start.3) | async-done | bytes 524320 | tf_op jit(solution)/shard_map/all_to_all | solution.py:281
  110.7 1.5 convolution_bitcast_fusion
  112.1 5.9 %collective-permute-start.15 = (f32[128,128]{1,0:T(8,128)S(1)}, f32[128,128]{1,0:T(8,128)S(1)}, u32[]{:S(2)}, u32[]{:S(2)}) collective-permute-start(f32[128,128]{1,0:T(8,128)S(1)} %convolution_bitcast_fusion), channel_id=1, source_target_pairs={{0,48},{16,32},{32,16},{48,0},{1,49},{17,33},{33,17},{49,1},{2,50}... | collective-permute-start | bytes 196616 | tf_op jit(solution)/shard_map/ppermute | solution.py:255
  118.5 2.3 collective-permute-done.15
  120.8 1.4 collective-permute-done.14
  122.2 2.8 collective-permute-start.18
  126.7 3.0 collective-permute-done.17.refs_3_
  129.7 3.1 forward_kernel2.1
  132.8 18.4 %all_to_all.50.parts_ref = f32[16,64,128]{2,1,0:T(8,128)S(1)} all-to-all(f32[16,64,128]{2,1,0:T(8,128)S(1)} %bitcast.75), channel_id=1, replica_groups=mesh['sub'=4,'row'=4,'col'=16] {'col'}, dimensions={0} | all-to-all | bytes 1048576 | tf_op jit(solution)/shard_map/all_to_all | solution.py:280
  151.2 19.3 %all_to_all.51 = f32[16,64,128]{2,1,0:T(8,128)S(1)} all-to-all(f32[16,64,128]{2,1,0:T(8,128)S(1)} %fold.7), channel_id=1, replica_groups=mesh['sub'=4,'row'=4,'col'=16] {'col'}, dimensions={0} | all-to-all | bytes 1048576 | tf_op jit(solution)/shard_map/all_to_all | solution.py:281
  170.5 3.7 %backward_kernel2.1 = (f32[128,128]{1,0:T(8,128)S(1)}, f32[128,128]{1,0:T(8,128)S(1)}, f32[128,128]{1,0:T(8,128)S(1)}, f32[128,128]{1,0:T(8,128)S(1)}, f32[4,128,256]{2,1,0:T(8,128)S(1)}) custom-call(s32[1]{0:T(128)} %bitcast.sub_ref, f32[4,520,128]{2,1,0:T(8,128)S(1)} %pad_maximum_fusion.seen_ref, f32[1024,128]{1,0:T(8,128)S(1)} %bitcast.74, ...), custom_call_target="tpu_custom_call" | custom-call | flops 805306368 | bytes 4194304 | tf_op jit(solution)/shard_map/backward_kernel2/pallas_call | solution.py:188
  174.5 4.5 %collective-permute-start.20 = (f32[128,128]{1,0:T(8,128)S(1)}, f32[128,128]{1,0:T(8,128)S(1)}, u32[]{:S(2)}, u32[]{:S(2)}) collective-permute-start(f32[128,128]{1,0:T(8,128)S(1)} %get-tuple-element.44), channel_id=1, source_target_pairs={{0,128},{64,192},{128,0},{192,64},{1,129},{65,193},{129,1},{193,65... | collective-permute-start | bytes 196616 | tf_op jit(solution)/shard_map/ppermute | solution.py:255
  179.2 2.1 collective-permute-done.20
  181.3 2.0 collective-permute-done.21
  183.3 6.1 %collective-permute-start.24 = (f32[128,128]{1,0:T(8,128)S(1)}, f32[128,128]{1,0:T(8,128)S(1)}, u32[]{:S(2)}, u32[]{:S(2)}) collective-permute-start(f32[128,128]{1,0:T(8,128)S(1)} %add_add_fusion.1.refs_0_), channel_id=1, source_target_pairs={{0,48},{16,32},{32,16},{48,0},{1,49},{17,33},{33,17},{49,1},{2,50}... | collective-permute-start | bytes 196616 | tf_op jit(solution)/shard_map/ppermute | solution.py:255
  190.1 1.8 collective-permute-done.24.refs_3_
  191.9 1.5 collective-permute-done.23.refs_2_
  194.5 20.2 %all_to_all.52.parts_ref = f32[16,64,128]{2,1,0:T(8,128)S(1)} all-to-all(f32[16,64,128]{2,1,0:T(8,128)S(1)} %bitcast.77), channel_id=1, replica_groups=mesh['sub'=4,'row'=4,'col'=16] {'col'}, dimensions={0} | all-to-all | bytes 1048576 | tf_op jit(solution)/shard_map/all_to_all | solution.py:280
  215.6 4.5 %all-to-all-start.7 = ((f32[16,64,128]{2,1,0:T(8,128)}), f32[16,64,128]{2,1,0:T(8,128)}, u32[]{:S(2)}, u32[]{:S(2)}) async-start(f32[16,64,128]{2,1,0:T(8,128)} %copy-done.4), calls=%async_computation.7 | async-start | bytes 1048576 | tf_op jit(solution)/shard_map/all_to_all | solution.py:281
  221.2 1.3 rest.1
  223.2 1.8 collective-permute-start.27
  225.0 2.1 collective-permute-start.28
  227.1 9.1 %all-to-all-done.7 = f32[16,64,128]{2,1,0:T(8,128)} async-done(((f32[16,64,128]{2,1,0:T(8,128)}), f32[16,64,128]{2,1,0:T(8,128)}, u32[]{:S(2)}, u32[]{:S(2)}) %all-to-all-start.7) | async-done | bytes 524320 | tf_op jit(solution)/shard_map/all_to_all | solution.py:281
  236.2 3.2 %backward_kernel1.1 = (f32[128,128]{1,0:T(8,128)S(1)}, f32[128,128]{1,0:T(8,128)S(1)}, f32[256,128]{1,0:T(8,128)S(1)}, f32[256,128]{1,0:T(8,128)S(1)}) custom-call(s32[1]{0:T(128)} %bitcast.sub_ref, f32[4,520,128]{2,1,0:T(8,128)S(1)} %pad_maximum_fusion.seen_ref, f32[1024,128]{1,0:T(8,128)} %bitcast.17.base_ref, f32[1024,128]{1,0:T(8,128)} %bitcast.24.refs_0_, ...), custom_call_target="tpu_custom_call" | custom-call | flops 402653184 | bytes 2097152 | tf_op jit(solution)/shard_map/backward_kernel1/pallas_call | solution.py:188
  239.6 1.2 add_add_fusion
  240.7 1.9 collective-permute-done.25
  242.7 5.6 %collective-permute-start.31 = (f32[256,128]{1,0:T(8,128)S(1)}, f32[256,128]{1,0:T(8,128)S(1)}, u32[]{:S(2)}, u32[]{:S(2)}) collective-permute-start(f32[256,128]{1,0:T(8,128)S(1)} %pad_maximum_fusion.2.refs_0_), channel_id=1, source_target_pairs={{0,48},{16,32},{32,16},{48,0},{1,49},{17,33},{33,17},{49,1},{2,50}... | collective-permute-start | bytes 393224 | tf_op jit(solution)/shard_map/ppermute | solution.py:255
  248.2 1.2 collective-permute-start.30
  249.4 2.3 collective-permute-done.31.refs_3_
  251.7 3.4 %collective-permute-done.30.refs_2_ = f32[256,128]{1,0:T(8,128)S(1)} collective-permute-done((f32[256,128]{1,0:T(8,128)S(1)}, f32[256,128]{1,0:T(8,128)S(1)}, u32[]{:S(2)}, u32[]{:S(2)}) %collective-permute-start.30) | collective-permute-done | bytes 131104 | tf_op jit(solution)/shard_map/ppermute | solution.py:255
  255.1 1.3 correct2.1
  256.4 20.8 %all_to_all.53.parts_ref = f32[16,64,128]{2,1,0:T(8,128)S(1)} all-to-all(f32[16,64,128]{2,1,0:T(8,128)S(1)} %bitcast.76), channel_id=1, replica_groups=mesh['sub'=4,'row'=4,'col'=16] {'col'}, dimensions={0} | all-to-all | bytes 1048576 | tf_op jit(solution)/shard_map/all_to_all | solution.py:280
  278.1 4.5 %all-to-all-start.9 = ((f32[16,64,128]{2,1,0:T(8,128)}), f32[16,64,128]{2,1,0:T(8,128)S(1)}, u32[]{:S(2)}, u32[]{:S(2)}) async-start(f32[16,64,128]{2,1,0:T(8,128)} %fold.9), calls=%async_computation.9 | async-start | bytes 1048576 | tf_op jit(solution)/shard_map/all_to_all | solution.py:281
  282.7 2.9 collective-permute-start.41
  286.5 4.0 %collective-permute-start.38 = (f32[256,128]{1,0:T(8,128)S(1)}, f32[256,128]{1,0:T(8,128)S(1)}, u32[]{:S(2)}, u32[]{:S(2)}) collective-permute-start(f32[256,128]{1,0:T(8,128)S(1)} %add.109), channel_id=1, source_target_pairs={{0,48},{16,32},{32,16},{48,0},{1,49},{17,33},{33,17},{49,1},{2,50}... | collective-permute-start | bytes 393224 | tf_op jit(solution)/shard_map/ppermute | solution.py:255
  291.6 3.7 %collective-permute-done.40 = f32[256,128]{1,0:T(8,128)S(1)} collective-permute-done((f32[256,128]{1,0:T(8,128)S(1)}, f32[256,128]{1,0:T(8,128)S(1)}, u32[]{:S(2)}, u32[]{:S(2)}) %collective-permute-start.40) | collective-permute-done | bytes 131104 | tf_op jit(solution)/shard_map/ppermute | solution.py:255
  295.4 3.9 %all-to-all-done.9 = f32[16,64,128]{2,1,0:T(8,128)S(1)} async-done(((f32[16,64,128]{2,1,0:T(8,128)}), f32[16,64,128]{2,1,0:T(8,128)S(1)}, u32[]{:S(2)}, u32[]{:S(2)}) %all-to-all-start.9) | async-done | bytes 524320 | tf_op jit(solution)/shard_map/all_to_all | solution.py:281
  299.3 2.4 backward_kernel0.1
  301.8 4.2 %collective-permute-start.34 = (f32[256,128]{1,0:T(8,128)S(1)}, f32[256,128]{1,0:T(8,128)S(1)}, u32[]{:S(2)}, u32[]{:S(2)}) collective-permute-start(f32[256,128]{1,0:T(8,128)S(1)} %backward_kernel0.1), channel_id=1, source_target_pairs={{0,48},{16,32},{32,16},{48,0},{1,49},{17,33},{33,17},{49,1},{2,50}... | collective-permute-start | bytes 393224 | tf_op jit(solution)/shard_map/ppermute | solution.py:255
  306.5 3.7 %collective-permute-done.34 = f32[256,128]{1,0:T(8,128)S(1)} collective-permute-done((f32[256,128]{1,0:T(8,128)S(1)}, f32[256,128]{1,0:T(8,128)S(1)}, u32[]{:S(2)}, u32[]{:S(2)}) %collective-permute-start.34) | collective-permute-done | bytes 131104 | tf_op jit(solution)/shard_map/ppermute | solution.py:255
  310.1 2.8 collective-permute-done.33
  (112 shorter events, 20.4 us)
Async XLA Ops:
  0.0 14.4 %copy-start.1 = (f32[3,1,256,128]{3,2,1,0:T(8,128)S(1)}, f32[3,1,256,128]{3,2,1,0:T(8,128)}, u32[]{:S(2)}) copy-start(f32[3,1,256,128]{3,2,1,0:T(8,128)} %param.4) | copy-start | bytes 1179652
  2.8 11.7 %copy-start.18 = (s32[3,1,128]{2,1,0:T(1,128)S(1)}, s32[3,1,128]{2,1,0:T(1,128)}, u32[]{:S(2)}) copy-start(s32[3,1,128]{2,1,0:T(1,128)} %param.7) | copy-start | bytes 4612
  2.9 28.8 %all-to-all-start = ((f32[16,64,128]{2,1,0:T(8,128)}), f32[16,64,128]{2,1,0:T(8,128)S(1)}, u32[]{:S(2)}, u32[]{:S(2)}) async-start(f32[16,64,128]{2,1,0:T(8,128)} %bitcast.84), calls=%async_computation | async-start | bytes 1048576 | tf_op jit(solution)/shard_map/all_to_all | solution.py:280
  14.5 40.1 %copy-start = (f32[3,1,128,1024]{3,2,1,0:T(8,128)S(1)}, f32[3,1,128,1024]{3,2,1,0:T(8,128)}, u32[]{:S(2)}) copy-start(f32[3,1,128,1024]{3,2,1,0:T(8,128)} %param.6) | copy-start | bytes 4718596
  14.7 40.2 %copy-start.14 = (f32[520,128]{1,0:T(8,128)}, f32[520,128]{1,0:T(8,128)S(1)}, u32[]{:S(2)}) copy-start(f32[520,128]{1,0:T(8,128)S(1)} %maximum_maximum_fusion) | copy-start | bytes 798724
  32.5 22.0 %all-to-all-start.1 = ((f32[16,64,128]{2,1,0:T(8,128)}), f32[16,64,128]{2,1,0:T(8,128)S(1)}, u32[]{:S(2)}, u32[]{:S(2)}) async-start(f32[16,64,128]{2,1,0:T(8,128)} %fold.5), calls=%async_computation.1 | async-start | bytes 1048576 | tf_op jit(solution)/shard_map/all_to_all | solution.py:281
  37.3 21.5 %collective-permute-start.2 = (f32[520,128]{1,0:T(8,128)S(1)}, f32[520,128]{1,0:T(8,128)S(1)}, u32[]{:S(2)}, u32[]{:S(2)}) collective-permute-start(f32[520,128]{1,0:T(8,128)S(1)} %maximum_maximum_fusion), channel_id=1, source_target_pairs={{0,192},{64,128},{128,64},{192,0},{1,193},{65,129},{129,65},{193,1... | collective-permute-start | bytes 798728 | tf_op jit(solution)/shard_map/ppermute | solution.py:255
  40.1 18.7 %collective-permute-start.1 = (f32[520,128]{1,0:T(8,128)S(1)}, f32[520,128]{1,0:T(8,128)S(1)}, u32[]{:S(2)}, u32[]{:S(2)}) collective-permute-start(f32[520,128]{1,0:T(8,128)S(1)} %maximum_maximum_fusion), channel_id=1, source_target_pairs={{0,128},{64,192},{128,0},{192,64},{1,129},{65,193},{129,1},{193,65... | collective-permute-start | bytes 798728 | tf_op jit(solution)/shard_map/ppermute | solution.py:255
  40.4 18.4 %collective-permute-start = (f32[520,128]{1,0:T(8,128)S(1)}, f32[520,128]{1,0:T(8,128)S(1)}, u32[]{:S(2)}, u32[]{:S(2)}) collective-permute-start(f32[520,128]{1,0:T(8,128)S(1)} %maximum_maximum_fusion), channel_id=1, source_target_pairs={{0,64},{64,0},{128,192},{192,128},{1,65},{65,1},{129,193},{193,129... | collective-permute-start | bytes 798728 | tf_op jit(solution)/shard_map/ppermute | solution.py:255
  55.0 6.0 %collective-permute-start.5 = (f32[128,128]{1,0:T(8,128)S(1)}, f32[128,128]{1,0:T(8,128)S(1)}, u32[]{:S(2)}, u32[]{:S(2)}) collective-permute-start(f32[128,128]{1,0:T(8,128)S(1)} %convolution_bitcast_fusion.2), channel_id=1, source_target_pairs={{0,48},{16,32},{32,16},{48,0},{1,49},{17,33},{33,17},{49,1},{2,50}... | collective-permute-start | bytes 196616 | tf_op jit(solution)/shard_map/ppermute | solution.py:255
  57.6 4.5 %collective-permute-start.4 = (f32[128,128]{1,0:T(8,128)S(1)}, f32[128,128]{1,0:T(8,128)S(1)}, u32[]{:S(2)}, u32[]{:S(2)}) collective-permute-start(f32[128,128]{1,0:T(8,128)S(1)} %convolution_bitcast_fusion.2), channel_id=1, source_target_pairs={{0,32},{16,48},{32,0},{48,16},{1,33},{17,49},{33,1},{49,17},{2,34}... | collective-permute-start | bytes 196616 | tf_op jit(solution)/shard_map/ppermute | solution.py:255
  58.8 3.3 %collective-permute-start.3 = (f32[128,128]{1,0:T(8,128)S(1)}, f32[128,128]{1,0:T(8,128)S(1)}, u32[]{:S(2)}, u32[]{:S(2)}) collective-permute-start(f32[128,128]{1,0:T(8,128)S(1)} %convolution_bitcast_fusion.2), channel_id=1, source_target_pairs={{0,16},{16,0},{32,48},{48,32},{1,17},{17,1},{33,49},{49,33},{2,18}... | collective-permute-start | bytes 196616 | tf_op jit(solution)/shard_map/ppermute | solution.py:255
  58.8 0.9 copy-start.17
  62.1 3.2 %collective-permute-start.6 = (f32[128,128]{1,0:T(8,128)S(1)}, f32[128,128]{1,0:T(8,128)S(1)}, u32[]{:S(2)}, u32[]{:S(2)}) collective-permute-start(f32[128,128]{1,0:T(8,128)S(1)} %add_add_fusion.4.refs_0_), channel_id=1, source_target_pairs={{0,64},{64,0},{128,192},{192,128},{1,65},{65,1},{129,193},{193,129... | collective-permute-start | bytes 196616 | tf_op jit(solution)/shard_map/ppermute | solution.py:255
  67.6 0.8 copy-start.2
  68.4 21.0 %all-to-all-start.2 = ((f32[16,64,128]{2,1,0:T(8,128)}), f32[16,64,128]{2,1,0:T(8,128)}, u32[]{:S(2)}, u32[]{:S(2)}) async-start(f32[16,64,128]{2,1,0:T(8,128)} %bitcast.73), calls=%async_computation.2 | async-start | bytes 1048576 | tf_op jit(solution)/shard_map/all_to_all | solution.py:280
  72.6 6.2 %collective-permute-start.9 = (f32[128,128]{1,0:T(8,128)}, f32[128,128]{1,0:T(8,128)S(1)}, u32[]{:S(2)}, u32[]{:S(2)}) collective-permute-start(f32[128,128]{1,0:T(8,128)} %convolution_bitcast_fusion.1), channel_id=1, source_target_pairs={{0,48},{16,32},{32,16},{48,0},{1,49},{17,33},{33,17},{49,1},{2,50}... | collective-permute-start | bytes 196616 | tf_op jit(solution)/shard_map/ppermute | solution.py:255
  75.2 5.6 %collective-permute-start.8 = (f32[128,128]{1,0:T(8,128)}, f32[128,128]{1,0:T(8,128)S(1)}, u32[]{:S(2)}, u32[]{:S(2)}) collective-permute-start(f32[128,128]{1,0:T(8,128)} %convolution_bitcast_fusion.1), channel_id=1, source_target_pairs={{0,32},{16,48},{32,0},{48,16},{1,33},{17,49},{33,1},{49,17},{2,34}... | collective-permute-start | bytes 196616 | tf_op jit(solution)/shard_map/ppermute | solution.py:255
  75.6 5.1 %collective-permute-start.7 = (f32[128,128]{1,0:T(8,128)}, f32[128,128]{1,0:T(8,128)S(1)}, u32[]{:S(2)}, u32[]{:S(2)}) collective-permute-start(f32[128,128]{1,0:T(8,128)} %convolution_bitcast_fusion.1), channel_id=1, source_target_pairs={{0,16},{16,0},{32,48},{48,32},{1,17},{17,1},{33,49},{49,33},{2,18}... | collective-permute-start | bytes 196616 | tf_op jit(solution)/shard_map/ppermute | solution.py:255
  90.5 0.8 copy-start.3
  91.3 19.4 %all-to-all-start.3 = ((f32[16,64,128]{2,1,0:T(8,128)}), f32[16,64,128]{2,1,0:T(8,128)}, u32[]{:S(2)}, u32[]{:S(2)}) async-start(f32[16,64,128]{2,1,0:T(8,128)} %copy-done.3), calls=%async_computation.3 | async-start | bytes 1048576 | tf_op jit(solution)/shard_map/all_to_all | solution.py:281
  95.8 5.1 %collective-permute-start.12 = (f32[128,128]{1,0:T(8,128)}, f32[128,128]{1,0:T(8,128)S(1)}, u32[]{:S(2)}, u32[]{:S(2)}) collective-permute-start(f32[128,128]{1,0:T(8,128)} %add_add_fusion.3), channel_id=1, source_target_pairs={{0,192},{64,128},{128,64},{192,0},{1,193},{65,129},{129,65},{193,1... | collective-permute-start | bytes 196616 | tf_op jit(solution)/shard_map/ppermute | solution.py:255
  98.6 4.8 %collective-permute-start.11 = (f32[128,128]{1,0:T(8,128)}, f32[128,128]{1,0:T(8,128)S(1)}, u32[]{:S(2)}, u32[]{:S(2)}) collective-permute-start(f32[128,128]{1,0:T(8,128)} %add_add_fusion.3), channel_id=1, source_target_pairs={{0,128},{64,192},{128,0},{192,64},{1,129},{65,193},{129,1},{193,65... | collective-permute-start | bytes 196616 | tf_op jit(solution)/shard_map/ppermute | solution.py:255
  99.0 4.5 %collective-permute-start.10 = (f32[128,128]{1,0:T(8,128)}, f32[128,128]{1,0:T(8,128)S(1)}, u32[]{:S(2)}, u32[]{:S(2)}) collective-permute-start(f32[128,128]{1,0:T(8,128)} %add_add_fusion.3), channel_id=1, source_target_pairs={{0,64},{64,0},{128,192},{192,128},{1,65},{65,1},{129,193},{193,129... | collective-permute-start | bytes 196616 | tf_op jit(solution)/shard_map/ppermute | solution.py:255
  110.7 19.0 %copy-start.5 = (f32[512,128]{1,0:T(8,128)S(1)}, f32[512,128]{1,0:T(8,128)}, u32[]{:S(2)}) copy-start(f32[512,128]{1,0:T(8,128)} %pad_maximum_fusion.1.refs_0_) | copy-start | bytes 786436
  112.1 8.7 %collective-permute-start.15 = (f32[128,128]{1,0:T(8,128)S(1)}, f32[128,128]{1,0:T(8,128)S(1)}, u32[]{:S(2)}, u32[]{:S(2)}) collective-permute-start(f32[128,128]{1,0:T(8,128)S(1)} %convolution_bitcast_fusion), channel_id=1, source_target_pairs={{0,48},{16,32},{32,16},{48,0},{1,49},{17,33},{33,17},{49,1},{2,50}... | collective-permute-start | bytes 196616 | tf_op jit(solution)/shard_map/ppermute | solution.py:255
  118.0 4.2 %collective-permute-start.14 = (f32[128,128]{1,0:T(8,128)S(1)}, f32[128,128]{1,0:T(8,128)S(1)}, u32[]{:S(2)}, u32[]{:S(2)}) collective-permute-start(f32[128,128]{1,0:T(8,128)S(1)} %convolution_bitcast_fusion), channel_id=1, source_target_pairs={{0,32},{16,48},{32,0},{48,16},{1,33},{17,49},{33,1},{49,17},{2,34}... | collective-permute-start | bytes 196616 | tf_op jit(solution)/shard_map/ppermute | solution.py:255
  118.4 3.8 %collective-permute-start.13 = (f32[128,128]{1,0:T(8,128)S(1)}, f32[128,128]{1,0:T(8,128)S(1)}, u32[]{:S(2)}, u32[]{:S(2)}) collective-permute-start(f32[128,128]{1,0:T(8,128)S(1)} %convolution_bitcast_fusion), channel_id=1, source_target_pairs={{0,16},{16,0},{32,48},{48,32},{1,17},{17,1},{33,49},{49,33},{2,18}... | collective-permute-start | bytes 196616 | tf_op jit(solution)/shard_map/ppermute | solution.py:255
  122.2 4.5 %collective-permute-start.18 = (f32[128,128]{1,0:T(8,128)S(1)}, f32[128,128]{1,0:T(8,128)S(1)}, u32[]{:S(2)}, u32[]{:S(2)}) collective-permute-start(f32[128,128]{1,0:T(8,128)S(1)} %add_add_fusion.2.refs_1_), channel_id=1, source_target_pairs={{0,192},{64,128},{128,64},{192,0},{1,193},{65,129},{129,65},{193,1... | collective-permute-start | bytes 196616 | tf_op jit(solution)/shard_map/ppermute | solution.py:255
  125.0 4.6 %collective-permute-start.17 = (f32[128,128]{1,0:T(8,128)S(1)}, f32[128,128]{1,0:T(8,128)S(1)}, u32[]{:S(2)}, u32[]{:S(2)}) collective-permute-start(f32[128,128]{1,0:T(8,128)S(1)} %add_add_fusion.2.refs_1_), channel_id=1, source_target_pairs={{0,128},{64,192},{128,0},{192,64},{1,129},{65,193},{129,1},{193,65... | collective-permute-start | bytes 196616 | tf_op jit(solution)/shard_map/ppermute | solution.py:255
  125.4 4.3 %collective-permute-start.16 = (f32[128,128]{1,0:T(8,128)S(1)}, f32[128,128]{1,0:T(8,128)S(1)}, u32[]{:S(2)}, u32[]{:S(2)}) collective-permute-start(f32[128,128]{1,0:T(8,128)S(1)} %add_add_fusion.2.refs_1_), channel_id=1, source_target_pairs={{0,64},{64,0},{128,192},{192,128},{1,65},{65,1},{129,193},{193,129... | collective-permute-start | bytes 196616 | tf_op jit(solution)/shard_map/ppermute | solution.py:255
  174.2 40.6 %copy-start.6 = (f32[4,128,256]{2,1,0:T(8,128)}, f32[4,128,256]{2,1,0:T(8,128)S(1)}, u32[]{:S(2)}) copy-start(f32[4,128,256]{2,1,0:T(8,128)S(1)} %get-tuple-element.50.total_ref) | copy-start | bytes 1572868
  174.2 5.0 %collective-permute-start.19 = (f32[128,128]{1,0:T(8,128)S(1)}, f32[128,128]{1,0:T(8,128)S(1)}, u32[]{:S(2)}, u32[]{:S(2)}) collective-permute-start(f32[128,128]{1,0:T(8,128)S(1)} %get-tuple-element.43), channel_id=1, source_target_pairs={{0,64},{64,0},{128,192},{192,128},{1,65},{65,1},{129,193},{193,129... | collective-permute-start | bytes 196616 | tf_op jit(solution)/shard_map/ppermute | solution.py:255
  174.5 6.8 %collective-permute-start.20 = (f32[128,128]{1,0:T(8,128)S(1)}, f32[128,128]{1,0:T(8,128)S(1)}, u32[]{:S(2)}, u32[]{:S(2)}) collective-permute-start(f32[128,128]{1,0:T(8,128)S(1)} %get-tuple-element.44), channel_id=1, source_target_pairs={{0,128},{64,192},{128,0},{192,64},{1,129},{65,193},{129,1},{193,65... | collective-permute-start | bytes 196616 | tf_op jit(solution)/shard_map/ppermute | solution.py:255
  179.0 4.3 %collective-permute-start.21 = (f32[128,128]{1,0:T(8,128)S(1)}, f32[128,128]{1,0:T(8,128)S(1)}, u32[]{:S(2)}, u32[]{:S(2)}) collective-permute-start(f32[128,128]{1,0:T(8,128)S(1)} %get-tuple-element.45), channel_id=1, source_target_pairs={{0,192},{64,128},{128,64},{192,0},{1,193},{65,129},{129,65},{193,1... | collective-permute-start | bytes 196616 | tf_op jit(solution)/shard_map/ppermute | solution.py:255
  183.3 8.6 %collective-permute-start.24 = (f32[128,128]{1,0:T(8,128)S(1)}, f32[128,128]{1,0:T(8,128)S(1)}, u32[]{:S(2)}, u32[]{:S(2)}) collective-permute-start(f32[128,128]{1,0:T(8,128)S(1)} %add_add_fusion.1.refs_0_), channel_id=1, source_target_pairs={{0,48},{16,32},{32,16},{48,0},{1,49},{17,33},{33,17},{49,1},{2,50}... | collective-permute-start | bytes 196616 | tf_op jit(solution)/shard_map/ppermute | solution.py:255
  189.4 4.1 %collective-permute-start.23 = (f32[128,128]{1,0:T(8,128)S(1)}, f32[128,128]{1,0:T(8,128)S(1)}, u32[]{:S(2)}, u32[]{:S(2)}) collective-permute-start(f32[128,128]{1,0:T(8,128)S(1)} %add_add_fusion.1.refs_0_), channel_id=1, source_target_pairs={{0,32},{16,48},{32,0},{48,16},{1,33},{17,49},{33,1},{49,17},{2,34}... | collective-permute-start | bytes 196616 | tf_op jit(solution)/shard_map/ppermute | solution.py:255
  190.1 3.3 %collective-permute-start.22 = (f32[128,128]{1,0:T(8,128)S(1)}, f32[128,128]{1,0:T(8,128)S(1)}, u32[]{:S(2)}, u32[]{:S(2)}) collective-permute-start(f32[128,128]{1,0:T(8,128)S(1)} %add_add_fusion.1.refs_0_), channel_id=1, source_target_pairs={{0,16},{16,0},{32,48},{48,32},{1,17},{17,1},{33,49},{49,33},{2,18}... | collective-permute-start | bytes 196616 | tf_op jit(solution)/shard_map/ppermute | solution.py:255
  214.8 0.8 copy-start.4
  215.6 20.6 %all-to-all-start.7 = ((f32[16,64,128]{2,1,0:T(8,128)}), f32[16,64,128]{2,1,0:T(8,128)}, u32[]{:S(2)}, u32[]{:S(2)}) async-start(f32[16,64,128]{2,1,0:T(8,128)} %copy-done.4), calls=%async_computation.7 | async-start | bytes 1048576 | tf_op jit(solution)/shard_map/all_to_all | solution.py:281
  220.2 1.0 copy-start.7
  223.2 16.3 %collective-permute-start.26 = (f32[384,128]{1,0:T(8,128)}, f32[384,128]{1,0:T(8,128)}, u32[]{:S(2)}, u32[]{:S(2)}) collective-permute-start(f32[384,128]{1,0:T(8,128)} %get-tuple-element.52), channel_id=1, source_target_pairs={{0,64},{64,0},{128,192},{192,128},{1,65},{65,1},{129,193},{193,129... | collective-permute-start | bytes 589832 | tf_op jit(solution)/shard_map/ppermute | solution.py:255
  223.2 16.3 %collective-permute-start.27 = (f32[384,128]{1,0:T(8,128)}, f32[384,128]{1,0:T(8,128)}, u32[]{:S(2)}, u32[]{:S(2)}) collective-permute-start(f32[384,128]{1,0:T(8,128)} %get-tuple-element.53), channel_id=1, source_target_pairs={{0,128},{64,192},{128,0},{192,64},{1,129},{65,193},{129,1},{193,65... | collective-permute-start | bytes 589832 | tf_op jit(solution)/shard_map/ppermute | solution.py:255
  225.0 14.5 %collective-permute-start.28 = (f32[384,128]{1,0:T(8,128)}, f32[384,128]{1,0:T(8,128)}, u32[]{:S(2)}, u32[]{:S(2)}) collective-permute-start(f32[384,128]{1,0:T(8,128)} %get-tuple-element.54), channel_id=1, source_target_pairs={{0,192},{64,128},{128,64},{192,0},{1,193},{65,129},{129,65},{193,1... | collective-permute-start | bytes 589832 | tf_op jit(solution)/shard_map/ppermute | solution.py:255
  236.2 3.4 %copy-start.9 = (f32[384,128]{1,0:T(8,128)S(1)}, f32[384,128]{1,0:T(8,128)}, u32[]{:S(2)}) copy-start(f32[384,128]{1,0:T(8,128)} %copy-done.8) | copy-start | bytes 589828
  239.4 17.0 %copy-start.10 = (f32[256,128]{1,0:T(8,128)}, f32[256,128]{1,0:T(8,128)S(1)}, u32[]{:S(2)}) copy-start(f32[256,128]{1,0:T(8,128)S(1)} %get-tuple-element.60) | copy-start | bytes 393220
  239.4 17.0 %copy-start.12 = (f32[256,128]{1,0:T(8,128)}, f32[256,128]{1,0:T(8,128)S(1)}, u32[]{:S(2)}) copy-start(f32[256,128]{1,0:T(8,128)S(1)} %get-tuple-element.61) | copy-start | bytes 393220
  239.4 3.2 %collective-permute-start.25 = (f32[128,128]{1,0:T(8,128)S(1)}, f32[128,128]{1,0:T(8,128)S(1)}, u32[]{:S(2)}, u32[]{:S(2)}) collective-permute-start(f32[128,128]{1,0:T(8,128)S(1)} %get-tuple-element.49), channel_id=1, source_target_pairs={{0,64},{64,0},{128,192},{192,128},{1,65},{65,1},{129,193},{193,129... | collective-permute-start | bytes 196616 | tf_op jit(solution)/shard_map/ppermute | solution.py:255
  242.7 9.0 %collective-permute-start.31 = (f32[256,128]{1,0:T(8,128)S(1)}, f32[256,128]{1,0:T(8,128)S(1)}, u32[]{:S(2)}, u32[]{:S(2)}) collective-permute-start(f32[256,128]{1,0:T(8,128)S(1)} %pad_maximum_fusion.2.refs_0_), channel_id=1, source_target_pairs={{0,48},{16,32},{32,16},{48,0},{1,49},{17,33},{33,17},{49,1},{2,50}... | collective-permute-start | bytes 393224 | tf_op jit(solution)/shard_map/ppermute | solution.py:255
  248.2 6.9 %collective-permute-start.30 = (f32[256,128]{1,0:T(8,128)S(1)}, f32[256,128]{1,0:T(8,128)S(1)}, u32[]{:S(2)}, u32[]{:S(2)}) collective-permute-start(f32[256,128]{1,0:T(8,128)S(1)} %pad_maximum_fusion.2.refs_0_), channel_id=1, source_target_pairs={{0,32},{16,48},{32,0},{48,16},{1,33},{17,49},{33,1},{49,17},{2,34}... | collective-permute-start | bytes 393224 | tf_op jit(solution)/shard_map/ppermute | solution.py:255
  249.4 5.7 %collective-permute-start.29 = (f32[256,128]{1,0:T(8,128)S(1)}, f32[256,128]{1,0:T(8,128)S(1)}, u32[]{:S(2)}, u32[]{:S(2)}) collective-permute-start(f32[256,128]{1,0:T(8,128)S(1)} %pad_maximum_fusion.2.refs_0_), channel_id=1, source_target_pairs={{0,16},{16,0},{32,48},{48,32},{1,17},{17,1},{33,49},{49,33},{2,18}... | collective-permute-start | bytes 393224 | tf_op jit(solution)/shard_map/ppermute | solution.py:255
  256.4 26.2 %copy-start.13 = (f32[256,128]{1,0:T(8,128)S(1)}, f32[256,128]{1,0:T(8,128)}, u32[]{:S(2)}) copy-start(f32[256,128]{1,0:T(8,128)} %copy-done.12) | copy-start | bytes 393220
  256.4 30.1 %copy-start.11 = (f32[256,128]{1,0:T(8,128)S(1)}, f32[256,128]{1,0:T(8,128)}, u32[]{:S(2)}) copy-start(f32[256,128]{1,0:T(8,128)} %copy-done.10) | copy-start | bytes 393220
  278.1 21.2 %all-to-all-start.9 = ((f32[16,64,128]{2,1,0:T(8,128)}), f32[16,64,128]{2,1,0:T(8,128)S(1)}, u32[]{:S(2)}, u32[]{:S(2)}) async-start(f32[16,64,128]{2,1,0:T(8,128)} %fold.9), calls=%async_computation.9 | async-start | bytes 1048576 | tf_op jit(solution)/shard_map/all_to_all | solution.py:281
  282.6 3.9 %collective-permute-start.35 = (f32[256,128]{1,0:T(8,128)S(1)}, f32[256,128]{1,0:T(8,128)S(1)}, u32[]{:S(2)}, u32[]{:S(2)}) collective-permute-start(f32[256,128]{1,0:T(8,128)S(1)} %copy-done.13), channel_id=1, source_target_pairs={{0,64},{64,0},{128,192},{192,128},{1,65},{65,1},{129,193},{193,129... | collective-permute-start | bytes 393224 | tf_op jit(solution)/shard_map/ppermute | solution.py:255
  282.7 8.9 %collective-permute-start.41 = (f32[256,128]{1,0:T(8,128)S(1)}, f32[256,128]{1,0:T(8,128)S(1)}, u32[]{:S(2)}, u32[]{:S(2)}) collective-permute-start(f32[256,128]{1,0:T(8,128)S(1)} %slice.29), channel_id=1, source_target_pairs={{0,48},{16,32},{32,16},{48,0},{1,49},{17,33},{33,17},{49,1},{2,50}... | collective-permute-start | bytes 393224 | tf_op jit(solution)/shard_map/ppermute | solution.py:255
  285.6 9.8 %collective-permute-start.40 = (f32[256,128]{1,0:T(8,128)S(1)}, f32[256,128]{1,0:T(8,128)S(1)}, u32[]{:S(2)}, u32[]{:S(2)}) collective-permute-start(f32[256,128]{1,0:T(8,128)S(1)} %slice.29), channel_id=1, source_target_pairs={{0,32},{16,48},{32,0},{48,16},{1,33},{17,49},{33,1},{49,17},{2,34}... | collective-permute-start | bytes 393224 | tf_op jit(solution)/shard_map/ppermute | solution.py:255
  285.9 9.5 %collective-permute-start.39 = (f32[256,128]{1,0:T(8,128)S(1)}, f32[256,128]{1,0:T(8,128)S(1)}, u32[]{:S(2)}, u32[]{:S(2)}) collective-permute-start(f32[256,128]{1,0:T(8,128)S(1)} %slice.29), channel_id=1, source_target_pairs={{0,16},{16,0},{32,48},{48,32},{1,17},{17,1},{33,49},{49,33},{2,18}... | collective-permute-start | bytes 393224 | tf_op jit(solution)/shard_map/ppermute | solution.py:255
  286.5 19.6 %collective-permute-start.38 = (f32[256,128]{1,0:T(8,128)S(1)}, f32[256,128]{1,0:T(8,128)S(1)}, u32[]{:S(2)}, u32[]{:S(2)}) collective-permute-start(f32[256,128]{1,0:T(8,128)S(1)} %add.109), channel_id=1, source_target_pairs={{0,48},{16,32},{32,16},{48,0},{1,49},{17,33},{33,17},{49,1},{2,50}... | collective-permute-start | bytes 393224 | tf_op jit(solution)/shard_map/ppermute | solution.py:255
  290.6 15.9 %collective-permute-start.37 = (f32[256,128]{1,0:T(8,128)S(1)}, f32[256,128]{1,0:T(8,128)S(1)}, u32[]{:S(2)}, u32[]{:S(2)}) collective-permute-start(f32[256,128]{1,0:T(8,128)S(1)} %add.109), channel_id=1, source_target_pairs={{0,32},{16,48},{32,0},{48,16},{1,33},{17,49},{33,1},{49,17},{2,34}... | collective-permute-start | bytes 393224 | tf_op jit(solution)/shard_map/ppermute | solution.py:255
  291.6 14.8 %collective-permute-start.36 = (f32[256,128]{1,0:T(8,128)S(1)}, f32[256,128]{1,0:T(8,128)S(1)}, u32[]{:S(2)}, u32[]{:S(2)}) collective-permute-start(f32[256,128]{1,0:T(8,128)S(1)} %add.109), channel_id=1, source_target_pairs={{0,16},{16,0},{32,48},{48,32},{1,17},{17,1},{33,49},{49,33},{2,18}... | collective-permute-start | bytes 393224 | tf_op jit(solution)/shard_map/ppermute | solution.py:255
  301.8 8.4 %collective-permute-start.34 = (f32[256,128]{1,0:T(8,128)S(1)}, f32[256,128]{1,0:T(8,128)S(1)}, u32[]{:S(2)}, u32[]{:S(2)}) collective-permute-start(f32[256,128]{1,0:T(8,128)S(1)} %backward_kernel0.1), channel_id=1, source_target_pairs={{0,48},{16,32},{32,16},{48,0},{1,49},{17,33},{33,17},{49,1},{2,50}... | collective-permute-start | bytes 393224 | tf_op jit(solution)/shard_map/ppermute | solution.py:255
  305.9 7.0 %collective-permute-start.33 = (f32[256,128]{1,0:T(8,128)S(1)}, f32[256,128]{1,0:T(8,128)S(1)}, u32[]{:S(2)}, u32[]{:S(2)}) collective-permute-start(f32[256,128]{1,0:T(8,128)S(1)} %backward_kernel0.1), channel_id=1, source_target_pairs={{0,32},{16,48},{32,0},{48,16},{1,33},{17,49},{33,1},{49,17},{2,34}... | collective-permute-start | bytes 393224 | tf_op jit(solution)/shard_map/ppermute | solution.py:255
  306.2 6.8 %collective-permute-start.32 = (f32[256,128]{1,0:T(8,128)S(1)}, f32[256,128]{1,0:T(8,128)S(1)}, u32[]{:S(2)}, u32[]{:S(2)}) collective-permute-start(f32[256,128]{1,0:T(8,128)S(1)} %backward_kernel0.1), channel_id=1, source_target_pairs={{0,16},{16,0},{32,48},{48,32},{1,17},{17,1},{33,49},{49,33},{2,18}... | collective-permute-start | bytes 393224 | tf_op jit(solution)/shard_map/ppermute | solution.py:255
  (3 other events, 2.2 us)

commit v10 on v9

--- a/solution.py
+++ b/solution.py
@@ -38,9 +38,6 @@
     shape = (panels * C, K * len(lists))
     rows = lax.broadcasted_iota(jnp.int32, shape, 0)
     return jnp.where(rows == targets, 1.0, 0.0).astype(jnp.bfloat16)
-
-
-SLOTS_OF = {1: (0,), 2: (1, 2)}
 
 
 def piece(spans, step, diag_ref, buffer_ref, sems):
@@ -71,18 +68,14 @@
         sub = sub_ref[0] % spans
         total = None
         for m in range(spans):
-            if level == 1:
-                own = update_refs[m][...]
-            else:
-                early = update_refs[0][m * K : (m + 1) * K, :]
-                own = jnp.concatenate([early, update_refs[m + 1][...]], axis=0)
-            high, low = halves(own)
+            place = m + level - 1
+            high, low = halves(update_refs[place][...])
             pair = jnp.concatenate([high, low], axis=1)
-            term = mm(hits(seen_ref, [(m, t) for t in SLOTS_OF[level]], spans), pair)
+            term = mm(hits(seen_ref, [(m, 2 * level - 2)], spans), pair)
             total = term if total is None else total + term
         total = total[:, :N] + total[:, N:]
         for a in range(spans):
-            rhs = seen_ref[a ^ sub, (level - 1) * C : level * C, :]
+            rhs = seen_ref[a ^ sub, :C, :] if level == 1 else update_refs[0][a]
             high, low = halves(rhs - total[a * C : (a + 1) * C])
             right_ref[a] = jnp.concatenate([high, low], axis=1)
 
@@ -162,6 +155,30 @@
         out_refs[m][K:, :] = total_ref[m ^ sub_ref[0]].T
 
 
+def early_kernel(sub_ref, seen_ref, update_ref, out_ref):
+    spans = 2 ** (LEVELS - 1)
+    total = None
+    for m in range(0, spans, 2):
+        high, low = halves(update_ref[m * K : (m + 2) * K, :])
+        term = mm(hits(seen_ref, [(m, 1), (m + 1, 1)], spans), jnp.concatenate([high, low], axis=1))
+        total = term if total is None else total + term
+    total = total[:, :N] + total[:, N:]
+    for a in range(spans):
+        out_ref[a] = seen_ref[a ^ sub_ref[0], C : 2 * C, :] - total[a * C : (a + 1) * C]
+
+
+def early(sub, seen, update):
+    vmem = pl.BlockSpec(memory_space=pltpu.VMEM)
+    return pl.pallas_call(
+        early_kernel,
+        in_specs=[pl.BlockSpec(memory_space=pltpu.SMEM), vmem, vmem],
+        out_specs=vmem,
+        out_shape=jax.ShapeDtypeStruct((4, C, N), jnp.float32),
+        compiler_params=pltpu.CompilerParams(vmem_limit_bytes=16 * 2**20),
+        name="early",
+    )(sub, seen, update)
+
+
 def rest(sub, seen, total):
     vmem = pl.BlockSpec(memory_space=pltpu.VMEM)
     shape = jax.ShapeDtypeStruct((K + C, N), jnp.float32)
@@ -323,7 +340,7 @@
     part1 = forward(1, sub, seen, [u01, swapped(u01, "sub", 1)], diag)
     part1, u02 = lax.optimization_barrier((part1, update(1, y0)))
     y1, u02 = col_sum(part1, row_sum(u02))
-    y1, u02 = lax.optimization_barrier((y1, jnp.concatenate(sub_parts(u02))))
+    y1, u02 = lax.optimization_barrier((y1, early(sub, seen, jnp.concatenate(sub_parts(u02)))))
     u12 = sub_parts(row_sum(update(2, y1)))
     (y2,) = col_sum(forward(2, sub, seen, [u02] + u12, diag))
 

time: 315 us -> 314 us (level)
  transfers between devices with their start and end apart: 48 -> 48, of which waited for: 28 -> 27; matrix products, arithmetic and copies ran while one was open for 2% -> 2% of each run, Pallas kernels for 2% -> 2%
where the time goes in v10:
time: 314 us; the launch traced here: 313 us
  waiting for transfers between devices  99.7 us (32%)
  starting transfers between devices  94.3 us (30%)
  blocking collectives  78.7 us (25%)
  Pallas kernels  24.8 us (8%)
  local copies, waits for them, and re-layouts  5.93 us (2%)
  other arithmetic  5.88 us (2%)
    ppermute x42, starting transfers between devices, swapped(): return lax.ppermute(value, axis, pairs)  60.3 us
    all_to_all x3, blocking collectives, col_sum(): lax.all_to_all(blocks, 'col', 0, 0)  59.4 us
    ppermute x42, waiting for transfers between devices, swapped(): return lax.ppermute(value, axis, pairs)  43.7 us
    all_to_all x4, waiting for transfers between devices, col_sum(): full = lax.all_to_all(own, 'col', 0, 0).reshape(part.shape)  31.9 us
    all_to_all x2, waiting for transfers between devices, col_sum(): lax.all_to_all(blocks, 'col', 0, 0)  24.1 us
    all_to_all x1, blocking collectives, col_sum(): full = lax.all_to_all(own, 'col', 0, 0).reshape(part.shape)  19.3 us
    all_to_all x4, starting transfers between devices, col_sum(): full = lax.all_to_all(own, 'col', 0, 0).reshape(part.shape)  18.2 us
    pallas_call x6, Pallas kernels, call(): pl.pallas_call(functools.partial(kernel, level), in_specs=[pl.BlockSpec(m...  17.7 us
  transfers between devices with their start and end apart: 48, of which 27 were waited for; matrix products, arithmetic and copies ran while one was open for 2% of the time, Pallas kernels for 2%

profile of v10, /device:TPU:1, one launch (start us, length us, event | category | flops | bytes accessed | tf_op | source)
XLA Modules:
  0.0 312.9 jit_solution(7911568411822057173)
XLA Ops:
  0.0 2.8 forward_kernel0.1
  2.9 11.6 %all-to-all-start = ((f32[16,64,128]{2,1,0:T(8,128)}), f32[16,64,128]{2,1,0:T(8,128)S(1)}, u32[]{:S(2)}, u32[]{:S(2)}) async-start(f32[16,64,128]{2,1,0:T(8,128)} %bitcast.84), calls=%async_computation | async-start | bytes 1048576 | tf_op jit(solution)/shard_map/all_to_all | solution.py:297
  14.7 16.9 %all-to-all-done.parts_ref = f32[16,64,128]{2,1,0:T(8,128)S(1)} async-done(((f32[16,64,128]{2,1,0:T(8,128)}), f32[16,64,128]{2,1,0:T(8,128)S(1)}, u32[]{:S(2)}, u32[]{:S(2)}) %all-to-all-start) | async-done | bytes 524320 | tf_op jit(solution)/shard_map/all_to_all | solution.py:297
  32.5 4.7 %all-to-all-start.1 = ((f32[16,64,128]{2,1,0:T(8,128)}), f32[16,64,128]{2,1,0:T(8,128)S(1)}, u32[]{:S(2)}, u32[]{:S(2)}) async-start(f32[16,64,128]{2,1,0:T(8,128)} %fold.5), calls=%async_computation.1 | async-start | bytes 1048576 | tf_op jit(solution)/shard_map/all_to_all | solution.py:298
  37.3 2.8 collective-permute-start.2
  40.8 13.8 %all-to-all-done.1 = f32[16,64,128]{2,1,0:T(8,128)S(1)} async-done(((f32[16,64,128]{2,1,0:T(8,128)}), f32[16,64,128]{2,1,0:T(8,128)S(1)}, u32[]{:S(2)}, u32[]{:S(2)}) %all-to-all-start.1) | async-done | bytes 524320 | tf_op jit(solution)/shard_map/all_to_all | solution.py:298
  55.0 2.6 collective-permute-start.5
  57.6 1.2 collective-permute-start.4
  59.7 1.3 pad_maximum_fusion.seen_ref
  60.9 1.1 collective-permute-done.4
  62.1 1.4 collective-permute-start.6
  65.3 2.3 forward_kernel1.1
  68.4 4.2 %all-to-all-start.2 = ((f32[16,64,128]{2,1,0:T(8,128)}), f32[16,64,128]{2,1,0:T(8,128)}, u32[]{:S(2)}, u32[]{:S(2)}) async-start(f32[16,64,128]{2,1,0:T(8,128)} %bitcast.73), calls=%async_computation.2 | async-start | bytes 1048576 | tf_op jit(solution)/shard_map/all_to_all | solution.py:297
  72.7 2.5 collective-permute-start.9
  75.7 3.2 %collective-permute-done.9 = f32[128,128]{1,0:T(8,128)S(1)} collective-permute-done((f32[128,128]{1,0:T(8,128)}, f32[128,128]{1,0:T(8,128)S(1)}, u32[]{:S(2)}, u32[]{:S(2)}) %collective-permute-start.9) | collective-permute-done | bytes 65568 | tf_op jit(solution)/shard_map/ppermute | solution.py:272
  78.9 1.8 collective-permute-done.8
  80.7 1.5 add_add_fusion.3
  82.2 7.2 %all-to-all-done.2.parts_ref = f32[16,64,128]{2,1,0:T(8,128)} async-done(((f32[16,64,128]{2,1,0:T(8,128)}), f32[16,64,128]{2,1,0:T(8,128)}, u32[]{:S(2)}, u32[]{:S(2)}) %all-to-all-start.2) | async-done | bytes 524320 | tf_op jit(solution)/shard_map/all_to_all | solution.py:297
  91.4 4.4 %all-to-all-start.3 = ((f32[16,64,128]{2,1,0:T(8,128)}), f32[16,64,128]{2,1,0:T(8,128)}, u32[]{:S(2)}, u32[]{:S(2)}) async-start(f32[16,64,128]{2,1,0:T(8,128)} %copy-done.5), calls=%async_computation.3 | async-start | bytes 1048576 | tf_op jit(solution)/shard_map/all_to_all | solution.py:298
  95.8 2.8 collective-permute-start.12
  99.3 1.6 collective-permute-done.12
  100.9 2.6 collective-permute-done.11
  105.6 5.1 %all-to-all-done.3 = f32[16,64,128]{2,1,0:T(8,128)} async-done(((f32[16,64,128]{2,1,0:T(8,128)}), f32[16,64,128]{2,1,0:T(8,128)}, u32[]{:S(2)}, u32[]{:S(2)}) %all-to-all-start.3) | async-done | bytes 524320 | tf_op jit(solution)/shard_map/all_to_all | solution.py:298
  110.7 1.5 convolution_bitcast_fusion
  112.2 5.8 %collective-permute-start.15 = (f32[128,128]{1,0:T(8,128)S(1)}, f32[128,128]{1,0:T(8,128)S(1)}, u32[]{:S(2)}, u32[]{:S(2)}) collective-permute-start(f32[128,128]{1,0:T(8,128)S(1)} %convolution_bitcast_fusion), channel_id=1, source_target_pairs={{0,48},{16,32},{32,16},{48,0},{1,49},{17,33},{33,17},{49,1},{2,50}... | collective-permute-start | bytes 196616 | tf_op jit(solution)/shard_map/ppermute | solution.py:272
  118.5 2.3 collective-permute-done.15
  120.8 1.4 collective-permute-done.14
  122.3 2.8 collective-permute-start.18
  126.8 3.0 collective-permute-done.17.refs_3_
  129.7 3.3 %forward_kernel2.1 = f32[1024,128]{1,0:T(8,128)S(1)} custom-call(s32[1]{0:T(128)} %bitcast.sub_ref, f32[4,520,128]{2,1,0:T(8,128)S(1)} %pad_maximum_fusion.seen_ref, f32[4,256,128]{2,1,0:T(8,128)S(1)} %copy-done.4, f32[128,128]{1,0:T(8,128)S(1)} %add_add_fusion.2.refs_1_, f32[128,128]{1,0:T(8,128)S(1)} %collective-permute-done.16.refs_2_, ...), custom_call_target="tpu_custom_call" | custom-call | flops 805306368 | bytes 4194304 | tf_op jit(solution)/shard_map/forward_kernel2/pallas_call | solution.py:205
  133.0 18.4 %all_to_all.50.parts_ref = f32[16,64,128]{2,1,0:T(8,128)S(1)} all-to-all(f32[16,64,128]{2,1,0:T(8,128)S(1)} %bitcast.75), channel_id=1, replica_groups=mesh['sub'=4,'row'=4,'col'=16] {'col'}, dimensions={0} | all-to-all | bytes 1048576 | tf_op jit(solution)/shard_map/all_to_all | solution.py:297
  151.5 19.3 %all_to_all.51 = f32[16,64,128]{2,1,0:T(8,128)S(1)} all-to-all(f32[16,64,128]{2,1,0:T(8,128)S(1)} %fold.7), channel_id=1, replica_groups=mesh['sub'=4,'row'=4,'col'=16] {'col'}, dimensions={0} | all-to-all | bytes 1048576 | tf_op jit(solution)/shard_map/all_to_all | solution.py:298
  170.8 3.7 %backward_kernel2.1 = (f32[128,128]{1,0:T(8,128)S(1)}, f32[128,128]{1,0:T(8,128)S(1)}, f32[128,128]{1,0:T(8,128)S(1)}, f32[128,128]{1,0:T(8,128)S(1)}, f32[4,128,256]{2,1,0:T(8,128)S(1)}) custom-call(s32[1]{0:T(128)} %bitcast.sub_ref, f32[4,520,128]{2,1,0:T(8,128)S(1)} %pad_maximum_fusion.seen_ref, f32[1024,128]{1,0:T(8,128)S(1)} %bitcast.74, ...), custom_call_target="tpu_custom_call" | custom-call | flops 805306368 | bytes 4194304 | tf_op jit(solution)/shard_map/backward_kernel2/pallas_call | solution.py:205
  174.5 3.4 %collective-permute-start.19 = (f32[128,128]{1,0:T(8,128)S(1)}, f32[128,128]{1,0:T(8,128)S(1)}, u32[]{:S(2)}, u32[]{:S(2)}) collective-permute-start(f32[128,128]{1,0:T(8,128)S(1)} %get-tuple-element.43), channel_id=1, source_target_pairs={{0,64},{64,0},{128,192},{192,128},{1,65},{65,1},{129,193},{193,129... | collective-permute-start | bytes 196616 | tf_op jit(solution)/shard_map/ppermute | solution.py:272
  177.9 1.3 collective-permute-start.20
  179.2 1.2 collective-permute-start.21
  180.4 2.1 collective-permute-done.20
  183.6 5.7 %collective-permute-start.24 = (f32[128,128]{1,0:T(8,128)S(1)}, f32[128,128]{1,0:T(8,128)S(1)}, u32[]{:S(2)}, u32[]{:S(2)}) collective-permute-start(f32[128,128]{1,0:T(8,128)S(1)} %add_add_fusion.1.refs_0_), channel_id=1, source_target_pairs={{0,48},{16,32},{32,16},{48,0},{1,49},{17,33},{33,17},{49,1},{2,50}... | collective-permute-start | bytes 196616 | tf_op jit(solution)/shard_map/ppermute | solution.py:272
  189.9 2.0 collective-permute-done.24.refs_3_
  191.9 1.4 collective-permute-done.23.refs_2_
  194.4 20.4 %all_to_all.52.parts_ref = f32[16,64,128]{2,1,0:T(8,128)S(1)} all-to-all(f32[16,64,128]{2,1,0:T(8,128)S(1)} %bitcast.77), channel_id=1, replica_groups=mesh['sub'=4,'row'=4,'col'=16] {'col'}, dimensions={0} | all-to-all | bytes 1048576 | tf_op jit(solution)/shard_map/all_to_all | solution.py:297
  215.7 4.6 %all-to-all-start.7 = ((f32[16,64,128]{2,1,0:T(8,128)}), f32[16,64,128]{2,1,0:T(8,128)}, u32[]{:S(2)}, u32[]{:S(2)}) async-start(f32[16,64,128]{2,1,0:T(8,128)} %copy-done.6), calls=%async_computation.7 | async-start | bytes 1048576 | tf_op jit(solution)/shard_map/all_to_all | solution.py:298
  221.3 1.3 rest.1
  223.3 2.0 collective-permute-start.27
  225.3 1.9 collective-permute-start.28
  227.2 9.1 %all-to-all-done.7 = f32[16,64,128]{2,1,0:T(8,128)} async-done(((f32[16,64,128]{2,1,0:T(8,128)}), f32[16,64,128]{2,1,0:T(8,128)}, u32[]{:S(2)}, u32[]{:S(2)}) %all-to-all-start.7) | async-done | bytes 524320 | tf_op jit(solution)/shard_map/all_to_all | solution.py:298
  236.3 3.2 %backward_kernel1.1 = (f32[128,128]{1,0:T(8,128)S(1)}, f32[128,128]{1,0:T(8,128)S(1)}, f32[256,128]{1,0:T(8,128)S(1)}, f32[256,128]{1,0:T(8,128)S(1)}) custom-call(s32[1]{0:T(128)} %bitcast.sub_ref, f32[4,520,128]{2,1,0:T(8,128)S(1)} %pad_maximum_fusion.seen_ref, f32[1024,128]{1,0:T(8,128)} %bitcast.17.base_ref, f32[1024,128]{1,0:T(8,128)} %bitcast.24.refs_0_, ...), custom_call_target="tpu_custom_call" | custom-call | flops 402653184 | bytes 2097152 | tf_op jit(solution)/shard_map/backward_kernel1/pallas_call | solution.py:205
  239.7 1.2 add_add_fusion
  240.9 1.9 collective-permute-done.25
  242.8 5.3 %collective-permute-start.31 = (f32[256,128]{1,0:T(8,128)S(1)}, f32[256,128]{1,0:T(8,128)S(1)}, u32[]{:S(2)}, u32[]{:S(2)}) collective-permute-start(f32[256,128]{1,0:T(8,128)S(1)} %pad_maximum_fusion.2.refs_0_), channel_id=1, source_target_pairs={{0,48},{16,32},{32,16},{48,0},{1,49},{17,33},{33,17},{49,1},{2,50}... | collective-permute-start | bytes 393224 | tf_op jit(solution)/shard_map/ppermute | solution.py:272
  248.1 1.4 collective-permute-start.30
  249.5 1.8 collective-permute-done.31.refs_3_
  251.3 3.6 %collective-permute-done.30.refs_2_ = f32[256,128]{1,0:T(8,128)S(1)} collective-permute-done((f32[256,128]{1,0:T(8,128)S(1)}, f32[256,128]{1,0:T(8,128)S(1)}, u32[]{:S(2)}, u32[]{:S(2)}) %collective-permute-start.30) | collective-permute-done | bytes 131104 | tf_op jit(solution)/shard_map/ppermute | solution.py:272
  254.9 1.3 correct2.1
  256.3 20.6 %all_to_all.53.parts_ref = f32[16,64,128]{2,1,0:T(8,128)S(1)} all-to-all(f32[16,64,128]{2,1,0:T(8,128)S(1)} %bitcast.76), channel_id=1, replica_groups=mesh['sub'=4,'row'=4,'col'=16] {'col'}, dimensions={0} | all-to-all | bytes 1048576 | tf_op jit(solution)/shard_map/all_to_all | solution.py:297
  277.8 4.5 %all-to-all-start.9 = ((f32[16,64,128]{2,1,0:T(8,128)}), f32[16,64,128]{2,1,0:T(8,128)S(1)}, u32[]{:S(2)}, u32[]{:S(2)}) async-start(f32[16,64,128]{2,1,0:T(8,128)} %fold.9), calls=%async_computation.9 | async-start | bytes 1048576 | tf_op jit(solution)/shard_map/all_to_all | solution.py:298
  282.4 2.5 collective-permute-start.41
  286.2 3.7 %collective-permute-start.38 = (f32[256,128]{1,0:T(8,128)S(1)}, f32[256,128]{1,0:T(8,128)S(1)}, u32[]{:S(2)}, u32[]{:S(2)}) collective-permute-start(f32[256,128]{1,0:T(8,128)S(1)} %add.109), channel_id=1, source_target_pairs={{0,48},{16,32},{32,16},{48,0},{1,49},{17,33},{33,17},{49,1},{2,50}... | collective-permute-start | bytes 393224 | tf_op jit(solution)/shard_map/ppermute | solution.py:272
  290.9 4.2 %collective-permute-done.40 = f32[256,128]{1,0:T(8,128)S(1)} collective-permute-done((f32[256,128]{1,0:T(8,128)S(1)}, f32[256,128]{1,0:T(8,128)S(1)}, u32[]{:S(2)}, u32[]{:S(2)}) %collective-permute-start.40) | collective-permute-done | bytes 131104 | tf_op jit(solution)/shard_map/ppermute | solution.py:272
  295.2 3.9 %all-to-all-done.9 = f32[16,64,128]{2,1,0:T(8,128)S(1)} async-done(((f32[16,64,128]{2,1,0:T(8,128)}), f32[16,64,128]{2,1,0:T(8,128)S(1)}, u32[]{:S(2)}, u32[]{:S(2)}) %all-to-all-start.9) | async-done | bytes 524320 | tf_op jit(solution)/shard_map/all_to_all | solution.py:298
  299.0 2.4 backward_kernel0.1
  301.5 3.7 %collective-permute-start.34 = (f32[256,128]{1,0:T(8,128)S(1)}, f32[256,128]{1,0:T(8,128)S(1)}, u32[]{:S(2)}, u32[]{:S(2)}) collective-permute-start(f32[256,128]{1,0:T(8,128)S(1)} %backward_kernel0.1), channel_id=1, source_target_pairs={{0,48},{16,32},{32,16},{48,0},{1,49},{17,33},{33,17},{49,1},{2,50}... | collective-permute-start | bytes 393224 | tf_op jit(solution)/shard_map/ppermute | solution.py:272
  305.9 3.2 %collective-permute-done.34 = f32[256,128]{1,0:T(8,128)S(1)} collective-permute-done((f32[256,128]{1,0:T(8,128)S(1)}, f32[256,128]{1,0:T(8,128)S(1)}, u32[]{:S(2)}, u32[]{:S(2)}) %collective-permute-start.34) | collective-permute-done | bytes 131104 | tf_op jit(solution)/shard_map/ppermute | solution.py:272
  309.1 2.9 collective-permute-done.33
  (115 shorter events, 23.4 us)
Async XLA Ops:
  0.0 14.4 %copy-start.1 = (f32[3,1,256,128]{3,2,1,0:T(8,128)S(1)}, f32[3,1,256,128]{3,2,1,0:T(8,128)}, u32[]{:S(2)}) copy-start(f32[3,1,256,128]{3,2,1,0:T(8,128)} %param.4) | copy-start | bytes 1179652
  2.8 11.7 %copy-start.19 = (s32[3,1,128]{2,1,0:T(1,128)S(1)}, s32[3,1,128]{2,1,0:T(1,128)}, u32[]{:S(2)}) copy-start(s32[3,1,128]{2,1,0:T(1,128)} %param.7) | copy-start | bytes 4612
  2.9 28.8 %all-to-all-start = ((f32[16,64,128]{2,1,0:T(8,128)}), f32[16,64,128]{2,1,0:T(8,128)S(1)}, u32[]{:S(2)}, u32[]{:S(2)}) async-start(f32[16,64,128]{2,1,0:T(8,128)} %bitcast.84), calls=%async_computation | async-start | bytes 1048576 | tf_op jit(solution)/shard_map/all_to_all | solution.py:297
  14.4 40.1 %copy-start = (f32[3,1,128,1024]{3,2,1,0:T(8,128)S(1)}, f32[3,1,128,1024]{3,2,1,0:T(8,128)}, u32[]{:S(2)}) copy-start(f32[3,1,128,1024]{3,2,1,0:T(8,128)} %param.6) | copy-start | bytes 4718596
  14.7 40.2 %copy-start.15 = (f32[520,128]{1,0:T(8,128)}, f32[520,128]{1,0:T(8,128)S(1)}, u32[]{:S(2)}) copy-start(f32[520,128]{1,0:T(8,128)S(1)} %maximum_maximum_fusion) | copy-start | bytes 798724
  32.5 22.0 %all-to-all-start.1 = ((f32[16,64,128]{2,1,0:T(8,128)}), f32[16,64,128]{2,1,0:T(8,128)S(1)}, u32[]{:S(2)}, u32[]{:S(2)}) async-start(f32[16,64,128]{2,1,0:T(8,128)} %fold.5), calls=%async_computation.1 | async-start | bytes 1048576 | tf_op jit(solution)/shard_map/all_to_all | solution.py:298
  37.3 21.5 %collective-permute-start.2 = (f32[520,128]{1,0:T(8,128)S(1)}, f32[520,128]{1,0:T(8,128)S(1)}, u32[]{:S(2)}, u32[]{:S(2)}) collective-permute-start(f32[520,128]{1,0:T(8,128)S(1)} %maximum_maximum_fusion), channel_id=1, source_target_pairs={{0,192},{64,128},{128,64},{192,0},{1,193},{65,129},{129,65},{193,1... | collective-permute-start | bytes 798728 | tf_op jit(solution)/shard_map/ppermute | solution.py:272
  40.1 18.7 %collective-permute-start.1 = (f32[520,128]{1,0:T(8,128)S(1)}, f32[520,128]{1,0:T(8,128)S(1)}, u32[]{:S(2)}, u32[]{:S(2)}) collective-permute-start(f32[520,128]{1,0:T(8,128)S(1)} %maximum_maximum_fusion), channel_id=1, source_target_pairs={{0,128},{64,192},{128,0},{192,64},{1,129},{65,193},{129,1},{193,65... | collective-permute-start | bytes 798728 | tf_op jit(solution)/shard_map/ppermute | solution.py:272
  40.4 18.4 %collective-permute-start = (f32[520,128]{1,0:T(8,128)S(1)}, f32[520,128]{1,0:T(8,128)S(1)}, u32[]{:S(2)}, u32[]{:S(2)}) collective-permute-start(f32[520,128]{1,0:T(8,128)S(1)} %maximum_maximum_fusion), channel_id=1, source_target_pairs={{0,64},{64,0},{128,192},{192,128},{1,65},{65,1},{129,193},{193,129... | collective-permute-start | bytes 798728 | tf_op jit(solution)/shard_map/ppermute | solution.py:272
  55.0 6.0 %collective-permute-start.5 = (f32[128,128]{1,0:T(8,128)S(1)}, f32[128,128]{1,0:T(8,128)S(1)}, u32[]{:S(2)}, u32[]{:S(2)}) collective-permute-start(f32[128,128]{1,0:T(8,128)S(1)} %convolution_bitcast_fusion.2), channel_id=1, source_target_pairs={{0,48},{16,32},{32,16},{48,0},{1,49},{17,33},{33,17},{49,1},{2,50}... | collective-permute-start | bytes 196616 | tf_op jit(solution)/shard_map/ppermute | solution.py:272
  57.6 4.5 %collective-permute-start.4 = (f32[128,128]{1,0:T(8,128)S(1)}, f32[128,128]{1,0:T(8,128)S(1)}, u32[]{:S(2)}, u32[]{:S(2)}) collective-permute-start(f32[128,128]{1,0:T(8,128)S(1)} %convolution_bitcast_fusion.2), channel_id=1, source_target_pairs={{0,32},{16,48},{32,0},{48,16},{1,33},{17,49},{33,1},{49,17},{2,34}... | collective-permute-start | bytes 196616 | tf_op jit(solution)/shard_map/ppermute | solution.py:272
  58.8 3.3 %collective-permute-start.3 = (f32[128,128]{1,0:T(8,128)S(1)}, f32[128,128]{1,0:T(8,128)S(1)}, u32[]{:S(2)}, u32[]{:S(2)}) collective-permute-start(f32[128,128]{1,0:T(8,128)S(1)} %convolution_bitcast_fusion.2), channel_id=1, source_target_pairs={{0,16},{16,0},{32,48},{48,32},{1,17},{17,1},{33,49},{49,33},{2,18}... | collective-permute-start | bytes 196616 | tf_op jit(solution)/shard_map/ppermute | solution.py:272
  58.8 0.9 copy-start.18
  62.1 3.2 %collective-permute-start.6 = (f32[128,128]{1,0:T(8,128)S(1)}, f32[128,128]{1,0:T(8,128)S(1)}, u32[]{:S(2)}, u32[]{:S(2)}) collective-permute-start(f32[128,128]{1,0:T(8,128)S(1)} %add_add_fusion.4.refs_0_), channel_id=1, source_target_pairs={{0,64},{64,0},{128,192},{192,128},{1,65},{65,1},{129,193},{193,129... | collective-permute-start | bytes 196616 | tf_op jit(solution)/shard_map/ppermute | solution.py:272
  68.4 21.0 %all-to-all-start.2 = ((f32[16,64,128]{2,1,0:T(8,128)}), f32[16,64,128]{2,1,0:T(8,128)}, u32[]{:S(2)}, u32[]{:S(2)}) async-start(f32[16,64,128]{2,1,0:T(8,128)} %bitcast.73), calls=%async_computation.2 | async-start | bytes 1048576 | tf_op jit(solution)/shard_map/all_to_all | solution.py:297
  72.7 6.2 %collective-permute-start.9 = (f32[128,128]{1,0:T(8,128)}, f32[128,128]{1,0:T(8,128)S(1)}, u32[]{:S(2)}, u32[]{:S(2)}) collective-permute-start(f32[128,128]{1,0:T(8,128)} %convolution_bitcast_fusion.1), channel_id=1, source_target_pairs={{0,48},{16,32},{32,16},{48,0},{1,49},{17,33},{33,17},{49,1},{2,50}... | collective-permute-start | bytes 196616 | tf_op jit(solution)/shard_map/ppermute | solution.py:272
  75.2 5.6 %collective-permute-start.8 = (f32[128,128]{1,0:T(8,128)}, f32[128,128]{1,0:T(8,128)S(1)}, u32[]{:S(2)}, u32[]{:S(2)}) collective-permute-start(f32[128,128]{1,0:T(8,128)} %convolution_bitcast_fusion.1), channel_id=1, source_target_pairs={{0,32},{16,48},{32,0},{48,16},{1,33},{17,49},{33,1},{49,17},{2,34}... | collective-permute-start | bytes 196616 | tf_op jit(solution)/shard_map/ppermute | solution.py:272
  75.6 5.1 %collective-permute-start.7 = (f32[128,128]{1,0:T(8,128)}, f32[128,128]{1,0:T(8,128)S(1)}, u32[]{:S(2)}, u32[]{:S(2)}) collective-permute-start(f32[128,128]{1,0:T(8,128)} %convolution_bitcast_fusion.1), channel_id=1, source_target_pairs={{0,16},{16,0},{32,48},{48,32},{1,17},{17,1},{33,49},{49,33},{2,18}... | collective-permute-start | bytes 196616 | tf_op jit(solution)/shard_map/ppermute | solution.py:272
  90.6 0.8 copy-start.5
  91.4 19.3 %all-to-all-start.3 = ((f32[16,64,128]{2,1,0:T(8,128)}), f32[16,64,128]{2,1,0:T(8,128)}, u32[]{:S(2)}, u32[]{:S(2)}) async-start(f32[16,64,128]{2,1,0:T(8,128)} %copy-done.5), calls=%async_computation.3 | async-start | bytes 1048576 | tf_op jit(solution)/shard_map/all_to_all | solution.py:298
  95.8 5.1 %collective-permute-start.12 = (f32[128,128]{1,0:T(8,128)}, f32[128,128]{1,0:T(8,128)S(1)}, u32[]{:S(2)}, u32[]{:S(2)}) collective-permute-start(f32[128,128]{1,0:T(8,128)} %add_add_fusion.3), channel_id=1, source_target_pairs={{0,192},{64,128},{128,64},{192,0},{1,193},{65,129},{129,65},{193,1... | collective-permute-start | bytes 196616 | tf_op jit(solution)/shard_map/ppermute | solution.py:272
  98.6 4.8 %collective-permute-start.11 = (f32[128,128]{1,0:T(8,128)}, f32[128,128]{1,0:T(8,128)S(1)}, u32[]{:S(2)}, u32[]{:S(2)}) collective-permute-start(f32[128,128]{1,0:T(8,128)} %add_add_fusion.3), channel_id=1, source_target_pairs={{0,128},{64,192},{128,0},{192,64},{1,129},{65,193},{129,1},{193,65... | collective-permute-start | bytes 196616 | tf_op jit(solution)/shard_map/ppermute | solution.py:272
  99.0 4.5 %collective-permute-start.10 = (f32[128,128]{1,0:T(8,128)}, f32[128,128]{1,0:T(8,128)S(1)}, u32[]{:S(2)}, u32[]{:S(2)}) collective-permute-start(f32[128,128]{1,0:T(8,128)} %add_add_fusion.3), channel_id=1, source_target_pairs={{0,64},{64,0},{128,192},{192,128},{1,65},{65,1},{129,193},{193,129... | collective-permute-start | bytes 196616 | tf_op jit(solution)/shard_map/ppermute | solution.py:272
  104.8 0.8 copy-start.3
  110.7 19.0 %copy-start.4 = (f32[4,256,128]{2,1,0:T(8,128)S(1)}, f32[4,256,128]{2,1,0:T(8,128)}, u32[]{:S(2)}) copy-start(f32[4,256,128]{2,1,0:T(8,128)} %copy-done.3) | copy-start | bytes 1572868
  112.2 8.6 %collective-permute-start.15 = (f32[128,128]{1,0:T(8,128)S(1)}, f32[128,128]{1,0:T(8,128)S(1)}, u32[]{:S(2)}, u32[]{:S(2)}) collective-permute-start(f32[128,128]{1,0:T(8,128)S(1)} %convolution_bitcast_fusion), channel_id=1, source_target_pairs={{0,48},{16,32},{32,16},{48,0},{1,49},{17,33},{33,17},{49,1},{2,50}... | collective-permute-start | bytes 196616 | tf_op jit(solution)/shard_map/ppermute | solution.py:272
  118.0 4.2 %collective-permute-start.14 = (f32[128,128]{1,0:T(8,128)S(1)}, f32[128,128]{1,0:T(8,128)S(1)}, u32[]{:S(2)}, u32[]{:S(2)}) collective-permute-start(f32[128,128]{1,0:T(8,128)S(1)} %convolution_bitcast_fusion), channel_id=1, source_target_pairs={{0,32},{16,48},{32,0},{48,16},{1,33},{17,49},{33,1},{49,17},{2,34}... | collective-permute-start | bytes 196616 | tf_op jit(solution)/shard_map/ppermute | solution.py:272
  118.5 3.7 %collective-permute-start.13 = (f32[128,128]{1,0:T(8,128)S(1)}, f32[128,128]{1,0:T(8,128)S(1)}, u32[]{:S(2)}, u32[]{:S(2)}) collective-permute-start(f32[128,128]{1,0:T(8,128)S(1)} %convolution_bitcast_fusion), channel_id=1, source_target_pairs={{0,16},{16,0},{32,48},{48,32},{1,17},{17,1},{33,49},{49,33},{2,18}... | collective-permute-start | bytes 196616 | tf_op jit(solution)/shard_map/ppermute | solution.py:272
  122.3 4.5 %collective-permute-start.18 = (f32[128,128]{1,0:T(8,128)S(1)}, f32[128,128]{1,0:T(8,128)S(1)}, u32[]{:S(2)}, u32[]{:S(2)}) collective-permute-start(f32[128,128]{1,0:T(8,128)S(1)} %add_add_fusion.2.refs_1_), channel_id=1, source_target_pairs={{0,192},{64,128},{128,64},{192,0},{1,193},{65,129},{129,65},{193,1... | collective-permute-start | bytes 196616 | tf_op jit(solution)/shard_map/ppermute | solution.py:272
  125.1 4.6 %collective-permute-start.17 = (f32[128,128]{1,0:T(8,128)S(1)}, f32[128,128]{1,0:T(8,128)S(1)}, u32[]{:S(2)}, u32[]{:S(2)}) collective-permute-start(f32[128,128]{1,0:T(8,128)S(1)} %add_add_fusion.2.refs_1_), channel_id=1, source_target_pairs={{0,128},{64,192},{128,0},{192,64},{1,129},{65,193},{129,1},{193,65... | collective-permute-start | bytes 196616 | tf_op jit(solution)/shard_map/ppermute | solution.py:272
  125.5 4.3 %collective-permute-start.16 = (f32[128,128]{1,0:T(8,128)S(1)}, f32[128,128]{1,0:T(8,128)S(1)}, u32[]{:S(2)}, u32[]{:S(2)}) collective-permute-start(f32[128,128]{1,0:T(8,128)S(1)} %add_add_fusion.2.refs_1_), channel_id=1, source_target_pairs={{0,64},{64,0},{128,192},{192,128},{1,65},{65,1},{129,193},{193,129... | collective-permute-start | bytes 196616 | tf_op jit(solution)/shard_map/ppermute | solution.py:272
  174.5 40.3 %copy-start.7 = (f32[4,128,256]{2,1,0:T(8,128)}, f32[4,128,256]{2,1,0:T(8,128)S(1)}, u32[]{:S(2)}) copy-start(f32[4,128,256]{2,1,0:T(8,128)S(1)} %get-tuple-element.50.total_ref) | copy-start | bytes 1572868
  174.5 5.9 %collective-permute-start.19 = (f32[128,128]{1,0:T(8,128)S(1)}, f32[128,128]{1,0:T(8,128)S(1)}, u32[]{:S(2)}, u32[]{:S(2)}) collective-permute-start(f32[128,128]{1,0:T(8,128)S(1)} %get-tuple-element.43), channel_id=1, source_target_pairs={{0,64},{64,0},{128,192},{192,128},{1,65},{65,1},{129,193},{193,129... | collective-permute-start | bytes 196616 | tf_op jit(solution)/shard_map/ppermute | solution.py:272
  177.9 4.6 %collective-permute-start.20 = (f32[128,128]{1,0:T(8,128)S(1)}, f32[128,128]{1,0:T(8,128)S(1)}, u32[]{:S(2)}, u32[]{:S(2)}) collective-permute-start(f32[128,128]{1,0:T(8,128)S(1)} %get-tuple-element.44), channel_id=1, source_target_pairs={{0,128},{64,192},{128,0},{192,64},{1,129},{65,193},{129,1},{193,65... | collective-permute-start | bytes 196616 | tf_op jit(solution)/shard_map/ppermute | solution.py:272
  179.2 4.3 %collective-permute-start.21 = (f32[128,128]{1,0:T(8,128)S(1)}, f32[128,128]{1,0:T(8,128)S(1)}, u32[]{:S(2)}, u32[]{:S(2)}) collective-permute-start(f32[128,128]{1,0:T(8,128)S(1)} %get-tuple-element.45), channel_id=1, source_target_pairs={{0,192},{64,128},{128,64},{192,0},{1,193},{65,129},{129,65},{193,1... | collective-permute-start | bytes 196616 | tf_op jit(solution)/shard_map/ppermute | solution.py:272
  183.6 8.3 %collective-permute-start.24 = (f32[128,128]{1,0:T(8,128)S(1)}, f32[128,128]{1,0:T(8,128)S(1)}, u32[]{:S(2)}, u32[]{:S(2)}) collective-permute-start(f32[128,128]{1,0:T(8,128)S(1)} %add_add_fusion.1.refs_0_), channel_id=1, source_target_pairs={{0,48},{16,32},{32,16},{48,0},{1,49},{17,33},{33,17},{49,1},{2,50}... | collective-permute-start | bytes 196616 | tf_op jit(solution)/shard_map/ppermute | solution.py:272
  189.3 4.1 %collective-permute-start.23 = (f32[128,128]{1,0:T(8,128)S(1)}, f32[128,128]{1,0:T(8,128)S(1)}, u32[]{:S(2)}, u32[]{:S(2)}) collective-permute-start(f32[128,128]{1,0:T(8,128)S(1)} %add_add_fusion.1.refs_0_), channel_id=1, source_target_pairs={{0,32},{16,48},{32,0},{48,16},{1,33},{17,49},{33,1},{49,17},{2,34}... | collective-permute-start | bytes 196616 | tf_op jit(solution)/shard_map/ppermute | solution.py:272
  189.9 3.5 %collective-permute-start.22 = (f32[128,128]{1,0:T(8,128)S(1)}, f32[128,128]{1,0:T(8,128)S(1)}, u32[]{:S(2)}, u32[]{:S(2)}) collective-permute-start(f32[128,128]{1,0:T(8,128)S(1)} %add_add_fusion.1.refs_0_), channel_id=1, source_target_pairs={{0,16},{16,0},{32,48},{48,32},{1,17},{17,1},{33,49},{49,33},{2,18}... | collective-permute-start | bytes 196616 | tf_op jit(solution)/shard_map/ppermute | solution.py:272
  214.9 0.8 copy-start.6
  215.7 20.6 %all-to-all-start.7 = ((f32[16,64,128]{2,1,0:T(8,128)}), f32[16,64,128]{2,1,0:T(8,128)}, u32[]{:S(2)}, u32[]{:S(2)}) async-start(f32[16,64,128]{2,1,0:T(8,128)} %copy-done.6), calls=%async_computation.7 | async-start | bytes 1048576 | tf_op jit(solution)/shard_map/all_to_all | solution.py:298
  220.3 1.0 copy-start.8
  223.3 16.3 %collective-permute-start.26 = (f32[384,128]{1,0:T(8,128)}, f32[384,128]{1,0:T(8,128)}, u32[]{:S(2)}, u32[]{:S(2)}) collective-permute-start(f32[384,128]{1,0:T(8,128)} %get-tuple-element.52), channel_id=1, source_target_pairs={{0,64},{64,0},{128,192},{192,128},{1,65},{65,1},{129,193},{193,129... | collective-permute-start | bytes 589832 | tf_op jit(solution)/shard_map/ppermute | solution.py:272
  223.3 16.3 %collective-permute-start.27 = (f32[384,128]{1,0:T(8,128)}, f32[384,128]{1,0:T(8,128)}, u32[]{:S(2)}, u32[]{:S(2)}) collective-permute-start(f32[384,128]{1,0:T(8,128)} %get-tuple-element.53), channel_id=1, source_target_pairs={{0,128},{64,192},{128,0},{192,64},{1,129},{65,193},{129,1},{193,65... | collective-permute-start | bytes 589832 | tf_op jit(solution)/shard_map/ppermute | solution.py:272
  225.3 14.3 %collective-permute-start.28 = (f32[384,128]{1,0:T(8,128)}, f32[384,128]{1,0:T(8,128)}, u32[]{:S(2)}, u32[]{:S(2)}) collective-permute-start(f32[384,128]{1,0:T(8,128)} %get-tuple-element.54), channel_id=1, source_target_pairs={{0,192},{64,128},{128,64},{192,0},{1,193},{65,129},{129,65},{193,1... | collective-permute-start | bytes 589832 | tf_op jit(solution)/shard_map/ppermute | solution.py:272
  236.3 3.4 %copy-start.10 = (f32[384,128]{1,0:T(8,128)S(1)}, f32[384,128]{1,0:T(8,128)}, u32[]{:S(2)}) copy-start(f32[384,128]{1,0:T(8,128)} %copy-done.9) | copy-start | bytes 589828
  239.5 16.7 %copy-start.11 = (f32[256,128]{1,0:T(8,128)}, f32[256,128]{1,0:T(8,128)S(1)}, u32[]{:S(2)}) copy-start(f32[256,128]{1,0:T(8,128)S(1)} %get-tuple-element.60) | copy-start | bytes 393220
  239.5 16.7 %copy-start.13 = (f32[256,128]{1,0:T(8,128)}, f32[256,128]{1,0:T(8,128)S(1)}, u32[]{:S(2)}) copy-start(f32[256,128]{1,0:T(8,128)S(1)} %get-tuple-element.61) | copy-start | bytes 393220
  239.5 3.2 %collective-permute-start.25 = (f32[128,128]{1,0:T(8,128)S(1)}, f32[128,128]{1,0:T(8,128)S(1)}, u32[]{:S(2)}, u32[]{:S(2)}) collective-permute-start(f32[128,128]{1,0:T(8,128)S(1)} %get-tuple-element.49), channel_id=1, source_target_pairs={{0,64},{64,0},{128,192},{192,128},{1,65},{65,1},{129,193},{193,129... | collective-permute-start | bytes 196616 | tf_op jit(solution)/shard_map/ppermute | solution.py:272
  242.8 8.5 %collective-permute-start.31 = (f32[256,128]{1,0:T(8,128)S(1)}, f32[256,128]{1,0:T(8,128)S(1)}, u32[]{:S(2)}, u32[]{:S(2)}) collective-permute-start(f32[256,128]{1,0:T(8,128)S(1)} %pad_maximum_fusion.2.refs_0_), channel_id=1, source_target_pairs={{0,48},{16,32},{32,16},{48,0},{1,49},{17,33},{33,17},{49,1},{2,50}... | collective-permute-start | bytes 393224 | tf_op jit(solution)/shard_map/ppermute | solution.py:272
  248.1 6.9 %collective-permute-start.30 = (f32[256,128]{1,0:T(8,128)S(1)}, f32[256,128]{1,0:T(8,128)S(1)}, u32[]{:S(2)}, u32[]{:S(2)}) collective-permute-start(f32[256,128]{1,0:T(8,128)S(1)} %pad_maximum_fusion.2.refs_0_), channel_id=1, source_target_pairs={{0,32},{16,48},{32,0},{48,16},{1,33},{17,49},{33,1},{49,17},{2,34}... | collective-permute-start | bytes 393224 | tf_op jit(solution)/shard_map/ppermute | solution.py:272
  249.5 5.5 %collective-permute-start.29 = (f32[256,128]{1,0:T(8,128)S(1)}, f32[256,128]{1,0:T(8,128)S(1)}, u32[]{:S(2)}, u32[]{:S(2)}) collective-permute-start(f32[256,128]{1,0:T(8,128)S(1)} %pad_maximum_fusion.2.refs_0_), channel_id=1, source_target_pairs={{0,16},{16,0},{32,48},{48,32},{1,17},{17,1},{33,49},{49,33},{2,18}... | collective-permute-start | bytes 393224 | tf_op jit(solution)/shard_map/ppermute | solution.py:272
  256.3 26.0 %copy-start.14 = (f32[256,128]{1,0:T(8,128)S(1)}, f32[256,128]{1,0:T(8,128)}, u32[]{:S(2)}) copy-start(f32[256,128]{1,0:T(8,128)} %copy-done.13) | copy-start | bytes 393220
  256.3 29.9 %copy-start.12 = (f32[256,128]{1,0:T(8,128)S(1)}, f32[256,128]{1,0:T(8,128)}, u32[]{:S(2)}) copy-start(f32[256,128]{1,0:T(8,128)} %copy-done.11) | copy-start | bytes 393220
  277.8 21.2 %all-to-all-start.9 = ((f32[16,64,128]{2,1,0:T(8,128)}), f32[16,64,128]{2,1,0:T(8,128)S(1)}, u32[]{:S(2)}, u32[]{:S(2)}) async-start(f32[16,64,128]{2,1,0:T(8,128)} %fold.9), calls=%async_computation.9 | async-start | bytes 1048576 | tf_op jit(solution)/shard_map/all_to_all | solution.py:298
  282.3 3.9 %collective-permute-start.35 = (f32[256,128]{1,0:T(8,128)S(1)}, f32[256,128]{1,0:T(8,128)S(1)}, u32[]{:S(2)}, u32[]{:S(2)}) collective-permute-start(f32[256,128]{1,0:T(8,128)S(1)} %copy-done.14), channel_id=1, source_target_pairs={{0,64},{64,0},{128,192},{192,128},{1,65},{65,1},{129,193},{193,129... | collective-permute-start | bytes 393224 | tf_op jit(solution)/shard_map/ppermute | solution.py:272
  282.4 8.2 %collective-permute-start.41 = (f32[256,128]{1,0:T(8,128)S(1)}, f32[256,128]{1,0:T(8,128)S(1)}, u32[]{:S(2)}, u32[]{:S(2)}) collective-permute-start(f32[256,128]{1,0:T(8,128)S(1)} %slice.29), channel_id=1, source_target_pairs={{0,48},{16,32},{32,16},{48,0},{1,49},{17,33},{33,17},{49,1},{2,50}... | collective-permute-start | bytes 393224 | tf_op jit(solution)/shard_map/ppermute | solution.py:272
  284.9 10.2 %collective-permute-start.40 = (f32[256,128]{1,0:T(8,128)S(1)}, f32[256,128]{1,0:T(8,128)S(1)}, u32[]{:S(2)}, u32[]{:S(2)}) collective-permute-start(f32[256,128]{1,0:T(8,128)S(1)} %slice.29), channel_id=1, source_target_pairs={{0,32},{16,48},{32,0},{48,16},{1,33},{17,49},{33,1},{49,17},{2,34}... | collective-permute-start | bytes 393224 | tf_op jit(solution)/shard_map/ppermute | solution.py:272
  285.6 9.6 %collective-permute-start.39 = (f32[256,128]{1,0:T(8,128)S(1)}, f32[256,128]{1,0:T(8,128)S(1)}, u32[]{:S(2)}, u32[]{:S(2)}) collective-permute-start(f32[256,128]{1,0:T(8,128)S(1)} %slice.29), channel_id=1, source_target_pairs={{0,16},{16,0},{32,48},{48,32},{1,17},{17,1},{33,49},{49,33},{2,18}... | collective-permute-start | bytes 393224 | tf_op jit(solution)/shard_map/ppermute | solution.py:272
  286.2 19.6 %collective-permute-start.38 = (f32[256,128]{1,0:T(8,128)S(1)}, f32[256,128]{1,0:T(8,128)S(1)}, u32[]{:S(2)}, u32[]{:S(2)}) collective-permute-start(f32[256,128]{1,0:T(8,128)S(1)} %add.109), channel_id=1, source_target_pairs={{0,48},{16,32},{32,16},{48,0},{1,49},{17,33},{33,17},{49,1},{2,50}... | collective-permute-start | bytes 393224 | tf_op jit(solution)/shard_map/ppermute | solution.py:272
  289.9 16.0 %collective-permute-start.37 = (f32[256,128]{1,0:T(8,128)S(1)}, f32[256,128]{1,0:T(8,128)S(1)}, u32[]{:S(2)}, u32[]{:S(2)}) collective-permute-start(f32[256,128]{1,0:T(8,128)S(1)} %add.109), channel_id=1, source_target_pairs={{0,32},{16,48},{32,0},{48,16},{1,33},{17,49},{33,1},{49,17},{2,34}... | collective-permute-start | bytes 393224 | tf_op jit(solution)/shard_map/ppermute | solution.py:272
  290.6 15.3 %collective-permute-start.36 = (f32[256,128]{1,0:T(8,128)S(1)}, f32[256,128]{1,0:T(8,128)S(1)}, u32[]{:S(2)}, u32[]{:S(2)}) collective-permute-start(f32[256,128]{1,0:T(8,128)S(1)} %add.109), channel_id=1, source_target_pairs={{0,16},{16,0},{32,48},{48,32},{1,17},{17,1},{33,49},{49,33},{2,18}... | collective-permute-start | bytes 393224 | tf_op jit(solution)/shard_map/ppermute | solution.py:272
  301.5 7.7 %collective-permute-start.34 = (f32[256,128]{1,0:T(8,128)S(1)}, f32[256,128]{1,0:T(8,128)S(1)}, u32[]{:S(2)}, u32[]{:S(2)}) collective-permute-start(f32[256,128]{1,0:T(8,128)S(1)} %backward_kernel0.1), channel_id=1, source_target_pairs={{0,48},{16,32},{32,16},{48,0},{1,49},{17,33},{33,17},{49,1},{2,50}... | collective-permute-start | bytes 393224 | tf_op jit(solution)/shard_map/ppermute | solution.py:272
  305.2 6.9 %collective-permute-start.33 = (f32[256,128]{1,0:T(8,128)S(1)}, f32[256,128]{1,0:T(8,128)S(1)}, u32[]{:S(2)}, u32[]{:S(2)}) collective-permute-start(f32[256,128]{1,0:T(8,128)S(1)} %backward_kernel0.1), channel_id=1, source_target_pairs={{0,32},{16,48},{32,0},{48,16},{1,33},{17,49},{33,1},{49,17},{2,34}... | collective-permute-start | bytes 393224 | tf_op jit(solution)/shard_map/ppermute | solution.py:272
  305.9 6.2 %collective-permute-start.32 = (f32[256,128]{1,0:T(8,128)S(1)}, f32[256,128]{1,0:T(8,128)S(1)}, u32[]{:S(2)}, u32[]{:S(2)}) collective-permute-start(f32[256,128]{1,0:T(8,128)S(1)} %backward_kernel0.1), channel_id=1, source_target_pairs={{0,16},{16,0},{32,48},{48,32},{1,17},{17,1},{33,49},{49,33},{2,18}... | collective-permute-start | bytes 393224 | tf_op jit(solution)/shard_map/ppermute | solution.py:272
  (4 other events, 3.0 us)
